TPU v7x, 256 devices: a whole 4x4x8 slice. The times are simulated.
256 devices in a mesh: radius: 16 (over z, core), polar: 4 (over x), group: 4 (over y).
Axes of the slice: x: 4, y: 4, z: 8, core: 2. Of those that a mesh axis runs over, the one named last changes fastest.
Arguments:
- density: float32 [768, 1024], P('radius', 'polar'), may hold values from 0.3 to 3
- opacity: bfloat16 [64, 768, 1024], P('group', 'radius', 'polar'), may hold values from 0.049804688 to 5
- radiation_old: float32 [64, 768, 1024], P('group', 'radius', 'polar'), may hold values from 0.5 to 2
- material_old: float32 [768, 1024], P('radius', 'polar'), may hold values from 0.5 to 2
- weights: float32 [64], P('group'), may hold values from 0.5 to 2
- stellar_flux: float32 [768], P('radius'), may hold values from 10 to 100
Outputs:
- energy: float32 [64, 768, 1024], P('group', 'radius', 'polar')
- material_now: float32 [768, 1024], P('radius', 'polar')
- column: float32 [768, 1024], P('radius', 'polar')
All inputs are finite; a program needn't handle non-finite values.
Results may differ from a plain program's by a relative error of at most 0.0003.
Values sent between devices are 32-bit elements; how exact they have to be, the bound alone decides.
No kernel may reach another device: no remote copies, remote signals or barrier semaphores. Data moves between devices by JAX's collectives and lax.ppermute only.
A program may use at most 64 MiB of HBM per device.

v0:
```python
import jax
import jax.numpy as jnp
from jax import lax
from jax.sharding import PartitionSpec as P

ITERS = 3
SWEEPS = 2


def padded_2(cells, sides, width):
    for axis, dim in sides:
        count = lax.axis_size(axis)
        ends = count - 1
        head = lax.slice_in_dim(cells, 0, width, axis=dim)
        tail = lax.slice_in_dim(cells, cells.shape[dim] - width, cells.shape[dim], axis=dim)
        cells = jnp.concatenate(
            [
                lax.ppermute(tail, axis, [(i, (i + 1) % count) for i in range(ends)]),
                cells,
                lax.ppermute(head, axis, [((i + 1) % count, i) for i in range(ends)]),
            ],
            axis=dim,
        )
    return cells


def prefix(part, axis, combine, identity):
    place = lax.axis_index(axis)
    gathered = lax.all_gather(part, axis)
    state = jnp.zeros_like(part) + jnp.asarray(identity, part.dtype)

    def one(turn, state):
        return combine(state, lax.dynamic_index_in_dim(gathered, turn, 0, False))

    return lax.fori_loop(0, place, one, state)


def harmonic(lower_value, upper_value):
    return 2.0 * lower_value * upper_value / (lower_value + upper_value)


def add_pair(earlier, following):
    return earlier + following


def apply_padded(padded, field, absorb, face_coeffs):
    return (
        (1.0 + absorb) * field
        + face_coeffs[0] * (field - padded[:, 2:, 1:-1])
        + face_coeffs[1] * (field - padded[:, :-2, 1:-1])
        + face_coeffs[2] * (field - padded[:, 1:-1, 2:])
        + face_coeffs[3] * (field - padded[:, 1:-1, :-2])
    )


def local_dot(left_field, right_field):
    return jnp.sum(left_field * right_field, axis=(1, 2))


def group_norms(residual):
    return lax.psum(local_dot(residual, residual), ("radius", "polar"))


def solve_classic(energy, residual, absorb, face_coeffs):
    norm_now = group_norms(residual)
    direction = residual
    for sweep_index in range(SWEEPS):
        padded = padded_2(direction, (("radius", 1), ("polar", 2)), 1)
        applied = apply_padded(padded, direction, absorb, face_coeffs)
        step_size = norm_now / lax.psum(local_dot(direction, applied), ("radius", "polar"))
        energy = energy + step_size[:, None, None] * direction
        residual = residual - step_size[:, None, None] * applied
        if sweep_index + 1 < SWEEPS:
            norm_next = group_norms(residual)
            direction = residual + (norm_next / norm_now)[:, None, None] * direction
            norm_now = norm_next
    return (energy, residual)


def per_device(density, opacity, radiation_old, material_old, weights, stellar_flux):
    polar_cells = density.shape[1]
    polar_total = polar_cells * lax.axis_size("polar")
    row_sums = jnp.sum(density, axis=1)
    carried = prefix(row_sums, "polar", add_pair, jnp.zeros_like(row_sums))
    upper_tri = (
        lax.broadcasted_iota(jnp.int32, (polar_cells, polar_cells), 0)
        <= lax.broadcasted_iota(jnp.int32, (polar_cells, polar_cells), 1)
    ).astype(jnp.float32)
    within = jnp.dot(
        density, upper_tri, precision=lax.Precision.HIGHEST, preferred_element_type=jnp.float32
    )
    column = 2.0 / polar_total * (carried[:, None] + within)
    heating = stellar_flux[:, None] * density * jnp.exp(-column)
    absorb = opacity.astype(jnp.float32) * density[None]
    group_weight = weights[:, None, None]
    old_padded = padded_2(radiation_old, (("radius", 1), ("polar", 2)), 1)
    radial_slope = 0.5 * (old_padded[:, 2:, 1:-1] - old_padded[:, :-2, 1:-1])
    polar_slope = 0.5 * (old_padded[:, 1:-1, 2:] - old_padded[:, 1:-1, :-2])
    ratio_value = jnp.sqrt(radial_slope * radial_slope + polar_slope * polar_slope) / (
        absorb * radiation_old
    )
    limiter = (2.0 + ratio_value) / (6.0 + 3.0 * ratio_value + ratio_value * ratio_value)
    diffusion = limiter / absorb
    coeff_padded = padded_2(diffusion, (("radius", 1), ("polar", 2)), 1)
    face_coeffs = (
        harmonic(diffusion, coeff_padded[:, 2:, 1:-1]),
        harmonic(coeff_padded[:, :-2, 1:-1], diffusion),
        harmonic(diffusion, coeff_padded[:, 1:-1, 2:]),
        harmonic(coeff_padded[:, 1:-1, :-2], diffusion),
    )
    residual = (
        absorb * group_weight * material_old[None]
        + radiation_old
        - apply_padded(old_padded, radiation_old, absorb, face_coeffs)
    )
    energy = radiation_old
    emission_local = jnp.sum(absorb * group_weight, axis=0)
    fixed_terms = 16.0 * density * material_old + heating
    capacity = 16.0 * density + lax.psum(emission_local, "group")
    material_now = material_old
    for round_index in range(ITERS):
        energy, residual = solve_classic(energy, residual, absorb, face_coeffs)
        absorbed_local = jnp.sum(absorb * energy, axis=0)
        material_next = (fixed_terms + lax.psum(absorbed_local, "group")) / capacity
        if round_index + 1 < ITERS:
            residual = residual + absorb * group_weight * (material_next - material_now)[None]
        material_now = material_next
    return (energy, material_now, column)


def solution(mesh):
    return jax.shard_map(
        per_device,
        mesh=mesh,
        in_specs=(
            P("radius", "polar"),
            P("group", "radius", "polar"),
            P("group", "radius", "polar"),
            P("radius", "polar"),
            P("group"),
            P("radius"),
        ),
        out_specs=(P("group", "radius", "polar"), P("radius", "polar"), P("radius", "polar")),
        check_vma=False,
    )
```

profile of v0, /device:TPU:8, one launch (start us, length us, event | category | flops | bytes accessed | tf_op | source)
XLA Modules:
  0.0 1479.8 jit_solution(10945650069616623366)
XLA Ops:
  9.5 3.0 collective-permute-start.1
  14.8 3.6 collective-permute-start.3
  19.7 9.0 collective-permute-done.3
  28.7 4.7 collective-permute-done.2
  34.5 2.0 collective-permute-start.5
  37.9 3.8 collective-permute-done.4
  42.0 3.4 collective-permute-start.7
  46.7 8.1 collective-permute-done.7
  54.7 4.7 collective-permute-done.6
  59.4 2.3 fusion.89
  61.8 3.0 collective-permute-start.9
  66.0 3.2 collective-permute-done.8
  70.8 4.6 collective-permute-start.11
  75.4 7.9 collective-permute-done.10
  85.1 3.0 multiply_reduce_fusion.12
  88.1 127.1 %all-reduce.3 = (f32[16]{0:T(128)}, f32[16]{0:T(128)}) all-reduce(f32[16]{0:T(128)} %get-tuple-element.32, f32[16]{0:T(128)} %get-tuple-element.31), channel_id=1, replica_groups=mesh['radius'=16,'polar'=4,'group'=4] {'radius','polar'}, use_global_device_ids=true, to_apply=%region_1.2 | all-reduce | flops 32 | bytes 256 | tf_op jit(solution)/shard_map/psum | solution.py:61
  218.4 124.7 %psum.114 = f32[16]{0:T(128)} all-reduce(f32[16]{0:T(128)} %multiply_reduce_fusion.11), channel_id=1, replica_groups=mesh['radius'=16,'polar'=4,'group'=4] {'radius','polar'}, use_global_device_ids=true, to_apply=%region_5.6 | all-reduce | flops 16 | bytes 128 | tf_op jit(solution)/shard_map/psum | solution.py:61
  352.6 5.6 collective-permute-start.15
  363.5 9.7 all-reduce
  374.5 5.7 multiply_reduce_fusion.10
  380.9 124.7 %psum.115 = f32[16]{0:T(128)S(1)} all-reduce(f32[16]{0:T(128)S(1)} %copy-done.46), channel_id=1, replica_groups=mesh['radius'=16,'polar'=4,'group'=4] {'radius','polar'}, use_global_device_ids=true, to_apply=%region_7.8 | all-reduce | flops 16 | bytes 128 | tf_op jit(solution)/shard_map/psum | solution.py:70
  506.2 3.3 fusion.100
  509.6 52.5 %all-reduce.7.cloned.1.call-done = (f32[48,256]{1,0:T(8,128)}, f32[48,256]{1,0:T(8,128)}) async-done(((f32[48,256]{1,0:T(8,128)}, f32[48,256]{1,0:T(8,128)}), (f32[48,256]{1,0:T(8,128)}, f32[48,256]{1,0:T(8,128)})) %all-reduce.7.cloned.1.call-update) | async-done | bytes 98320 | tf_op jit(solution)/shard_map/psum | solution.py:124
  569.4 3.6 collective-permute-done.16
  574.7 4.6 collective-permute-start.19
  579.3 7.9 collective-permute-done.18
  588.9 3.1 multiply_reduce_fusion.7
  592.1 127.1 %all-reduce.2 = (f32[16]{0:T(128)}, f32[16]{0:T(128)}) all-reduce(f32[16]{0:T(128)} %get-tuple-element.30, f32[16]{0:T(128)} %get-tuple-element.29), channel_id=1, replica_groups=mesh['radius'=16,'polar'=4,'group'=4] {'radius','polar'}, use_global_device_ids=true, to_apply=%region_16.17 | all-reduce | flops 32 | bytes 256 | tf_op jit(solution)/shard_map/psum | solution.py:61
  720.4 2.0 multiply_reduce_fusion.6
  722.3 124.6 %psum.120 = f32[16]{0:T(128)} all-reduce(f32[16]{0:T(128)} %multiply_reduce_fusion.6), channel_id=1, replica_groups=mesh['radius'=16,'polar'=4,'group'=4] {'radius','polar'}, use_global_device_ids=true, to_apply=%region_20.21 | all-reduce | flops 16 | bytes 128 | tf_op jit(solution)/shard_map/psum | solution.py:61
  855.0 4.8 collective-permute-start.23
  859.8 8.9 collective-permute-done.22
  869.9 2.8 multiply_reduce_fusion.5
  872.7 127.1 %psum.121 = f32[16]{0:T(128)} all-reduce(f32[16]{0:T(128)} %get-tuple-element.56), channel_id=1, replica_groups=mesh['radius'=16,'polar'=4,'group'=4] {'radius','polar'}, use_global_device_ids=true, to_apply=%region_22.23 | all-reduce | flops 16 | bytes 128 | tf_op jit(solution)/shard_map/psum | solution.py:70
  1001.1 3.2 multiply_reduce_fusion.4
  1004.2 16.2 %psum.122 = f32[48,256]{1,0:T(8,128)} all-reduce(f32[48,256]{1,0:T(8,128)} %get-tuple-element.54), channel_id=1, replica_groups=mesh['radius'=16,'polar'=4,'group'=4] {'group'}, use_global_device_ids=true, to_apply=%region_24.25 | all-reduce | flops 12288 | bytes 98304 | tf_op jit(solution)/shard_map/psum | solution.py:124
  1029.8 4.6 collective-permute-start.27
  1034.4 8.6 collective-permute-done.26
  1044.2 2.5 multiply_reduce_fusion.2
  1046.7 126.5 %all-reduce.1 = (f32[16]{0:T(128)S(1)}, f32[16]{0:T(128)S(1)}) all-reduce(f32[16]{0:T(128)S(1)} %get-tuple-element.28, f32[16]{0:T(128)S(1)} %get-tuple-element.27), channel_id=1, replica_groups=mesh['radius'=16,'polar'=4,'group'=4] {'radius','polar'}, use_global_device_ids=true, to_apply=%region_26.27 | all-reduce | flops 32 | bytes 256 | tf_op jit(solution)/shard_map/psum | solution.py:61
  1174.4 2.2 multiply_reduce_fusion.1
  1176.7 124.5 %psum.125 = f32[16]{0:T(128)} all-reduce(f32[16]{0:T(128)} %multiply_reduce_fusion.1), channel_id=1, replica_groups=mesh['radius'=16,'polar'=4,'group'=4] {'radius','polar'}, use_global_device_ids=true, to_apply=%region_30.31 | all-reduce | flops 16 | bytes 128 | tf_op jit(solution)/shard_map/psum | solution.py:61
  1309.3 4.8 collective-permute-start.31
  1314.1 8.9 collective-permute-done.30
  1324.2 2.0 fusion.6
  1326.2 126.5 %psum.126 = f32[16]{0:T(128)S(1)} all-reduce(f32[16]{0:T(128)} %fusion.6), channel_id=1, replica_groups=mesh['radius'=16,'polar'=4,'group'=4] {'radius','polar'}, use_global_device_ids=true, to_apply=%region_32.33 | all-reduce | flops 16 | bytes 128 | tf_op jit(solution)/shard_map/psum | solution.py:70
  1453.4 2.5 multiply_reduce_fusion
  1456.0 16.3 %psum.127 = f32[48,256]{1,0:T(8,128)S(1)} all-reduce(f32[48,256]{1,0:T(8,128)S(1)} %get-tuple-element.51), channel_id=1, replica_groups=mesh['radius'=16,'polar'=4,'group'=4] {'group'}, use_global_device_ids=true, to_apply=%region_34.35 | all-reduce | flops 12288 | bytes 98304 | tf_op jit(solution)/shard_map/psum | solution.py:124
  (203 shorter events, 79.1 us)
Async XLA Ops:
  7.2 554.9 %all-reduce.7.cloned.1.call-start = ((), (), s32[]{:S(2)}) async-start(), calls=%async_computation | async-start | bytes 196608 | tf_op jit(solution)/shard_map/psum | solution.py:124
  8.2 4.3 collective-permute-start
  9.5 3.9 collective-permute-start.1
  14.6 18.8 %copy-start = (bf16[16,48,256]{2,1,0:T(8,128)(2,1)S(1)}, bf16[16,48,256]{2,1,0:T(8,128)(2,1)}, u32[]{:S(2)}) copy-start(bf16[16,48,256]{2,1,0:T(8,128)(2,1)} %param.9) | copy-start | bytes 1179652
  14.6 18.7 %copy-start.5 = (f32[16,48,256]{2,1,0:T(8,128)S(1)}, f32[16,48,256]{2,1,0:T(8,128)}, u32[]{:S(2)}) copy-start(f32[16,48,256]{2,1,0:T(8,128)} %param.10) | copy-start | bytes 2359300
  14.6 18.7 %copy-start.9 = (f32[48,256]{1,0:T(8,128)S(1)}, f32[48,256]{1,0:T(8,128)}, u32[]{:S(2)}) copy-start(f32[48,256]{1,0:T(8,128)} %param.8) | copy-start | bytes 147460
  14.8 13.8 collective-permute-start.3
  18.4 15.0 %collective-permute-start.2 = (f32[16,50,1]{2,1,0:T(8,128)S(1)}, f32[16,50,1]{2,1,0:T(8,128)S(1)}, u32[]{:S(2)}, u32[]{:S(2)}) collective-permute-start(f32[16,50,1]{2,1,0:T(8,128)S(1)} %get-tuple-element.83), channel_id=1, source_target_pairs={{4,0},{8,4},{12,8},{5,1},{9,5},{13,9},{6,2},{10,6},{14,10},{7,3},{... | collective-permute-start | bytes 9608 | tf_op jit(solution)/shard_map/ppermute | solution.py:20
  34.5 3.4 collective-permute-start.5
  36.5 5.1 collective-permute-start.4
  41.7 43.4 %copy-start.16 = (f32[16,1,256]{2,1,0:T(1,128)}, f32[16,1,256]{2,1,0:T(1,128)S(1)}, u32[]{:S(2)}) copy-start(f32[16,1,256]{2,1,0:T(1,128)S(1)} %collective-permute-done.4) | copy-start | bytes 49156
  41.8 17.7 %copy-start.25 = (f32[48,256]{1,0:T(8,128)S(1)}, f32[48,256]{1,0:T(8,128)}, u32[]{:S(2)}) copy-start(f32[48,256]{1,0:T(8,128)} %param.11) | copy-start | bytes 147460
  42.0 12.8 collective-permute-start.7
  45.4 14.1 collective-permute-start.6
  61.7 312.8 %copy-start.1 = (f32[16,48,256]{2,1,0:T(8,128)}, f32[16,48,256]{2,1,0:T(8,128)S(1)}, u32[]{:S(2)}) copy-start(f32[16,48,256]{2,1,0:T(8,128)S(1)} %get-tuple-element.67) | copy-start | bytes 2359300
  61.8 4.3 collective-permute-start.9
  64.7 4.5 collective-permute-start.8
  69.5 13.8 collective-permute-start.10
  70.8 14.2 collective-permute-start.11
  345.2 2.6 collective-permute-start.13
  346.5 3.1 collective-permute-start.12
  351.3 23.2 %collective-permute-start.14 = (f32[16,50,1]{2,1,0:T(8,128)}, f32[16,50,1]{2,1,0:T(8,128)}, u32[]{:S(2)}, u32[]{:S(2)}) collective-permute-start(f32[16,50,1]{2,1,0:T(8,128)} %get-tuple-element.76), channel_id=1, source_target_pairs={{4,0},{8,4},{12,8},{5,1},{9,5},{13,9},{6,2},{10,6},{14,10},{7,3},{... | collective-permute-start | bytes 9608 | tf_op jit(solution)/shard_map/ppermute | solution.py:20
  352.6 21.9 %collective-permute-start.15 = (f32[16,50,1]{2,1,0:T(8,128)}, f32[16,50,1]{2,1,0:T(8,128)}, u32[]{:S(2)}, u32[]{:S(2)}) collective-permute-start(f32[16,50,1]{2,1,0:T(8,128)} %get-tuple-element.77), channel_id=1, source_target_pairs={{0,4},{4,8},{8,12},{1,5},{5,9},{9,13},{2,6},{6,10},{10,14},{3,7},{... | collective-permute-start | bytes 9608 | tf_op jit(solution)/shard_map/ppermute | solution.py:18
  380.9 124.7 %copy-start.48 = (f32[16]{0:T(128)S(1)}, f32[16]{0:T(128)}, u32[]{:S(2)}) copy-start(f32[16]{0:T(128)} %psum.114) | copy-start | bytes 196
  509.5 52.5 %copy-start.10 = (f32[48,256]{1,0:T(8,128)S(1)}, f32[48,256]{1,0:T(8,128)}, u32[]{:S(2)}) copy-start(f32[48,256]{1,0:T(8,128)} %param.8) | copy-start | bytes 147460
  509.5 52.5 %copy-start.26 = (f32[48,256]{1,0:T(8,128)S(1)}, f32[48,256]{1,0:T(8,128)}, u32[]{:S(2)}) copy-start(f32[48,256]{1,0:T(8,128)} %param.11) | copy-start | bytes 147460
  566.8 2.6 collective-permute-start.17
  568.1 4.9 collective-permute-start.16
  573.3 13.9 collective-permute-start.18
  574.7 14.2 collective-permute-start.19
  849.0 20.9 %copy-start.8 = (f32[16,48,256]{2,1,0:T(8,128)}, f32[16,48,256]{2,1,0:T(8,128)S(1)}, u32[]{:S(2)}) copy-start(f32[16,48,256]{2,1,0:T(8,128)S(1)} %multiply_add_fusion.4) | copy-start | bytes 2359300
  849.0 2.8 collective-permute-start.21
  850.3 3.1 collective-permute-start.20
  853.7 15.0 %collective-permute-start.22 = (f32[16,50,1]{2,1,0:T(8,128)S(1)}, f32[16,50,1]{2,1,0:T(8,128)S(1)}, u32[]{:S(2)}, u32[]{:S(2)}) collective-permute-start(f32[16,50,1]{2,1,0:T(8,128)S(1)} %get-tuple-element.72), channel_id=1, source_target_pairs={{4,0},{8,4},{12,8},{5,1},{9,5},{13,9},{6,2},{10,6},{14,10},{7,3},{... | collective-permute-start | bytes 9608 | tf_op jit(solution)/shard_map/ppermute | solution.py:20
  855.0 14.9 %collective-permute-start.23 = (f32[16,50,1]{2,1,0:T(8,128)S(1)}, f32[16,50,1]{2,1,0:T(8,128)S(1)}, u32[]{:S(2)}, u32[]{:S(2)}) collective-permute-start(f32[16,50,1]{2,1,0:T(8,128)S(1)} %get-tuple-element.73), channel_id=1, source_target_pairs={{0,4},{4,8},{8,12},{1,5},{5,9},{9,13},{2,6},{6,10},{10,14},{3,7},{... | collective-permute-start | bytes 9608 | tf_op jit(solution)/shard_map/ppermute | solution.py:18
  1023.8 20.4 %copy-start.3 = (f32[16,48,256]{2,1,0:T(8,128)}, f32[16,48,256]{2,1,0:T(8,128)S(1)}, u32[]{:S(2)}) copy-start(f32[16,48,256]{2,1,0:T(8,128)S(1)} %multiply_add_fusion.2) | copy-start | bytes 2359300
  1023.8 2.6 collective-permute-start.25
  1025.1 3.1 collective-permute-start.24
  1028.5 14.5 collective-permute-start.26
  1029.8 14.4 collective-permute-start.27
  1174.4 127.5 %copy-start.4 = (f32[16,48,256]{2,1,0:T(8,128)S(1)}, f32[16,48,256]{2,1,0:T(8,128)}, u32[]{:S(2)}) copy-start(f32[16,48,256]{2,1,0:T(8,128)} %copy-done.3) | copy-start | bytes 2359300
  1303.3 20.9 %copy-start.6 = (f32[16,48,256]{2,1,0:T(8,128)}, f32[16,48,256]{2,1,0:T(8,128)S(1)}, u32[]{:S(2)}) copy-start(f32[16,48,256]{2,1,0:T(8,128)S(1)} %multiply_add_fusion.1) | copy-start | bytes 2359300
  1303.3 2.6 collective-permute-start.29
  1304.6 3.1 collective-permute-start.28
  1308.0 15.0 %collective-permute-start.30 = (f32[16,50,1]{2,1,0:T(8,128)S(1)}, f32[16,50,1]{2,1,0:T(8,128)S(1)}, u32[]{:S(2)}, u32[]{:S(2)}) collective-permute-start(f32[16,50,1]{2,1,0:T(8,128)S(1)} %get-tuple-element.68), channel_id=1, source_target_pairs={{4,0},{8,4},{12,8},{5,1},{9,5},{13,9},{6,2},{10,6},{14,10},{7,3},{... | collective-permute-start | bytes 9608 | tf_op jit(solution)/shard_map/ppermute | solution.py:20
  1309.3 14.9 %collective-permute-start.31 = (f32[16,50,1]{2,1,0:T(8,128)S(1)}, f32[16,50,1]{2,1,0:T(8,128)S(1)}, u32[]{:S(2)}, u32[]{:S(2)}) collective-permute-start(f32[16,50,1]{2,1,0:T(8,128)S(1)} %get-tuple-element.69), channel_id=1, source_target_pairs={{0,4},{4,8},{8,12},{1,5},{5,9},{9,13},{2,6},{6,10},{10,14},{3,7},{... | collective-permute-start | bytes 9608 | tf_op jit(solution)/shard_map/ppermute | solution.py:18
  1326.2 126.5 %copy-start.49 = (f32[16]{0:T(128)S(1)}, f32[16]{0:T(128)}, u32[]{:S(2)}) copy-start(f32[16]{0:T(128)} %psum.125) | copy-start | bytes 196
  1453.4 18.8 %copy-start.22 = (f32[48,256]{1,0:T(8,128)S(1)}, f32[48,256]{1,0:T(8,128)}, u32[]{:S(2)}) copy-start(f32[48,256]{1,0:T(8,128)} %get-tuple-element.60) | copy-start | bytes 147460
  (40 other events, 191.7 us)
Sparse Core Ops, SparseCore 0:
  509.7 52.3 all-reduce.6
where the time goes:
time: 1490 us; the launch traced here: 1480 us
  blocking collectives  1170 us (79%)
  waiting for transfers between devices  146 us (10%)
  starting transfers between devices  71.5 us (5%)
  other arithmetic  52.9 us (4%)
  local copies, waits for them, and re-layouts  17 us (1%)
  between operations  15.5 us (1%)
    psum x6, blocking collectives, group_norms(): return lax.psum(local_dot(residual, residual), ('radius', 'polar'))  755 us
    psum x3, blocking collectives, solve_classic(): lax.psum(local_dot(direction, applied), ('radius', 'polar'))  378 us
    ppermute x16, waiting for transfers between devices, padded_2(): lax.ppermute(head, axis, [((i + 1) % count, i) for i in range(ends)])  69 us
    psum x1, waiting for transfers between devices, per_device(): material_next = (fixed_terms + lax.psum(absorbed_local, 'group')) / capacity  52.5 us
    ppermute x16, starting transfers between devices, padded_2(): lax.ppermute(tail, axis, [(i, (i + 1) % count) for i in range(ends)])  50.5 us
    psum x2, blocking collectives, per_device(): material_next = (fixed_terms + lax.psum(absorbed_local, 'group')) / capacity  32.5 us
  transfers between devices with their start and end apart: 33, of which 23 were waited for; matrix products, arithmetic and copies ran while one was open for 0% of the time, Pallas kernels for 0%

commit v1 on v0

v1 whole, which is shorter than its diff:
```python
import functools
import jax
import jax.numpy as jnp
from jax import lax
from jax.experimental import pallas as pl
from jax.experimental.pallas import tpu as pltpu
from jax.sharding import PartitionSpec as P

ITERS = 3
HALO = 8
LANES = 128
VMEM_LIMIT = 12 * 1024 * 1024
HIGHEST = lax.Precision.HIGHEST


def vspec():
    return pl.BlockSpec(memory_space=pltpu.VMEM)


def sspec():
    return pl.BlockSpec(memory_space=pltpu.SMEM)


def call(kernel, outs, args, specs, scratch=(), flops=1000000, nbytes=1000000, name=None):
    return pl.pallas_call(
        kernel,
        out_shape=[jax.ShapeDtypeStruct(s, jnp.float32) for s in outs],
        in_specs=specs,
        out_specs=[vspec() for _ in outs],
        scratch_shapes=list(scratch),
        compiler_params=pltpu.CompilerParams(vmem_limit_bytes=VMEM_LIMIT),
        cost_estimate=pl.CostEstimate(flops=flops, bytes_accessed=nbytes, transcendentals=0),
        name=name,
    )(*args)


def pack_rows_kernel(groups, rows, opacity, old, density, material, flux, up, down):
    for out, lo in ((up, 0), (down, rows - HALO)):
        base = (lo // 16) * 16
        dens = density[lo : lo + HALO, :]
        for g in range(groups):
            part = opacity[g, base : base + 16, :].astype(jnp.float32)
            out[g] = part[lo - base : lo - base + HALO, :] * dens
            out[groups + g] = old[g, lo : lo + HALO, :]
        out[2 * groups] = dens
        out[2 * groups + 1] = material[lo : lo + HALO, :]
        out[2 * groups + 2] = jnp.broadcast_to(flux[lo : lo + HALO, :], dens.shape)


def pack_columns_kernel(groups, rows, cols, opacity, old, density, material, top, bottom, left, right):
    full = rows + 2 * HALO
    lane = lax.broadcasted_iota(jnp.int32, (full, LANES), 1)
    for out, lo, edge in ((left, 0, 0), (right, cols - LANES, LANES - HALO)):
        hi = lo + LANES

        def tile(plane, own):
            return jnp.concatenate([top[plane, :, lo:hi], own, bottom[plane, :, lo:hi]], axis=0)

        packed_a = jnp.zeros((full, LANES), jnp.float32)
        packed_e = jnp.zeros((full, LANES), jnp.float32)
        dens = density[:, lo:hi]
        for g in range(groups):
            mine = (lane >= HALO * g) & (lane < HALO * (g + 1))
            shift = (HALO * g - edge) % LANES
            a = tile(g, opacity[g, :, lo:hi].astype(jnp.float32) * dens)
            e = tile(groups + g, old[g, :, lo:hi])
            if shift:
                a = pltpu.roll(a, shift, 1)
                e = pltpu.roll(e, shift, 1)
            packed_a = jnp.where(mine, a, packed_a)
            packed_e = jnp.where(mine, e, packed_e)
        out[0] = packed_a
        out[1] = packed_e
        d = tile(2 * groups, dens)
        m = tile(2 * groups + 1, material[:, lo:hi])
        d = pltpu.roll(d, (-edge) % LANES, 1) if edge else d
        m = pltpu.roll(m, (HALO - edge) % LANES, 1)
        out[2] = jnp.where(lane < HALO, d, jnp.where(lane < 2 * HALO, m, 0.0))


def next_row(v):
    return pltpu.roll(v, v.shape[0] - 1, 0)


def prev_row(v):
    return pltpu.roll(v, 1, 0)


def next_col(v):
    return pltpu.roll(v, v.shape[1] - 1, 1)


def prev_col(v):
    return pltpu.roll(v, 1, 1)


def flux_sum(v, face_r, face_p):
    fr = face_r * (v - next_row(v))
    fp = face_p * (v - next_col(v))
    return fr - prev_row(fr) + fp - prev_col(fp)


def harmonic(a, b):
    return 2.0 * a * b / jnp.maximum(a + b, 1e-30)


def own_sum(v, rows, cols):
    own = v[HALO : HALO + rows, :cols]
    acc = own[:, :LANES]
    for lo in range(LANES, cols, LANES):
        acc = acc + own[:, lo : lo + LANES]
    return jnp.sum(acc, axis=0, keepdims=True)


def krylov(g, groups, rows, cols, r, a, face_r, face_p, r_ref, q_ref, t_ref, mom):
    q = r + a * r + flux_sum(r, face_r, face_p)
    r_ref[g] = r
    q_ref[g] = q
    mom[pl.ds(g, 1), :] = own_sum(r * r, rows, cols)
    mom[pl.ds(groups + g, 1), :] = own_sum(r * q, rows, cols)
    mom[pl.ds(2 * groups + g, 1), :] = own_sum(q * q, rows, cols)
    t = q + a * q + flux_sum(q, face_r, face_p)
    if t_ref is not None:
        t_ref[g] = t
    mom[pl.ds(3 * groups + g, 1), :] = own_sum(q * t, rows, cols)


def broadcast_moments(mom, out):
    out[...] = lax.dot_general(
        jnp.ones((out.shape[0], LANES), jnp.float32),
        mom[...],
        (((1,), (1,)), ((), ())),
        precision=HIGHEST,
        preferred_element_type=jnp.float32,
    )


def start_kernel(
    groups, rows, cols,
    weights, opacity, old, density, material, flux, top, bottom, left, right,
    a_ref, e_ref, fr_ref, fp_ref, r_ref, q_ref, t_ref, dens_ref, mat_ref, flux_ref, emit_ref, out,
    mom,
):
    full, wide = a_ref.shape[1:]
    lane = lax.broadcasted_iota(jnp.int32, (full, LANES), 1)
    at_right = lane < HALO
    at_left = lane >= LANES - HALO

    def halo_tile(plane, shift_right, shift_left):
        from_right = pltpu.roll(right[plane], shift_right, 1)
        from_left = pltpu.roll(left[plane], shift_left, 1)
        return jnp.where(at_right, from_right, jnp.where(at_left, from_left, 0.0))

    def field(own, plane, tile):
        inner = jnp.concatenate([top[plane], own, bottom[plane]], axis=0)
        return jnp.concatenate([inner, tile], axis=1)

    dens = field(density[...], 2 * groups, halo_tile(2, 0, LANES - HALO))
    mat = field(material[...], 2 * groups + 1, halo_tile(2, LANES - HALO, LANES - 2 * HALO))
    valid = dens > 0.0
    dens_ref[...] = dens
    mat_ref[...] = mat
    flux_ref[0:HALO, :] = top[2 * groups + 2][:, :LANES]
    flux_ref[HALO : HALO + rows, :] = jnp.broadcast_to(flux[...], (rows, LANES))
    flux_ref[HALO + rows :, :] = bottom[2 * groups + 2][:, :LANES]
    partial = dens[:, :LANES]
    for lo in range(LANES, cols, LANES):
        partial = partial + dens[:, lo : lo + LANES]
    mom[4 * groups : 4 * groups + full, :] = partial

    def one(g, emit):
        shift_right = lax.rem(LANES - HALO * g, LANES)
        shift_left = lax.rem(2 * LANES - HALO - HALO * g, LANES)
        own = opacity[g].astype(jnp.float32) * density[...]
        a = field(own, g, halo_tile(0, shift_right, shift_left))
        e = field(old[g], groups + g, halo_tile(1, shift_right, shift_left))
        a = jnp.where(valid, a, 1.0)
        a_ref[g] = a
        e_ref[g] = e
        w = weights[g]
        emit = emit + a * w
        slope_r = 0.5 * (next_row(e) - prev_row(e))
        slope_p = 0.5 * (next_col(e) - prev_col(e))
        n = jnp.sqrt(slope_r * slope_r + slope_p * slope_p)
        u = a * e
        s = 2.0 * u + n
        d = jnp.where(valid, e * s / (n * n + 3.0 * u * s), 0.0)
        face_r = harmonic(d, next_row(d))
        face_p = harmonic(d, next_col(d))
        fr_ref[g] = face_r
        fp_ref[g] = face_p
        r = a * (w * mat - e) - flux_sum(e, face_r, face_p)
        krylov(g, groups, rows, cols, r, a, face_r, face_p, r_ref, q_ref, t_ref, mom)
        return emit

    emit_ref[...] = lax.fori_loop(0, groups, one, jnp.zeros((full, wide), jnp.float32))
    broadcast_moments(mom, out)


def steps(groups, gathered):
    total = jnp.sum(gathered[...], axis=0, keepdims=True)
    lane = lax.broadcasted_iota(jnp.int32, (groups, LANES), 1)
    sub = lax.broadcasted_iota(jnp.int32, (groups, LANES), 0)
    m0, m1, m2, m3 = (
        jnp.sum(jnp.where(lane == sub + k * groups, total, 0.0), axis=1, keepdims=True)
        for k in range(4)
    )
    k1, k2, k3 = m1 / m0, m2 / m0, m3 / m0
    first = 1.0 / k1
    det = k2 - k1 * k1
    beta = jnp.maximum(det, 0.0) / (k1 * k1)
    low = k1 * k3 - k2 * k2
    second = jnp.where(low > 0.0, k1 * jnp.maximum(det, 0.0) / low, 0.0)
    second = jnp.minimum(second, 1.0)
    return first + second * (1.0 + beta), first * second


def update_kernel(groups, gathered, a_ref, e_ref, r_ref, q_ref, e_out, s_out, c1_ref, c2_ref):
    c1, c2 = steps(groups, gathered)
    wide = a_ref.shape[2]
    c1_ref[...] = jnp.broadcast_to(c1, (groups, wide))
    c2_ref[...] = jnp.broadcast_to(c2, (groups, wide))

    def one(g, total):
        e = e_ref[g] + c1_ref[pl.ds(g, 1), :] * r_ref[g] - c2_ref[pl.ds(g, 1), :] * q_ref[g]
        e_out[g] = e
        return total + a_ref[g] * e

    s_out[...] = lax.fori_loop(0, groups, one, jnp.zeros(s_out.shape, jnp.float32))


def last_update_kernel(groups, rows, cols, gathered, a_ref, e_ref, r_ref, q_ref, e_out, s_out, c1_ref, c2_ref):
    c1, c2 = steps(groups, gathered)
    c1_ref[...] = jnp.broadcast_to(c1, (groups, cols))
    c2_ref[...] = jnp.broadcast_to(c2, (groups, cols))

    def one(g, total):
        here = (g, slice(HALO, HALO + rows), slice(0, cols))
        e = e_ref[here] + c1_ref[pl.ds(g, 1), :] * r_ref[here] - c2_ref[pl.ds(g, 1), :] * q_ref[here]
        e_out[g] = e
        return total + a_ref[here] * e

    s_out[...] = lax.fori_loop(0, groups, one, jnp.zeros((rows, cols), jnp.float32))


def heating_kernel(groups, rows, cols, polar_count, polar_total, place, gathered, dens_ref, flux_ref, mat_ref, column_out, fixed_out):
    full, wide = dens_ref.shape
    radius, polar = place[0], place[1]
    dens = dens_ref[...]
    count = gathered.shape[0]
    row_id = lax.broadcasted_iota(jnp.int32, (count, LANES), 0)
    ahead = (row_id >= radius * polar_count) & (row_id < radius * polar_count + polar)
    carried = jnp.sum(jnp.where(ahead, gathered[...], 0.0), axis=0, keepdims=True)
    lane = lax.broadcasted_iota(jnp.int32, (full, LANES), 1)
    sub = lax.broadcasted_iota(jnp.int32, (full, LANES), 0)
    carried = jnp.sum(jnp.where(lane == sub + 4 * groups, carried, 0.0), axis=1, keepdims=True)
    src = lax.broadcasted_iota(jnp.int32, (wide, wide), 0)
    dst = lax.broadcasted_iota(jnp.int32, (wide, wide), 1)
    middle = cols + LANES // 2
    ahead_of = (dst < middle) & (src <= dst)
    behind = (dst >= middle) & (src > dst)
    coeff = jnp.where(ahead_of, 1.0, jnp.where(behind, -1.0, 0.0))
    within = lax.dot_general(
        dens, coeff, (((1,), (0,)), ((), ())), precision=HIGHEST, preferred_element_type=jnp.float32
    )
    column = 2.0 / polar_total * (carried + within)
    column_out[...] = column[HALO : HALO + rows, :cols]
    flux = jnp.concatenate([flux_ref[...]] * (wide // LANES), axis=1)
    fixed_out[...] = 16.0 * dens * mat_ref[...] + flux * dens * jnp.exp(-column)


def next_kernel(
    groups, rows, cols, count, last,
    weights, c1_ref, c2_ref, a_ref, fr_ref, fp_ref, r_in, q_in, t_in,
    fixed, capacity, mat_ref, *rest,
):
    sums = rest[:count]
    r_ref, q_ref, t_ref, m_ref, out, delta_ref, mom = rest[count:]
    total = sums[0][...]
    for s in sums[1:]:
        total = total + s[...]
    nxt = (fixed[...] + total) / capacity[...]
    m_ref[...] = nxt
    delta_ref[...] = nxt - mat_ref[...]

    def one(g, carry):
        a = a_ref[g]
        r = (
            r_in[g]
            - c1_ref[pl.ds(g, 1), :] * q_in[g]
            + c2_ref[pl.ds(g, 1), :] * t_in[g]
            + a * (weights[g] * delta_ref[...])
        )
        krylov(g, groups, rows, cols, r, a, fr_ref[g], fp_ref[g], r_ref, q_ref, None if last else t_ref, mom)
        return carry

    mom[4 * groups :, :] = jnp.zeros((mom.shape[0] - 4 * groups, LANES), jnp.float32)
    lax.fori_loop(0, groups, one, 0)
    broadcast_moments(mom, out)


def capacity_kernel(count, dens_ref, *rest):
    sums = rest[:count]
    out = rest[count]
    total = sums[0][...]
    for s in sums[1:]:
        total = total + s[...]
    dens = dens_ref[...]
    out[...] = 16.0 * jnp.where(dens > 0.0, dens, 1.0) + total


def material_kernel(count, rows, cols, fixed, capacity, *rest):
    sums = rest[:count]
    out = rest[count]
    total = sums[0][...]
    for s in sums[1:]:
        total = total + s[...]
    here = (slice(HALO, HALO + rows), slice(0, cols))
    out[...] = (fixed[here] + total) / capacity[here]


def spread(part, axis):
    count = lax.axis_size(axis)
    return [part] + [
        lax.ppermute(part, axis, [(i, (i + s) % count) for i in range(count)]) for s in range(1, count)
    ]


def shifted(upward, downward, axis):
    count = lax.axis_size(axis)
    from_lower = lax.ppermute(downward, axis, [(i, i + 1) for i in range(count - 1)])
    from_upper = lax.ppermute(upward, axis, [(i + 1, i) for i in range(count - 1)])
    return from_lower, from_upper


def per_device(density, opacity, radiation_old, material_old, weights, stellar_flux):
    groups, rows, cols = opacity.shape
    full, wide = rows + 2 * HALO, cols + LANES
    polar_count = lax.axis_size("polar")
    group_count = lax.axis_size("group")
    devices = lax.axis_size("radius") * polar_count
    place = jnp.stack([lax.axis_index("radius"), lax.axis_index("polar")]).astype(jnp.int32)
    flux = stellar_flux[:, None]
    planes = 2 * groups + 3
    big = (groups, full, wide)
    flat = (full, wide)

    up, down = call(
        functools.partial(pack_rows_kernel, groups, rows),
        [(planes, HALO, cols)] * 2,
        (opacity, radiation_old, density, material_old, flux),
        [vspec()] * 5,
        name="pack_rows",
    )
    top, bottom = shifted(up, down, "radius")
    to_left, to_right = call(
        functools.partial(pack_columns_kernel, groups, rows, cols),
        [(3, full, LANES)] * 2,
        (opacity, radiation_old, density, material_old, top, bottom),
        [vspec()] * 6,
        name="pack_columns",
    )
    left, right = shifted(to_left, to_right, "polar")
    a, e, fr, fp, r, q, t, dens, mat, flux_rows, emit, out = call(
        functools.partial(start_kernel, groups, rows, cols),
        [big] * 7 + [flat, flat, (full, LANES), flat, (devices, LANES)],
        (weights, opacity, radiation_old, density, material_old, flux, top, bottom, left, right),
        [sspec()] + [vspec()] * 9,
        scratch=[pltpu.VMEM((LANES, LANES), jnp.float32)],
        name="start",
    )
    for turn in range(ITERS):
        gathered = lax.all_to_all(out, ("radius", "polar"), 0, 0, tiled=True)
        if turn + 1 == ITERS:
            e, part = call(
                functools.partial(last_update_kernel, groups, rows, cols),
                [(groups, rows, cols), (rows, cols)],
                (gathered, a, e, r, q),
                [vspec()] * 5,
                scratch=[pltpu.VMEM((groups, cols), jnp.float32)] * 2,
                name="last_update",
            )
            sums = spread(part, "group")
            (mat,) = call(
                functools.partial(material_kernel, group_count, rows, cols),
                [(rows, cols)],
                (fixed, capacity, *sums),
                [vspec()] * (2 + group_count),
                name="material",
            )
            break
        e, part, c1, c2 = call(
            functools.partial(update_kernel, groups),
            [big, flat, (groups, wide), (groups, wide)],
            (gathered, a, e, r, q),
            [vspec()] * 5,
            name="update",
        )
        sums = spread(part, "group")
        if turn == 0:
            emits = spread(emit, "group")
            column, fixed = call(
                functools.partial(heating_kernel, groups, rows, cols, polar_count, cols * polar_count),
                [(rows, cols), flat],
                (place, gathered, dens, flux_rows, mat),
                [sspec()] + [vspec()] * 4,
                name="heating",
            )
            (capacity,) = call(
                functools.partial(capacity_kernel, group_count),
                [flat],
                (dens, *emits),
                [vspec()] * (1 + group_count),
                name="capacity",
            )
        r, q, t, mat, out = call(
            functools.partial(next_kernel, groups, rows, cols, group_count, turn + 2 == ITERS),
            [big] * 3 + [flat, (devices, LANES)],
            (weights, c1, c2, a, fr, fp, r, q, t, fixed, capacity, mat, *sums),
            [sspec()] + [vspec()] * (11 + group_count),
            scratch=[pltpu.VMEM(flat, jnp.float32), pltpu.VMEM((LANES, LANES), jnp.float32)],
            name="next",
        )
    return (e, mat, column)


def solution(mesh):
    return jax.shard_map(
        per_device,
        mesh=mesh,
        in_specs=(
            P("radius", "polar"),
            P("group", "radius", "polar"),
            P("group", "radius", "polar"),
            P("radius", "polar"),
            P("group"),
            P("radius"),
        ),
        out_specs=(P("group", "radius", "polar"), P("radius", "polar"), P("radius", "polar")),
        check_vma=False,
    )
```

time: 1490 us -> 141 us (0.09)
  blocking collectives: 1170 us -> 27.2 us
  waiting for transfers between devices: 146 us -> 22.3 us
  other arithmetic: 52.9 us -> 0.07 us
  Pallas kernels: 0 us -> 31.8 us
  starting transfers between devices: 71.5 us -> 43.1 us
    psum x11 -> x0, blocking collectives: 1170 us -> none  [the longest x6 755 us: group_norms(): return lax.psum(local_dot(residual, residual), ('radius', 'polar'))]
    ppermute x32 -> x16, waiting for transfers between devices: 93.9 us -> 17.3 us  [the longest x12 8.26 us: spread(): lax.ppermute(part, axis, [(i, (i + s) % count) for i in range(count)])]
    psum x1 -> x0, waiting for transfers between devices: 52.5 us -> none  [per_device(): material_next = (fixed_terms + lax.psum(absorbed_local, 'group')) / capacity]
    ppermute x32 -> x16, starting transfers between devices: 71.4 us -> 27.4 us  [the longest x12 19.7 us: spread(): lax.ppermute(part, axis, [(i, (i + s) % count) for i in range(count)])]
    reduce_sum x13 -> x0, other arithmetic: 35.8 us -> none  [the longest x9 25.3 us: local_dot(): return jnp.sum(left_field * right_field, axis=(1, 2))]
    pallas_call x0 -> x11, Pallas kernels: none -> 31.8 us  [call(): pl.pallas_call(kernel, out_shape=[jax.ShapeDtypeStruct(s, jnp.float32) fo...]
    all_to_all x0 -> x2, blocking collectives: none -> 27.2 us  [per_device(): gathered = lax.all_to_all(out, ('radius', 'polar'), 0, 0, tiled=True)]
    all_to_all x0 -> x1, starting transfers between devices: none -> 15.6 us  [per_device(): gathered = lax.all_to_all(out, ('radius', 'polar'), 0, 0, tiled=True)]
  transfers between devices with their start and end apart: 33 -> 17, of which waited for: 23 -> 8; matrix products, arithmetic and copies ran while one was open for 0% -> 0% of each run, Pallas kernels for 0% -> 2%
where the time goes in v1:
time: 141 us; the launch traced here: 140 us
  starting transfers between devices  43.1 us (31%)
  Pallas kernels  31.8 us (23%)
  blocking collectives  27.2 us (19%)
  waiting for transfers between devices  22.3 us (16%)
  local copies, waits for them, and re-layouts  14.6 us (10%)
    pallas_call x11, Pallas kernels, call(): pl.pallas_call(kernel, out_shape=[jax.ShapeDtypeStruct(s, jnp.float32) fo...  31.8 us
    all_to_all x2, blocking collectives, per_device(): gathered = lax.all_to_all(out, ('radius', 'polar'), 0, 0, tiled=True)  27.2 us
    ppermute x12, starting transfers between devices, spread(): lax.ppermute(part, axis, [(i, (i + s) % count) for i in range(count)])  19.7 us
    all_to_all x1, starting transfers between devices, per_device(): gathered = lax.all_to_all(out, ('radius', 'polar'), 0, 0, tiled=True)  15.6 us
    unnamed x32, local copies, waits for them, and re-layouts  13.8 us
    ppermute x12, waiting for transfers between devices, spread(): lax.ppermute(part, axis, [(i, (i + s) % count) for i in range(count)])  8.26 us
    ppermute x2, waiting for transfers between devices, shifted(): lax.ppermute(upward, axis, [(i + 1, i) for i in range(count - 1)])  8.16 us
    ppermute x2, starting transfers between devices, shifted(): lax.ppermute(downward, axis, [(i, i + 1) for i in range(count - 1)])  5.14 us
  transfers between devices with their start and end apart: 17, of which 8 were waited for; matrix products, arithmetic and copies ran while one was open for 0% of the time, Pallas kernels for 2%

profile of v1, /device:TPU:8, one launch (start us, length us, event | category | flops | bytes accessed | tf_op | source)
XLA Modules:
  0.0 139.8 jit_solution(2108171339891261633)
XLA Ops:
  0.6 0.7 copy.12.flux
  1.4 1.1 copy-done
  2.5 1.0 copy-done.8
  3.5 0.8 copy-done.13
  4.3 0.8 copy-done.14
  5.2 1.7 %collective-permute-start = (f32[35,8,256]{2,1,0:T(8,128)S(1)}, f32[35,8,256]{2,1,0:T(8,128)S(1)}, u32[]{:S(2)}, u32[]{:S(2)}) collective-permute-start(f32[35,8,256]{2,1,0:T(8,128)S(1)} %get-tuple-element.39), channel_id=1, source_target_pairs={{0,16},{16,32},{32,48},{48,64},{64,80},{80,96},{96,112},{112,128},... | collective-permute-start | bytes 860168 | tf_op jit(solution)/shard_map/ppermute | solution.py:331
  6.9 1.3 collective-permute-start.1
  8.2 3.8 %collective-permute-done.1.bottom = f32[35,8,256]{2,1,0:T(8,128)S(1)} collective-permute-done((f32[35,8,256]{2,1,0:T(8,128)S(1)}, f32[35,8,256]{2,1,0:T(8,128)S(1)}, u32[]{:S(2)}, u32[]{:S(2)}) %collective-permute-start.1) | collective-permute-done | bytes 286752 | tf_op jit(solution)/shard_map/ppermute | solution.py:332
  12.1 0.6 pack_columns.1
  12.7 3.4 %collective-permute-start.2 = (f32[3,64,128]{2,1,0:T(8,128)S(1)}, f32[3,64,128]{2,1,0:T(8,128)S(1)}, u32[]{:S(2)}, u32[]{:S(2)}) collective-permute-start(f32[3,64,128]{2,1,0:T(8,128)S(1)} %get-tuple-element.41), channel_id=1, source_target_pairs={{0,4},{4,8},{8,12},{1,5},{5,9},{9,13},{2,6},{6,10},{10,14},{3,7},{... | collective-permute-start | bytes 294920 | tf_op jit(solution)/shard_map/ppermute | solution.py:331
  16.1 1.3 collective-permute-start.3
  17.4 0.9 collective-permute-done.2.left
  18.3 4.3 %collective-permute-done.3.right = f32[3,64,128]{2,1,0:T(8,128)S(1)} collective-permute-done((f32[3,64,128]{2,1,0:T(8,128)S(1)}, f32[3,64,128]{2,1,0:T(8,128)S(1)}, u32[]{:S(2)}, u32[]{:S(2)}) %collective-permute-start.3) | collective-permute-done | bytes 98336 | tf_op jit(solution)/shard_map/ppermute | solution.py:332
  22.6 12.5 %start.1 = (f32[16,64,384]{2,1,0:T(8,128)S(1)}, f32[16,64,384]{2,1,0:T(8,128)S(1)}, f32[16,64,384]{2,1,0:T(8,128)S(1)}, f32[16,64,384]{2,1,0:T(8,128)S(1)}, f32[...) custom-call(f32[16]{0:T(128)S(1)} %copy-done.15, ...), custom_call_target="tpu_custom_call" | custom-call | flops 1000000 | bytes 1000000 | tf_op jit(solution)/shard_map/start/pallas_call | solution.py:25
  35.1 1.2 copy-done.1
  36.2 1.2 copy-done.3
  37.4 1.2 copy-done.6
  38.6 1.1 copy-done.9
  39.7 1.2 copy-done.11
  40.9 0.4 collective-permute-start.6
  41.4 15.6 %all-to-all-start = ((f32[64,1,128]{2,1,0:T(1,128)}), f32[64,1,128]{2,1,0:T(1,128)S(1)}, u32[]{:S(2)}, u32[]{:S(2)}) async-start(f32[64,1,128]{2,1,0:T(1,128)} %bitcast.2), calls=%async_computation | async-start | bytes 65536 | tf_op jit(solution)/shard_map/all_to_all | solution.py:373
  57.0 2.7 %collective-permute-start.5 = (f32[64,384]{1,0:T(8,128)S(1)}, f32[64,384]{1,0:T(8,128)}, u32[]{:S(2)}, u32[]{:S(2)}) collective-permute-start(f32[64,384]{1,0:T(8,128)S(1)} %get-tuple-element.57.rest_0_), channel_id=1, source_target_pairs={{0,2},{1,3},{2,0},{3,1},{4,6},{5,7},{6,4},{7,5},{8,10},{9,11},{10,... | collective-permute-start | bytes 294920 | tf_op jit(solution)/shard_map/ppermute | solution.py:325
  59.7 1.9 %collective-permute-start.4 = (f32[64,384]{1,0:T(8,128)S(1)}, f32[64,384]{1,0:T(8,128)}, u32[]{:S(2)}, u32[]{:S(2)}) collective-permute-start(f32[64,384]{1,0:T(8,128)S(1)} %get-tuple-element.57.rest_0_), channel_id=1, source_target_pairs={{0,1},{1,2},{2,3},{3,0},{4,5},{5,6},{6,7},{7,4},{8,9},{9,10},{10,1... | collective-permute-start | bytes 294920 | tf_op jit(solution)/shard_map/ppermute | solution.py:325
  61.6 5.0 %all-to-all-done = f32[64,1,128]{2,1,0:T(1,128)S(1)} async-done(((f32[64,1,128]{2,1,0:T(1,128)}), f32[64,1,128]{2,1,0:T(1,128)S(1)}, u32[]{:S(2)}, u32[]{:S(2)}) %all-to-all-start) | async-done | bytes 32800 | tf_op jit(solution)/shard_map/all_to_all | solution.py:373
  66.6 1.4 %copy-done.4 = f32[16,64,384]{2,1,0:T(8,128)S(1)} copy-done((f32[16,64,384]{2,1,0:T(8,128)S(1)}, f32[16,64,384]{2,1,0:T(8,128)}, u32[]{:S(2)}) %copy-start.4) | copy-done | bytes 1572888
  68.0 1.4 %copy-done.7 = f32[16,64,384]{2,1,0:T(8,128)S(1)} copy-done((f32[16,64,384]{2,1,0:T(8,128)S(1)}, f32[16,64,384]{2,1,0:T(8,128)}, u32[]{:S(2)}) %copy-start.7) | copy-done | bytes 1572888
  69.4 1.4 %copy-done.12 = f32[16,64,384]{2,1,0:T(8,128)S(1)} copy-done((f32[16,64,384]{2,1,0:T(8,128)S(1)}, f32[16,64,384]{2,1,0:T(8,128)}, u32[]{:S(2)}) %copy-start.12) | copy-done | bytes 1572888
  70.9 0.6 update.2
  71.4 3.1 %collective-permute-start.9 = (f32[64,384]{1,0:T(8,128)S(1)}, f32[64,384]{1,0:T(8,128)S(1)}, u32[]{:S(2)}, u32[]{:S(2)}) collective-permute-start(f32[64,384]{1,0:T(8,128)S(1)} %get-tuple-element.58.rest_0_), channel_id=1, source_target_pairs={{0,3},{1,0},{2,1},{3,2},{4,7},{5,4},{6,5},{7,6},{8,11},{9,8},{10,9... | collective-permute-start | bytes 294920 | tf_op jit(solution)/shard_map/ppermute | solution.py:325
  74.6 2.2 %collective-permute-start.7 = (f32[64,384]{1,0:T(8,128)S(1)}, f32[64,384]{1,0:T(8,128)S(1)}, u32[]{:S(2)}, u32[]{:S(2)}) collective-permute-start(f32[64,384]{1,0:T(8,128)S(1)} %get-tuple-element.58.rest_0_), channel_id=1, source_target_pairs={{0,1},{1,2},{2,3},{3,0},{4,5},{5,6},{6,7},{7,4},{8,9},{9,10},{10,1... | collective-permute-start | bytes 294920 | tf_op jit(solution)/shard_map/ppermute | solution.py:325
  76.8 1.5 %heating.1 = (f32[48,256]{1,0:T(8,128)}, f32[64,384]{1,0:T(8,128)S(1)}) custom-call(s32[2]{0:T(128)S(1)} %pad_add_fusion.place, f32[64,128]{1,0:T(8,128)S(1)} %bitcast.16, f32[64,384]{1,0:T(8,128)S(1)} %get-tuple-element.53.dens_ref, f32[64,128]{1,0:T(8,128)S(1)} %get-tuple-element.54.flux_ref, f32[64,384]{1,0:T(8,128)S(1)} %get-tuple-element.55.mat_ref), custom_call_target="tpu_custom_call" | custom-call | flops 1000000 | bytes 1000000 | tf_op jit(solution)/shard_map/heating/pallas_call | solution.py:25
  78.4 1.0 capacity.1
  79.4 1.3 collective-permute-done.8.rest_2_
  80.7 6.2 %next.2 = (f32[16,64,384]{2,1,0:T(8,128)S(1)}, f32[16,64,384]{2,1,0:T(8,128)S(1)}, f32[16,64,384]{2,1,0:T(8,128)S(1)}, f32[64,384]{1,0:T(8,128)S(1)}, f32[64,128]{1,0:T(8,128)S(1)}) custom-call(f32[16]{0:T(128)S(1)} %copy-done.15, f32[16,384]{1,0:T(8,128)S(1)} %get-tuple-element.48.c1_ref, f32[16,384]{1,0:T(8,128)S(1)} %get-tuple-element.49.c2_ref, ...), custom_call_target="tpu_custom_call" | custom-call | flops 1000000 | bytes 1000000 | tf_op jit(solution)/shard_map/next/pallas_call | solution.py:25
  86.9 13.8 %all_to_all.33 = f32[64,1,128]{2,1,0:T(1,128)S(1)} all-to-all(f32[64,1,128]{2,1,0:T(1,128)S(1)} %bitcast.20), channel_id=1, replica_groups=mesh['radius'=16,'polar'=4,'group'=4] {'radius','polar'}, dimensions={0} | all-to-all | bytes 65536 | tf_op jit(solution)/shard_map/all_to_all | solution.py:373
  100.7 0.6 update.3
  101.3 2.2 %collective-permute-start.12 = (f32[64,384]{1,0:T(8,128)S(1)}, f32[64,384]{1,0:T(8,128)S(1)}, u32[]{:S(2)}, u32[]{:S(2)}) collective-permute-start(f32[64,384]{1,0:T(8,128)S(1)} %get-tuple-element.67.rest_0_), channel_id=1, source_target_pairs={{0,3},{1,0},{2,1},{3,2},{4,7},{5,4},{6,5},{7,6},{8,11},{9,8},{10,9... | collective-permute-start | bytes 294920 | tf_op jit(solution)/shard_map/ppermute | solution.py:325
  103.5 0.8 collective-permute-start.11
  104.3 1.6 %collective-permute-start.10 = (f32[64,384]{1,0:T(8,128)S(1)}, f32[64,384]{1,0:T(8,128)S(1)}, u32[]{:S(2)}, u32[]{:S(2)}) collective-permute-start(f32[64,384]{1,0:T(8,128)S(1)} %get-tuple-element.67.rest_0_), channel_id=1, source_target_pairs={{0,1},{1,2},{2,3},{3,0},{4,5},{5,6},{6,7},{7,4},{8,9},{9,10},{10,1... | collective-permute-start | bytes 294920 | tf_op jit(solution)/shard_map/ppermute | solution.py:325
  105.9 0.4 collective-permute-done.12.rest_3_
  106.3 3.3 %collective-permute-done.11.rest_2_ = f32[64,384]{1,0:T(8,128)S(1)} collective-permute-done((f32[64,384]{1,0:T(8,128)S(1)}, f32[64,384]{1,0:T(8,128)S(1)}, u32[]{:S(2)}, u32[]{:S(2)}) %collective-permute-start.11) | collective-permute-done | bytes 98336 | tf_op jit(solution)/shard_map/ppermute | solution.py:325
  109.6 6.8 %next.3 = (f32[16,64,384]{2,1,0:T(8,128)S(1)}, f32[16,64,384]{2,1,0:T(8,128)S(1)}, f32[16,64,384]{2,1,0:T(8,128)}, f32[64,384]{1,0:T(8,128)}, f32[64,128]{1,0:T(8,128)S(1)}) custom-call(f32[16]{0:T(128)S(1)} %copy-done.15, f32[16,384]{1,0:T(8,128)S(1)} %get-tuple-element.63.c1_ref, f32[16,384]{1,0:T(8,128)S(1)} %get-tuple-element.64.c2_ref, ...), custom_call_target="tpu_custom_call" | custom-call | flops 1000000 | bytes 1000000 | tf_op jit(solution)/shard_map/next/pallas_call | solution.py:25
  116.4 13.4 %all_to_all.34 = f32[64,1,128]{2,1,0:T(1,128)S(1)} all-to-all(f32[64,1,128]{2,1,0:T(1,128)S(1)} %bitcast.19), channel_id=1, replica_groups=mesh['radius'=16,'polar'=4,'group'=4] {'radius','polar'}, dimensions={0} | all-to-all | bytes 65536 | tf_op jit(solution)/shard_map/all_to_all | solution.py:373
  129.8 1.3 last_update.1
  131.1 2.4 %collective-permute-start.15 = (f32[48,256]{1,0:T(8,128)S(1)}, f32[48,256]{1,0:T(8,128)S(1)}, u32[]{:S(2)}, u32[]{:S(2)}) collective-permute-start(f32[48,256]{1,0:T(8,128)S(1)} %get-tuple-element.73.rest_0_), channel_id=1, source_target_pairs={{0,3},{1,0},{2,1},{3,2},{4,7},{5,4},{6,5},{7,6},{8,11},{9,8},{10,9... | collective-permute-start | bytes 147464 | tf_op jit(solution)/shard_map/ppermute | solution.py:325
  134.0 1.9 %collective-permute-start.13 = (f32[48,256]{1,0:T(8,128)S(1)}, f32[48,256]{1,0:T(8,128)S(1)}, u32[]{:S(2)}, u32[]{:S(2)}) collective-permute-start(f32[48,256]{1,0:T(8,128)S(1)} %get-tuple-element.73.rest_0_), channel_id=1, source_target_pairs={{0,1},{1,2},{2,3},{3,0},{4,5},{5,6},{6,7},{7,4},{8,9},{9,10},{10,1... | collective-permute-start | bytes 147464 | tf_op jit(solution)/shard_map/ppermute | solution.py:325
  135.9 3.2 %collective-permute-done.14.rest_2_ = f32[48,256]{1,0:T(8,128)S(1)} collective-permute-done((f32[48,256]{1,0:T(8,128)S(1)}, f32[48,256]{1,0:T(8,128)S(1)}, u32[]{:S(2)}, u32[]{:S(2)}) %collective-permute-start.14) | collective-permute-done | bytes 49184 | tf_op jit(solution)/shard_map/ppermute | solution.py:325
  139.2 0.6 material.7
  (33 shorter events, 0.6 us)
Async XLA Ops:
  1.4 1.1 copy-start
  2.5 1.0 copy-start.8
  3.5 0.8 copy-start.13
  4.3 0.8 copy-start.14
  5.1 17.5 %copy-start.15 = (f32[16]{0:T(128)S(1)}, f32[16]{0:T(128)}, u32[]{:S(2)}) copy-start(f32[16]{0:T(128)} %weights.5) | copy-start | bytes 196
  5.2 3.1 %collective-permute-start = (f32[35,8,256]{2,1,0:T(8,128)S(1)}, f32[35,8,256]{2,1,0:T(8,128)S(1)}, u32[]{:S(2)}, u32[]{:S(2)}) collective-permute-start(f32[35,8,256]{2,1,0:T(8,128)S(1)} %get-tuple-element.39), channel_id=1, source_target_pairs={{0,16},{16,32},{32,48},{48,64},{64,80},{80,96},{96,112},{112,128},... | collective-permute-start | bytes 860168 | tf_op jit(solution)/shard_map/ppermute | solution.py:331
  6.9 5.2 %collective-permute-start.1 = (f32[35,8,256]{2,1,0:T(8,128)S(1)}, f32[35,8,256]{2,1,0:T(8,128)S(1)}, u32[]{:S(2)}, u32[]{:S(2)}) collective-permute-start(f32[35,8,256]{2,1,0:T(8,128)S(1)} %get-tuple-element.40), channel_id=1, source_target_pairs={{16,0},{32,16},{48,32},{64,48},{80,64},{96,80},{112,96},{128,112},... | collective-permute-start | bytes 860168 | tf_op jit(solution)/shard_map/ppermute | solution.py:332
  12.7 5.6 %collective-permute-start.2 = (f32[3,64,128]{2,1,0:T(8,128)S(1)}, f32[3,64,128]{2,1,0:T(8,128)S(1)}, u32[]{:S(2)}, u32[]{:S(2)}) collective-permute-start(f32[3,64,128]{2,1,0:T(8,128)S(1)} %get-tuple-element.41), channel_id=1, source_target_pairs={{0,4},{4,8},{8,12},{1,5},{5,9},{9,13},{2,6},{6,10},{10,14},{3,7},{... | collective-permute-start | bytes 294920 | tf_op jit(solution)/shard_map/ppermute | solution.py:331
  16.1 6.5 %collective-permute-start.3 = (f32[3,64,128]{2,1,0:T(8,128)S(1)}, f32[3,64,128]{2,1,0:T(8,128)S(1)}, u32[]{:S(2)}, u32[]{:S(2)}) collective-permute-start(f32[3,64,128]{2,1,0:T(8,128)S(1)} %get-tuple-element.42), channel_id=1, source_target_pairs={{4,0},{8,4},{12,8},{5,1},{9,5},{13,9},{6,2},{10,6},{14,10},{7,3},{... | collective-permute-start | bytes 294920 | tf_op jit(solution)/shard_map/ppermute | solution.py:332
  35.1 1.2 copy-start.1
  36.2 1.2 copy-start.3
  37.4 1.2 copy-start.6
  38.6 1.1 copy-start.9
  39.7 1.2 copy-start.11
  40.9 33.6 %collective-permute-start.6 = (f32[64,384]{1,0:T(8,128)S(1)}, f32[64,384]{1,0:T(8,128)}, u32[]{:S(2)}, u32[]{:S(2)}) collective-permute-start(f32[64,384]{1,0:T(8,128)S(1)} %get-tuple-element.57.rest_0_), channel_id=1, source_target_pairs={{0,3},{1,0},{2,1},{3,2},{4,7},{5,4},{6,5},{7,6},{8,11},{9,8},{10,9... | collective-permute-start | bytes 294920 | tf_op jit(solution)/shard_map/ppermute | solution.py:325
  41.4 25.3 %all-to-all-start = ((f32[64,1,128]{2,1,0:T(1,128)}), f32[64,1,128]{2,1,0:T(1,128)S(1)}, u32[]{:S(2)}, u32[]{:S(2)}) async-start(f32[64,1,128]{2,1,0:T(1,128)} %bitcast.2), calls=%async_computation | async-start | bytes 65536 | tf_op jit(solution)/shard_map/all_to_all | solution.py:373
  57.0 21.3 %collective-permute-start.5 = (f32[64,384]{1,0:T(8,128)S(1)}, f32[64,384]{1,0:T(8,128)}, u32[]{:S(2)}, u32[]{:S(2)}) collective-permute-start(f32[64,384]{1,0:T(8,128)S(1)} %get-tuple-element.57.rest_0_), channel_id=1, source_target_pairs={{0,2},{1,3},{2,0},{3,1},{4,6},{5,7},{6,4},{7,5},{8,10},{9,11},{10,... | collective-permute-start | bytes 294920 | tf_op jit(solution)/shard_map/ppermute | solution.py:325
  59.7 18.7 %collective-permute-start.4 = (f32[64,384]{1,0:T(8,128)S(1)}, f32[64,384]{1,0:T(8,128)}, u32[]{:S(2)}, u32[]{:S(2)}) collective-permute-start(f32[64,384]{1,0:T(8,128)S(1)} %get-tuple-element.57.rest_0_), channel_id=1, source_target_pairs={{0,1},{1,2},{2,3},{3,0},{4,5},{5,6},{6,7},{7,4},{8,9},{9,10},{10,1... | collective-permute-start | bytes 294920 | tf_op jit(solution)/shard_map/ppermute | solution.py:325
  66.6 1.4 %copy-start.4 = (f32[16,64,384]{2,1,0:T(8,128)S(1)}, f32[16,64,384]{2,1,0:T(8,128)}, u32[]{:S(2)}) copy-start(f32[16,64,384]{2,1,0:T(8,128)} %copy-done.3) | copy-start | bytes 4718596
  68.0 1.4 %copy-start.7 = (f32[16,64,384]{2,1,0:T(8,128)S(1)}, f32[16,64,384]{2,1,0:T(8,128)}, u32[]{:S(2)}) copy-start(f32[16,64,384]{2,1,0:T(8,128)} %copy-done.6) | copy-start | bytes 4718596
  69.4 1.4 %copy-start.12 = (f32[16,64,384]{2,1,0:T(8,128)S(1)}, f32[16,64,384]{2,1,0:T(8,128)}, u32[]{:S(2)}) copy-start(f32[16,64,384]{2,1,0:T(8,128)} %copy-done.11) | copy-start | bytes 4718596
  70.9 9.8 %copy-start.2 = (f32[16,64,384]{2,1,0:T(8,128)S(1)}, f32[16,64,384]{2,1,0:T(8,128)}, u32[]{:S(2)}) copy-start(f32[16,64,384]{2,1,0:T(8,128)} %copy-done.1) | copy-start | bytes 4718596
  70.9 9.8 %copy-start.5 = (f32[16,64,384]{2,1,0:T(8,128)S(1)}, f32[16,64,384]{2,1,0:T(8,128)}, u32[]{:S(2)}) copy-start(f32[16,64,384]{2,1,0:T(8,128)} %copy-done.3) | copy-start | bytes 4718596
  70.9 9.8 %copy-start.10 = (f32[16,64,384]{2,1,0:T(8,128)S(1)}, f32[16,64,384]{2,1,0:T(8,128)}, u32[]{:S(2)}) copy-start(f32[16,64,384]{2,1,0:T(8,128)} %copy-done.9) | copy-start | bytes 4718596
  71.4 7.9 %collective-permute-start.9 = (f32[64,384]{1,0:T(8,128)S(1)}, f32[64,384]{1,0:T(8,128)S(1)}, u32[]{:S(2)}, u32[]{:S(2)}) collective-permute-start(f32[64,384]{1,0:T(8,128)S(1)} %get-tuple-element.58.rest_0_), channel_id=1, source_target_pairs={{0,3},{1,0},{2,1},{3,2},{4,7},{5,4},{6,5},{7,6},{8,11},{9,8},{10,9... | collective-permute-start | bytes 294920 | tf_op jit(solution)/shard_map/ppermute | solution.py:325
  74.5 6.1 %collective-permute-start.8 = (f32[64,384]{1,0:T(8,128)S(1)}, f32[64,384]{1,0:T(8,128)S(1)}, u32[]{:S(2)}, u32[]{:S(2)}) collective-permute-start(f32[64,384]{1,0:T(8,128)S(1)} %get-tuple-element.58.rest_0_), channel_id=1, source_target_pairs={{0,2},{1,3},{2,0},{3,1},{4,6},{5,7},{6,4},{7,5},{8,10},{9,11},{10,... | collective-permute-start | bytes 294920 | tf_op jit(solution)/shard_map/ppermute | solution.py:325
  74.6 6.1 %collective-permute-start.7 = (f32[64,384]{1,0:T(8,128)S(1)}, f32[64,384]{1,0:T(8,128)S(1)}, u32[]{:S(2)}, u32[]{:S(2)}) collective-permute-start(f32[64,384]{1,0:T(8,128)S(1)} %get-tuple-element.58.rest_0_), channel_id=1, source_target_pairs={{0,1},{1,2},{2,3},{3,0},{4,5},{5,6},{6,7},{7,4},{8,9},{9,10},{10,1... | collective-permute-start | bytes 294920 | tf_op jit(solution)/shard_map/ppermute | solution.py:325
  101.3 5.0 %collective-permute-start.12 = (f32[64,384]{1,0:T(8,128)S(1)}, f32[64,384]{1,0:T(8,128)S(1)}, u32[]{:S(2)}, u32[]{:S(2)}) collective-permute-start(f32[64,384]{1,0:T(8,128)S(1)} %get-tuple-element.67.rest_0_), channel_id=1, source_target_pairs={{0,3},{1,0},{2,1},{3,2},{4,7},{5,4},{6,5},{7,6},{8,11},{9,8},{10,9... | collective-permute-start | bytes 294920 | tf_op jit(solution)/shard_map/ppermute | solution.py:325
  103.5 6.1 %collective-permute-start.11 = (f32[64,384]{1,0:T(8,128)S(1)}, f32[64,384]{1,0:T(8,128)S(1)}, u32[]{:S(2)}, u32[]{:S(2)}) collective-permute-start(f32[64,384]{1,0:T(8,128)S(1)} %get-tuple-element.67.rest_0_), channel_id=1, source_target_pairs={{0,2},{1,3},{2,0},{3,1},{4,6},{5,7},{6,4},{7,5},{8,10},{9,11},{10,... | collective-permute-start | bytes 294920 | tf_op jit(solution)/shard_map/ppermute | solution.py:325
  104.3 5.3 %collective-permute-start.10 = (f32[64,384]{1,0:T(8,128)S(1)}, f32[64,384]{1,0:T(8,128)S(1)}, u32[]{:S(2)}, u32[]{:S(2)}) collective-permute-start(f32[64,384]{1,0:T(8,128)S(1)} %get-tuple-element.67.rest_0_), channel_id=1, source_target_pairs={{0,1},{1,2},{2,3},{3,0},{4,5},{5,6},{6,7},{7,4},{8,9},{9,10},{10,1... | collective-permute-start | bytes 294920 | tf_op jit(solution)/shard_map/ppermute | solution.py:325
  131.1 4.8 %collective-permute-start.15 = (f32[48,256]{1,0:T(8,128)S(1)}, f32[48,256]{1,0:T(8,128)S(1)}, u32[]{:S(2)}, u32[]{:S(2)}) collective-permute-start(f32[48,256]{1,0:T(8,128)S(1)} %get-tuple-element.73.rest_0_), channel_id=1, source_target_pairs={{0,3},{1,0},{2,1},{3,2},{4,7},{5,4},{6,5},{7,6},{8,11},{9,8},{10,9... | collective-permute-start | bytes 147464 | tf_op jit(solution)/shard_map/ppermute | solution.py:325
  133.6 5.6 %collective-permute-start.14 = (f32[48,256]{1,0:T(8,128)S(1)}, f32[48,256]{1,0:T(8,128)S(1)}, u32[]{:S(2)}, u32[]{:S(2)}) collective-permute-start(f32[48,256]{1,0:T(8,128)S(1)} %get-tuple-element.73.rest_0_), channel_id=1, source_target_pairs={{0,2},{1,3},{2,0},{3,1},{4,6},{5,7},{6,4},{7,5},{8,10},{9,11},{10,... | collective-permute-start | bytes 147464 | tf_op jit(solution)/shard_map/ppermute | solution.py:325
  134.0 5.2 %collective-permute-start.13 = (f32[48,256]{1,0:T(8,128)S(1)}, f32[48,256]{1,0:T(8,128)S(1)}, u32[]{:S(2)}, u32[]{:S(2)}) collective-permute-start(f32[48,256]{1,0:T(8,128)S(1)} %get-tuple-element.73.rest_0_), channel_id=1, source_target_pairs={{0,1},{1,2},{2,3},{3,0},{4,5},{5,6},{6,7},{7,4},{8,9},{9,10},{10,1... | collective-permute-start | bytes 147464 | tf_op jit(solution)/shard_map/ppermute | solution.py:325

commit v2 on v0

v2 whole, which is shorter than its diff:
```python
import functools
import jax
import jax.numpy as jnp
from jax import lax
from jax.experimental import pallas as pl
from jax.experimental.pallas import tpu as pltpu
from jax.sharding import PartitionSpec as P


ITERS = 3
HALO = 8
LANES = 128
HALF = LANES // 2
STEP = 64
VMEM_LIMIT = 12 * 1024 * 1024
HIGHEST = lax.Precision.HIGHEST
OUTSIDE = 1.6e38


def vspec():
    return pl.BlockSpec(memory_space=pltpu.VMEM)


def sspec():
    return pl.BlockSpec(memory_space=pltpu.SMEM)


def hspec():
    return pl.BlockSpec(memory_space=pl.ANY)


def call(kernel, outs, args, specs, scratch=(), flops=1000000, nbytes=1000000, name=None):
    return pl.pallas_call(
        kernel,
        out_shape=[jax.ShapeDtypeStruct(s, jnp.float32) for s in outs],
        in_specs=specs,
        out_specs=[vspec() for _ in outs],
        scratch_shapes=list(scratch),
        compiler_params=pltpu.CompilerParams(vmem_limit_bytes=VMEM_LIMIT),
        cost_estimate=pl.CostEstimate(flops=flops, bytes_accessed=nbytes, transcendentals=0),
        name=name,
    )(*args)


def lane_of(height=1):
    return lax.broadcasted_iota(jnp.int32, (height, LANES), 1)


def pieces(tall):
    cuts = [0, HALO]
    while cuts[-1] + STEP < tall - HALO:
        cuts.append(cuts[-1] + STEP)
    cuts += [tall - HALO, tall]
    return list(zip(cuts[:-1], cuts[1:]))


def pack_rows_kernel(groups, rows, flux, opacity, old, density, material, up, down, *scratch):
    copies = []
    sems = scratch[-1]
    for side, (lo, base) in enumerate(((0, 0), (rows - HALO, rows - 2 * HALO))):
        op_buf, old_buf, dens_buf, mat_buf = scratch[4 * side : 4 * side + 4]
        pairs = (
            (opacity.at[:, pl.ds(base, 2 * HALO), :], op_buf),
            (old.at[:, pl.ds(lo, HALO), :], old_buf),
            (density.at[pl.ds(lo, HALO), :], dens_buf),
            (material.at[pl.ds(lo, HALO), :], mat_buf),
        )
        for k, (src, dst) in enumerate(pairs):
            copies.append(pltpu.make_async_copy(src, dst, sems.at[4 * side + k]))
    for c in copies:
        c.start()
    for c in copies:
        c.wait()
    lane = lane_of(HALO)
    for side, (out, lo, inside, first) in enumerate(
        ((up, 0, 0, rows + HALO), (down, rows - HALO, HALO, 0))
    ):
        op_buf, old_buf, dens_buf, mat_buf = scratch[4 * side : 4 * side + 4]
        dens = dens_buf[...]
        for g in range(groups):
            out[g] = op_buf[g].astype(jnp.float32)[inside : inside + HALO, :] * dens
            out[groups + g] = old_buf[g]
        out[2 * groups] = dens
        out[2 * groups + 1] = mat_buf[...]
        vec = jnp.zeros((HALO, LANES), jnp.float32)
        for i in range(HALO):
            vec = jnp.where(lane % HALF == first + i, flux[lo + i], vec)
        out[2 * groups + 2, :, :LANES] = vec
        for at in range(LANES, out.shape[2], LANES):
            out[2 * groups + 2, :, at : at + LANES] = vec


def turn_kernel(
    groups, rows, cols, opacity, old, density, material, top, bottom,
    a_ref, e_ref, dens_ref, mat_ref, flux_ref, to_left, to_right,
):
    pairs = groups // 2
    flux_ref[...] = top[2 * groups + 2, :, :LANES] + bottom[2 * groups + 2, :, :LANES]
    for lo in range(0, cols, LANES):
        hi = lo + LANES

        def tile(plane, own):
            return jnp.concatenate([top[plane, :, lo:hi], own, bottom[plane, :, lo:hi]], axis=0)

        d = tile(2 * groups, density[:, lo:hi])
        d = jnp.concatenate([d, d], axis=0).T
        m = tile(2 * groups + 1, material[:, lo:hi])
        m = jnp.concatenate([m, m], axis=0).T
        dens_ref[lo:hi, :] = d
        mat_ref[lo:hi, :] = m

        def one(p, carry):
            both = []
            for h in range(2):
                g = 2 * p + h
                both.append(tile(g, opacity[g, :, lo:hi].astype(jnp.float32) * density[:, lo:hi]))
            a = jnp.concatenate(both, axis=0).T
            a_ref[p, lo:hi, :] = jnp.where(dens_ref[lo:hi, :] > 0.0, a, 1.0)
            both = [tile(groups + 2 * p + h, old[2 * p + h, :, lo:hi]) for h in range(2)]
            e_ref[p, lo:hi, :] = jnp.concatenate(both, axis=0).T
            return carry

        lax.fori_loop(0, pairs, one, 0)
    for out, lo in ((to_left, 0), (to_right, cols - HALO)):
        hi = lo + HALO
        for p in range(pairs):
            out[p] = a_ref[p, lo:hi, :]
            out[pairs + p] = e_ref[p, lo:hi, :]
        out[2 * pairs] = dens_ref[lo:hi, :]
        out[2 * pairs + 1] = mat_ref[lo:hi, :]


def next_row(v):
    return pltpu.roll(v, LANES - 1, 1)


def prev_row(v):
    return pltpu.roll(v, 1, 1)


def after(ref, lead, lo, hi, here):
    if hi < ref.shape[-2]:
        return ref[(*lead, slice(lo + 1, hi + 1), slice(None))]
    return pltpu.roll(here, hi - lo - 1, 0)


def before(ref, lead, lo, hi, here):
    if lo > 0:
        return ref[(*lead, slice(lo - 1, hi - 1), slice(None))]
    return pltpu.roll(here, 1, 0)


def at(lo, hi):
    return (slice(lo, hi), slice(None))


def flux_sum(p, lo, hi, v_ref, v, fr_ref, fp_ref):
    fp = fp_ref[(p, *at(lo, hi))]
    fp_before = before(fp_ref, (p,), lo, hi, fp)
    polar = fp * (v - after(v_ref, (p,), lo, hi, v)) + fp_before * (v - before(v_ref, (p,), lo, hi, v))
    fr = fr_ref[(p, *at(lo, hi))] * (v - next_row(v))
    return polar + (fr - prev_row(fr))


def tile_sum(v):
    acc = v[:HALO]
    for lo in range(HALO, v.shape[0], HALO):
        acc = acc + v[lo : lo + HALO]
    return acc


def krylov(p, pairs, a_ref, fr_ref, fp_ref, r_ref, q_ref, t_ref, mom):
    tall = r_ref.shape[1]
    sums = [jnp.zeros((HALO, LANES), jnp.float32) for _ in range(4)]
    for lo, hi in pieces(tall):
        r = r_ref[(p, *at(lo, hi))]
        q = r + a_ref[(p, *at(lo, hi))] * r + flux_sum(p, lo, hi, r_ref, r, fr_ref, fp_ref)
        q_ref[(p, *at(lo, hi))] = q
        if lo >= HALO and hi <= tall - HALO:
            sums[0] = sums[0] + tile_sum(r * r)
            sums[1] = sums[1] + tile_sum(r * q)
            sums[2] = sums[2] + tile_sum(q * q)
    for lo, hi in pieces(tall):
        own = lo >= HALO and hi <= tall - HALO
        if not own and t_ref is None:
            continue
        q = q_ref[(p, *at(lo, hi))]
        t = q + a_ref[(p, *at(lo, hi))] * q + flux_sum(p, lo, hi, q_ref, q, fr_ref, fp_ref)
        if t_ref is not None:
            t_ref[(p, *at(lo, hi))] = t
        if own:
            sums[3] = sums[3] + tile_sum(q * t)
    for k in range(4):
        mom[pl.ds(k * pairs + p, 1), :] = jnp.sum(sums[k], axis=0, keepdims=True)


def send_moments(pairs, rows, mom, out, row_sums):
    lane = lane_of(4 * pairs)
    x = mom[...]
    first = jnp.where((lane >= HALO) & (lane < HALO + rows), x, 0.0)
    second = jnp.where((lane >= HALF + HALO) & (lane < HALF + HALO + rows), x, 0.0)
    both = jnp.concatenate([first, second, jnp.zeros((LANES - 8 * pairs, LANES), jnp.float32)], axis=0)
    line = lax.dot_general(
        jnp.ones((HALO, LANES), jnp.float32), both, (((1,), (1,)), ((), ())),
        precision=HIGHEST, preferred_element_type=jnp.float32,
    )
    if row_sums is not None:
        line = jnp.where(lane_of(HALO) < HALF, line, row_sums)
    for lo in range(0, out.shape[0], HALO):
        out[lo : lo + HALO, :] = line


def weight_of(weights, p):
    return jnp.where(lane_of(HALO) < HALF, weights[2 * p], weights[2 * p + 1])[:1]


def fold(s):
    s = s + pltpu.roll(s, HALF, 1)
    middle = s.shape[0] // 2
    return jnp.where(lane_of(middle) < HALF, s[:middle], s[middle:])


def unfold(s):
    other = pltpu.roll(s, HALF, 1)
    low = lane_of(s.shape[0]) < HALF
    return jnp.where(low, s, other), jnp.where(low, other, s)


def start_kernel(
    groups, rows, cols, weights, a_in, e_in, dens_in, mat_in, left, right,
    a_ref, e_ref, fr_ref, fp_ref, r_ref, q_ref, t_ref, dens_ref, mat_ref, emit_out, out,
    inv, emit, mom,
):
    pairs = groups // 2
    tall = cols + 2 * HALO
    dens_ref[0:HALO, :] = left[2 * pairs]
    dens_ref[HALO : HALO + cols, :] = dens_in[...]
    dens_ref[HALO + cols :, :] = right[2 * pairs]
    mat_ref[0:HALO, :] = left[2 * pairs + 1]
    mat_ref[HALO : HALO + cols, :] = mat_in[...]
    mat_ref[HALO + cols :, :] = right[2 * pairs + 1]
    emit[...] = jnp.zeros(emit.shape, jnp.float32)

    def one(p, carry):
        w = weight_of(weights, p)
        for lo, hi in pieces(tall):
            if lo < HALO:
                a, e = left[p], left[pairs + p]
            elif hi > tall - HALO:
                a, e = right[p], right[pairs + p]
            else:
                a, e = (ref[(p, *at(lo - HALO, hi - HALO))] for ref in (a_in, e_in))
            if lo < HALO or hi > tall - HALO:
                a = jnp.where(dens_ref[lo:hi, :] > 0.0, a, 1.0)
            a_ref[(p, *at(lo, hi))] = a
            e_ref[(p, *at(lo, hi))] = e
            emit[lo:hi, :] += a * w
        for lo, hi in pieces(tall):
            a, e = a_ref[(p, *at(lo, hi))], e_ref[(p, *at(lo, hi))]
            slope_r = 0.5 * (next_row(e) - prev_row(e))
            slope_p = 0.5 * (after(e_ref, (p,), lo, hi, e) - before(e_ref, (p,), lo, hi, e))
            n2 = slope_r * slope_r + slope_p * slope_p
            u = a * e
            s = 2.0 * u + jnp.sqrt(n2)
            inv[lo:hi, :] = jnp.where(dens_ref[lo:hi, :] > 0.0, (n2 + 3.0 * u * s) / (e * s), OUTSIDE)
        for lo, hi in pieces(tall):
            d = inv[lo:hi, :]
            fr_ref[(p, *at(lo, hi))] = 2.0 / (d + next_row(d))
            fp_ref[(p, *at(lo, hi))] = 2.0 / (d + after(inv, (), lo, hi, d))
        for lo, hi in pieces(tall):
            a, e = a_ref[(p, *at(lo, hi))], e_ref[(p, *at(lo, hi))]
            r_ref[(p, *at(lo, hi))] = a * (w * mat_ref[lo:hi, :] - e) - flux_sum(
                p, lo, hi, e_ref, e, fr_ref, fp_ref
            )
        krylov(p, pairs, a_ref, fr_ref, fp_ref, r_ref, q_ref, t_ref, mom)
        return carry

    lax.fori_loop(0, pairs, one, 0)
    emit_out[...] = fold(emit[...])
    row_sums = jnp.sum(tile_sum(dens_in[...]), axis=0, keepdims=True)
    send_moments(pairs, rows, mom, out, row_sums)


def steps(pairs, gathered):
    total = jnp.sum(gathered[...], axis=0, keepdims=True)
    lane = lane_of(pairs)
    sub = lax.broadcasted_iota(jnp.int32, (pairs, LANES), 0)

    def moment(k):
        first, second = (
            jnp.sum(jnp.where(lane == sub + (4 * h + k) * pairs, total, 0.0), axis=1, keepdims=True)
            for h in range(2)
        )
        return jnp.where(lane < HALF, first, second)

    m0, m1, m2, m3 = (moment(k) for k in range(4))
    k1, k2, k3 = m1 / m0, m2 / m0, m3 / m0
    first = 1.0 / k1
    det = jnp.maximum(k2 - k1 * k1, 0.0)
    beta = det / (k1 * k1)
    low = k1 * k3 - k2 * k2
    second = jnp.minimum(jnp.where(low > 0.0, k1 * det / low, 0.0), 1.0)
    return first + second * (1.0 + beta), first * second


def absorbed(pairs, c1, c2, a_ref, e_ref, r_ref, q_ref, e_out, s):
    tall = a_ref.shape[1]
    for lo, hi in pieces(tall):
        total = jnp.zeros((hi - lo, LANES), jnp.float32)
        for p in range(pairs):
            e = (
                e_ref[(p, *at(lo, hi))]
                + c1[p : p + 1, :] * r_ref[(p, *at(lo, hi))]
                - c2[p : p + 1, :] * q_ref[(p, *at(lo, hi))]
            )
            e_out[(p, *at(lo, hi))] = e
            total = total + a_ref[(p, *at(lo, hi))] * e
        s[lo:hi, :] = total


def update_kernel(pairs, gathered, a_ref, e_ref, r_ref, q_ref, *rest):
    if len(rest) == 6:
        emit, *rest = rest
    else:
        emit = None
    e_out, s_out, c1_ref, c2_ref, s = rest
    c1, c2 = steps(pairs, gathered)
    c1_ref[...] = c1
    c2_ref[...] = c2
    absorbed(pairs, c1, c2, a_ref, e_ref, r_ref, q_ref, e_out, s)
    s_out[0] = fold(s[...])
    if emit is not None:
        s_out[1] = emit[...]


def last_update_kernel(pairs, cols, gathered, a_ref, e_ref, r_ref, q_ref, e_out, s_out, s):
    c1, c2 = steps(pairs, gathered)
    absorbed(pairs, c1, c2, a_ref, e_ref, r_ref, q_ref, e_out, s)
    s_out[...] = fold(s[HALO : HALO + cols, :])


def energy_kernel(pairs, rows, cols, e_ref, out):
    def one(p, carry):
        for lo in range(0, cols, LANES):
            block = e_ref[p, HALO + lo : HALO + lo + LANES, :].T
            out[2 * p, :, lo : lo + LANES] = block[HALO : HALO + rows]
            out[2 * p + 1, :, lo : lo + LANES] = block[HALF + HALO : HALF + HALO + rows]
        return carry

    lax.fori_loop(0, pairs, one, 0)


def turned_back(v, rows):
    parts = [v[lo : lo + LANES].T[HALO : HALO + rows] for lo in range(0, v.shape[0], LANES)]
    return jnp.concatenate(parts, axis=1)


def heating_kernel(
    groups, rows, cols, polar_count, place, flux, gathered, dens_ref, mat_ref, flux_ref, column_out, fixed_out
):
    tall = dens_ref.shape[0]
    radius, polar = place[0], place[1]
    dens = dens_ref[...]
    row_id = lax.broadcasted_iota(jnp.int32, gathered.shape, 0)
    ahead = (row_id >= radius * polar_count) & (row_id < radius * polar_count + polar)
    carried = jnp.sum(jnp.where(ahead, gathered[...], 0.0), axis=0, keepdims=True)
    lane = lane_of()
    carried = jnp.where(lane < HALF, pltpu.roll(carried, HALF, 1), carried)
    dst = lax.broadcasted_iota(jnp.int32, (tall, tall), 0)
    src = lax.broadcasted_iota(jnp.int32, (tall, tall), 1)
    coeff = jnp.where(
        (src >= HALO) & (src <= dst), 1.0, jnp.where((src < HALO) & (src > dst), -1.0, 0.0)
    )
    within = lax.dot_general(
        coeff, dens, (((1,), (0,)), ((), ())), precision=HIGHEST, preferred_element_type=jnp.float32
    )
    column = 2.0 / (cols * polar_count) * (carried + within)
    vec = flux_ref[0:1, :]
    for i in range(rows):
        vec = jnp.where(lane % HALF == HALO + i, flux[i], vec)
    fixed_out[...] = 16.0 * dens * mat_ref[...] + vec * dens * jnp.exp(-column)
    column_out[...] = turned_back(column[HALO : HALO + cols], rows)


def summed(refs, lead=()):
    total = refs[0][(*lead, ...)]
    for s in refs[1:]:
        total = total + s[(*lead, ...)]
    return total


def next_kernel(groups, rows, count, turn, last, weights, c1_ref, c2_ref, a_ref, fr_ref, fp_ref, r_in, q_in, t_in, fixed, cap_in, mat_ref, *rest):
    pairs = groups // 2
    sums = rest[:count]
    rest = rest[count:]
    outs, (delta, mom) = rest[:-2], rest[-2:]
    r_ref, q_ref, out, *outs = outs
    t_ref = None if last else outs.pop(0)
    m_ref = None if last else outs.pop(0)
    half = fixed.shape[0] // 2
    folded = summed(sums, (0,))
    if turn == 0:
        cap_out = outs.pop(0)
        dens = cap_in[...]
        emits = jnp.concatenate(unfold(summed(sums, (1,))), axis=0)
        cap_out[...] = 16.0 * jnp.where(dens > 0.0, dens, 1.0) + emits
        cap_in = cap_out
    for k, total in enumerate(unfold(folded)):
        here = at(k * half, (k + 1) * half)
        nxt = (fixed[here] + total) / cap_in[here]
        delta[here] = nxt - mat_ref[here]
        if m_ref is not None:
            m_ref[here] = nxt

    def one(p, carry):
        w = weight_of(weights, p)
        c1 = c1_ref[pl.ds(p, 1), :]
        c2 = c2_ref[pl.ds(p, 1), :]
        for lo, hi in pieces(r_ref.shape[1]):
            here = (p, *at(lo, hi))
            r_ref[here] = (
                r_in[here] - c1 * q_in[here] + c2 * t_in[here] + a_ref[here] * (w * delta[lo:hi, :])
            )
        krylov(p, pairs, a_ref, fr_ref, fp_ref, r_ref, q_ref, t_ref, mom)
        return carry

    lax.fori_loop(0, pairs, one, 0)
    send_moments(pairs, rows, mom, out, None)


def material_kernel(count, rows, cols, fixed, capacity, *rest):
    sums, out = rest[:count], rest[count]
    total = jnp.concatenate(unfold(summed(sums)), axis=0)
    here = at(HALO, HALO + cols)
    out[...] = turned_back((fixed[here] + total) / capacity[here], rows)


def spread(part, axis):
    count = lax.axis_size(axis)
    return [part] + [
        lax.ppermute(part, axis, [(i, (i + s) % count) for i in range(count)]) for s in range(1, count)
    ]


def shifted(upward, downward, axis):
    count = lax.axis_size(axis)
    from_lower = lax.ppermute(downward, axis, [(i, i + 1) for i in range(count - 1)])
    from_upper = lax.ppermute(upward, axis, [(i + 1, i) for i in range(count - 1)])
    return from_lower, from_upper


def per_device(density, opacity, radiation_old, material_old, weights, stellar_flux):
    groups, rows, cols = opacity.shape
    pairs, tall = groups // 2, cols + 2 * HALO
    assert rows + 2 * HALO == HALF
    polar_count = lax.axis_size("polar")
    count = lax.axis_size("group")
    devices = lax.axis_size("radius") * polar_count
    place = jnp.stack([lax.axis_index("radius"), lax.axis_index("polar")]).astype(jnp.int32)
    planes = 2 * groups + 3
    big, flat, core = (pairs, tall, LANES), (tall, LANES), (cols, LANES)
    line = (devices, LANES)
    vmem = lambda shape: pltpu.VMEM(shape, jnp.float32)

    strips = [
        pltpu.VMEM((groups, 2 * HALO, cols), jnp.bfloat16),
        vmem((groups, HALO, cols)),
        vmem((HALO, cols)),
        vmem((HALO, cols)),
    ]
    up, down = call(
        functools.partial(pack_rows_kernel, groups, rows),
        [(planes, HALO, cols)] * 2,
        (stellar_flux, opacity, radiation_old, density, material_old),
        [sspec()] + [hspec()] * 4,
        scratch=strips * 2 + [pltpu.SemaphoreType.DMA((8,))],
        name="pack_rows",
    )
    top, bottom = shifted(up, down, "radius")
    a, e, dens, mat, flux_lanes, to_left, to_right = call(
        functools.partial(turn_kernel, groups, rows, cols),
        [(pairs, *core)] * 2 + [core, core, (HALO, LANES)] + [(2 * pairs + 2, HALO, LANES)] * 2,
        (opacity, radiation_old, density, material_old, top, bottom),
        [vspec()] * 6,
        name="turn",
    )
    left, right = shifted(to_left, to_right, "polar")
    a, e, fr, fp, r, q, t, dens, mat, emit, out = call(
        functools.partial(start_kernel, groups, rows, cols),
        [big] * 7 + [flat, flat, (tall // 2, LANES), line],
        (weights, a, e, dens, mat, left, right),
        [sspec()] + [vspec()] * 6,
        scratch=[vmem(flat), vmem(flat), vmem((4 * pairs, LANES))],
        name="start",
    )
    capacity = dens
    for turn in range(ITERS):
        gathered = lax.all_to_all(out, ("radius", "polar"), 0, 0, tiled=True)
        if turn + 1 == ITERS:
            e, part = call(
                functools.partial(last_update_kernel, pairs, cols),
                [big, (cols // 2, LANES)],
                (gathered, a, e, r, q),
                [vspec()] * 5,
                scratch=[vmem(flat)],
                name="last_update",
            )
            sums = spread(part, "group")
            (energy,) = call(
                functools.partial(energy_kernel, pairs, rows, cols),
                [(groups, rows, cols)],
                (e,),
                [vspec()],
                name="energy",
            )
            (mat,) = call(
                functools.partial(material_kernel, count, rows, cols),
                [(rows, cols)],
                (fixed, capacity, *sums),
                [vspec()] * (2 + count),
                name="material",
            )
            break
        first, last = turn == 0, turn + 2 == ITERS
        extra = [emit] if first else []
        e, part, c1, c2 = call(
            functools.partial(update_kernel, pairs),
            [big, (1 + len(extra), tall // 2, LANES), (pairs, LANES), (pairs, LANES)],
            (gathered, a, e, r, q, *extra),
            [vspec()] * (5 + len(extra)),
            scratch=[vmem(flat)],
            name="update",
        )
        sums = spread(part, "group")
        if first:
            column, fixed = call(
                functools.partial(heating_kernel, groups, rows, cols, polar_count),
                [(rows, cols), flat],
                (place, stellar_flux, gathered, dens, mat, flux_lanes),
                [sspec()] * 2 + [vspec()] * 4,
                name="heating",
            )
        r, q, out, *more = call(
            functools.partial(next_kernel, groups, rows, count, turn, last),
            [big, big, line] + ([] if last else [big, flat]) + ([flat] if first else []),
            (weights, c1, c2, a, fr, fp, r, q, t, fixed, capacity, mat, *sums),
            [sspec()] + [vspec()] * (11 + count),
            scratch=[vmem(flat), vmem((4 * pairs, LANES))],
            name="next",
        )
        if not last:
            t, mat, *more = more
        if first:
            (capacity,) = more
    return (energy, mat, column)


def solution(mesh):
    return jax.shard_map(
        per_device,
        mesh=mesh,
        in_specs=(
            P("radius", "polar"),
            P("group", "radius", "polar"),
            P("group", "radius", "polar"),
            P("radius", "polar"),
            P("group"),
            P("radius"),
        ),
        out_specs=(P("group", "radius", "polar"), P("radius", "polar"), P("radius", "polar")),
        check_vma=False,
    )
```

time: 1490 us -> 129 us (0.09)
  blocking collectives: 1170 us -> 52.1 us
  waiting for transfers between devices: 146 us -> 16.1 us
  other arithmetic: 52.9 us -> 0.07 us
  starting transfers between devices: 71.5 us -> 22.4 us
  Pallas kernels: 0 us -> 23.5 us
    psum x11 -> x0, blocking collectives: 1170 us -> none  [the longest x6 755 us: group_norms(): return lax.psum(local_dot(residual, residual), ('radius', 'polar'))]
    ppermute x32 -> x13, waiting for transfers between devices: 93.9 us -> 16.1 us  [the longest x2 8.13 us: shifted(): lax.ppermute(upward, axis, [(i + 1, i) for i in range(count - 1)])]
    psum x1 -> x0, waiting for transfers between devices: 52.5 us -> none  [per_device(): material_next = (fixed_terms + lax.psum(absorbed_local, 'group')) / capacity]
    all_to_all x0 -> x3, blocking collectives: none -> 52.1 us  [per_device(): gathered = lax.all_to_all(out, ('radius', 'polar'), 0, 0, tiled=True)]
    ppermute x32 -> x13, starting transfers between devices: 71.4 us -> 22.4 us  [the longest x9 14.6 us: spread(): lax.ppermute(part, axis, [(i, (i + s) % count) for i in range(count)])]
    reduce_sum x13 -> x0, other arithmetic: 35.8 us -> none  [the longest x9 25.3 us: local_dot(): return jnp.sum(left_field * right_field, axis=(1, 2))]
    pallas_call x0 -> x11, Pallas kernels: none -> 23.5 us  [call(): pl.pallas_call(kernel, out_shape=[jax.ShapeDtypeStruct(s, jnp.float32) fo...]
  transfers between devices with their start and end apart: 33 -> 13, of which waited for: 23 -> 7; matrix products, arithmetic and copies ran while one was open for 0% -> 0% of each run, Pallas kernels for 0% -> 3%
where the time goes in v2:
time: 129 us; the launch traced here: 127 us
  blocking collectives  52.1 us (40%)
  Pallas kernels  23.5 us (18%)
  starting transfers between devices  22.4 us (17%)
  waiting for transfers between devices  16.1 us (12%)
  local copies, waits for them, and re-layouts  12 us (9%)
    all_to_all x3, blocking collectives, per_device(): gathered = lax.all_to_all(out, ('radius', 'polar'), 0, 0, tiled=True)  52.1 us
    pallas_call x11, Pallas kernels, call(): pl.pallas_call(kernel, out_shape=[jax.ShapeDtypeStruct(s, jnp.float32) fo...  23.5 us
    ppermute x9, starting transfers between devices, spread(): lax.ppermute(part, axis, [(i, (i + s) % count) for i in range(count)])  14.6 us
    unnamed x46, local copies, waits for them, and re-layouts  12 us
    ppermute x2, waiting for transfers between devices, shifted(): lax.ppermute(upward, axis, [(i + 1, i) for i in range(count - 1)])  8.13 us
    ppermute x9, waiting for transfers between devices, spread(): lax.ppermute(part, axis, [(i, (i + s) % count) for i in range(count)])  7.36 us
    ppermute x2, starting transfers between devices, shifted(): lax.ppermute(downward, axis, [(i, i + 1) for i in range(count - 1)])  5.16 us
    ppermute x2, starting transfers between devices, shifted(): lax.ppermute(upward, axis, [(i + 1, i) for i in range(count - 1)])  2.58 us
  transfers between devices with their start and end apart: 13, of which 7 were waited for; matrix products, arithmetic and copies ran while one was open for 0% of the time, Pallas kernels for 3%

profile of v2, /device:TPU:8, one launch (start us, length us, event | category | flops | bytes accessed | tf_op | source)
XLA Modules:
  0.0 126.9 jit_solution(15986892024072849602)
XLA Ops:
  0.6 1.1 copy-done.6
  1.8 1.0 copy-done.8
  2.8 0.8 copy-done.16
  3.6 0.8 copy-done.18
  4.4 0.7 copy-done.21
  5.0 0.8 pack_rows.1
  5.8 0.0 copy-start.20
  5.8 1.8 %collective-permute-start = (f32[35,8,256]{2,1,0:T(8,128)S(1)}, f32[35,8,256]{2,1,0:T(8,128)S(1)}, u32[]{:S(2)}, u32[]{:S(2)}) collective-permute-start(f32[35,8,256]{2,1,0:T(8,128)S(1)} %get-tuple-element.44), channel_id=1, source_target_pairs={{0,16},{16,32},{32,48},{48,64},{64,80},{80,96},{96,112},{112,128},... | collective-permute-start | bytes 860168 | tf_op jit(solution)/shard_map/ppermute | solution.py:447
  7.6 1.3 %collective-permute-start.1 = (f32[35,8,256]{2,1,0:T(8,128)S(1)}, f32[35,8,256]{2,1,0:T(8,128)S(1)}, u32[]{:S(2)}, u32[]{:S(2)}) collective-permute-start(f32[35,8,256]{2,1,0:T(8,128)S(1)} %get-tuple-element.45), channel_id=1, source_target_pairs={{16,0},{32,16},{48,32},{64,48},{80,64},{96,80},{112,96},{128,112},... | collective-permute-start | bytes 860168 | tf_op jit(solution)/shard_map/ppermute | solution.py:448
  8.9 3.8 %collective-permute-done.1.bottom = f32[35,8,256]{2,1,0:T(8,128)S(1)} collective-permute-done((f32[35,8,256]{2,1,0:T(8,128)S(1)}, f32[35,8,256]{2,1,0:T(8,128)S(1)}, u32[]{:S(2)}, u32[]{:S(2)}) %collective-permute-start.1) | collective-permute-done | bytes 286752 | tf_op jit(solution)/shard_map/ppermute | solution.py:448
  12.7 1.8 %turn.1 = (f32[8,256,128]{2,1,0:T(8,128)S(1)}, f32[8,256,128]{2,1,0:T(8,128)S(1)}, f32[256,128]{1,0:T(8,128)S(1)}, f32[256,128]{1,0:T(8,128)S(1)}, f32[8,128]{1,...) custom-call(bf16[16,48,256]{2,1,0:T(8,128)(2,1)S(1)} %copy-done.8, f32[16,48,256]{2,1,0:T(8,128)S(1)} %copy-done.7, ...), custom_call_target="tpu_custom_call" | custom-call | flops 1000000 | bytes 1000000 | tf_op jit(solution)/shard_map/turn/pallas_call | solution.py:33
  14.6 3.4 %collective-permute-start.2 = (f32[18,8,128]{2,1,0:T(8,128)S(1)}, f32[18,8,128]{2,1,0:T(8,128)S(1)}, u32[]{:S(2)}, u32[]{:S(2)}) collective-permute-start(f32[18,8,128]{2,1,0:T(8,128)S(1)} %get-tuple-element.50), channel_id=1, source_target_pairs={{0,4},{4,8},{8,12},{1,5},{5,9},{9,13},{2,6},{6,10},{10,14},{3,7},{... | collective-permute-start | bytes 221192 | tf_op jit(solution)/shard_map/ppermute | solution.py:447
  18.0 1.3 %collective-permute-start.3 = (f32[18,8,128]{2,1,0:T(8,128)S(1)}, f32[18,8,128]{2,1,0:T(8,128)S(1)}, u32[]{:S(2)}, u32[]{:S(2)}) collective-permute-start(f32[18,8,128]{2,1,0:T(8,128)S(1)} %get-tuple-element.51), channel_id=1, source_target_pairs={{4,0},{8,4},{12,8},{5,1},{9,5},{13,9},{6,2},{10,6},{14,10},{7,3},{... | collective-permute-start | bytes 221192 | tf_op jit(solution)/shard_map/ppermute | solution.py:448
  19.3 0.7 collective-permute-done.2.left
  19.9 4.3 %collective-permute-done.3.right = f32[18,8,128]{2,1,0:T(8,128)S(1)} collective-permute-done((f32[18,8,128]{2,1,0:T(8,128)S(1)}, f32[18,8,128]{2,1,0:T(8,128)S(1)}, u32[]{:S(2)}, u32[]{:S(2)}) %collective-permute-start.3) | collective-permute-done | bytes 73760 | tf_op jit(solution)/shard_map/ppermute | solution.py:448
  24.2 6.5 %start.1 = (f32[8,272,128]{2,1,0:T(8,128)S(1)}, f32[8,272,128]{2,1,0:T(8,128)S(1)}, f32[8,272,128]{2,1,0:T(8,128)S(1)}, f32[8,272,128]{2,1,0:T(8,128)S(1)}, f32[...) custom-call(f32[16]{0:T(128)S(1)} %copy-done.20, ...), custom_call_target="tpu_custom_call" | custom-call | flops 1000000 | bytes 1000000 | tf_op jit(solution)/shard_map/start/pallas_call | solution.py:33
  30.8 1.0 copy-done.3
  31.8 25.1 %all_to_all.33 = f32[64,1,128]{2,1,0:T(1,128)S(1)} all-to-all(f32[64,1,128]{2,1,0:T(1,128)S(1)} %bitcast.18), channel_id=1, replica_groups=mesh['radius'=16,'polar'=4,'group'=4] {'radius','polar'}, dimensions={0} | all-to-all | bytes 65536 | tf_op jit(solution)/shard_map/all_to_all | solution.py:498
  56.9 1.1 update.2
  58.0 1.0 copy-done.11
  59.0 0.4 collective-permute-start.6
  59.5 2.6 %collective-permute-start.5 = (f32[2,136,128]{2,1,0:T(8,128)}, f32[2,136,128]{2,1,0:T(8,128)}, u32[]{:S(2)}, u32[]{:S(2)}) collective-permute-start(f32[2,136,128]{2,1,0:T(8,128)} %get-tuple-element.67.rest_0_), channel_id=1, source_target_pairs={{0,2},{1,3},{2,0},{3,1},{4,6},{5,7},{6,4},{7,5},{8,10},{9,11},{10,... | collective-permute-start | bytes 417800 | tf_op jit(solution)/shard_map/ppermute | solution.py:441
  62.1 1.9 %collective-permute-start.4 = (f32[2,136,128]{2,1,0:T(8,128)}, f32[2,136,128]{2,1,0:T(8,128)}, u32[]{:S(2)}, u32[]{:S(2)}) collective-permute-start(f32[2,136,128]{2,1,0:T(8,128)} %get-tuple-element.67.rest_0_), channel_id=1, source_target_pairs={{0,1},{1,2},{2,3},{3,0},{4,5},{5,6},{6,7},{7,4},{8,9},{9,10},{10,1... | collective-permute-start | bytes 417800 | tf_op jit(solution)/shard_map/ppermute | solution.py:441
  64.0 0.1 pad_add_fusion.place
  64.1 0.9 copy-done.14
  65.0 1.7 %heating.1 = (f32[48,256]{1,0:T(8,128)}, f32[272,128]{1,0:T(8,128)S(1)}) custom-call(s32[2]{0:T(128)S(1)} %pad_add_fusion.place, f32[48]{0:T(128)S(1)} %copy-done.22, f32[64,128]{1,0:T(8,128)S(1)} %bitcast.15, f32[272,128]{1,0:T(8,128)S(1)} %get-tuple-element.63.dens_ref.cap_in, f32[272,128]{1,0:T(8,128)S(1)} %copy-done.14, ...), custom_call_target="tpu_custom_call" | custom-call | flops 1000000 | bytes 1000000 | tf_op jit(solution)/shard_map/heating/pallas_call | solution.py:33
  66.7 1.8 %collective-permute-done.5.rest_2_ = f32[2,136,128]{2,1,0:T(8,128)} collective-permute-done((f32[2,136,128]{2,1,0:T(8,128)}, f32[2,136,128]{2,1,0:T(8,128)}, u32[]{:S(2)}, u32[]{:S(2)}) %collective-permute-start.5) | collective-permute-done | bytes 139296 | tf_op jit(solution)/shard_map/ppermute | solution.py:441
  68.5 0.8 collective-permute-done.4.rest_1_
  69.3 1.2 copy-done.1
  70.5 1.2 copy-done.4
  71.8 1.2 copy-done.10
  73.0 0.9 copy-done.15
  73.9 4.3 %next.2 = (f32[8,272,128]{2,1,0:T(8,128)S(1)}, f32[8,272,128]{2,1,0:T(8,128)S(1)}, f32[64,128]{1,0:T(8,128)S(1)}, f32[8,272,128]{2,1,0:T(8,128)S(1)}, f32[272,128]{1,0:T(8,128)S(1)}, /*index=5*/f32[272,128]{1,0:T(8,128)S(1)}) custom-call(f32[16]{0:T(128)S(1)} %copy-done.20, f32[8,128]{1,0:T(8,128)S(1)} %get-tuple-element.58.c1_ref, ...), custom_call_target="tpu_custom_call" | custom-call | flops 1000000 | bytes 1000000 | tf_op jit(solution)/shard_map/next/pallas_call | solution.py:33
  78.3 13.5 %all_to_all.34 = f32[64,1,128]{2,1,0:T(1,128)S(1)} all-to-all(f32[64,1,128]{2,1,0:T(1,128)S(1)} %bitcast.19), channel_id=1, replica_groups=mesh['radius'=16,'polar'=4,'group'=4] {'radius','polar'}, dimensions={0} | all-to-all | bytes 65536 | tf_op jit(solution)/shard_map/all_to_all | solution.py:498
  91.8 0.5 update.3
  92.3 3.0 %collective-permute-start.9 = (f32[1,136,128]{2,1,0:T(8,128)S(1)}, f32[1,136,128]{2,1,0:T(8,128)S(1)}, u32[]{:S(2)}, u32[]{:S(2)}) collective-permute-start(f32[1,136,128]{2,1,0:T(8,128)S(1)} %get-tuple-element.77.rest_0_), channel_id=1, source_target_pairs={{0,3},{1,0},{2,1},{3,2},{4,7},{5,4},{6,5},{7,6},{8,11},{9,8},{10,9... | collective-permute-start | bytes 208904 | tf_op jit(solution)/shard_map/ppermute | solution.py:441
  95.2 0.0 collective-permute-start.8
  95.3 2.0 %collective-permute-start.7 = (f32[1,136,128]{2,1,0:T(8,128)S(1)}, f32[1,136,128]{2,1,0:T(8,128)S(1)}, u32[]{:S(2)}, u32[]{:S(2)}) collective-permute-start(f32[1,136,128]{2,1,0:T(8,128)S(1)} %get-tuple-element.77.rest_0_), channel_id=1, source_target_pairs={{0,1},{1,2},{2,3},{3,0},{4,5},{5,6},{6,7},{7,4},{8,9},{9,10},{10,1... | collective-permute-start | bytes 208904 | tf_op jit(solution)/shard_map/ppermute | solution.py:441
  97.3 3.8 %collective-permute-done.8.rest_2_ = f32[1,136,128]{2,1,0:T(8,128)S(1)} collective-permute-done((f32[1,136,128]{2,1,0:T(8,128)S(1)}, f32[1,136,128]{2,1,0:T(8,128)S(1)}, u32[]{:S(2)}, u32[]{:S(2)}) %collective-permute-start.8) | collective-permute-done | bytes 69664 | tf_op jit(solution)/shard_map/ppermute | solution.py:441
  101.1 3.7 %next.3 = (f32[8,272,128]{2,1,0:T(8,128)S(1)}, f32[8,272,128]{2,1,0:T(8,128)S(1)}, f32[64,128]{1,0:T(8,128)S(1)}) custom-call(f32[16]{0:T(128)S(1)} %copy-done.20, f32[8,128]{1,0:T(8,128)S(1)} %get-tuple-element.72.c1_ref, f32[8,128]{1,0:T(8,128)S(1)} %get-tuple-element.73.c2_ref, f32[8,272,128]{2,1,0:T(8,128)S(1)} %get-tuple-element.53.a_ref, ...), custom_call_target="tpu_custom_call" | custom-call | flops 1000000 | bytes 1000000 | tf_op jit(solution)/shard_map/next/pallas_call | solution.py:33
  104.8 13.5 %all_to_all.35 = f32[64,1,128]{2,1,0:T(1,128)S(1)} all-to-all(f32[64,1,128]{2,1,0:T(1,128)S(1)} %bitcast.20), channel_id=1, replica_groups=mesh['radius'=16,'polar'=4,'group'=4] {'radius','polar'}, dimensions={0} | all-to-all | bytes 65536 | tf_op jit(solution)/shard_map/all_to_all | solution.py:498
  118.3 0.5 last_update.1
  118.7 1.6 %collective-permute-start.12 = (f32[128,128]{1,0:T(8,128)S(1)}, f32[128,128]{1,0:T(8,128)S(1)}, u32[]{:S(2)}, u32[]{:S(2)}) collective-permute-start(f32[128,128]{1,0:T(8,128)S(1)} %get-tuple-element.83.rest_0_), channel_id=1, source_target_pairs={{0,3},{1,0},{2,1},{3,2},{4,7},{5,4},{6,5},{7,6},{8,11},{9,8},{10,9... | collective-permute-start | bytes 196616 | tf_op jit(solution)/shard_map/ppermute | solution.py:441
  120.3 0.6 collective-permute-start.11
  120.9 2.5 %collective-permute-start.10 = (f32[128,128]{1,0:T(8,128)S(1)}, f32[128,128]{1,0:T(8,128)S(1)}, u32[]{:S(2)}, u32[]{:S(2)}) collective-permute-start(f32[128,128]{1,0:T(8,128)S(1)} %get-tuple-element.83.rest_0_), channel_id=1, source_target_pairs={{0,1},{1,2},{2,3},{3,0},{4,5},{5,6},{6,7},{7,4},{8,9},{9,10},{10,1... | collective-permute-start | bytes 196616 | tf_op jit(solution)/shard_map/ppermute | solution.py:441
  123.4 1.7 %energy.1 = f32[16,48,256]{2,1,0:T(8,128)} custom-call(f32[8,272,128]{2,1,0:T(8,128)S(1)} %get-tuple-element.82.e_ref), custom_call_target="tpu_custom_call" | custom-call | flops 1000000 | bytes 1000000 | tf_op jit(solution)/shard_map/energy/pallas_call | solution.py:33
  125.1 1.0 collective-permute-done.11.rest_2_
  126.1 0.8 material.5
  (39 shorter events, 0.1 us)
Async XLA Ops:
  0.6 1.1 copy-start.6
  1.8 1.0 copy-start.8
  2.8 0.8 copy-start.16
  3.6 0.8 copy-start.18
  4.4 0.7 copy-start.21
  5.0 7.7 %copy-start.7 = (f32[16,48,256]{2,1,0:T(8,128)S(1)}, f32[16,48,256]{2,1,0:T(8,128)}, u32[]{:S(2)}) copy-start(f32[16,48,256]{2,1,0:T(8,128)} %old.3) | copy-start | bytes 2359300
  5.0 7.7 %copy-start.17 = (f32[48,256]{1,0:T(8,128)S(1)}, f32[48,256]{1,0:T(8,128)}, u32[]{:S(2)}) copy-start(f32[48,256]{1,0:T(8,128)} %density.3) | copy-start | bytes 147460
  5.0 7.7 %copy-start.19 = (f32[48,256]{1,0:T(8,128)S(1)}, f32[48,256]{1,0:T(8,128)}, u32[]{:S(2)}) copy-start(f32[48,256]{1,0:T(8,128)} %material.4) | copy-start | bytes 147460
  5.8 18.4 %copy-start.20 = (f32[16]{0:T(128)S(1)}, f32[16]{0:T(128)}, u32[]{:S(2)}) copy-start(f32[16]{0:T(128)} %weights.5) | copy-start | bytes 196
  5.8 3.1 %collective-permute-start = (f32[35,8,256]{2,1,0:T(8,128)S(1)}, f32[35,8,256]{2,1,0:T(8,128)S(1)}, u32[]{:S(2)}, u32[]{:S(2)}) collective-permute-start(f32[35,8,256]{2,1,0:T(8,128)S(1)} %get-tuple-element.44), channel_id=1, source_target_pairs={{0,16},{16,32},{32,48},{48,64},{64,80},{80,96},{96,112},{112,128},... | collective-permute-start | bytes 860168 | tf_op jit(solution)/shard_map/ppermute | solution.py:447
  7.6 5.2 %collective-permute-start.1 = (f32[35,8,256]{2,1,0:T(8,128)S(1)}, f32[35,8,256]{2,1,0:T(8,128)S(1)}, u32[]{:S(2)}, u32[]{:S(2)}) collective-permute-start(f32[35,8,256]{2,1,0:T(8,128)S(1)} %get-tuple-element.45), channel_id=1, source_target_pairs={{16,0},{32,16},{48,32},{64,48},{80,64},{96,80},{112,96},{128,112},... | collective-permute-start | bytes 860168 | tf_op jit(solution)/shard_map/ppermute | solution.py:448
  14.6 5.4 %collective-permute-start.2 = (f32[18,8,128]{2,1,0:T(8,128)S(1)}, f32[18,8,128]{2,1,0:T(8,128)S(1)}, u32[]{:S(2)}, u32[]{:S(2)}) collective-permute-start(f32[18,8,128]{2,1,0:T(8,128)S(1)} %get-tuple-element.50), channel_id=1, source_target_pairs={{0,4},{4,8},{8,12},{1,5},{5,9},{9,13},{2,6},{6,10},{10,14},{3,7},{... | collective-permute-start | bytes 221192 | tf_op jit(solution)/shard_map/ppermute | solution.py:447
  18.0 6.2 %collective-permute-start.3 = (f32[18,8,128]{2,1,0:T(8,128)S(1)}, f32[18,8,128]{2,1,0:T(8,128)S(1)}, u32[]{:S(2)}, u32[]{:S(2)}) collective-permute-start(f32[18,8,128]{2,1,0:T(8,128)S(1)} %get-tuple-element.51), channel_id=1, source_target_pairs={{4,0},{8,4},{12,8},{5,1},{9,5},{13,9},{6,2},{10,6},{14,10},{7,3},{... | collective-permute-start | bytes 221192 | tf_op jit(solution)/shard_map/ppermute | solution.py:448
  30.8 1.0 copy-start.3
  31.8 26.2 %copy-start = (f32[8,272,128]{2,1,0:T(8,128)}, f32[8,272,128]{2,1,0:T(8,128)S(1)}, u32[]{:S(2)}) copy-start(f32[8,272,128]{2,1,0:T(8,128)S(1)} %get-tuple-element.60.fr_ref) | copy-start | bytes 3342340
  31.8 26.2 %copy-start.9 = (f32[8,272,128]{2,1,0:T(8,128)}, f32[8,272,128]{2,1,0:T(8,128)S(1)}, u32[]{:S(2)}) copy-start(f32[8,272,128]{2,1,0:T(8,128)S(1)} %get-tuple-element.62.t_in) | copy-start | bytes 3342340
  31.8 26.2 %copy-start.13 = (f32[272,128]{1,0:T(8,128)}, f32[272,128]{1,0:T(8,128)S(1)}, u32[]{:S(2)}) copy-start(f32[272,128]{1,0:T(8,128)S(1)} %get-tuple-element.64.mat_ref) | copy-start | bytes 417796
  56.9 7.1 %copy-start.22 = (f32[48]{0:T(128)S(1)}, f32[48]{0:T(128)}, u32[]{:S(2)}) copy-start(f32[48]{0:T(128)} %flux.3) | copy-start | bytes 580
  58.0 1.0 copy-start.11
  59.0 7.7 %collective-permute-start.6 = (f32[2,136,128]{2,1,0:T(8,128)}, f32[2,136,128]{2,1,0:T(8,128)}, u32[]{:S(2)}, u32[]{:S(2)}) collective-permute-start(f32[2,136,128]{2,1,0:T(8,128)} %get-tuple-element.67.rest_0_), channel_id=1, source_target_pairs={{0,3},{1,0},{2,1},{3,2},{4,7},{5,4},{6,5},{7,6},{8,11},{9,8},{10,9... | collective-permute-start | bytes 417800 | tf_op jit(solution)/shard_map/ppermute | solution.py:441
  59.5 9.0 %collective-permute-start.5 = (f32[2,136,128]{2,1,0:T(8,128)}, f32[2,136,128]{2,1,0:T(8,128)}, u32[]{:S(2)}, u32[]{:S(2)}) collective-permute-start(f32[2,136,128]{2,1,0:T(8,128)} %get-tuple-element.67.rest_0_), channel_id=1, source_target_pairs={{0,2},{1,3},{2,0},{3,1},{4,6},{5,7},{6,4},{7,5},{8,10},{9,11},{10,... | collective-permute-start | bytes 417800 | tf_op jit(solution)/shard_map/ppermute | solution.py:441
  62.1 7.2 %collective-permute-start.4 = (f32[2,136,128]{2,1,0:T(8,128)}, f32[2,136,128]{2,1,0:T(8,128)}, u32[]{:S(2)}, u32[]{:S(2)}) collective-permute-start(f32[2,136,128]{2,1,0:T(8,128)} %get-tuple-element.67.rest_0_), channel_id=1, source_target_pairs={{0,1},{1,2},{2,3},{3,0},{4,5},{5,6},{6,7},{7,4},{8,9},{9,10},{10,1... | collective-permute-start | bytes 417800 | tf_op jit(solution)/shard_map/ppermute | solution.py:441
  64.1 0.9 copy-start.14
  69.3 1.2 copy-start.1
  70.5 1.2 copy-start.4
  71.8 1.2 copy-start.10
  73.0 0.9 copy-start.15
  73.9 17.8 %copy-start.12 = (f32[8,272,128]{2,1,0:T(8,128)S(1)}, f32[8,272,128]{2,1,0:T(8,128)}, u32[]{:S(2)}) copy-start(f32[8,272,128]{2,1,0:T(8,128)} %copy-done.11) | copy-start | bytes 3342340
  91.8 9.3 %copy-start.2 = (f32[8,272,128]{2,1,0:T(8,128)S(1)}, f32[8,272,128]{2,1,0:T(8,128)}, u32[]{:S(2)}) copy-start(f32[8,272,128]{2,1,0:T(8,128)} %copy-done) | copy-start | bytes 3342340
  91.8 9.3 %copy-start.5 = (f32[8,272,128]{2,1,0:T(8,128)S(1)}, f32[8,272,128]{2,1,0:T(8,128)}, u32[]{:S(2)}) copy-start(f32[8,272,128]{2,1,0:T(8,128)} %copy-done.3) | copy-start | bytes 3342340
  92.3 5.0 %collective-permute-start.9 = (f32[1,136,128]{2,1,0:T(8,128)S(1)}, f32[1,136,128]{2,1,0:T(8,128)S(1)}, u32[]{:S(2)}, u32[]{:S(2)}) collective-permute-start(f32[1,136,128]{2,1,0:T(8,128)S(1)} %get-tuple-element.77.rest_0_), channel_id=1, source_target_pairs={{0,3},{1,0},{2,1},{3,2},{4,7},{5,4},{6,5},{7,6},{8,11},{9,8},{10,9... | collective-permute-start | bytes 208904 | tf_op jit(solution)/shard_map/ppermute | solution.py:441
  95.2 5.8 %collective-permute-start.8 = (f32[1,136,128]{2,1,0:T(8,128)S(1)}, f32[1,136,128]{2,1,0:T(8,128)S(1)}, u32[]{:S(2)}, u32[]{:S(2)}) collective-permute-start(f32[1,136,128]{2,1,0:T(8,128)S(1)} %get-tuple-element.77.rest_0_), channel_id=1, source_target_pairs={{0,2},{1,3},{2,0},{3,1},{4,6},{5,7},{6,4},{7,5},{8,10},{9,11},{10,... | collective-permute-start | bytes 208904 | tf_op jit(solution)/shard_map/ppermute | solution.py:441
  95.3 5.8 %collective-permute-start.7 = (f32[1,136,128]{2,1,0:T(8,128)S(1)}, f32[1,136,128]{2,1,0:T(8,128)S(1)}, u32[]{:S(2)}, u32[]{:S(2)}) collective-permute-start(f32[1,136,128]{2,1,0:T(8,128)S(1)} %get-tuple-element.77.rest_0_), channel_id=1, source_target_pairs={{0,1},{1,2},{2,3},{3,0},{4,5},{5,6},{6,7},{7,4},{8,9},{9,10},{10,1... | collective-permute-start | bytes 208904 | tf_op jit(solution)/shard_map/ppermute | solution.py:441
  118.7 6.4 %collective-permute-start.12 = (f32[128,128]{1,0:T(8,128)S(1)}, f32[128,128]{1,0:T(8,128)S(1)}, u32[]{:S(2)}, u32[]{:S(2)}) collective-permute-start(f32[128,128]{1,0:T(8,128)S(1)} %get-tuple-element.83.rest_0_), channel_id=1, source_target_pairs={{0,3},{1,0},{2,1},{3,2},{4,7},{5,4},{6,5},{7,6},{8,11},{9,8},{10,9... | collective-permute-start | bytes 196616 | tf_op jit(solution)/shard_map/ppermute | solution.py:441
  120.3 5.8 %collective-permute-start.11 = (f32[128,128]{1,0:T(8,128)S(1)}, f32[128,128]{1,0:T(8,128)S(1)}, u32[]{:S(2)}, u32[]{:S(2)}) collective-permute-start(f32[128,128]{1,0:T(8,128)S(1)} %get-tuple-element.83.rest_0_), channel_id=1, source_target_pairs={{0,2},{1,3},{2,0},{3,1},{4,6},{5,7},{6,4},{7,5},{8,10},{9,11},{10,... | collective-permute-start | bytes 196616 | tf_op jit(solution)/shard_map/ppermute | solution.py:441
  120.9 5.2 %collective-permute-start.10 = (f32[128,128]{1,0:T(8,128)S(1)}, f32[128,128]{1,0:T(8,128)S(1)}, u32[]{:S(2)}, u32[]{:S(2)}) collective-permute-start(f32[128,128]{1,0:T(8,128)S(1)} %get-tuple-element.83.rest_0_), channel_id=1, source_target_pairs={{0,1},{1,2},{2,3},{3,0},{4,5},{5,6},{6,7},{7,4},{8,9},{9,10},{10,1... | collective-permute-start | bytes 196616 | tf_op jit(solution)/shard_map/ppermute | solution.py:441

commit v3 on v2

--- a/solution.py
+++ b/solution.py
@@ -26,17 +26,17 @@
 
 
 def hspec():
-    return pl.BlockSpec(memory_space=pl.ANY)
-
-
-def call(kernel, outs, args, specs, scratch=(), flops=1000000, nbytes=1000000, name=None):
+    return pl.BlockSpec(memory_space=pltpu.HBM)
+
+
+def call(kernel, outs, args, specs, scratch=(), flops=1000000, nbytes=1000000, name=None, limit=VMEM_LIMIT):
     return pl.pallas_call(
         kernel,
         out_shape=[jax.ShapeDtypeStruct(s, jnp.float32) for s in outs],
         in_specs=specs,
         out_specs=[vspec() for _ in outs],
         scratch_shapes=list(scratch),
-        compiler_params=pltpu.CompilerParams(vmem_limit_bytes=VMEM_LIMIT),
+        compiler_params=pltpu.CompilerParams(vmem_limit_bytes=limit),
         cost_estimate=pl.CostEstimate(flops=flops, bytes_accessed=nbytes, transcendentals=0),
         name=name,
     )(*args)
@@ -356,10 +356,10 @@
 
 
 def heating_kernel(
-    groups, rows, cols, polar_count, place, flux, gathered, dens_ref, mat_ref, flux_ref, column_out, fixed_out
+    groups, rows, cols, polar_count, flux, gathered, dens_ref, mat_ref, flux_ref, column_out, fixed_out
 ):
     tall = dens_ref.shape[0]
-    radius, polar = place[0], place[1]
+    radius, polar = lax.axis_index("radius"), lax.axis_index("polar")
     dens = dens_ref[...]
     row_id = lax.broadcasted_iota(jnp.int32, gathered.shape, 0)
     ahead = (row_id >= radius * polar_count) & (row_id < radius * polar_count + polar)
@@ -456,7 +456,6 @@
     polar_count = lax.axis_size("polar")
     count = lax.axis_size("group")
     devices = lax.axis_size("radius") * polar_count
-    place = jnp.stack([lax.axis_index("radius"), lax.axis_index("polar")]).astype(jnp.int32)
     planes = 2 * groups + 3
     big, flat, core = (pairs, tall, LANES), (tall, LANES), (cols, LANES)
     line = (devices, LANES)
@@ -475,6 +474,7 @@
         [sspec()] + [hspec()] * 4,
         scratch=strips * 2 + [pltpu.SemaphoreType.DMA((8,))],
         name="pack_rows",
+        limit=60 * 1024 * 1024,
     )
     top, bottom = shifted(up, down, "radius")
     a, e, dens, mat, flux_lanes, to_left, to_right = call(
@@ -536,8 +536,8 @@
             column, fixed = call(
                 functools.partial(heating_kernel, groups, rows, cols, polar_count),
                 [(rows, cols), flat],
-                (place, stellar_flux, gathered, dens, mat, flux_lanes),
-                [sspec()] * 2 + [vspec()] * 4,
+                (stellar_flux, gathered, dens, mat, flux_lanes),
+                [sspec()] + [vspec()] * 4,
                 name="heating",
             )
         r, q, out, *more = call(

time: 129 us -> 118 us (0.915)
  local copies, waits for them, and re-layouts: 12 us -> 0.03 us
    unnamed x46 -> x12, local copies, waits for them, and re-layouts: 12 us -> 0.03 us
  transfers between devices with their start and end apart: 13 -> 13, of which waited for: 7 -> 8; matrix products, arithmetic and copies ran while one was open for 0% -> 0% of each run, Pallas kernels for 3% -> 3%
where the time goes in v3:
time: 118 us; the launch traced here: 116 us
  blocking collectives  52.2 us (44%)
  Pallas kernels  24.1 us (20%)
  starting transfers between devices  22.4 us (19%)
  waiting for transfers between devices  17 us (14%)
    all_to_all x3, blocking collectives, per_device(): gathered = lax.all_to_all(out, ('radius', 'polar'), 0, 0, tiled=True)  52.2 us
    pallas_call x11, Pallas kernels, call(): pl.pallas_call(kernel, out_shape=[jax.ShapeDtypeStruct(s, jnp.float32) fo...  24.1 us
    ppermute x9, starting transfers between devices, spread(): lax.ppermute(part, axis, [(i, (i + s) % count) for i in range(count)])  14.7 us
    ppermute x2, waiting for transfers between devices, shifted(): lax.ppermute(upward, axis, [(i + 1, i) for i in range(count - 1)])  8.27 us
    ppermute x9, waiting for transfers between devices, spread(): lax.ppermute(part, axis, [(i, (i + s) % count) for i in range(count)])  8.02 us
    ppermute x2, starting transfers between devices, shifted(): lax.ppermute(downward, axis, [(i, i + 1) for i in range(count - 1)])  5.15 us
    ppermute x2, starting transfers between devices, shifted(): lax.ppermute(upward, axis, [(i + 1, i) for i in range(count - 1)])  2.58 us
  transfers between devices with their start and end apart: 13, of which 8 were waited for; matrix products, arithmetic and copies ran while one was open for 0% of the time, Pallas kernels for 3%

profile of v3, /device:TPU:8, one launch (start us, length us, event | category | flops | bytes accessed | tf_op | source)
XLA Modules:
  0.0 116.5 jit_solution(8005034897929625148)
XLA Ops:
  0.6 0.0 copy-start.3
  0.6 0.0 copy-start
  0.7 0.0 copy-start.1
  0.7 0.0 copy-start.2
  0.7 2.8 %pack_rows.1 = (f32[35,8,256]{2,1,0:T(8,128)}, f32[35,8,256]{2,1,0:T(8,128)}) custom-call(f32[48]{0:T(128)} %flux.3, bf16[16,48,256]{2,1,0:T(8,128)(2,1)} %opacity.3, f32[16,48,256]{2,1,0:T(8,128)} %old.3, f32[48,256]{1,0:T(8,128)} %density.3, f32[48,256]{1,0:T(8,128)} %material.4), custom_call_target="tpu_custom_call" | custom-call | flops 1000000 | bytes 1000000 | tf_op jit(solution)/shard_map/pack_rows/pallas_call | solution.py:33
  3.5 0.0 copy-start.4
  3.5 1.8 %collective-permute-start = (f32[35,8,256]{2,1,0:T(8,128)}, f32[35,8,256]{2,1,0:T(8,128)S(1)}, u32[]{:S(2)}, u32[]{:S(2)}) collective-permute-start(f32[35,8,256]{2,1,0:T(8,128)} %get-tuple-element.44), channel_id=1, source_target_pairs={{0,16},{16,32},{32,48},{48,64},{64,80},{80,96},{96,112},{112,128},... | collective-permute-start | bytes 860168 | tf_op jit(solution)/shard_map/ppermute | solution.py:447
  5.3 1.3 %collective-permute-start.1 = (f32[35,8,256]{2,1,0:T(8,128)}, f32[35,8,256]{2,1,0:T(8,128)S(1)}, u32[]{:S(2)}, u32[]{:S(2)}) collective-permute-start(f32[35,8,256]{2,1,0:T(8,128)} %get-tuple-element.45), channel_id=1, source_target_pairs={{16,0},{32,16},{48,32},{64,48},{80,64},{96,80},{112,96},{128,112},... | collective-permute-start | bytes 860168 | tf_op jit(solution)/shard_map/ppermute | solution.py:448
  6.6 0.1 collective-permute-done.top
  6.7 4.0 %collective-permute-done.1.bottom = f32[35,8,256]{2,1,0:T(8,128)S(1)} collective-permute-done((f32[35,8,256]{2,1,0:T(8,128)}, f32[35,8,256]{2,1,0:T(8,128)S(1)}, u32[]{:S(2)}, u32[]{:S(2)}) %collective-permute-start.1) | collective-permute-done | bytes 286752 | tf_op jit(solution)/shard_map/ppermute | solution.py:448
  10.6 0.0 copy-done.3
  10.6 0.0 copy-done
  10.6 0.0 copy-done.1
  10.7 1.9 %turn.1 = (f32[8,256,128]{2,1,0:T(8,128)S(1)}, f32[8,256,128]{2,1,0:T(8,128)S(1)}, f32[256,128]{1,0:T(8,128)S(1)}, f32[256,128]{1,0:T(8,128)S(1)}, f32[8,128]{1,...) custom-call(bf16[16,48,256]{2,1,0:T(8,128)(2,1)S(1)} %copy-done.1, f32[16,48,256]{2,1,0:T(8,128)S(1)} %copy-done, ...), custom_call_target="tpu_custom_call" | custom-call | flops 1000000 | bytes 1000000 | tf_op jit(solution)/shard_map/turn/pallas_call | solution.py:33
  12.5 3.4 %collective-permute-start.2 = (f32[18,8,128]{2,1,0:T(8,128)S(1)}, f32[18,8,128]{2,1,0:T(8,128)S(1)}, u32[]{:S(2)}, u32[]{:S(2)}) collective-permute-start(f32[18,8,128]{2,1,0:T(8,128)S(1)} %get-tuple-element.50), channel_id=1, source_target_pairs={{0,4},{4,8},{8,12},{1,5},{5,9},{9,13},{2,6},{6,10},{10,14},{3,7},{... | collective-permute-start | bytes 221192 | tf_op jit(solution)/shard_map/ppermute | solution.py:447
  15.9 1.3 %collective-permute-start.3 = (f32[18,8,128]{2,1,0:T(8,128)S(1)}, f32[18,8,128]{2,1,0:T(8,128)S(1)}, u32[]{:S(2)}, u32[]{:S(2)}) collective-permute-start(f32[18,8,128]{2,1,0:T(8,128)S(1)} %get-tuple-element.51), channel_id=1, source_target_pairs={{4,0},{8,4},{12,8},{5,1},{9,5},{13,9},{6,2},{10,6},{14,10},{7,3},{... | collective-permute-start | bytes 221192 | tf_op jit(solution)/shard_map/ppermute | solution.py:448
  17.2 0.7 collective-permute-done.2.left
  17.9 4.3 %collective-permute-done.3.right = f32[18,8,128]{2,1,0:T(8,128)S(1)} collective-permute-done((f32[18,8,128]{2,1,0:T(8,128)S(1)}, f32[18,8,128]{2,1,0:T(8,128)S(1)}, u32[]{:S(2)}, u32[]{:S(2)}) %collective-permute-start.3) | collective-permute-done | bytes 73760 | tf_op jit(solution)/shard_map/ppermute | solution.py:448
  22.2 6.4 %start.1 = (f32[8,272,128]{2,1,0:T(8,128)S(1)}, f32[8,272,128]{2,1,0:T(8,128)S(1)}, f32[8,272,128]{2,1,0:T(8,128)S(1)}, f32[8,272,128]{2,1,0:T(8,128)S(1)}, f32[...) custom-call(f32[16]{0:T(128)S(1)} %copy-done.4, ...), custom_call_target="tpu_custom_call" | custom-call | flops 1000000 | bytes 1000000 | tf_op jit(solution)/shard_map/start/pallas_call | solution.py:33
  28.6 25.2 %all_to_all.33 = f32[64,1,128]{2,1,0:T(1,128)S(1)} all-to-all(f32[64,1,128]{2,1,0:T(1,128)S(1)} %bitcast.16), channel_id=1, replica_groups=mesh['radius'=16,'polar'=4,'group'=4] {'radius','polar'}, dimensions={0} | all-to-all | bytes 65536 | tf_op jit(solution)/shard_map/all_to_all | solution.py:498
  53.8 0.4 update.2
  54.3 0.5 collective-permute-start.6
  54.8 2.6 %collective-permute-start.5 = (f32[2,136,128]{2,1,0:T(8,128)S(1)}, f32[2,136,128]{2,1,0:T(8,128)S(1)}, u32[]{:S(2)}, u32[]{:S(2)}) collective-permute-start(f32[2,136,128]{2,1,0:T(8,128)S(1)} %get-tuple-element.67.rest_0_), channel_id=1, source_target_pairs={{0,2},{1,3},{2,0},{3,1},{4,6},{5,7},{6,4},{7,5},{8,10},{9,11},{10,... | collective-permute-start | bytes 417800 | tf_op jit(solution)/shard_map/ppermute | solution.py:441
  57.4 1.9 %collective-permute-start.4 = (f32[2,136,128]{2,1,0:T(8,128)S(1)}, f32[2,136,128]{2,1,0:T(8,128)S(1)}, u32[]{:S(2)}, u32[]{:S(2)}) collective-permute-start(f32[2,136,128]{2,1,0:T(8,128)S(1)} %get-tuple-element.67.rest_0_), channel_id=1, source_target_pairs={{0,1},{1,2},{2,3},{3,0},{4,5},{5,6},{6,7},{7,4},{8,9},{9,10},{10,1... | collective-permute-start | bytes 417800 | tf_op jit(solution)/shard_map/ppermute | solution.py:441
  59.3 1.7 %heating.1 = (f32[48,256]{1,0:T(8,128)}, f32[272,128]{1,0:T(8,128)S(1)}) custom-call(f32[48]{0:T(128)S(1)} %copy-done.5, f32[64,128]{1,0:T(8,128)S(1)} %bitcast.13, f32[272,128]{1,0:T(8,128)S(1)} %get-tuple-element.63.dens_ref.cap_in, f32[272,128]{1,0:T(8,128)S(1)} %get-tuple-element.64.mat_ref, f32[8,128]{1,0:T(8,128)S(1)} %get-tuple-element.65.flux_ref), custom_call_target="tpu_custom_call" | custom-call | flops 1000000 | bytes 1000000 | tf_op jit(solution)/shard_map/heating/pallas_call | solution.py:33
  61.0 0.0 collective-permute-done.6.rest_3_
  61.0 2.5 %collective-permute-done.5.rest_2_ = f32[2,136,128]{2,1,0:T(8,128)S(1)} collective-permute-done((f32[2,136,128]{2,1,0:T(8,128)S(1)}, f32[2,136,128]{2,1,0:T(8,128)S(1)}, u32[]{:S(2)}, u32[]{:S(2)}) %collective-permute-start.5) | collective-permute-done | bytes 139296 | tf_op jit(solution)/shard_map/ppermute | solution.py:441
  63.5 0.8 collective-permute-done.4.rest_1_
  64.2 3.7 %next.2 = (f32[8,272,128]{2,1,0:T(8,128)S(1)}, f32[8,272,128]{2,1,0:T(8,128)S(1)}, f32[64,128]{1,0:T(8,128)S(1)}, f32[8,272,128]{2,1,0:T(8,128)S(1)}, f32[272,128]{1,0:T(8,128)S(1)}, /*index=5*/f32[272,128]{1,0:T(8,128)S(1)}) custom-call(f32[16]{0:T(128)S(1)} %copy-done.4, f32[8,128]{1,0:T(8,128)S(1)} %get-tuple-element.58.c1_ref, ...), custom_call_target="tpu_custom_call" | custom-call | flops 1000000 | bytes 1000000 | tf_op jit(solution)/shard_map/next/pallas_call | solution.py:33
  67.9 13.5 %all_to_all.34 = f32[64,1,128]{2,1,0:T(1,128)S(1)} all-to-all(f32[64,1,128]{2,1,0:T(1,128)S(1)} %bitcast.17), channel_id=1, replica_groups=mesh['radius'=16,'polar'=4,'group'=4] {'radius','polar'}, dimensions={0} | all-to-all | bytes 65536 | tf_op jit(solution)/shard_map/all_to_all | solution.py:498
  81.4 0.5 update.3
  81.9 3.0 %collective-permute-start.9 = (f32[1,136,128]{2,1,0:T(8,128)S(1)}, f32[1,136,128]{2,1,0:T(8,128)S(1)}, u32[]{:S(2)}, u32[]{:S(2)}) collective-permute-start(f32[1,136,128]{2,1,0:T(8,128)S(1)} %get-tuple-element.77.rest_0_), channel_id=1, source_target_pairs={{0,3},{1,0},{2,1},{3,2},{4,7},{5,4},{6,5},{7,6},{8,11},{9,8},{10,9... | collective-permute-start | bytes 208904 | tf_op jit(solution)/shard_map/ppermute | solution.py:441
  84.8 0.0 collective-permute-start.8
  84.9 2.0 %collective-permute-start.7 = (f32[1,136,128]{2,1,0:T(8,128)S(1)}, f32[1,136,128]{2,1,0:T(8,128)S(1)}, u32[]{:S(2)}, u32[]{:S(2)}) collective-permute-start(f32[1,136,128]{2,1,0:T(8,128)S(1)} %get-tuple-element.77.rest_0_), channel_id=1, source_target_pairs={{0,1},{1,2},{2,3},{3,0},{4,5},{5,6},{6,7},{7,4},{8,9},{9,10},{10,1... | collective-permute-start | bytes 208904 | tf_op jit(solution)/shard_map/ppermute | solution.py:441
  86.9 0.0 collective-permute-done.9.rest_3_
  86.9 3.8 %collective-permute-done.8.rest_2_ = f32[1,136,128]{2,1,0:T(8,128)S(1)} collective-permute-done((f32[1,136,128]{2,1,0:T(8,128)S(1)}, f32[1,136,128]{2,1,0:T(8,128)S(1)}, u32[]{:S(2)}, u32[]{:S(2)}) %collective-permute-start.8) | collective-permute-done | bytes 69664 | tf_op jit(solution)/shard_map/ppermute | solution.py:441
  90.7 0.0 collective-permute-done.7.rest_1_
  90.7 3.7 %next.3 = (f32[8,272,128]{2,1,0:T(8,128)S(1)}, f32[8,272,128]{2,1,0:T(8,128)S(1)}, f32[64,128]{1,0:T(8,128)S(1)}) custom-call(f32[16]{0:T(128)S(1)} %copy-done.4, f32[8,128]{1,0:T(8,128)S(1)} %get-tuple-element.72.c1_ref, f32[8,128]{1,0:T(8,128)S(1)} %get-tuple-element.73.c2_ref, f32[8,272,128]{2,1,0:T(8,128)S(1)} %get-tuple-element.53.a_ref, ...), custom_call_target="tpu_custom_call" | custom-call | flops 1000000 | bytes 1000000 | tf_op jit(solution)/shard_map/next/pallas_call | solution.py:33
  94.4 13.5 %all_to_all.35 = f32[64,1,128]{2,1,0:T(1,128)S(1)} all-to-all(f32[64,1,128]{2,1,0:T(1,128)S(1)} %bitcast.18), channel_id=1, replica_groups=mesh['radius'=16,'polar'=4,'group'=4] {'radius','polar'}, dimensions={0} | all-to-all | bytes 65536 | tf_op jit(solution)/shard_map/all_to_all | solution.py:498
  107.8 0.5 last_update.1
  108.3 1.6 %collective-permute-start.12 = (f32[128,128]{1,0:T(8,128)S(1)}, f32[128,128]{1,0:T(8,128)S(1)}, u32[]{:S(2)}, u32[]{:S(2)}) collective-permute-start(f32[128,128]{1,0:T(8,128)S(1)} %get-tuple-element.83.rest_0_), channel_id=1, source_target_pairs={{0,3},{1,0},{2,1},{3,2},{4,7},{5,4},{6,5},{7,6},{8,11},{9,8},{10,9... | collective-permute-start | bytes 196616 | tf_op jit(solution)/shard_map/ppermute | solution.py:441
  109.9 0.6 collective-permute-start.11
  110.5 2.5 %collective-permute-start.10 = (f32[128,128]{1,0:T(8,128)S(1)}, f32[128,128]{1,0:T(8,128)S(1)}, u32[]{:S(2)}, u32[]{:S(2)}) collective-permute-start(f32[128,128]{1,0:T(8,128)S(1)} %get-tuple-element.83.rest_0_), channel_id=1, source_target_pairs={{0,1},{1,2},{2,3},{3,0},{4,5},{5,6},{6,7},{7,4},{8,9},{9,10},{10,1... | collective-permute-start | bytes 196616 | tf_op jit(solution)/shard_map/ppermute | solution.py:441
  113.1 1.7 %energy.1 = f32[16,48,256]{2,1,0:T(8,128)} custom-call(f32[8,272,128]{2,1,0:T(8,128)S(1)} %get-tuple-element.82.e_ref), custom_call_target="tpu_custom_call" | custom-call | flops 1000000 | bytes 1000000 | tf_op jit(solution)/shard_map/energy/pallas_call | solution.py:33
  114.7 0.0 collective-permute-done.12.rest_3_
  114.7 1.0 collective-permute-done.11.rest_2_
  115.7 0.0 collective-permute-done.10.rest_1_
  115.7 0.8 material.5
  (4 shorter events, 0.0 us)
Async XLA Ops:
  0.6 10.0 %copy-start.3 = (f32[48,256]{1,0:T(8,128)S(1)}, f32[48,256]{1,0:T(8,128)}, u32[]{:S(2)}) copy-start(f32[48,256]{1,0:T(8,128)} %material.4) | copy-start | bytes 147460
  0.6 10.0 %copy-start = (f32[16,48,256]{2,1,0:T(8,128)S(1)}, f32[16,48,256]{2,1,0:T(8,128)}, u32[]{:S(2)}) copy-start(f32[16,48,256]{2,1,0:T(8,128)} %old.3) | copy-start | bytes 2359300
  0.7 10.0 %copy-start.1 = (bf16[16,48,256]{2,1,0:T(8,128)(2,1)S(1)}, bf16[16,48,256]{2,1,0:T(8,128)(2,1)}, u32[]{:S(2)}) copy-start(bf16[16,48,256]{2,1,0:T(8,128)(2,1)} %opacity.3) | copy-start | bytes 1179652
  0.7 10.0 %copy-start.2 = (f32[48,256]{1,0:T(8,128)S(1)}, f32[48,256]{1,0:T(8,128)}, u32[]{:S(2)}) copy-start(f32[48,256]{1,0:T(8,128)} %density.3) | copy-start | bytes 147460
  3.5 18.7 %copy-start.4 = (f32[16]{0:T(128)S(1)}, f32[16]{0:T(128)}, u32[]{:S(2)}) copy-start(f32[16]{0:T(128)} %weights.5) | copy-start | bytes 196
  3.5 3.1 %collective-permute-start = (f32[35,8,256]{2,1,0:T(8,128)}, f32[35,8,256]{2,1,0:T(8,128)S(1)}, u32[]{:S(2)}, u32[]{:S(2)}) collective-permute-start(f32[35,8,256]{2,1,0:T(8,128)} %get-tuple-element.44), channel_id=1, source_target_pairs={{0,16},{16,32},{32,48},{48,64},{64,80},{80,96},{96,112},{112,128},... | collective-permute-start | bytes 860168 | tf_op jit(solution)/shard_map/ppermute | solution.py:447
  5.3 5.4 %collective-permute-start.1 = (f32[35,8,256]{2,1,0:T(8,128)}, f32[35,8,256]{2,1,0:T(8,128)S(1)}, u32[]{:S(2)}, u32[]{:S(2)}) collective-permute-start(f32[35,8,256]{2,1,0:T(8,128)} %get-tuple-element.45), channel_id=1, source_target_pairs={{16,0},{32,16},{48,32},{64,48},{80,64},{96,80},{112,96},{128,112},... | collective-permute-start | bytes 860168 | tf_op jit(solution)/shard_map/ppermute | solution.py:448
  12.5 5.4 %collective-permute-start.2 = (f32[18,8,128]{2,1,0:T(8,128)S(1)}, f32[18,8,128]{2,1,0:T(8,128)S(1)}, u32[]{:S(2)}, u32[]{:S(2)}) collective-permute-start(f32[18,8,128]{2,1,0:T(8,128)S(1)} %get-tuple-element.50), channel_id=1, source_target_pairs={{0,4},{4,8},{8,12},{1,5},{5,9},{9,13},{2,6},{6,10},{10,14},{3,7},{... | collective-permute-start | bytes 221192 | tf_op jit(solution)/shard_map/ppermute | solution.py:447
  15.9 6.2 %collective-permute-start.3 = (f32[18,8,128]{2,1,0:T(8,128)S(1)}, f32[18,8,128]{2,1,0:T(8,128)S(1)}, u32[]{:S(2)}, u32[]{:S(2)}) collective-permute-start(f32[18,8,128]{2,1,0:T(8,128)S(1)} %get-tuple-element.51), channel_id=1, source_target_pairs={{4,0},{8,4},{12,8},{5,1},{9,5},{13,9},{6,2},{10,6},{14,10},{7,3},{... | collective-permute-start | bytes 221192 | tf_op jit(solution)/shard_map/ppermute | solution.py:448
  53.8 5.4 %copy-start.5 = (f32[48]{0:T(128)S(1)}, f32[48]{0:T(128)}, u32[]{:S(2)}) copy-start(f32[48]{0:T(128)} %flux.3) | copy-start | bytes 580
  54.3 6.7 %collective-permute-start.6 = (f32[2,136,128]{2,1,0:T(8,128)S(1)}, f32[2,136,128]{2,1,0:T(8,128)S(1)}, u32[]{:S(2)}, u32[]{:S(2)}) collective-permute-start(f32[2,136,128]{2,1,0:T(8,128)S(1)} %get-tuple-element.67.rest_0_), channel_id=1, source_target_pairs={{0,3},{1,0},{2,1},{3,2},{4,7},{5,4},{6,5},{7,6},{8,11},{9,8},{10,9... | collective-permute-start | bytes 417800 | tf_op jit(solution)/shard_map/ppermute | solution.py:441
  54.8 8.7 %collective-permute-start.5 = (f32[2,136,128]{2,1,0:T(8,128)S(1)}, f32[2,136,128]{2,1,0:T(8,128)S(1)}, u32[]{:S(2)}, u32[]{:S(2)}) collective-permute-start(f32[2,136,128]{2,1,0:T(8,128)S(1)} %get-tuple-element.67.rest_0_), channel_id=1, source_target_pairs={{0,2},{1,3},{2,0},{3,1},{4,6},{5,7},{6,4},{7,5},{8,10},{9,11},{10,... | collective-permute-start | bytes 417800 | tf_op jit(solution)/shard_map/ppermute | solution.py:441
  57.4 6.9 %collective-permute-start.4 = (f32[2,136,128]{2,1,0:T(8,128)S(1)}, f32[2,136,128]{2,1,0:T(8,128)S(1)}, u32[]{:S(2)}, u32[]{:S(2)}) collective-permute-start(f32[2,136,128]{2,1,0:T(8,128)S(1)} %get-tuple-element.67.rest_0_), channel_id=1, source_target_pairs={{0,1},{1,2},{2,3},{3,0},{4,5},{5,6},{6,7},{7,4},{8,9},{9,10},{10,1... | collective-permute-start | bytes 417800 | tf_op jit(solution)/shard_map/ppermute | solution.py:441
  81.9 5.0 %collective-permute-start.9 = (f32[1,136,128]{2,1,0:T(8,128)S(1)}, f32[1,136,128]{2,1,0:T(8,128)S(1)}, u32[]{:S(2)}, u32[]{:S(2)}) collective-permute-start(f32[1,136,128]{2,1,0:T(8,128)S(1)} %get-tuple-element.77.rest_0_), channel_id=1, source_target_pairs={{0,3},{1,0},{2,1},{3,2},{4,7},{5,4},{6,5},{7,6},{8,11},{9,8},{10,9... | collective-permute-start | bytes 208904 | tf_op jit(solution)/shard_map/ppermute | solution.py:441
  84.8 5.8 %collective-permute-start.8 = (f32[1,136,128]{2,1,0:T(8,128)S(1)}, f32[1,136,128]{2,1,0:T(8,128)S(1)}, u32[]{:S(2)}, u32[]{:S(2)}) collective-permute-start(f32[1,136,128]{2,1,0:T(8,128)S(1)} %get-tuple-element.77.rest_0_), channel_id=1, source_target_pairs={{0,2},{1,3},{2,0},{3,1},{4,6},{5,7},{6,4},{7,5},{8,10},{9,11},{10,... | collective-permute-start | bytes 208904 | tf_op jit(solution)/shard_map/ppermute | solution.py:441
  84.9 5.8 %collective-permute-start.7 = (f32[1,136,128]{2,1,0:T(8,128)S(1)}, f32[1,136,128]{2,1,0:T(8,128)S(1)}, u32[]{:S(2)}, u32[]{:S(2)}) collective-permute-start(f32[1,136,128]{2,1,0:T(8,128)S(1)} %get-tuple-element.77.rest_0_), channel_id=1, source_target_pairs={{0,1},{1,2},{2,3},{3,0},{4,5},{5,6},{6,7},{7,4},{8,9},{9,10},{10,1... | collective-permute-start | bytes 208904 | tf_op jit(solution)/shard_map/ppermute | solution.py:441
  108.3 6.4 %collective-permute-start.12 = (f32[128,128]{1,0:T(8,128)S(1)}, f32[128,128]{1,0:T(8,128)S(1)}, u32[]{:S(2)}, u32[]{:S(2)}) collective-permute-start(f32[128,128]{1,0:T(8,128)S(1)} %get-tuple-element.83.rest_0_), channel_id=1, source_target_pairs={{0,3},{1,0},{2,1},{3,2},{4,7},{5,4},{6,5},{7,6},{8,11},{9,8},{10,9... | collective-permute-start | bytes 196616 | tf_op jit(solution)/shard_map/ppermute | solution.py:441
  109.9 5.8 %collective-permute-start.11 = (f32[128,128]{1,0:T(8,128)S(1)}, f32[128,128]{1,0:T(8,128)S(1)}, u32[]{:S(2)}, u32[]{:S(2)}) collective-permute-start(f32[128,128]{1,0:T(8,128)S(1)} %get-tuple-element.83.rest_0_), channel_id=1, source_target_pairs={{0,2},{1,3},{2,0},{3,1},{4,6},{5,7},{6,4},{7,5},{8,10},{9,11},{10,... | collective-permute-start | bytes 196616 | tf_op jit(solution)/shard_map/ppermute | solution.py:441
  110.5 5.2 %collective-permute-start.10 = (f32[128,128]{1,0:T(8,128)S(1)}, f32[128,128]{1,0:T(8,128)S(1)}, u32[]{:S(2)}, u32[]{:S(2)}) collective-permute-start(f32[128,128]{1,0:T(8,128)S(1)} %get-tuple-element.83.rest_0_), channel_id=1, source_target_pairs={{0,1},{1,2},{2,3},{3,0},{4,5},{5,6},{6,7},{7,4},{8,9},{9,10},{10,1... | collective-permute-start | bytes 196616 | tf_op jit(solution)/shard_map/ppermute | solution.py:441

commit v4 on v3

--- a/solution.py
+++ b/solution.py
@@ -29,7 +29,7 @@
     return pl.BlockSpec(memory_space=pltpu.HBM)
 
 
-def call(kernel, outs, args, specs, scratch=(), flops=1000000, nbytes=1000000, name=None, limit=VMEM_LIMIT):
+def call(kernel, outs, args, specs, scratch=(), flops=1000000, nbytes=1000000, name=None, limit=VMEM_LIMIT, aliases=None):
     return pl.pallas_call(
         kernel,
         out_shape=[jax.ShapeDtypeStruct(s, jnp.float32) for s in outs],
@@ -39,6 +39,7 @@
         compiler_params=pltpu.CompilerParams(vmem_limit_bytes=limit),
         cost_estimate=pl.CostEstimate(flops=flops, bytes_accessed=nbytes, transcendentals=0),
         name=name,
+        input_output_aliases=aliases or {},
     )(*args)
 
 
@@ -54,60 +55,71 @@
     return list(zip(cuts[:-1], cuts[1:]))
 
 
-def pack_rows_kernel(groups, rows, flux, opacity, old, density, material, up, down, *scratch):
+def partner(axis, inner, outer):
+    even = lax.rem(lax.axis_index(axis), 2) == 0
+    return even, jnp.where(even, inner, outer), jnp.where(even, outer, inner)
+
+
+def pack_rows_kernel(groups, rows, flux, opacity, old, density, material, first, second, *scratch):
+    even, lo_first, lo_second = partner("radius", rows - HALO, 0)
+    sems = scratch[-1]
+    sides = ((first, lo_first, even), (second, lo_second, jnp.logical_not(even)))
     copies = []
-    sems = scratch[-1]
-    for side, (lo, base) in enumerate(((0, 0), (rows - HALO, rows - 2 * HALO))):
+    for side, (_, lo, at_end) in enumerate(sides):
         op_buf, old_buf, dens_buf, mat_buf = scratch[4 * side : 4 * side + 4]
-        pairs = (
+        lo = pl.multiple_of(lo, HALO)
+        base = pl.multiple_of(jnp.where(at_end, rows - 2 * HALO, 0), 2 * HALO)
+        moves = (
             (opacity.at[:, pl.ds(base, 2 * HALO), :], op_buf),
             (old.at[:, pl.ds(lo, HALO), :], old_buf),
             (density.at[pl.ds(lo, HALO), :], dens_buf),
             (material.at[pl.ds(lo, HALO), :], mat_buf),
         )
-        for k, (src, dst) in enumerate(pairs):
+        for k, (src, dst) in enumerate(moves):
             copies.append(pltpu.make_async_copy(src, dst, sems.at[4 * side + k]))
     for c in copies:
         c.start()
     for c in copies:
         c.wait()
-    lane = lane_of(HALO)
-    for side, (out, lo, inside, first) in enumerate(
-        ((up, 0, 0, rows + HALO), (down, rows - HALO, HALO, 0))
-    ):
+    lane = lane_of(HALO) % HALF
+    for side, (out, lo, at_end) in enumerate(sides):
         op_buf, old_buf, dens_buf, mat_buf = scratch[4 * side : 4 * side + 4]
         dens = dens_buf[...]
         for g in range(groups):
-            out[g] = op_buf[g].astype(jnp.float32)[inside : inside + HALO, :] * dens
+            part = op_buf[g].astype(jnp.float32)
+            out[g] = jnp.where(at_end, part[HALO:], part[:HALO]) * dens
             out[groups + g] = old_buf[g]
         out[2 * groups] = dens
         out[2 * groups + 1] = mat_buf[...]
+        place = jnp.where(at_end, 0, rows + HALO)
         vec = jnp.zeros((HALO, LANES), jnp.float32)
         for i in range(HALO):
-            vec = jnp.where(lane % HALF == first + i, flux[lo + i], vec)
-        out[2 * groups + 2, :, :LANES] = vec
-        for at in range(LANES, out.shape[2], LANES):
-            out[2 * groups + 2, :, at : at + LANES] = vec
+            vec = jnp.where(lane == place + i, flux[lo + i], vec)
+        for at_lane in range(0, out.shape[2], LANES):
+            out[2 * groups + 2, :, at_lane : at_lane + LANES] = vec
 
 
 def turn_kernel(
-    groups, rows, cols, opacity, old, density, material, top, bottom,
-    a_ref, e_ref, dens_ref, mat_ref, flux_ref, to_left, to_right,
+    groups, rows, cols, opacity, old, density, material, got_first, got_second,
+    a_ref, e_ref, dens_ref, mat_ref, flux_ref, to_first, to_second,
 ):
     pairs = groups // 2
-    flux_ref[...] = top[2 * groups + 2, :, :LANES] + bottom[2 * groups + 2, :, :LANES]
+    plane_of_flux = 2 * groups + 2
+    flux_ref[...] = got_first[plane_of_flux, :, :LANES] + got_second[plane_of_flux, :, :LANES]
+    even, _, _ = partner("radius", 0, 0)
     for lo in range(0, cols, LANES):
         hi = lo + LANES
 
         def tile(plane, own):
-            return jnp.concatenate([top[plane, :, lo:hi], own, bottom[plane, :, lo:hi]], axis=0)
+            one, two = got_first[plane, :, lo:hi], got_second[plane, :, lo:hi]
+            return jnp.concatenate([jnp.where(even, two, one), own, jnp.where(even, one, two)], axis=0)
 
         d = tile(2 * groups, density[:, lo:hi])
         d = jnp.concatenate([d, d], axis=0).T
         m = tile(2 * groups + 1, material[:, lo:hi])
         m = jnp.concatenate([m, m], axis=0).T
-        dens_ref[lo:hi, :] = d
-        mat_ref[lo:hi, :] = m
+        dens_ref[HALO + lo : HALO + hi, :] = d
+        mat_ref[HALO + lo : HALO + hi, :] = m
 
         def one(p, carry):
             both = []
@@ -115,19 +127,20 @@
                 g = 2 * p + h
                 both.append(tile(g, opacity[g, :, lo:hi].astype(jnp.float32) * density[:, lo:hi]))
             a = jnp.concatenate(both, axis=0).T
-            a_ref[p, lo:hi, :] = jnp.where(dens_ref[lo:hi, :] > 0.0, a, 1.0)
+            a_ref[p, HALO + lo : HALO + hi, :] = jnp.where(dens_ref[HALO + lo : HALO + hi, :] > 0.0, a, 1.0)
             both = [tile(groups + 2 * p + h, old[2 * p + h, :, lo:hi]) for h in range(2)]
-            e_ref[p, lo:hi, :] = jnp.concatenate(both, axis=0).T
+            e_ref[p, HALO + lo : HALO + hi, :] = jnp.concatenate(both, axis=0).T
             return carry
 
         lax.fori_loop(0, pairs, one, 0)
-    for out, lo in ((to_left, 0), (to_right, cols - HALO)):
-        hi = lo + HALO
+    _, lo_first, lo_second = partner("polar", cols, HALO)
+    for out, lo in ((to_first, lo_first), (to_second, lo_second)):
+        edge = pl.ds(pl.multiple_of(lo, HALO), HALO)
         for p in range(pairs):
-            out[p] = a_ref[p, lo:hi, :]
-            out[pairs + p] = e_ref[p, lo:hi, :]
-        out[2 * pairs] = dens_ref[lo:hi, :]
-        out[2 * pairs + 1] = mat_ref[lo:hi, :]
+            out[p] = a_ref[p, edge, :]
+            out[pairs + p] = e_ref[p, edge, :]
+        out[2 * pairs] = dens_ref[edge, :]
+        out[2 * pairs + 1] = mat_ref[edge, :]
 
 
 def next_row(v):
@@ -138,14 +151,14 @@
     return pltpu.roll(v, 1, 1)
 
 
-def after(ref, lead, lo, hi, here):
-    if hi < ref.shape[-2]:
+def after(ref, lead, lo, hi, here, end):
+    if hi < end:
         return ref[(*lead, slice(lo + 1, hi + 1), slice(None))]
     return pltpu.roll(here, hi - lo - 1, 0)
 
 
-def before(ref, lead, lo, hi, here):
-    if lo > 0:
+def before(ref, lead, lo, hi, here, begin):
+    if lo > begin:
         return ref[(*lead, slice(lo - 1, hi - 1), slice(None))]
     return pltpu.roll(here, 1, 0)
 
@@ -154,10 +167,13 @@
     return (slice(lo, hi), slice(None))
 
 
-def flux_sum(p, lo, hi, v_ref, v, fr_ref, fp_ref):
+def flux_sum(p, lo, hi, v_ref, v, fr_ref, fp_ref, span):
+    begin, end = span
     fp = fp_ref[(p, *at(lo, hi))]
-    fp_before = before(fp_ref, (p,), lo, hi, fp)
-    polar = fp * (v - after(v_ref, (p,), lo, hi, v)) + fp_before * (v - before(v_ref, (p,), lo, hi, v))
+    fp_before = before(fp_ref, (p,), lo, hi, fp, begin)
+    polar = fp * (v - after(v_ref, (p,), lo, hi, v, end)) + fp_before * (
+        v - before(v_ref, (p,), lo, hi, v, begin)
+    )
     fr = fr_ref[(p, *at(lo, hi))] * (v - next_row(v))
     return polar + (fr - prev_row(fr))
 
@@ -169,29 +185,31 @@
     return acc
 
 
-def krylov(p, pairs, a_ref, fr_ref, fp_ref, r_ref, q_ref, t_ref, mom):
-    tall = r_ref.shape[1]
+def krylov(p, pairs, parts, span, own, a_ref, fr_ref, fp_ref, r_ref, q_ref, t_ref, mom, old_mom=None):
     sums = [jnp.zeros((HALO, LANES), jnp.float32) for _ in range(4)]
-    for lo, hi in pieces(tall):
+    for lo, hi in parts:
         r = r_ref[(p, *at(lo, hi))]
-        q = r + a_ref[(p, *at(lo, hi))] * r + flux_sum(p, lo, hi, r_ref, r, fr_ref, fp_ref)
+        q = r + a_ref[(p, *at(lo, hi))] * r + flux_sum(p, lo, hi, r_ref, r, fr_ref, fp_ref, span)
         q_ref[(p, *at(lo, hi))] = q
-        if lo >= HALO and hi <= tall - HALO:
+        if lo >= own[0] and hi <= own[1]:
             sums[0] = sums[0] + tile_sum(r * r)
             sums[1] = sums[1] + tile_sum(r * q)
             sums[2] = sums[2] + tile_sum(q * q)
-    for lo, hi in pieces(tall):
-        own = lo >= HALO and hi <= tall - HALO
-        if not own and t_ref is None:
+    for lo, hi in parts:
+        inside = lo >= own[0] and hi <= own[1]
+        if not inside and t_ref is None:
             continue
         q = q_ref[(p, *at(lo, hi))]
-        t = q + a_ref[(p, *at(lo, hi))] * q + flux_sum(p, lo, hi, q_ref, q, fr_ref, fp_ref)
+        t = q + a_ref[(p, *at(lo, hi))] * q + flux_sum(p, lo, hi, q_ref, q, fr_ref, fp_ref, span)
         if t_ref is not None:
             t_ref[(p, *at(lo, hi))] = t
-        if own:
+        if inside:
             sums[3] = sums[3] + tile_sum(q * t)
     for k in range(4):
-        mom[pl.ds(k * pairs + p, 1), :] = jnp.sum(sums[k], axis=0, keepdims=True)
+        total = jnp.sum(sums[k], axis=0, keepdims=True)
+        if old_mom is not None:
+            total = total + old_mom[pl.ds(k * pairs + p, 1), :]
+        mom[pl.ds(k * pairs + p, 1), :] = total
 
 
 def send_moments(pairs, rows, mom, out, row_sums):
@@ -226,58 +244,86 @@
     return jnp.where(low, s, other), jnp.where(low, other, s)
 
 
-def start_kernel(
-    groups, rows, cols, weights, a_in, e_in, dens_in, mat_in, left, right,
-    a_ref, e_ref, fr_ref, fp_ref, r_ref, q_ref, t_ref, dens_ref, mat_ref, emit_out, out,
-    inv, emit, mom,
+def first_residual(p, w, inverse_parts, parts, span, dens_ref, mat_ref, a_ref, e_ref, fr_ref, fp_ref, r_ref, inv):
+    begin, end = span
+    for lo, hi in inverse_parts:
+        a, e = a_ref[(p, *at(lo, hi))], e_ref[(p, *at(lo, hi))]
+        slope_r = 0.5 * (next_row(e) - prev_row(e))
+        slope_p = 0.5 * (after(e_ref, (p,), lo, hi, e, end) - before(e_ref, (p,), lo, hi, e, begin))
+        n2 = slope_r * slope_r + slope_p * slope_p
+        u = a * e
+        s = 2.0 * u + jnp.sqrt(n2)
+        inv[lo:hi, :] = jnp.where(dens_ref[lo:hi, :] > 0.0, (n2 + 3.0 * u * s) / (e * s), OUTSIDE)
+    for lo, hi in parts:
+        d = inv[lo:hi, :]
+        fr_ref[(p, *at(lo, hi))] = 2.0 / (d + next_row(d))
+        fp_ref[(p, *at(lo, hi))] = 2.0 / (d + after(inv, (), lo, hi, d, end))
+    for lo, hi in parts:
+        a, e = a_ref[(p, *at(lo, hi))], e_ref[(p, *at(lo, hi))]
+        r_ref[(p, *at(lo, hi))] = a * (w * mat_ref[lo:hi, :] - e) - flux_sum(
+            p, lo, hi, e_ref, e, fr_ref, fp_ref, span
+        )
+
+
+def inner_kernel(
+    groups, cols, weights, a_ref, e_ref, dens_ref, mat_ref,
+    fr_ref, fp_ref, r_ref, q_ref, t_ref, emit, mom, inv,
 ):
     pairs = groups // 2
-    tall = cols + 2 * HALO
-    dens_ref[0:HALO, :] = left[2 * pairs]
-    dens_ref[HALO : HALO + cols, :] = dens_in[...]
-    dens_ref[HALO + cols :, :] = right[2 * pairs]
-    mat_ref[0:HALO, :] = left[2 * pairs + 1]
-    mat_ref[HALO : HALO + cols, :] = mat_in[...]
-    mat_ref[HALO + cols :, :] = right[2 * pairs + 1]
+    span = (HALO, HALO + cols)
+    parts = [(lo + HALO, hi + HALO) for lo, hi in pieces(cols)]
+    own = (2 * HALO, cols)
     emit[...] = jnp.zeros(emit.shape, jnp.float32)
 
     def one(p, carry):
         w = weight_of(weights, p)
-        for lo, hi in pieces(tall):
-            if lo < HALO:
-                a, e = left[p], left[pairs + p]
-            elif hi > tall - HALO:
-                a, e = right[p], right[pairs + p]
-            else:
-                a, e = (ref[(p, *at(lo - HALO, hi - HALO))] for ref in (a_in, e_in))
-            if lo < HALO or hi > tall - HALO:
-                a = jnp.where(dens_ref[lo:hi, :] > 0.0, a, 1.0)
+        for lo, hi in parts:
+            emit[lo:hi, :] += a_ref[(p, *at(lo, hi))] * w
+        first_residual(p, w, parts, parts, span, dens_ref, mat_ref, a_ref, e_ref, fr_ref, fp_ref, r_ref, inv)
+        krylov(p, pairs, parts, span, own, a_ref, fr_ref, fp_ref, r_ref, q_ref, t_ref, mom)
+        return carry
+
+    lax.fori_loop(0, pairs, one, 0)
+
+
+def frame_kernel(groups, rows, cols, weights, got_first, got_second, emit, old_mom, *rest):
+    a_ref, e_ref, fr_ref, fp_ref, r_ref, q_ref, t_ref, dens_ref, mat_ref, emit_out, out, inv, mom = rest[9:]
+    pairs = groups // 2
+    tall = cols + 2 * HALO
+    span = (0, tall)
+    even, _, _ = partner("polar", 0, 0)
+    ends = ((0, HALO), (tall - HALO, tall))
+
+    def halo(side, plane):
+        one, two = got_first[plane], got_second[plane]
+        return jnp.where(even, two, one) if side == 0 else jnp.where(even, one, two)
+
+    for side, (lo, hi) in enumerate(ends):
+        dens_ref[lo:hi, :] = halo(side, 2 * pairs)
+        mat_ref[lo:hi, :] = halo(side, 2 * pairs + 1)
+    parts = [(0, HALO), (HALO, 2 * HALO), (cols, cols + HALO), (cols + HALO, tall)]
+    inverse_parts = parts[:2] + [(2 * HALO, 3 * HALO)] + parts[2:]
+
+    def one(p, emitted):
+        w = weight_of(weights, p)
+        sums = []
+        for side, (lo, hi) in enumerate(ends):
+            a = jnp.where(dens_ref[lo:hi, :] > 0.0, halo(side, p), 1.0)
             a_ref[(p, *at(lo, hi))] = a
-            e_ref[(p, *at(lo, hi))] = e
-            emit[lo:hi, :] += a * w
-        for lo, hi in pieces(tall):
-            a, e = a_ref[(p, *at(lo, hi))], e_ref[(p, *at(lo, hi))]
-            slope_r = 0.5 * (next_row(e) - prev_row(e))
-            slope_p = 0.5 * (after(e_ref, (p,), lo, hi, e) - before(e_ref, (p,), lo, hi, e))
-            n2 = slope_r * slope_r + slope_p * slope_p
-            u = a * e
-            s = 2.0 * u + jnp.sqrt(n2)
-            inv[lo:hi, :] = jnp.where(dens_ref[lo:hi, :] > 0.0, (n2 + 3.0 * u * s) / (e * s), OUTSIDE)
-        for lo, hi in pieces(tall):
-            d = inv[lo:hi, :]
-            fr_ref[(p, *at(lo, hi))] = 2.0 / (d + next_row(d))
-            fp_ref[(p, *at(lo, hi))] = 2.0 / (d + after(inv, (), lo, hi, d))
-        for lo, hi in pieces(tall):
-            a, e = a_ref[(p, *at(lo, hi))], e_ref[(p, *at(lo, hi))]
-            r_ref[(p, *at(lo, hi))] = a * (w * mat_ref[lo:hi, :] - e) - flux_sum(
-                p, lo, hi, e_ref, e, fr_ref, fp_ref
-            )
-        krylov(p, pairs, a_ref, fr_ref, fp_ref, r_ref, q_ref, t_ref, mom)
-        return carry
-
-    lax.fori_loop(0, pairs, one, 0)
-    emit_out[...] = fold(emit[...])
-    row_sums = jnp.sum(tile_sum(dens_in[...]), axis=0, keepdims=True)
+            e_ref[(p, *at(lo, hi))] = halo(side, pairs + p)
+            sums.append(emitted[side] + a * w)
+        first_residual(
+            p, w, inverse_parts, parts, span, dens_ref, mat_ref, a_ref, e_ref, fr_ref, fp_ref, r_ref, inv
+        )
+        krylov(
+            p, pairs, parts, span, (HALO, HALO + cols), a_ref, fr_ref, fp_ref, r_ref, q_ref, t_ref, mom, old_mom
+        )
+        return tuple(sums)
+
+    zero = jnp.zeros((HALO, LANES), jnp.float32)
+    low, high = lax.fori_loop(0, pairs, one, (zero, zero))
+    emit_out[...] = fold(jnp.concatenate([low, emit[HALO : HALO + cols, :], high], axis=0))
+    row_sums = jnp.sum(tile_sum(dens_ref[HALO : HALO + cols, :]), axis=0, keepdims=True)
     send_moments(pairs, rows, mom, out, row_sums)
 
 
@@ -397,7 +443,9 @@
     r_ref, q_ref, out, *outs = outs
     t_ref = None if last else outs.pop(0)
     m_ref = None if last else outs.pop(0)
-    half = fixed.shape[0] // 2
+    tall = fixed.shape[0]
+    parts = pieces(tall)
+    half = tall // 2
     folded = summed(sums, (0,))
     if turn == 0:
         cap_out = outs.pop(0)
@@ -416,12 +464,12 @@
         w = weight_of(weights, p)
         c1 = c1_ref[pl.ds(p, 1), :]
         c2 = c2_ref[pl.ds(p, 1), :]
-        for lo, hi in pieces(r_ref.shape[1]):
+        for lo, hi in parts:
             here = (p, *at(lo, hi))
             r_ref[here] = (
                 r_in[here] - c1 * q_in[here] + c2 * t_in[here] + a_ref[here] * (w * delta[lo:hi, :])
             )
-        krylov(p, pairs, a_ref, fr_ref, fp_ref, r_ref, q_ref, t_ref, mom)
+        krylov(p, pairs, parts, (0, tall), (HALO, tall - HALO), a_ref, fr_ref, fp_ref, r_ref, q_ref, t_ref, mom)
         return carry
 
     lax.fori_loop(0, pairs, one, 0)
@@ -437,16 +485,15 @@
 
 def spread(part, axis):
     count = lax.axis_size(axis)
-    return [part] + [
-        lax.ppermute(part, axis, [(i, (i + s) % count) for i in range(count)]) for s in range(1, count)
-    ]
-
-
-def shifted(upward, downward, axis):
+    return [part] + [lax.ppermute(part, axis, [(i, i ^ s) for i in range(count)]) for s in range(1, count)]
+
+
+def exchanged(first, second, axis):
     count = lax.axis_size(axis)
-    from_lower = lax.ppermute(downward, axis, [(i, i + 1) for i in range(count - 1)])
-    from_upper = lax.ppermute(upward, axis, [(i + 1, i) for i in range(count - 1)])
-    return from_lower, from_upper
+    got_first = lax.ppermute(first, axis, [(i, i ^ 1) for i in range(count)])
+    links = [(i, i + 1) for i in range(1, count - 1, 2)]
+    got_second = lax.ppermute(second, axis, links + [(j, i) for i, j in links])
+    return got_first, got_second
 
 
 def per_device(density, opacity, radiation_old, material_old, weights, stellar_flux):
@@ -467,7 +514,7 @@
         vmem((HALO, cols)),
         vmem((HALO, cols)),
     ]
-    up, down = call(
+    first, second = call(
         functools.partial(pack_rows_kernel, groups, rows),
         [(planes, HALO, cols)] * 2,
         (stellar_flux, opacity, radiation_old, density, material_old),
@@ -476,22 +523,31 @@
         name="pack_rows",
         limit=60 * 1024 * 1024,
     )
-    top, bottom = shifted(up, down, "radius")
-    a, e, dens, mat, flux_lanes, to_left, to_right = call(
+    first, second = exchanged(first, second, "radius")
+    a, e, dens, mat, flux_lanes, first, second = call(
         functools.partial(turn_kernel, groups, rows, cols),
-        [(pairs, *core)] * 2 + [core, core, (HALO, LANES)] + [(2 * pairs + 2, HALO, LANES)] * 2,
-        (opacity, radiation_old, density, material_old, top, bottom),
+        [big] * 2 + [flat, flat, (HALO, LANES)] + [(2 * pairs + 2, HALO, LANES)] * 2,
+        (opacity, radiation_old, density, material_old, first, second),
         [vspec()] * 6,
         name="turn",
     )
-    left, right = shifted(to_left, to_right, "polar")
+    first, second = exchanged(first, second, "polar")
+    fr, fp, r, q, t, emit, mom = call(
+        functools.partial(inner_kernel, groups, cols),
+        [big] * 5 + [flat, (4 * pairs, LANES)],
+        (weights, a, e, dens, mat),
+        [sspec()] + [vspec()] * 4,
+        scratch=[vmem(flat)],
+        name="inner",
+    )
     a, e, fr, fp, r, q, t, dens, mat, emit, out = call(
-        functools.partial(start_kernel, groups, rows, cols),
+        functools.partial(frame_kernel, groups, rows, cols),
         [big] * 7 + [flat, flat, (tall // 2, LANES), line],
-        (weights, a, e, dens, mat, left, right),
-        [sspec()] + [vspec()] * 6,
-        scratch=[vmem(flat), vmem(flat), vmem((4 * pairs, LANES))],
-        name="start",
+        (weights, first, second, emit, mom, a, e, fr, fp, r, q, t, dens, mat),
+        [sspec()] + [vspec()] * 13,
+        scratch=[vmem(flat), vmem((4 * pairs, LANES))],
+        name="frame",
+        aliases={5 + k: k for k in range(9)},
     )
     capacity = dens
     for turn in range(ITERS):

time: 118 us -> 113 us (0.958); the launches traced: 116 us -> 113 us
  starting transfers between devices: 22.4 us -> 15.5 us
  waiting for transfers between devices: 17 us -> 10.9 us
  blocking collectives: 52.2 us -> 56.9 us
  Pallas kernels: 24.1 us -> 28.6 us
    ppermute x13, starting transfers between devices: 22.4 us -> 15.5 us  [the longest x9 12.5 us: spread(): lax.ppermute(part, axis, [(i, i ^ s) for i in range(count)])]
    ppermute x13, waiting for transfers between devices: 17 us -> 10.9 us  [the longest x9 9.85 us: spread(): lax.ppermute(part, axis, [(i, i ^ s) for i in range(count)])]
    all_to_all x3, blocking collectives: 52.2 us -> 56.9 us  [per_device(): gathered = lax.all_to_all(out, ('radius', 'polar'), 0, 0, tiled=True)]
    pallas_call x11 -> x12, Pallas kernels: 24.1 us -> 28.6 us  [call(): pl.pallas_call(kernel, out_shape=[jax.ShapeDtypeStruct(s, jnp.float32) fo...]
  transfers between devices with their start and end apart: 13 -> 13, of which waited for: 8 -> 9; matrix products, arithmetic and copies ran while one was open for 0% -> 0% of each run, Pallas kernels for 3% -> 8%
where the time goes in v4:
time: 113 us
  blocking collectives  56.9 us (50%)
  Pallas kernels  28.6 us (25%)
  starting transfers between devices  15.5 us (14%)
  waiting for transfers between devices  10.9 us (10%)
    all_to_all x3, blocking collectives, per_device(): gathered = lax.all_to_all(out, ('radius', 'polar'), 0, 0, tiled=True)  56.9 us
    pallas_call x12, Pallas kernels, call(): pl.pallas_call(kernel, out_shape=[jax.ShapeDtypeStruct(s, jnp.float32) fo...  28.6 us
    ppermute x9, starting transfers between devices, spread(): lax.ppermute(part, axis, [(i, i ^ s) for i in range(count)])  12.5 us
    ppermute x9, waiting for transfers between devices, spread(): lax.ppermute(part, axis, [(i, i ^ s) for i in range(count)])  9.85 us
  transfers between devices with their start and end apart: 13, of which 9 were waited for; matrix products, arithmetic and copies ran while one was open for 0% of the time, Pallas kernels for 8%

profile of v4, /device:TPU:8, one launch (start us, length us, event | category | flops | bytes accessed | tf_op | source)
XLA Modules:
  0.0 112.8 jit_solution(14521071218315702578)
XLA Ops:
  0.6 0.0 copy-start.3
  0.6 0.0 copy-start
  0.7 0.0 copy-start.1
  0.7 0.0 copy-start.2
  0.7 2.8 %pack_rows.1 = (f32[35,8,256]{2,1,0:T(8,128)}, f32[35,8,256]{2,1,0:T(8,128)}) custom-call(f32[48]{0:T(128)} %flux.3, bf16[16,48,256]{2,1,0:T(8,128)(2,1)} %opacity.3, f32[16,48,256]{2,1,0:T(8,128)} %old.3, f32[48,256]{1,0:T(8,128)} %density.3, f32[48,256]{1,0:T(8,128)} %material.4), custom_call_target="tpu_custom_call" | custom-call | flops 1000000 | bytes 1000000 | tf_op jit(solution)/shard_map/pack_rows/pallas_call | solution.py:33
  3.5 0.0 copy-start.4
  3.5 0.1 collective-permute-start
  3.6 0.7 collective-permute-start.1
  4.3 1.1 collective-permute-done.got_first
  5.4 0.0 collective-permute-done.1.got_second
  5.4 0.0 copy-done.3
  5.4 0.0 copy-done
  5.4 1.9 %turn.1 = (f32[8,272,128]{2,1,0:T(8,128)S(1)}, f32[8,272,128]{2,1,0:T(8,128)S(1)}, f32[272,128]{1,0:T(8,128)S(1)}, f32[272,128]{1,0:T(8,128)S(1)}, f32[8,128]{1,...) custom-call(bf16[16,48,256]{2,1,0:T(8,128)(2,1)S(1)} %copy-done.1, f32[16,48,256]{2,1,0:T(8,128)S(1)} %copy-done, ...), custom_call_target="tpu_custom_call" | custom-call | flops 1000000 | bytes 1000000 | tf_op jit(solution)/shard_map/turn/pallas_call | solution.py:33
  7.3 1.6 %collective-permute-start.2 = (f32[18,8,128]{2,1,0:T(8,128)S(1)}, f32[18,8,128]{2,1,0:T(8,128)S(1)}, u32[]{:S(2)}, u32[]{:S(2)}) collective-permute-start(f32[18,8,128]{2,1,0:T(8,128)S(1)} %get-tuple-element.53), channel_id=1, source_target_pairs={{0,4},{4,0},{8,12},{12,8},{1,5},{5,1},{9,13},{13,9},{2,6},{6,2},{1... | collective-permute-start | bytes 221192 | tf_op jit(solution)/shard_map/ppermute | solution.py:493
  8.9 0.7 collective-permute-start.3
  9.6 6.1 %inner.1 = (f32[8,272,128]{2,1,0:T(8,128)S(1)}, f32[8,272,128]{2,1,0:T(8,128)S(1)}, f32[8,272,128]{2,1,0:T(8,128)S(1)}, f32[8,272,128]{2,1,0:T(8,128)S(1)}, f32[...) custom-call(f32[16]{0:T(128)S(1)} %copy-done.4, ...), custom_call_target="tpu_custom_call" | custom-call | flops 1000000 | bytes 1000000 | tf_op jit(solution)/shard_map/inner/pallas_call | solution.py:33
  15.7 0.0 collective-permute-done.2.got_first
  15.7 0.0 collective-permute-done.3.got_second
  15.7 5.0 %frame.1 = (f32[8,272,128]{2,1,0:T(8,128)S(1)}, f32[8,272,128]{2,1,0:T(8,128)S(1)}, f32[8,272,128]{2,1,0:T(8,128)S(1)}, f32[8,272,128]{2,1,0:T(8,128)S(1)}, f32[...) custom-call(f32[16]{0:T(128)S(1)} %copy-done.4, ...), custom_call_target="tpu_custom_call", output_to_operand_aliasing={{0}: (5, {}), {1}: (6, {}), {2}: (7, {}), {3}: (8, {}), {4}... | custom-call | flops 1000000 | bytes 1000000 | tf_op jit(solution)/shard_map/frame/pallas_call | solution.py:33
  20.7 30.0 %all_to_all.33 = f32[64,1,128]{2,1,0:T(1,128)S(1)} all-to-all(f32[64,1,128]{2,1,0:T(1,128)S(1)} %bitcast.16), channel_id=1, replica_groups=mesh['radius'=16,'polar'=4,'group'=4] {'radius','polar'}, dimensions={0} | all-to-all | bytes 65536 | tf_op jit(solution)/shard_map/all_to_all | solution.py:554
  50.7 0.5 update.2
  51.1 1.6 %collective-permute-start.6 = (f32[2,136,128]{2,1,0:T(8,128)S(1)}, f32[2,136,128]{2,1,0:T(8,128)S(1)}, u32[]{:S(2)}, u32[]{:S(2)}) collective-permute-start(f32[2,136,128]{2,1,0:T(8,128)S(1)} %get-tuple-element.81.rest_0_), channel_id=1, source_target_pairs={{0,3},{1,2},{2,1},{3,0},{4,7},{5,6},{6,5},{7,4},{8,11},{9,10},{10,... | collective-permute-start | bytes 417800 | tf_op jit(solution)/shard_map/ppermute | solution.py:488
  52.8 0.9 collective-permute-start.5
  53.7 1.6 %collective-permute-start.4 = (f32[2,136,128]{2,1,0:T(8,128)S(1)}, f32[2,136,128]{2,1,0:T(8,128)S(1)}, u32[]{:S(2)}, u32[]{:S(2)}) collective-permute-start(f32[2,136,128]{2,1,0:T(8,128)S(1)} %get-tuple-element.81.rest_0_), channel_id=1, source_target_pairs={{0,1},{1,0},{2,3},{3,2},{4,5},{5,4},{6,7},{7,6},{8,9},{9,8},{10,11... | collective-permute-start | bytes 417800 | tf_op jit(solution)/shard_map/ppermute | solution.py:488
  55.3 1.7 %heating.1 = (f32[48,256]{1,0:T(8,128)}, f32[272,128]{1,0:T(8,128)S(1)}) custom-call(f32[48]{0:T(128)S(1)} %copy-done.5, f32[64,128]{1,0:T(8,128)S(1)} %bitcast.13, f32[272,128]{1,0:T(8,128)S(1)} %get-tuple-element.77.dens_ref.cap_in, f32[272,128]{1,0:T(8,128)S(1)} %get-tuple-element.78.mat_ref, f32[8,128]{1,0:T(8,128)S(1)} %get-tuple-element.79.flux_ref), custom_call_target="tpu_custom_call" | custom-call | flops 1000000 | bytes 1000000 | tf_op jit(solution)/shard_map/heating/pallas_call | solution.py:33
  57.0 0.9 collective-permute-done.6.rest_3_
  57.9 2.8 %collective-permute-done.5.rest_2_ = f32[2,136,128]{2,1,0:T(8,128)S(1)} collective-permute-done((f32[2,136,128]{2,1,0:T(8,128)S(1)}, f32[2,136,128]{2,1,0:T(8,128)S(1)}, u32[]{:S(2)}, u32[]{:S(2)}) %collective-permute-start.5) | collective-permute-done | bytes 139296 | tf_op jit(solution)/shard_map/ppermute | solution.py:488
  60.7 0.5 collective-permute-done.4.rest_1_
  61.2 3.7 %next.2 = (f32[8,272,128]{2,1,0:T(8,128)S(1)}, f32[8,272,128]{2,1,0:T(8,128)S(1)}, f32[64,128]{1,0:T(8,128)S(1)}, f32[8,272,128]{2,1,0:T(8,128)S(1)}, f32[272,128]{1,0:T(8,128)S(1)}, /*index=5*/f32[272,128]{1,0:T(8,128)S(1)}) custom-call(f32[16]{0:T(128)S(1)} %copy-done.4, f32[8,128]{1,0:T(8,128)S(1)} %get-tuple-element.72.c1_ref, ...), custom_call_target="tpu_custom_call" | custom-call | flops 1000000 | bytes 1000000 | tf_op jit(solution)/shard_map/next/pallas_call | solution.py:33
  64.9 13.5 %all_to_all.34 = f32[64,1,128]{2,1,0:T(1,128)S(1)} all-to-all(f32[64,1,128]{2,1,0:T(1,128)S(1)} %bitcast.17), channel_id=1, replica_groups=mesh['radius'=16,'polar'=4,'group'=4] {'radius','polar'}, dimensions={0} | all-to-all | bytes 65536 | tf_op jit(solution)/shard_map/all_to_all | solution.py:554
  78.3 0.5 update.3
  78.8 1.6 %collective-permute-start.9 = (f32[1,136,128]{2,1,0:T(8,128)S(1)}, f32[1,136,128]{2,1,0:T(8,128)S(1)}, u32[]{:S(2)}, u32[]{:S(2)}) collective-permute-start(f32[1,136,128]{2,1,0:T(8,128)S(1)} %get-tuple-element.91.rest_0_), channel_id=1, source_target_pairs={{0,3},{1,2},{2,1},{3,0},{4,7},{5,6},{6,5},{7,4},{8,11},{9,10},{10,... | collective-permute-start | bytes 208904 | tf_op jit(solution)/shard_map/ppermute | solution.py:488
  80.4 1.9 %collective-permute-start.8 = (f32[1,136,128]{2,1,0:T(8,128)S(1)}, f32[1,136,128]{2,1,0:T(8,128)S(1)}, u32[]{:S(2)}, u32[]{:S(2)}) collective-permute-start(f32[1,136,128]{2,1,0:T(8,128)S(1)} %get-tuple-element.91.rest_0_), channel_id=1, source_target_pairs={{0,2},{1,3},{2,0},{3,1},{4,6},{5,7},{6,4},{7,5},{8,10},{9,11},{10,... | collective-permute-start | bytes 208904 | tf_op jit(solution)/shard_map/ppermute | solution.py:488
  82.3 0.7 collective-permute-start.7
  83.0 0.2 collective-permute-done.9.rest_3_
  83.2 3.1 %collective-permute-done.8.rest_2_ = f32[1,136,128]{2,1,0:T(8,128)S(1)} collective-permute-done((f32[1,136,128]{2,1,0:T(8,128)S(1)}, f32[1,136,128]{2,1,0:T(8,128)S(1)}, u32[]{:S(2)}, u32[]{:S(2)}) %collective-permute-start.8) | collective-permute-done | bytes 69664 | tf_op jit(solution)/shard_map/ppermute | solution.py:488
  86.3 0.3 collective-permute-done.7.rest_1_
  86.6 3.6 %next.3 = (f32[8,272,128]{2,1,0:T(8,128)S(1)}, f32[8,272,128]{2,1,0:T(8,128)S(1)}, f32[64,128]{1,0:T(8,128)S(1)}) custom-call(f32[16]{0:T(128)S(1)} %copy-done.4, f32[8,128]{1,0:T(8,128)S(1)} %get-tuple-element.86.c1_ref, f32[8,128]{1,0:T(8,128)S(1)} %get-tuple-element.87.c2_ref, f32[8,272,128]{2,1,0:T(8,128)S(1)} %get-tuple-element.67.a_ref, ...), custom_call_target="tpu_custom_call" | custom-call | flops 1000000 | bytes 1000000 | tf_op jit(solution)/shard_map/next/pallas_call | solution.py:33
  90.2 13.5 %all_to_all.35 = f32[64,1,128]{2,1,0:T(1,128)S(1)} all-to-all(f32[64,1,128]{2,1,0:T(1,128)S(1)} %bitcast.18), channel_id=1, replica_groups=mesh['radius'=16,'polar'=4,'group'=4] {'radius','polar'}, dimensions={0} | all-to-all | bytes 65536 | tf_op jit(solution)/shard_map/all_to_all | solution.py:554
  103.7 0.4 last_update.1
  104.1 1.5 %collective-permute-start.12 = (f32[128,128]{1,0:T(8,128)S(1)}, f32[128,128]{1,0:T(8,128)S(1)}, u32[]{:S(2)}, u32[]{:S(2)}) collective-permute-start(f32[128,128]{1,0:T(8,128)S(1)} %get-tuple-element.97.rest_0_), channel_id=1, source_target_pairs={{0,3},{1,2},{2,1},{3,0},{4,7},{5,6},{6,5},{7,4},{8,11},{9,10},{10,... | collective-permute-start | bytes 196616 | tf_op jit(solution)/shard_map/ppermute | solution.py:488
  105.6 2.1 %collective-permute-start.11 = (f32[128,128]{1,0:T(8,128)S(1)}, f32[128,128]{1,0:T(8,128)S(1)}, u32[]{:S(2)}, u32[]{:S(2)}) collective-permute-start(f32[128,128]{1,0:T(8,128)S(1)} %get-tuple-element.97.rest_0_), channel_id=1, source_target_pairs={{0,2},{1,3},{2,0},{3,1},{4,6},{5,7},{6,4},{7,5},{8,10},{9,11},{10,... | collective-permute-start | bytes 196616 | tf_op jit(solution)/shard_map/ppermute | solution.py:488
  107.7 0.5 collective-permute-start.10
  108.3 1.7 %energy.1 = f32[16,48,256]{2,1,0:T(8,128)} custom-call(f32[8,272,128]{2,1,0:T(8,128)S(1)} %get-tuple-element.96.e_ref), custom_call_target="tpu_custom_call" | custom-call | flops 1000000 | bytes 1000000 | tf_op jit(solution)/shard_map/energy/pallas_call | solution.py:33
  109.9 0.0 collective-permute-done.12.rest_3_
  109.9 1.5 %collective-permute-done.11.rest_2_ = f32[128,128]{1,0:T(8,128)S(1)} collective-permute-done((f32[128,128]{1,0:T(8,128)S(1)}, f32[128,128]{1,0:T(8,128)S(1)}, u32[]{:S(2)}, u32[]{:S(2)}) %collective-permute-start.11) | collective-permute-done | bytes 65568 | tf_op jit(solution)/shard_map/ppermute | solution.py:488
  111.4 0.6 collective-permute-done.10.rest_1_
  112.0 0.8 material.5
  (5 shorter events, 0.0 us)
Async XLA Ops:
  0.6 4.8 %copy-start.3 = (f32[48,256]{1,0:T(8,128)S(1)}, f32[48,256]{1,0:T(8,128)}, u32[]{:S(2)}) copy-start(f32[48,256]{1,0:T(8,128)} %material.4) | copy-start | bytes 147460
  0.6 4.8 %copy-start = (f32[16,48,256]{2,1,0:T(8,128)S(1)}, f32[16,48,256]{2,1,0:T(8,128)}, u32[]{:S(2)}) copy-start(f32[16,48,256]{2,1,0:T(8,128)} %old.3) | copy-start | bytes 2359300
  0.7 4.8 %copy-start.1 = (bf16[16,48,256]{2,1,0:T(8,128)(2,1)S(1)}, bf16[16,48,256]{2,1,0:T(8,128)(2,1)}, u32[]{:S(2)}) copy-start(bf16[16,48,256]{2,1,0:T(8,128)(2,1)} %opacity.3) | copy-start | bytes 1179652
  0.7 4.8 %copy-start.2 = (f32[48,256]{1,0:T(8,128)S(1)}, f32[48,256]{1,0:T(8,128)}, u32[]{:S(2)}) copy-start(f32[48,256]{1,0:T(8,128)} %density.3) | copy-start | bytes 147460
  3.5 6.0 %copy-start.4 = (f32[16]{0:T(128)S(1)}, f32[16]{0:T(128)}, u32[]{:S(2)}) copy-start(f32[16]{0:T(128)} %weights.7) | copy-start | bytes 196
  3.5 1.9 %collective-permute-start = (f32[35,8,256]{2,1,0:T(8,128)}, f32[35,8,256]{2,1,0:T(8,128)S(1)}, u32[]{:S(2)}, u32[]{:S(2)}) collective-permute-start(f32[35,8,256]{2,1,0:T(8,128)} %get-tuple-element.51), channel_id=1, source_target_pairs={{0,16},{16,0},{32,48},{48,32},{64,80},{80,64},{96,112},{112,96},{1... | collective-permute-start | bytes 860168 | tf_op jit(solution)/shard_map/ppermute | solution.py:493
  3.6 1.8 %collective-permute-start.1 = (f32[35,8,256]{2,1,0:T(8,128)}, f32[35,8,256]{2,1,0:T(8,128)S(1)}, u32[]{:S(2)}, u32[]{:S(2)}) collective-permute-start(f32[35,8,256]{2,1,0:T(8,128)} %get-tuple-element.52), channel_id=1, source_target_pairs={{16,32},{48,64},{80,96},{112,128},{144,160},{176,192},{208,224},{3... | collective-permute-start | bytes 860168 | tf_op jit(solution)/shard_map/ppermute | solution.py:495
  7.3 8.4 %collective-permute-start.2 = (f32[18,8,128]{2,1,0:T(8,128)S(1)}, f32[18,8,128]{2,1,0:T(8,128)S(1)}, u32[]{:S(2)}, u32[]{:S(2)}) collective-permute-start(f32[18,8,128]{2,1,0:T(8,128)S(1)} %get-tuple-element.53), channel_id=1, source_target_pairs={{0,4},{4,0},{8,12},{12,8},{1,5},{5,1},{9,13},{13,9},{2,6},{6,2},{1... | collective-permute-start | bytes 221192 | tf_op jit(solution)/shard_map/ppermute | solution.py:493
  8.9 6.8 %collective-permute-start.3 = (f32[18,8,128]{2,1,0:T(8,128)S(1)}, f32[18,8,128]{2,1,0:T(8,128)S(1)}, u32[]{:S(2)}, u32[]{:S(2)}) collective-permute-start(f32[18,8,128]{2,1,0:T(8,128)S(1)} %get-tuple-element.54), channel_id=1, source_target_pairs={{4,8},{8,4},{5,9},{9,5},{6,10},{10,6},{7,11},{11,7},{20,24},{24,20... | collective-permute-start | bytes 221192 | tf_op jit(solution)/shard_map/ppermute | solution.py:495
  50.7 4.6 %copy-start.5 = (f32[48]{0:T(128)S(1)}, f32[48]{0:T(128)}, u32[]{:S(2)}) copy-start(f32[48]{0:T(128)} %flux.3) | copy-start | bytes 580
  51.1 6.8 %collective-permute-start.6 = (f32[2,136,128]{2,1,0:T(8,128)S(1)}, f32[2,136,128]{2,1,0:T(8,128)S(1)}, u32[]{:S(2)}, u32[]{:S(2)}) collective-permute-start(f32[2,136,128]{2,1,0:T(8,128)S(1)} %get-tuple-element.81.rest_0_), channel_id=1, source_target_pairs={{0,3},{1,2},{2,1},{3,0},{4,7},{5,6},{6,5},{7,4},{8,11},{9,10},{10,... | collective-permute-start | bytes 417800 | tf_op jit(solution)/shard_map/ppermute | solution.py:488
  52.8 7.9 %collective-permute-start.5 = (f32[2,136,128]{2,1,0:T(8,128)S(1)}, f32[2,136,128]{2,1,0:T(8,128)S(1)}, u32[]{:S(2)}, u32[]{:S(2)}) collective-permute-start(f32[2,136,128]{2,1,0:T(8,128)S(1)} %get-tuple-element.81.rest_0_), channel_id=1, source_target_pairs={{0,2},{1,3},{2,0},{3,1},{4,6},{5,7},{6,4},{7,5},{8,10},{9,11},{10,... | collective-permute-start | bytes 417800 | tf_op jit(solution)/shard_map/ppermute | solution.py:488
  53.7 7.4 %collective-permute-start.4 = (f32[2,136,128]{2,1,0:T(8,128)S(1)}, f32[2,136,128]{2,1,0:T(8,128)S(1)}, u32[]{:S(2)}, u32[]{:S(2)}) collective-permute-start(f32[2,136,128]{2,1,0:T(8,128)S(1)} %get-tuple-element.81.rest_0_), channel_id=1, source_target_pairs={{0,1},{1,0},{2,3},{3,2},{4,5},{5,4},{6,7},{7,6},{8,9},{9,8},{10,11... | collective-permute-start | bytes 417800 | tf_op jit(solution)/shard_map/ppermute | solution.py:488
  78.8 4.4 %collective-permute-start.9 = (f32[1,136,128]{2,1,0:T(8,128)S(1)}, f32[1,136,128]{2,1,0:T(8,128)S(1)}, u32[]{:S(2)}, u32[]{:S(2)}) collective-permute-start(f32[1,136,128]{2,1,0:T(8,128)S(1)} %get-tuple-element.91.rest_0_), channel_id=1, source_target_pairs={{0,3},{1,2},{2,1},{3,0},{4,7},{5,6},{6,5},{7,4},{8,11},{9,10},{10,... | collective-permute-start | bytes 208904 | tf_op jit(solution)/shard_map/ppermute | solution.py:488
  80.4 5.9 %collective-permute-start.8 = (f32[1,136,128]{2,1,0:T(8,128)S(1)}, f32[1,136,128]{2,1,0:T(8,128)S(1)}, u32[]{:S(2)}, u32[]{:S(2)}) collective-permute-start(f32[1,136,128]{2,1,0:T(8,128)S(1)} %get-tuple-element.91.rest_0_), channel_id=1, source_target_pairs={{0,2},{1,3},{2,0},{3,1},{4,6},{5,7},{6,4},{7,5},{8,10},{9,11},{10,... | collective-permute-start | bytes 208904 | tf_op jit(solution)/shard_map/ppermute | solution.py:488
  82.3 4.3 %collective-permute-start.7 = (f32[1,136,128]{2,1,0:T(8,128)S(1)}, f32[1,136,128]{2,1,0:T(8,128)S(1)}, u32[]{:S(2)}, u32[]{:S(2)}) collective-permute-start(f32[1,136,128]{2,1,0:T(8,128)S(1)} %get-tuple-element.91.rest_0_), channel_id=1, source_target_pairs={{0,1},{1,0},{2,3},{3,2},{4,5},{5,4},{6,7},{7,6},{8,9},{9,8},{10,11... | collective-permute-start | bytes 208904 | tf_op jit(solution)/shard_map/ppermute | solution.py:488
  104.1 5.8 %collective-permute-start.12 = (f32[128,128]{1,0:T(8,128)S(1)}, f32[128,128]{1,0:T(8,128)S(1)}, u32[]{:S(2)}, u32[]{:S(2)}) collective-permute-start(f32[128,128]{1,0:T(8,128)S(1)} %get-tuple-element.97.rest_0_), channel_id=1, source_target_pairs={{0,3},{1,2},{2,1},{3,0},{4,7},{5,6},{6,5},{7,4},{8,11},{9,10},{10,... | collective-permute-start | bytes 196616 | tf_op jit(solution)/shard_map/ppermute | solution.py:488
  105.6 5.8 %collective-permute-start.11 = (f32[128,128]{1,0:T(8,128)S(1)}, f32[128,128]{1,0:T(8,128)S(1)}, u32[]{:S(2)}, u32[]{:S(2)}) collective-permute-start(f32[128,128]{1,0:T(8,128)S(1)} %get-tuple-element.97.rest_0_), channel_id=1, source_target_pairs={{0,2},{1,3},{2,0},{3,1},{4,6},{5,7},{6,4},{7,5},{8,10},{9,11},{10,... | collective-permute-start | bytes 196616 | tf_op jit(solution)/shard_map/ppermute | solution.py:488
  107.7 4.3 %collective-permute-start.10 = (f32[128,128]{1,0:T(8,128)S(1)}, f32[128,128]{1,0:T(8,128)S(1)}, u32[]{:S(2)}, u32[]{:S(2)}) collective-permute-start(f32[128,128]{1,0:T(8,128)S(1)} %get-tuple-element.97.rest_0_), channel_id=1, source_target_pairs={{0,1},{1,0},{2,3},{3,2},{4,5},{5,4},{6,7},{7,6},{8,9},{9,8},{10,11... | collective-permute-start | bytes 196616 | tf_op jit(solution)/shard_map/ppermute | solution.py:488

commit v5 on v4

--- a/solution.py
+++ b/solution.py
@@ -132,7 +132,7 @@
             e_ref[p, HALO + lo : HALO + hi, :] = jnp.concatenate(both, axis=0).T
             return carry
 
-        lax.fori_loop(0, pairs, one, 0)
+        lax.fori_loop(0, pairs, one, 0, unroll=8)
     _, lo_first, lo_second = partner("polar", cols, HALO)
     for out, lo in ((to_first, lo_first), (to_second, lo_second)):
         edge = pl.ds(pl.multiple_of(lo, HALO), HALO)
@@ -283,7 +283,7 @@
         krylov(p, pairs, parts, span, own, a_ref, fr_ref, fp_ref, r_ref, q_ref, t_ref, mom)
         return carry
 
-    lax.fori_loop(0, pairs, one, 0)
+    lax.fori_loop(0, pairs, one, 0, unroll=2)
 
 
 def frame_kernel(groups, rows, cols, weights, got_first, got_second, emit, old_mom, *rest):
@@ -321,7 +321,7 @@
         return tuple(sums)
 
     zero = jnp.zeros((HALO, LANES), jnp.float32)
-    low, high = lax.fori_loop(0, pairs, one, (zero, zero))
+    low, high = lax.fori_loop(0, pairs, one, (zero, zero), unroll=8)
     emit_out[...] = fold(jnp.concatenate([low, emit[HALO : HALO + cols, :], high], axis=0))
     row_sums = jnp.sum(tile_sum(dens_ref[HALO : HALO + cols, :]), axis=0, keepdims=True)
     send_moments(pairs, rows, mom, out, row_sums)
@@ -393,7 +393,7 @@
             out[2 * p + 1, :, lo : lo + LANES] = block[HALF + HALO : HALF + HALO + rows]
         return carry
 
-    lax.fori_loop(0, pairs, one, 0)
+    lax.fori_loop(0, pairs, one, 0, unroll=4)
 
 
 def turned_back(v, rows):
@@ -472,7 +472,7 @@
         krylov(p, pairs, parts, (0, tall), (HALO, tall - HALO), a_ref, fr_ref, fp_ref, r_ref, q_ref, t_ref, mom)
         return carry
 
-    lax.fori_loop(0, pairs, one, 0)
+    lax.fori_loop(0, pairs, one, 0, unroll=2)
     send_moments(pairs, rows, mom, out, None)
 
 

time: 113 us -> 106 us (0.938)
  Pallas kernels: 28.6 us -> 21.1 us
    pallas_call x12, Pallas kernels: 28.6 us -> 21.1 us  [call(): pl.pallas_call(kernel, out_shape=[jax.ShapeDtypeStruct(s, jnp.float32) fo...]
where the time goes in v5:
time: 106 us
  blocking collectives  57.1 us (54%)
  Pallas kernels  21.1 us (20%)
  starting transfers between devices  15.5 us (15%)
  waiting for transfers between devices  11.3 us (11%)
    all_to_all x3, blocking collectives, per_device(): gathered = lax.all_to_all(out, ('radius', 'polar'), 0, 0, tiled=True)  57.1 us
    pallas_call x12, Pallas kernels, call(): pl.pallas_call(kernel, out_shape=[jax.ShapeDtypeStruct(s, jnp.float32) fo...  21.1 us
    ppermute x9, starting transfers between devices, spread(): lax.ppermute(part, axis, [(i, i ^ s) for i in range(count)])  12.5 us
    ppermute x9, waiting for transfers between devices, spread(): lax.ppermute(part, axis, [(i, i ^ s) for i in range(count)])  10.2 us
  transfers between devices with their start and end apart: 13, of which 9 were waited for; matrix products, arithmetic and copies ran while one was open for 0% of the time, Pallas kernels for 8%

profile of v5, /device:TPU:8, one launch (start us, length us, event | category | flops | bytes accessed | tf_op | source)
XLA Modules:
  0.0 105.8 jit_solution(10019009441698217598)
XLA Ops:
  0.6 0.0 copy-start.3
  0.6 0.0 copy-start
  0.7 0.0 copy-start.1
  0.7 0.0 copy-start.2
  0.7 2.8 %pack_rows.1 = (f32[35,8,256]{2,1,0:T(8,128)}, f32[35,8,256]{2,1,0:T(8,128)}) custom-call(f32[48]{0:T(128)} %flux.3, bf16[16,48,256]{2,1,0:T(8,128)(2,1)} %opacity.3, f32[16,48,256]{2,1,0:T(8,128)} %old.3, f32[48,256]{1,0:T(8,128)} %density.3, f32[48,256]{1,0:T(8,128)} %material.4), custom_call_target="tpu_custom_call" | custom-call | flops 1000000 | bytes 1000000 | tf_op jit(solution)/shard_map/pack_rows/pallas_call | solution.py:33
  3.5 0.0 copy-start.4
  3.5 0.1 collective-permute-start
  3.6 0.7 collective-permute-start.1
  4.3 1.1 %collective-permute-done.got_first = f32[35,8,256]{2,1,0:T(8,128)S(1)} collective-permute-done((f32[35,8,256]{2,1,0:T(8,128)}, f32[35,8,256]{2,1,0:T(8,128)S(1)}, u32[]{:S(2)}, u32[]{:S(2)}) %collective-permute-start) | collective-permute-done | bytes 286752 | tf_op jit(solution)/shard_map/ppermute | solution.py:493
  5.4 0.0 collective-permute-done.1.got_second
  5.4 0.0 copy-done.3
  5.4 0.0 copy-done
  5.4 0.7 turn.1
  6.1 1.6 %collective-permute-start.2 = (f32[18,8,128]{2,1,0:T(8,128)S(1)}, f32[18,8,128]{2,1,0:T(8,128)S(1)}, u32[]{:S(2)}, u32[]{:S(2)}) collective-permute-start(f32[18,8,128]{2,1,0:T(8,128)S(1)} %get-tuple-element.53), channel_id=1, source_target_pairs={{0,4},{4,0},{8,12},{12,8},{1,5},{5,1},{9,13},{13,9},{2,6},{6,2},{1... | collective-permute-start | bytes 221192 | tf_op jit(solution)/shard_map/ppermute | solution.py:493
  7.7 0.7 collective-permute-start.3
  8.4 5.1 %inner.1 = (f32[8,272,128]{2,1,0:T(8,128)S(1)}, f32[8,272,128]{2,1,0:T(8,128)S(1)}, f32[8,272,128]{2,1,0:T(8,128)S(1)}, f32[8,272,128]{2,1,0:T(8,128)S(1)}, f32[...) custom-call(f32[16]{0:T(128)S(1)} %copy-done.4, ...), custom_call_target="tpu_custom_call" | custom-call | flops 1000000 | bytes 1000000 | tf_op jit(solution)/shard_map/inner/pallas_call | solution.py:33
  13.5 0.0 collective-permute-done.2.got_first
  13.5 0.0 collective-permute-done.3.got_second
  13.5 1.4 %frame.1 = (f32[8,272,128]{2,1,0:T(8,128)S(1)}, f32[8,272,128]{2,1,0:T(8,128)S(1)}, f32[8,272,128]{2,1,0:T(8,128)S(1)}, f32[8,272,128]{2,1,0:T(8,128)S(1)}, f32[...) custom-call(f32[16]{0:T(128)S(1)} %copy-done.4, ...), custom_call_target="tpu_custom_call", output_to_operand_aliasing={{0}: (5, {}), {1}: (6, {}), {2}: (7, {}), {3}: (8, {}), {4}... | custom-call | flops 1000000 | bytes 1000000 | tf_op jit(solution)/shard_map/frame/pallas_call | solution.py:33
  14.9 30.0 %all_to_all.33 = f32[64,1,128]{2,1,0:T(1,128)S(1)} all-to-all(f32[64,1,128]{2,1,0:T(1,128)S(1)} %bitcast.16), channel_id=1, replica_groups=mesh['radius'=16,'polar'=4,'group'=4] {'radius','polar'}, dimensions={0} | all-to-all | bytes 65536 | tf_op jit(solution)/shard_map/all_to_all | solution.py:554
  44.9 0.5 update.2
  45.3 1.6 %collective-permute-start.6 = (f32[2,136,128]{2,1,0:T(8,128)S(1)}, f32[2,136,128]{2,1,0:T(8,128)S(1)}, u32[]{:S(2)}, u32[]{:S(2)}) collective-permute-start(f32[2,136,128]{2,1,0:T(8,128)S(1)} %get-tuple-element.81.rest_0_), channel_id=1, source_target_pairs={{0,3},{1,2},{2,1},{3,0},{4,7},{5,6},{6,5},{7,4},{8,11},{9,10},{10,... | collective-permute-start | bytes 417800 | tf_op jit(solution)/shard_map/ppermute | solution.py:488
  46.9 0.9 collective-permute-start.5
  47.9 1.6 %collective-permute-start.4 = (f32[2,136,128]{2,1,0:T(8,128)S(1)}, f32[2,136,128]{2,1,0:T(8,128)S(1)}, u32[]{:S(2)}, u32[]{:S(2)}) collective-permute-start(f32[2,136,128]{2,1,0:T(8,128)S(1)} %get-tuple-element.81.rest_0_), channel_id=1, source_target_pairs={{0,1},{1,0},{2,3},{3,2},{4,5},{5,4},{6,7},{7,6},{8,9},{9,8},{10,11... | collective-permute-start | bytes 417800 | tf_op jit(solution)/shard_map/ppermute | solution.py:488
  49.5 1.7 %heating.1 = (f32[48,256]{1,0:T(8,128)}, f32[272,128]{1,0:T(8,128)S(1)}) custom-call(f32[48]{0:T(128)S(1)} %copy-done.5, f32[64,128]{1,0:T(8,128)S(1)} %bitcast.13, f32[272,128]{1,0:T(8,128)S(1)} %get-tuple-element.77.dens_ref.cap_in, f32[272,128]{1,0:T(8,128)S(1)} %get-tuple-element.78.mat_ref, f32[8,128]{1,0:T(8,128)S(1)} %get-tuple-element.79.flux_ref), custom_call_target="tpu_custom_call" | custom-call | flops 1000000 | bytes 1000000 | tf_op jit(solution)/shard_map/heating/pallas_call | solution.py:33
  51.2 0.9 collective-permute-done.6.rest_3_
  52.1 2.8 %collective-permute-done.5.rest_2_ = f32[2,136,128]{2,1,0:T(8,128)S(1)} collective-permute-done((f32[2,136,128]{2,1,0:T(8,128)S(1)}, f32[2,136,128]{2,1,0:T(8,128)S(1)}, u32[]{:S(2)}, u32[]{:S(2)}) %collective-permute-start.5) | collective-permute-done | bytes 139296 | tf_op jit(solution)/shard_map/ppermute | solution.py:488
  54.9 0.5 collective-permute-done.4.rest_1_
  55.3 3.1 %next.2 = (f32[8,272,128]{2,1,0:T(8,128)S(1)}, f32[8,272,128]{2,1,0:T(8,128)S(1)}, f32[64,128]{1,0:T(8,128)S(1)}, f32[8,272,128]{2,1,0:T(8,128)S(1)}, f32[272,128]{1,0:T(8,128)S(1)}, /*index=5*/f32[272,128]{1,0:T(8,128)S(1)}) custom-call(f32[16]{0:T(128)S(1)} %copy-done.4, f32[8,128]{1,0:T(8,128)S(1)} %get-tuple-element.72.c1_ref, ...), custom_call_target="tpu_custom_call" | custom-call | flops 1000000 | bytes 1000000 | tf_op jit(solution)/shard_map/next/pallas_call | solution.py:33
  58.4 13.5 %all_to_all.34 = f32[64,1,128]{2,1,0:T(1,128)S(1)} all-to-all(f32[64,1,128]{2,1,0:T(1,128)S(1)} %bitcast.17), channel_id=1, replica_groups=mesh['radius'=16,'polar'=4,'group'=4] {'radius','polar'}, dimensions={0} | all-to-all | bytes 65536 | tf_op jit(solution)/shard_map/all_to_all | solution.py:554
  71.9 0.5 update.3
  72.4 1.6 %collective-permute-start.9 = (f32[1,136,128]{2,1,0:T(8,128)S(1)}, f32[1,136,128]{2,1,0:T(8,128)S(1)}, u32[]{:S(2)}, u32[]{:S(2)}) collective-permute-start(f32[1,136,128]{2,1,0:T(8,128)S(1)} %get-tuple-element.91.rest_0_), channel_id=1, source_target_pairs={{0,3},{1,2},{2,1},{3,0},{4,7},{5,6},{6,5},{7,4},{8,11},{9,10},{10,... | collective-permute-start | bytes 208904 | tf_op jit(solution)/shard_map/ppermute | solution.py:488
  74.0 1.9 %collective-permute-start.8 = (f32[1,136,128]{2,1,0:T(8,128)S(1)}, f32[1,136,128]{2,1,0:T(8,128)S(1)}, u32[]{:S(2)}, u32[]{:S(2)}) collective-permute-start(f32[1,136,128]{2,1,0:T(8,128)S(1)} %get-tuple-element.91.rest_0_), channel_id=1, source_target_pairs={{0,2},{1,3},{2,0},{3,1},{4,6},{5,7},{6,4},{7,5},{8,10},{9,11},{10,... | collective-permute-start | bytes 208904 | tf_op jit(solution)/shard_map/ppermute | solution.py:488
  75.9 0.7 collective-permute-start.7
  76.5 0.2 collective-permute-done.9.rest_3_
  76.7 3.1 %collective-permute-done.8.rest_2_ = f32[1,136,128]{2,1,0:T(8,128)S(1)} collective-permute-done((f32[1,136,128]{2,1,0:T(8,128)S(1)}, f32[1,136,128]{2,1,0:T(8,128)S(1)}, u32[]{:S(2)}, u32[]{:S(2)}) %collective-permute-start.8) | collective-permute-done | bytes 69664 | tf_op jit(solution)/shard_map/ppermute | solution.py:488
  79.9 0.3 collective-permute-done.7.rest_1_
  80.2 2.9 %next.3 = (f32[8,272,128]{2,1,0:T(8,128)S(1)}, f32[8,272,128]{2,1,0:T(8,128)S(1)}, f32[64,128]{1,0:T(8,128)S(1)}) custom-call(f32[16]{0:T(128)S(1)} %copy-done.4, f32[8,128]{1,0:T(8,128)S(1)} %get-tuple-element.86.c1_ref, f32[8,128]{1,0:T(8,128)S(1)} %get-tuple-element.87.c2_ref, f32[8,272,128]{2,1,0:T(8,128)S(1)} %get-tuple-element.67.a_ref, ...), custom_call_target="tpu_custom_call" | custom-call | flops 1000000 | bytes 1000000 | tf_op jit(solution)/shard_map/next/pallas_call | solution.py:33
  83.1 13.7 %all_to_all.35 = f32[64,1,128]{2,1,0:T(1,128)S(1)} all-to-all(f32[64,1,128]{2,1,0:T(1,128)S(1)} %bitcast.18), channel_id=1, replica_groups=mesh['radius'=16,'polar'=4,'group'=4] {'radius','polar'}, dimensions={0} | all-to-all | bytes 65536 | tf_op jit(solution)/shard_map/all_to_all | solution.py:554
  96.8 0.4 last_update.1
  97.2 1.5 %collective-permute-start.12 = (f32[128,128]{1,0:T(8,128)S(1)}, f32[128,128]{1,0:T(8,128)S(1)}, u32[]{:S(2)}, u32[]{:S(2)}) collective-permute-start(f32[128,128]{1,0:T(8,128)S(1)} %get-tuple-element.97.rest_0_), channel_id=1, source_target_pairs={{0,3},{1,2},{2,1},{3,0},{4,7},{5,6},{6,5},{7,4},{8,11},{9,10},{10,... | collective-permute-start | bytes 196616 | tf_op jit(solution)/shard_map/ppermute | solution.py:488
  98.7 2.1 %collective-permute-start.11 = (f32[128,128]{1,0:T(8,128)S(1)}, f32[128,128]{1,0:T(8,128)S(1)}, u32[]{:S(2)}, u32[]{:S(2)}) collective-permute-start(f32[128,128]{1,0:T(8,128)S(1)} %get-tuple-element.97.rest_0_), channel_id=1, source_target_pairs={{0,2},{1,3},{2,0},{3,1},{4,6},{5,7},{6,4},{7,5},{8,10},{9,11},{10,... | collective-permute-start | bytes 196616 | tf_op jit(solution)/shard_map/ppermute | solution.py:488
  100.8 0.5 collective-permute-start.10
  101.3 1.3 %energy.1 = f32[16,48,256]{2,1,0:T(8,128)} custom-call(f32[8,272,128]{2,1,0:T(8,128)S(1)} %get-tuple-element.96.e_ref), custom_call_target="tpu_custom_call" | custom-call | flops 1000000 | bytes 1000000 | tf_op jit(solution)/shard_map/energy/pallas_call | solution.py:33
  102.6 0.0 collective-permute-done.12.rest_3_
  102.6 1.8 %collective-permute-done.11.rest_2_ = f32[128,128]{1,0:T(8,128)S(1)} collective-permute-done((f32[128,128]{1,0:T(8,128)S(1)}, f32[128,128]{1,0:T(8,128)S(1)}, u32[]{:S(2)}, u32[]{:S(2)}) %collective-permute-start.11) | collective-permute-done | bytes 65568 | tf_op jit(solution)/shard_map/ppermute | solution.py:488
  104.5 0.6 collective-permute-done.10.rest_1_
  105.1 0.8 material.5
  (5 shorter events, 0.0 us)
Async XLA Ops:
  0.6 4.8 %copy-start.3 = (f32[48,256]{1,0:T(8,128)S(1)}, f32[48,256]{1,0:T(8,128)}, u32[]{:S(2)}) copy-start(f32[48,256]{1,0:T(8,128)} %material.4) | copy-start | bytes 147460
  0.6 4.8 %copy-start = (f32[16,48,256]{2,1,0:T(8,128)S(1)}, f32[16,48,256]{2,1,0:T(8,128)}, u32[]{:S(2)}) copy-start(f32[16,48,256]{2,1,0:T(8,128)} %old.3) | copy-start | bytes 2359300
  0.7 4.8 %copy-start.1 = (bf16[16,48,256]{2,1,0:T(8,128)(2,1)S(1)}, bf16[16,48,256]{2,1,0:T(8,128)(2,1)}, u32[]{:S(2)}) copy-start(bf16[16,48,256]{2,1,0:T(8,128)(2,1)} %opacity.3) | copy-start | bytes 1179652
  0.7 4.8 %copy-start.2 = (f32[48,256]{1,0:T(8,128)S(1)}, f32[48,256]{1,0:T(8,128)}, u32[]{:S(2)}) copy-start(f32[48,256]{1,0:T(8,128)} %density.3) | copy-start | bytes 147460
  3.5 4.9 %copy-start.4 = (f32[16]{0:T(128)S(1)}, f32[16]{0:T(128)}, u32[]{:S(2)}) copy-start(f32[16]{0:T(128)} %weights.7) | copy-start | bytes 196
  3.5 1.9 %collective-permute-start = (f32[35,8,256]{2,1,0:T(8,128)}, f32[35,8,256]{2,1,0:T(8,128)S(1)}, u32[]{:S(2)}, u32[]{:S(2)}) collective-permute-start(f32[35,8,256]{2,1,0:T(8,128)} %get-tuple-element.51), channel_id=1, source_target_pairs={{0,16},{16,0},{32,48},{48,32},{64,80},{80,64},{96,112},{112,96},{1... | collective-permute-start | bytes 860168 | tf_op jit(solution)/shard_map/ppermute | solution.py:493
  3.6 1.8 %collective-permute-start.1 = (f32[35,8,256]{2,1,0:T(8,128)}, f32[35,8,256]{2,1,0:T(8,128)S(1)}, u32[]{:S(2)}, u32[]{:S(2)}) collective-permute-start(f32[35,8,256]{2,1,0:T(8,128)} %get-tuple-element.52), channel_id=1, source_target_pairs={{16,32},{48,64},{80,96},{112,128},{144,160},{176,192},{208,224},{3... | collective-permute-start | bytes 860168 | tf_op jit(solution)/shard_map/ppermute | solution.py:495
  6.1 7.3 %collective-permute-start.2 = (f32[18,8,128]{2,1,0:T(8,128)S(1)}, f32[18,8,128]{2,1,0:T(8,128)S(1)}, u32[]{:S(2)}, u32[]{:S(2)}) collective-permute-start(f32[18,8,128]{2,1,0:T(8,128)S(1)} %get-tuple-element.53), channel_id=1, source_target_pairs={{0,4},{4,0},{8,12},{12,8},{1,5},{5,1},{9,13},{13,9},{2,6},{6,2},{1... | collective-permute-start | bytes 221192 | tf_op jit(solution)/shard_map/ppermute | solution.py:493
  7.7 5.8 %collective-permute-start.3 = (f32[18,8,128]{2,1,0:T(8,128)S(1)}, f32[18,8,128]{2,1,0:T(8,128)S(1)}, u32[]{:S(2)}, u32[]{:S(2)}) collective-permute-start(f32[18,8,128]{2,1,0:T(8,128)S(1)} %get-tuple-element.54), channel_id=1, source_target_pairs={{4,8},{8,4},{5,9},{9,5},{6,10},{10,6},{7,11},{11,7},{20,24},{24,20... | collective-permute-start | bytes 221192 | tf_op jit(solution)/shard_map/ppermute | solution.py:495
  44.8 4.6 %copy-start.5 = (f32[48]{0:T(128)S(1)}, f32[48]{0:T(128)}, u32[]{:S(2)}) copy-start(f32[48]{0:T(128)} %flux.3) | copy-start | bytes 580
  45.3 6.8 %collective-permute-start.6 = (f32[2,136,128]{2,1,0:T(8,128)S(1)}, f32[2,136,128]{2,1,0:T(8,128)S(1)}, u32[]{:S(2)}, u32[]{:S(2)}) collective-permute-start(f32[2,136,128]{2,1,0:T(8,128)S(1)} %get-tuple-element.81.rest_0_), channel_id=1, source_target_pairs={{0,3},{1,2},{2,1},{3,0},{4,7},{5,6},{6,5},{7,4},{8,11},{9,10},{10,... | collective-permute-start | bytes 417800 | tf_op jit(solution)/shard_map/ppermute | solution.py:488
  46.9 7.9 %collective-permute-start.5 = (f32[2,136,128]{2,1,0:T(8,128)S(1)}, f32[2,136,128]{2,1,0:T(8,128)S(1)}, u32[]{:S(2)}, u32[]{:S(2)}) collective-permute-start(f32[2,136,128]{2,1,0:T(8,128)S(1)} %get-tuple-element.81.rest_0_), channel_id=1, source_target_pairs={{0,2},{1,3},{2,0},{3,1},{4,6},{5,7},{6,4},{7,5},{8,10},{9,11},{10,... | collective-permute-start | bytes 417800 | tf_op jit(solution)/shard_map/ppermute | solution.py:488
  47.9 7.4 %collective-permute-start.4 = (f32[2,136,128]{2,1,0:T(8,128)S(1)}, f32[2,136,128]{2,1,0:T(8,128)S(1)}, u32[]{:S(2)}, u32[]{:S(2)}) collective-permute-start(f32[2,136,128]{2,1,0:T(8,128)S(1)} %get-tuple-element.81.rest_0_), channel_id=1, source_target_pairs={{0,1},{1,0},{2,3},{3,2},{4,5},{5,4},{6,7},{7,6},{8,9},{9,8},{10,11... | collective-permute-start | bytes 417800 | tf_op jit(solution)/shard_map/ppermute | solution.py:488
  72.4 4.4 %collective-permute-start.9 = (f32[1,136,128]{2,1,0:T(8,128)S(1)}, f32[1,136,128]{2,1,0:T(8,128)S(1)}, u32[]{:S(2)}, u32[]{:S(2)}) collective-permute-start(f32[1,136,128]{2,1,0:T(8,128)S(1)} %get-tuple-element.91.rest_0_), channel_id=1, source_target_pairs={{0,3},{1,2},{2,1},{3,0},{4,7},{5,6},{6,5},{7,4},{8,11},{9,10},{10,... | collective-permute-start | bytes 208904 | tf_op jit(solution)/shard_map/ppermute | solution.py:488
  74.0 5.9 %collective-permute-start.8 = (f32[1,136,128]{2,1,0:T(8,128)S(1)}, f32[1,136,128]{2,1,0:T(8,128)S(1)}, u32[]{:S(2)}, u32[]{:S(2)}) collective-permute-start(f32[1,136,128]{2,1,0:T(8,128)S(1)} %get-tuple-element.91.rest_0_), channel_id=1, source_target_pairs={{0,2},{1,3},{2,0},{3,1},{4,6},{5,7},{6,4},{7,5},{8,10},{9,11},{10,... | collective-permute-start | bytes 208904 | tf_op jit(solution)/shard_map/ppermute | solution.py:488
  75.9 4.3 %collective-permute-start.7 = (f32[1,136,128]{2,1,0:T(8,128)S(1)}, f32[1,136,128]{2,1,0:T(8,128)S(1)}, u32[]{:S(2)}, u32[]{:S(2)}) collective-permute-start(f32[1,136,128]{2,1,0:T(8,128)S(1)} %get-tuple-element.91.rest_0_), channel_id=1, source_target_pairs={{0,1},{1,0},{2,3},{3,2},{4,5},{5,4},{6,7},{7,6},{8,9},{9,8},{10,11... | collective-permute-start | bytes 208904 | tf_op jit(solution)/shard_map/ppermute | solution.py:488
  97.2 5.4 %collective-permute-start.12 = (f32[128,128]{1,0:T(8,128)S(1)}, f32[128,128]{1,0:T(8,128)S(1)}, u32[]{:S(2)}, u32[]{:S(2)}) collective-permute-start(f32[128,128]{1,0:T(8,128)S(1)} %get-tuple-element.97.rest_0_), channel_id=1, source_target_pairs={{0,3},{1,2},{2,1},{3,0},{4,7},{5,6},{6,5},{7,4},{8,11},{9,10},{10,... | collective-permute-start | bytes 196616 | tf_op jit(solution)/shard_map/ppermute | solution.py:488
  98.7 5.8 %collective-permute-start.11 = (f32[128,128]{1,0:T(8,128)S(1)}, f32[128,128]{1,0:T(8,128)S(1)}, u32[]{:S(2)}, u32[]{:S(2)}) collective-permute-start(f32[128,128]{1,0:T(8,128)S(1)} %get-tuple-element.97.rest_0_), channel_id=1, source_target_pairs={{0,2},{1,3},{2,0},{3,1},{4,6},{5,7},{6,4},{7,5},{8,10},{9,11},{10,... | collective-permute-start | bytes 196616 | tf_op jit(solution)/shard_map/ppermute | solution.py:488
  100.8 4.3 %collective-permute-start.10 = (f32[128,128]{1,0:T(8,128)S(1)}, f32[128,128]{1,0:T(8,128)S(1)}, u32[]{:S(2)}, u32[]{:S(2)}) collective-permute-start(f32[128,128]{1,0:T(8,128)S(1)} %get-tuple-element.97.rest_0_), channel_id=1, source_target_pairs={{0,1},{1,0},{2,3},{3,2},{4,5},{5,4},{6,7},{7,6},{8,9},{9,8},{10,11... | collective-permute-start | bytes 196616 | tf_op jit(solution)/shard_map/ppermute | solution.py:488

commit v6 on v5

--- a/solution.py
+++ b/solution.py
@@ -60,11 +60,11 @@
     return even, jnp.where(even, inner, outer), jnp.where(even, outer, inner)
 
 
-def pack_rows_kernel(groups, rows, flux, opacity, old, density, material, first, second, *scratch):
+def pack_rows_kernel(groups, rows, flux_in, opacity, old, density, material, first, second, *scratch):
     even, lo_first, lo_second = partner("radius", rows - HALO, 0)
-    sems = scratch[-1]
+    flux, sems = scratch[-2:]
     sides = ((first, lo_first, even), (second, lo_second, jnp.logical_not(even)))
-    copies = []
+    copies = [pltpu.make_async_copy(flux_in, flux, sems.at[8])]
     for side, (_, lo, at_end) in enumerate(sides):
         op_buf, old_buf, dens_buf, mat_buf = scratch[4 * side : 4 * side + 4]
         lo = pl.multiple_of(lo, HALO)
@@ -265,15 +265,18 @@
         )
 
 
-def inner_kernel(
-    groups, cols, weights, a_ref, e_ref, dens_ref, mat_ref,
-    fr_ref, fp_ref, r_ref, q_ref, t_ref, emit, mom, inv,
-):
+def inner_kernel(groups, cols, half, weights, a_ref, e_ref, dens_ref, mat_ref, *rest):
     pairs = groups // 2
+    if half == 0:
+        edge, fr_ref, fp_ref, r_ref, q_ref, t_ref, emit, mom, edge_out, inv = rest
+        edge_out[...] = edge[...]
+        emit[...] = jnp.zeros(emit.shape, jnp.float32)
+    else:
+        fr_ref, fp_ref, r_ref, q_ref, t_ref, emit, mom, inv = rest[7:]
+    bounds = (0, pairs // 2) if half == 0 else (pairs // 2, pairs)
     span = (HALO, HALO + cols)
     parts = [(lo + HALO, hi + HALO) for lo, hi in pieces(cols)]
     own = (2 * HALO, cols)
-    emit[...] = jnp.zeros(emit.shape, jnp.float32)
 
     def one(p, carry):
         w = weight_of(weights, p)
@@ -283,7 +286,7 @@
         krylov(p, pairs, parts, span, own, a_ref, fr_ref, fp_ref, r_ref, q_ref, t_ref, mom)
         return carry
 
-    lax.fori_loop(0, pairs, one, 0, unroll=2)
+    lax.fori_loop(*bounds, one, 0, unroll=2)
 
 
 def frame_kernel(groups, rows, cols, weights, got_first, got_second, emit, old_mom, *rest):
@@ -488,12 +491,13 @@
     return [part] + [lax.ppermute(part, axis, [(i, i ^ s) for i in range(count)]) for s in range(1, count)]
 
 
-def exchanged(first, second, axis):
-    count = lax.axis_size(axis)
-    got_first = lax.ppermute(first, axis, [(i, i ^ 1) for i in range(count)])
-    links = [(i, i + 1) for i in range(1, count - 1, 2)]
-    got_second = lax.ppermute(second, axis, links + [(j, i) for i, j in links])
-    return got_first, got_second
+def pair_up(first, axis):
+    return lax.ppermute(first, axis, [(i, i ^ 1) for i in range(lax.axis_size(axis))])
+
+
+def pair_across(second, axis):
+    links = [(i, i + 1) for i in range(1, lax.axis_size(axis) - 1, 2)]
+    return lax.ppermute(second, axis, links + [(j, i) for i, j in links])
 
 
 def per_device(density, opacity, radiation_old, material_old, weights, stellar_flux):
@@ -506,6 +510,7 @@
     planes = 2 * groups + 3
     big, flat, core = (pairs, tall, LANES), (tall, LANES), (cols, LANES)
     line = (devices, LANES)
+    edge = (2 * pairs + 2, HALO, LANES)
     vmem = lambda shape: pltpu.VMEM(shape, jnp.float32)
 
     strips = [
@@ -517,28 +522,41 @@
     first, second = call(
         functools.partial(pack_rows_kernel, groups, rows),
         [(planes, HALO, cols)] * 2,
-        (stellar_flux, opacity, radiation_old, density, material_old),
-        [sspec()] + [hspec()] * 4,
-        scratch=strips * 2 + [pltpu.SemaphoreType.DMA((8,))],
+        tuple(
+            pltpu.with_memory_space_constraint(v, pltpu.HBM)
+            for v in (stellar_flux, opacity, radiation_old, density, material_old)
+        ),
+        [hspec()] * 5,
+        scratch=strips * 2 + [pltpu.SMEM((rows,), jnp.float32), pltpu.SemaphoreType.DMA((9,))],
         name="pack_rows",
-        limit=60 * 1024 * 1024,
-    )
-    first, second = exchanged(first, second, "radius")
+        limit=20 * 1024 * 1024,
+    )
+    first, second = pair_up(first, "radius"), pair_across(second, "radius")
     a, e, dens, mat, flux_lanes, first, second = call(
         functools.partial(turn_kernel, groups, rows, cols),
-        [big] * 2 + [flat, flat, (HALO, LANES)] + [(2 * pairs + 2, HALO, LANES)] * 2,
+        [big] * 2 + [flat, flat, (HALO, LANES), edge, edge],
         (opacity, radiation_old, density, material_old, first, second),
         [vspec()] * 6,
         name="turn",
     )
-    first, second = exchanged(first, second, "polar")
+    first = pair_up(first, "polar")
+    *state, second = call(
+        functools.partial(inner_kernel, groups, cols, 0),
+        [big] * 5 + [flat, (4 * pairs, LANES), edge],
+        (weights, a, e, dens, mat, second),
+        [sspec()] + [vspec()] * 5,
+        scratch=[vmem(flat)],
+        name="inner_first",
+    )
+    second = pair_across(second, "polar")
     fr, fp, r, q, t, emit, mom = call(
-        functools.partial(inner_kernel, groups, cols),
+        functools.partial(inner_kernel, groups, cols, 1),
         [big] * 5 + [flat, (4 * pairs, LANES)],
-        (weights, a, e, dens, mat),
-        [sspec()] + [vspec()] * 4,
+        (weights, a, e, dens, mat, *state),
+        [sspec()] + [vspec()] * 11,
         scratch=[vmem(flat)],
-        name="inner",
+        name="inner_second",
+        aliases={5 + k: k for k in range(7)},
     )
     a, e, fr, fp, r, q, t, dens, mat, emit, out = call(
         functools.partial(frame_kernel, groups, rows, cols),

time: 106 us -> 106 us (level)
  blocking collectives: 57.1 us -> 58.4 us
    all_to_all x3, blocking collectives: 57.1 us -> 58.4 us  [per_device(): gathered = lax.all_to_all(out, ('radius', 'polar'), 0, 0, tiled=True)]
    pallas_call x12 -> x13, Pallas kernels: 21.1 us -> 20.2 us  [call(): pl.pallas_call(kernel, out_shape=[jax.ShapeDtypeStruct(s, jnp.float32) fo...]
where the time goes in v6:
time: 106 us
  blocking collectives  58.4 us (55%)
  Pallas kernels  20.2 us (19%)
  starting transfers between devices  15.5 us (15%)
  waiting for transfers between devices  11.1 us (10%)
    all_to_all x3, blocking collectives, per_device(): gathered = lax.all_to_all(out, ('radius', 'polar'), 0, 0, tiled=True)  58.4 us
    pallas_call x13, Pallas kernels, call(): pl.pallas_call(kernel, out_shape=[jax.ShapeDtypeStruct(s, jnp.float32) fo...  20.2 us
    ppermute x9, starting transfers between devices, spread(): lax.ppermute(part, axis, [(i, i ^ s) for i in range(count)])  12.5 us
    ppermute x9, waiting for transfers between devices, spread(): lax.ppermute(part, axis, [(i, i ^ s) for i in range(count)])  10.2 us
  transfers between devices with their start and end apart: 13, of which 9 were waited for; matrix products, arithmetic and copies ran while one was open for 0% of the time, Pallas kernels for 8%

profile of v6, /device:TPU:8, one launch (start us, length us, event | category | flops | bytes accessed | tf_op | source)
XLA Modules:
  0.0 106.0 jit_solution(5019762828566843840)
XLA Ops:
  0.6 0.0 copy-start.3
  0.6 0.0 copy-start
  0.7 0.0 copy-start.1
  0.7 1.4 %pack_rows.1 = (f32[35,8,256]{2,1,0:T(8,128)S(1)}, f32[35,8,256]{2,1,0:T(8,128)S(1)}) custom-call(f32[48]{0:T(128)} %flux.1, bf16[16,48,256]{2,1,0:T(8,128)(2,1)} %opacity.3, f32[16,48,256]{2,1,0:T(8,128)} %old.3, f32[48,256]{1,0:T(8,128)} %density.3, f32[48,256]{1,0:T(8,128)} %material.4), custom_call_target="tpu_custom_call" | custom-call | flops 1000000 | bytes 1000000 | tf_op jit(solution)/shard_map/pack_rows/pallas_call | solution.py:33
  2.0 0.0 copy-start.4
  2.1 0.1 collective-permute-start
  2.2 0.7 collective-permute-start.1
  2.8 0.9 collective-permute-done.got_first
  3.7 0.0 collective-permute-done.1.got_second
  3.7 0.0 copy-done.3
  3.7 0.7 turn.1
  4.4 1.6 %collective-permute-start.2 = (f32[18,8,128]{2,1,0:T(8,128)S(1)}, f32[18,8,128]{2,1,0:T(8,128)S(1)}, u32[]{:S(2)}, u32[]{:S(2)}) collective-permute-start(f32[18,8,128]{2,1,0:T(8,128)S(1)} %get-tuple-element.61), channel_id=1, source_target_pairs={{0,4},{4,0},{8,12},{12,8},{1,5},{5,1},{9,13},{13,9},{2,6},{6,2},{1... | collective-permute-start | bytes 221192 | tf_op jit(solution)/shard_map/ppermute | solution.py:495
  6.0 2.8 %inner_first.1 = (f32[8,272,128]{2,1,0:T(8,128)S(1)}, f32[8,272,128]{2,1,0:T(8,128)S(1)}, f32[8,272,128]{2,1,0:T(8,128)S(1)}, f32[8,272,128]{2,1,0:T(8,128)S(1)}...) custom-call(f32[16]{0:T(128)S(1)} %copy-done.4, ...), custom_call_target="tpu_custom_call" | custom-call | flops 1000000 | bytes 1000000 | tf_op jit(solution)/shard_map/inner_first/pallas_call | solution.py:33
  8.8 0.7 collective-permute-start.3
  9.5 2.8 %inner_second.1 = (f32[8,272,128]{2,1,0:T(8,128)S(1)}, f32[8,272,128]{2,1,0:T(8,128)S(1)}, f32[8,272,128]{2,1,0:T(8,128)S(1)}, f32[8,272,128]{2,1,0:T(8,128)S(1)...) custom-call(f32[16]{0:T(128)S(1)} %copy-done.4, ...), custom_call_target="tpu_custom_call", output_to_operand_aliasing={{0}: (5, {}), {1}: (6, {}), {2}: (7, {}), {3}: (8, {}), {4}... | custom-call | flops 1000000 | bytes 1000000 | tf_op jit(solution)/shard_map/inner_second/pallas_call | solution.py:33
  12.3 0.0 collective-permute-done.2.got_first
  12.3 0.0 collective-permute-done.3.got_second
  12.4 1.4 %frame.1 = (f32[8,272,128]{2,1,0:T(8,128)S(1)}, f32[8,272,128]{2,1,0:T(8,128)S(1)}, f32[8,272,128]{2,1,0:T(8,128)S(1)}, f32[8,272,128]{2,1,0:T(8,128)S(1)}, f32[...) custom-call(f32[16]{0:T(128)S(1)} %copy-done.4, ...), custom_call_target="tpu_custom_call", output_to_operand_aliasing={{0}: (5, {}), {1}: (6, {}), {2}: (7, {}), {3}: (8, {}), {4}... | custom-call | flops 1000000 | bytes 1000000 | tf_op jit(solution)/shard_map/frame/pallas_call | solution.py:33
  13.8 31.4 %all_to_all.33 = f32[64,1,128]{2,1,0:T(1,128)S(1)} all-to-all(f32[64,1,128]{2,1,0:T(1,128)S(1)} %bitcast.16), channel_id=1, replica_groups=mesh['radius'=16,'polar'=4,'group'=4] {'radius','polar'}, dimensions={0} | all-to-all | bytes 65536 | tf_op jit(solution)/shard_map/all_to_all | solution.py:572
  45.2 0.5 update.2
  45.6 1.6 %collective-permute-start.6 = (f32[2,136,128]{2,1,0:T(8,128)S(1)}, f32[2,136,128]{2,1,0:T(8,128)S(1)}, u32[]{:S(2)}, u32[]{:S(2)}) collective-permute-start(f32[2,136,128]{2,1,0:T(8,128)S(1)} %get-tuple-element.97.rest_0_), channel_id=1, source_target_pairs={{0,3},{1,2},{2,1},{3,0},{4,7},{5,6},{6,5},{7,4},{8,11},{9,10},{10,... | collective-permute-start | bytes 417800 | tf_op jit(solution)/shard_map/ppermute | solution.py:491
  47.3 0.9 collective-permute-start.5
  48.2 1.6 %collective-permute-start.4 = (f32[2,136,128]{2,1,0:T(8,128)S(1)}, f32[2,136,128]{2,1,0:T(8,128)S(1)}, u32[]{:S(2)}, u32[]{:S(2)}) collective-permute-start(f32[2,136,128]{2,1,0:T(8,128)S(1)} %get-tuple-element.97.rest_0_), channel_id=1, source_target_pairs={{0,1},{1,0},{2,3},{3,2},{4,5},{5,4},{6,7},{7,6},{8,9},{9,8},{10,11... | collective-permute-start | bytes 417800 | tf_op jit(solution)/shard_map/ppermute | solution.py:491
  49.8 0.0 copy-done.5
  49.8 1.7 %heating.1 = (f32[48,256]{1,0:T(8,128)}, f32[272,128]{1,0:T(8,128)S(1)}) custom-call(f32[48]{0:T(128)S(1)} %copy-done.5, f32[64,128]{1,0:T(8,128)S(1)} %bitcast.13, f32[272,128]{1,0:T(8,128)S(1)} %get-tuple-element.93.dens_ref.cap_in, f32[272,128]{1,0:T(8,128)S(1)} %get-tuple-element.94.mat_ref, f32[8,128]{1,0:T(8,128)S(1)} %get-tuple-element.95.flux_ref), custom_call_target="tpu_custom_call" | custom-call | flops 1000000 | bytes 1000000 | tf_op jit(solution)/shard_map/heating/pallas_call | solution.py:33
  51.5 0.9 collective-permute-done.6.rest_3_
  52.4 2.8 %collective-permute-done.5.rest_2_ = f32[2,136,128]{2,1,0:T(8,128)S(1)} collective-permute-done((f32[2,136,128]{2,1,0:T(8,128)S(1)}, f32[2,136,128]{2,1,0:T(8,128)S(1)}, u32[]{:S(2)}, u32[]{:S(2)}) %collective-permute-start.5) | collective-permute-done | bytes 139296 | tf_op jit(solution)/shard_map/ppermute | solution.py:491
  55.2 0.5 collective-permute-done.4.rest_1_
  55.7 3.1 %next.2 = (f32[8,272,128]{2,1,0:T(8,128)S(1)}, f32[8,272,128]{2,1,0:T(8,128)S(1)}, f32[64,128]{1,0:T(8,128)S(1)}, f32[8,272,128]{2,1,0:T(8,128)S(1)}, f32[272,128]{1,0:T(8,128)S(1)}, /*index=5*/f32[272,128]{1,0:T(8,128)S(1)}) custom-call(f32[16]{0:T(128)S(1)} %copy-done.4, f32[8,128]{1,0:T(8,128)S(1)} %get-tuple-element.88.c1_ref, ...), custom_call_target="tpu_custom_call" | custom-call | flops 1000000 | bytes 1000000 | tf_op jit(solution)/shard_map/next/pallas_call | solution.py:33
  58.8 13.5 %all_to_all.34 = f32[64,1,128]{2,1,0:T(1,128)S(1)} all-to-all(f32[64,1,128]{2,1,0:T(1,128)S(1)} %bitcast.17), channel_id=1, replica_groups=mesh['radius'=16,'polar'=4,'group'=4] {'radius','polar'}, dimensions={0} | all-to-all | bytes 65536 | tf_op jit(solution)/shard_map/all_to_all | solution.py:572
  72.3 0.5 update.3
  72.8 1.6 %collective-permute-start.9 = (f32[1,136,128]{2,1,0:T(8,128)S(1)}, f32[1,136,128]{2,1,0:T(8,128)S(1)}, u32[]{:S(2)}, u32[]{:S(2)}) collective-permute-start(f32[1,136,128]{2,1,0:T(8,128)S(1)} %get-tuple-element.107.rest_0_), channel_id=1, source_target_pairs={{0,3},{1,2},{2,1},{3,0},{4,7},{5,6},{6,5},{7,4},{8,11},{9,10},{10,... | collective-permute-start | bytes 208904 | tf_op jit(solution)/shard_map/ppermute | solution.py:491
  74.4 1.9 %collective-permute-start.8 = (f32[1,136,128]{2,1,0:T(8,128)S(1)}, f32[1,136,128]{2,1,0:T(8,128)S(1)}, u32[]{:S(2)}, u32[]{:S(2)}) collective-permute-start(f32[1,136,128]{2,1,0:T(8,128)S(1)} %get-tuple-element.107.rest_0_), channel_id=1, source_target_pairs={{0,2},{1,3},{2,0},{3,1},{4,6},{5,7},{6,4},{7,5},{8,10},{9,11},{10,... | collective-permute-start | bytes 208904 | tf_op jit(solution)/shard_map/ppermute | solution.py:491
  76.3 0.7 collective-permute-start.7
  76.9 0.2 collective-permute-done.9.rest_3_
  77.1 3.1 %collective-permute-done.8.rest_2_ = f32[1,136,128]{2,1,0:T(8,128)S(1)} collective-permute-done((f32[1,136,128]{2,1,0:T(8,128)S(1)}, f32[1,136,128]{2,1,0:T(8,128)S(1)}, u32[]{:S(2)}, u32[]{:S(2)}) %collective-permute-start.8) | collective-permute-done | bytes 69664 | tf_op jit(solution)/shard_map/ppermute | solution.py:491
  80.3 0.3 collective-permute-done.7.rest_1_
  80.6 2.9 %next.3 = (f32[8,272,128]{2,1,0:T(8,128)S(1)}, f32[8,272,128]{2,1,0:T(8,128)S(1)}, f32[64,128]{1,0:T(8,128)S(1)}) custom-call(f32[16]{0:T(128)S(1)} %copy-done.4, f32[8,128]{1,0:T(8,128)S(1)} %get-tuple-element.102.c1_ref, f32[8,128]{1,0:T(8,128)S(1)} %get-tuple-element.103.c2_ref, f32[8,272,128]{2,1,0:T(8,128)S(1)} %get-tuple-element.83.a_ref, ...), custom_call_target="tpu_custom_call" | custom-call | flops 1000000 | bytes 1000000 | tf_op jit(solution)/shard_map/next/pallas_call | solution.py:33
  83.5 13.5 %all_to_all.35 = f32[64,1,128]{2,1,0:T(1,128)S(1)} all-to-all(f32[64,1,128]{2,1,0:T(1,128)S(1)} %bitcast.18), channel_id=1, replica_groups=mesh['radius'=16,'polar'=4,'group'=4] {'radius','polar'}, dimensions={0} | all-to-all | bytes 65536 | tf_op jit(solution)/shard_map/all_to_all | solution.py:572
  97.0 0.4 last_update.1
  97.4 1.5 %collective-permute-start.12 = (f32[128,128]{1,0:T(8,128)S(1)}, f32[128,128]{1,0:T(8,128)S(1)}, u32[]{:S(2)}, u32[]{:S(2)}) collective-permute-start(f32[128,128]{1,0:T(8,128)S(1)} %get-tuple-element.113.rest_0_), channel_id=1, source_target_pairs={{0,3},{1,2},{2,1},{3,0},{4,7},{5,6},{6,5},{7,4},{8,11},{9,10},{10,... | collective-permute-start | bytes 196616 | tf_op jit(solution)/shard_map/ppermute | solution.py:491
  98.9 2.1 %collective-permute-start.11 = (f32[128,128]{1,0:T(8,128)S(1)}, f32[128,128]{1,0:T(8,128)S(1)}, u32[]{:S(2)}, u32[]{:S(2)}) collective-permute-start(f32[128,128]{1,0:T(8,128)S(1)} %get-tuple-element.113.rest_0_), channel_id=1, source_target_pairs={{0,2},{1,3},{2,0},{3,1},{4,6},{5,7},{6,4},{7,5},{8,10},{9,11},{10,... | collective-permute-start | bytes 196616 | tf_op jit(solution)/shard_map/ppermute | solution.py:491
  101.0 0.5 collective-permute-start.10
  101.5 1.3 %energy.1 = f32[16,48,256]{2,1,0:T(8,128)} custom-call(f32[8,272,128]{2,1,0:T(8,128)S(1)} %get-tuple-element.112.e_ref), custom_call_target="tpu_custom_call" | custom-call | flops 1000000 | bytes 1000000 | tf_op jit(solution)/shard_map/energy/pallas_call | solution.py:33
  102.8 0.0 collective-permute-done.12.rest_3_
  102.8 1.8 %collective-permute-done.11.rest_2_ = f32[128,128]{1,0:T(8,128)S(1)} collective-permute-done((f32[128,128]{1,0:T(8,128)S(1)}, f32[128,128]{1,0:T(8,128)S(1)}, u32[]{:S(2)}, u32[]{:S(2)}) %collective-permute-start.11) | collective-permute-done | bytes 65568 | tf_op jit(solution)/shard_map/ppermute | solution.py:491
  104.7 0.6 collective-permute-done.10.rest_1_
  105.3 0.8 material.5
  (6 shorter events, 0.0 us)
Async XLA Ops:
  0.6 3.1 %copy-start.3 = (f32[48,256]{1,0:T(8,128)S(1)}, f32[48,256]{1,0:T(8,128)}, u32[]{:S(2)}) copy-start(f32[48,256]{1,0:T(8,128)} %material.4) | copy-start | bytes 147460
  0.6 3.1 %copy-start = (f32[16,48,256]{2,1,0:T(8,128)S(1)}, f32[16,48,256]{2,1,0:T(8,128)}, u32[]{:S(2)}) copy-start(f32[16,48,256]{2,1,0:T(8,128)} %old.3) | copy-start | bytes 2359300
  0.7 3.1 %copy-start.1 = (bf16[16,48,256]{2,1,0:T(8,128)(2,1)S(1)}, bf16[16,48,256]{2,1,0:T(8,128)(2,1)}, u32[]{:S(2)}) copy-start(bf16[16,48,256]{2,1,0:T(8,128)(2,1)} %opacity.3) | copy-start | bytes 1179652
  0.7 3.1 %copy-start.2 = (f32[48,256]{1,0:T(8,128)S(1)}, f32[48,256]{1,0:T(8,128)}, u32[]{:S(2)}) copy-start(f32[48,256]{1,0:T(8,128)} %density.3) | copy-start | bytes 147460
  2.0 4.0 %copy-start.4 = (f32[16]{0:T(128)S(1)}, f32[16]{0:T(128)}, u32[]{:S(2)}) copy-start(f32[16]{0:T(128)} %weights.9) | copy-start | bytes 196
  2.1 1.7 %collective-permute-start = (f32[35,8,256]{2,1,0:T(8,128)S(1)}, f32[35,8,256]{2,1,0:T(8,128)S(1)}, u32[]{:S(2)}, u32[]{:S(2)}) collective-permute-start(f32[35,8,256]{2,1,0:T(8,128)S(1)} %get-tuple-element.59), channel_id=1, source_target_pairs={{0,16},{16,0},{32,48},{48,32},{64,80},{80,64},{96,112},{112,96},{1... | collective-permute-start | bytes 860168 | tf_op jit(solution)/shard_map/ppermute | solution.py:495
  2.2 1.6 %collective-permute-start.1 = (f32[35,8,256]{2,1,0:T(8,128)S(1)}, f32[35,8,256]{2,1,0:T(8,128)S(1)}, u32[]{:S(2)}, u32[]{:S(2)}) collective-permute-start(f32[35,8,256]{2,1,0:T(8,128)S(1)} %get-tuple-element.60), channel_id=1, source_target_pairs={{16,32},{48,64},{80,96},{112,128},{144,160},{176,192},{208,224},{3... | collective-permute-start | bytes 860168 | tf_op jit(solution)/shard_map/ppermute | solution.py:500
  4.4 7.9 %collective-permute-start.2 = (f32[18,8,128]{2,1,0:T(8,128)S(1)}, f32[18,8,128]{2,1,0:T(8,128)S(1)}, u32[]{:S(2)}, u32[]{:S(2)}) collective-permute-start(f32[18,8,128]{2,1,0:T(8,128)S(1)} %get-tuple-element.61), channel_id=1, source_target_pairs={{0,4},{4,0},{8,12},{12,8},{1,5},{5,1},{9,13},{13,9},{2,6},{6,2},{1... | collective-permute-start | bytes 221192 | tf_op jit(solution)/shard_map/ppermute | solution.py:495
  8.8 3.5 %collective-permute-start.3 = (f32[18,8,128]{2,1,0:T(8,128)S(1)}, f32[18,8,128]{2,1,0:T(8,128)S(1)}, u32[]{:S(2)}, u32[]{:S(2)}) collective-permute-start(f32[18,8,128]{2,1,0:T(8,128)S(1)} %get-tuple-element.67), channel_id=1, source_target_pairs={{4,8},{8,4},{5,9},{9,5},{6,10},{10,6},{7,11},{11,7},{20,24},{24,20... | collective-permute-start | bytes 221192 | tf_op jit(solution)/shard_map/ppermute | solution.py:500
  45.2 4.6 %copy-start.5 = (f32[48]{0:T(128)S(1)}, f32[48]{0:T(128)}, u32[]{:S(2)}) copy-start(f32[48]{0:T(128)} %flux.1) | copy-start | bytes 580
  45.6 6.8 %collective-permute-start.6 = (f32[2,136,128]{2,1,0:T(8,128)S(1)}, f32[2,136,128]{2,1,0:T(8,128)S(1)}, u32[]{:S(2)}, u32[]{:S(2)}) collective-permute-start(f32[2,136,128]{2,1,0:T(8,128)S(1)} %get-tuple-element.97.rest_0_), channel_id=1, source_target_pairs={{0,3},{1,2},{2,1},{3,0},{4,7},{5,6},{6,5},{7,4},{8,11},{9,10},{10,... | collective-permute-start | bytes 417800 | tf_op jit(solution)/shard_map/ppermute | solution.py:491
  47.3 7.9 %collective-permute-start.5 = (f32[2,136,128]{2,1,0:T(8,128)S(1)}, f32[2,136,128]{2,1,0:T(8,128)S(1)}, u32[]{:S(2)}, u32[]{:S(2)}) collective-permute-start(f32[2,136,128]{2,1,0:T(8,128)S(1)} %get-tuple-element.97.rest_0_), channel_id=1, source_target_pairs={{0,2},{1,3},{2,0},{3,1},{4,6},{5,7},{6,4},{7,5},{8,10},{9,11},{10,... | collective-permute-start | bytes 417800 | tf_op jit(solution)/shard_map/ppermute | solution.py:491
  48.2 7.4 %collective-permute-start.4 = (f32[2,136,128]{2,1,0:T(8,128)S(1)}, f32[2,136,128]{2,1,0:T(8,128)S(1)}, u32[]{:S(2)}, u32[]{:S(2)}) collective-permute-start(f32[2,136,128]{2,1,0:T(8,128)S(1)} %get-tuple-element.97.rest_0_), channel_id=1, source_target_pairs={{0,1},{1,0},{2,3},{3,2},{4,5},{5,4},{6,7},{7,6},{8,9},{9,8},{10,11... | collective-permute-start | bytes 417800 | tf_op jit(solution)/shard_map/ppermute | solution.py:491
  72.8 4.4 %collective-permute-start.9 = (f32[1,136,128]{2,1,0:T(8,128)S(1)}, f32[1,136,128]{2,1,0:T(8,128)S(1)}, u32[]{:S(2)}, u32[]{:S(2)}) collective-permute-start(f32[1,136,128]{2,1,0:T(8,128)S(1)} %get-tuple-element.107.rest_0_), channel_id=1, source_target_pairs={{0,3},{1,2},{2,1},{3,0},{4,7},{5,6},{6,5},{7,4},{8,11},{9,10},{10,... | collective-permute-start | bytes 208904 | tf_op jit(solution)/shard_map/ppermute | solution.py:491
  74.4 5.9 %collective-permute-start.8 = (f32[1,136,128]{2,1,0:T(8,128)S(1)}, f32[1,136,128]{2,1,0:T(8,128)S(1)}, u32[]{:S(2)}, u32[]{:S(2)}) collective-permute-start(f32[1,136,128]{2,1,0:T(8,128)S(1)} %get-tuple-element.107.rest_0_), channel_id=1, source_target_pairs={{0,2},{1,3},{2,0},{3,1},{4,6},{5,7},{6,4},{7,5},{8,10},{9,11},{10,... | collective-permute-start | bytes 208904 | tf_op jit(solution)/shard_map/ppermute | solution.py:491
  76.3 4.3 %collective-permute-start.7 = (f32[1,136,128]{2,1,0:T(8,128)S(1)}, f32[1,136,128]{2,1,0:T(8,128)S(1)}, u32[]{:S(2)}, u32[]{:S(2)}) collective-permute-start(f32[1,136,128]{2,1,0:T(8,128)S(1)} %get-tuple-element.107.rest_0_), channel_id=1, source_target_pairs={{0,1},{1,0},{2,3},{3,2},{4,5},{5,4},{6,7},{7,6},{8,9},{9,8},{10,11... | collective-permute-start | bytes 208904 | tf_op jit(solution)/shard_map/ppermute | solution.py:491
  97.4 5.4 %collective-permute-start.12 = (f32[128,128]{1,0:T(8,128)S(1)}, f32[128,128]{1,0:T(8,128)S(1)}, u32[]{:S(2)}, u32[]{:S(2)}) collective-permute-start(f32[128,128]{1,0:T(8,128)S(1)} %get-tuple-element.113.rest_0_), channel_id=1, source_target_pairs={{0,3},{1,2},{2,1},{3,0},{4,7},{5,6},{6,5},{7,4},{8,11},{9,10},{10,... | collective-permute-start | bytes 196616 | tf_op jit(solution)/shard_map/ppermute | solution.py:491
  98.9 5.8 %collective-permute-start.11 = (f32[128,128]{1,0:T(8,128)S(1)}, f32[128,128]{1,0:T(8,128)S(1)}, u32[]{:S(2)}, u32[]{:S(2)}) collective-permute-start(f32[128,128]{1,0:T(8,128)S(1)} %get-tuple-element.113.rest_0_), channel_id=1, source_target_pairs={{0,2},{1,3},{2,0},{3,1},{4,6},{5,7},{6,4},{7,5},{8,10},{9,11},{10,... | collective-permute-start | bytes 196616 | tf_op jit(solution)/shard_map/ppermute | solution.py:491
  101.0 4.3 %collective-permute-start.10 = (f32[128,128]{1,0:T(8,128)S(1)}, f32[128,128]{1,0:T(8,128)S(1)}, u32[]{:S(2)}, u32[]{:S(2)}) collective-permute-start(f32[128,128]{1,0:T(8,128)S(1)} %get-tuple-element.113.rest_0_), channel_id=1, source_target_pairs={{0,1},{1,0},{2,3},{3,2},{4,5},{5,4},{6,7},{7,6},{8,9},{9,8},{10,11... | collective-permute-start | bytes 196616 | tf_op jit(solution)/shard_map/ppermute | solution.py:491

commit v7 on v6

--- a/solution.py
+++ b/solution.py
@@ -100,7 +100,7 @@
 
 
 def turn_kernel(
-    groups, rows, cols, opacity, old, density, material, got_first, got_second,
+    groups, rows, cols, opacity, old, density, material, got_second, got_first,
     a_ref, e_ref, dens_ref, mat_ref, flux_ref, to_first, to_second,
 ):
     pairs = groups // 2
@@ -273,7 +273,7 @@
         emit[...] = jnp.zeros(emit.shape, jnp.float32)
     else:
         fr_ref, fp_ref, r_ref, q_ref, t_ref, emit, mom, inv = rest[7:]
-    bounds = (0, pairs // 2) if half == 0 else (pairs // 2, pairs)
+    bounds = (0, pairs // 4) if half == 0 else (pairs // 4, pairs)
     span = (HALO, HALO + cols)
     parts = [(lo + HALO, hi + HALO) for lo, hi in pieces(cols)]
     own = (2 * HALO, cols)
@@ -531,11 +531,12 @@
         name="pack_rows",
         limit=20 * 1024 * 1024,
     )
-    first, second = pair_up(first, "radius"), pair_across(second, "radius")
+    second = pair_across(second, "radius")
+    first = pair_up(first, "radius")
     a, e, dens, mat, flux_lanes, first, second = call(
         functools.partial(turn_kernel, groups, rows, cols),
         [big] * 2 + [flat, flat, (HALO, LANES), edge, edge],
-        (opacity, radiation_old, density, material_old, first, second),
+        (opacity, radiation_old, density, material_old, second, first),
         [vspec()] * 6,
         name="turn",
     )

time: 106 us -> 105 us (level)
  blocking collectives: 58.4 us -> 53.6 us
  starting transfers between devices: 15.5 us -> 18.8 us
    all_to_all x3, blocking collectives: 58.4 us -> 53.6 us  [per_device(): gathered = lax.all_to_all(out, ('radius', 'polar'), 0, 0, tiled=True)]
    ppermute x2, starting transfers between devices: 1.67 us -> 4.93 us  [pair_up(): lax.ppermute(first, axis, [(i, i ^ 1) for i in range(lax.axis_size(axis))])]
where the time goes in v7:
time: 105 us
  blocking collectives  53.6 us (51%)
  Pallas kernels  20.3 us (19%)
  starting transfers between devices  18.8 us (18%)
  waiting for transfers between devices  11.4 us (11%)
    all_to_all x3, blocking collectives, per_device(): gathered = lax.all_to_all(out, ('radius', 'polar'), 0, 0, tiled=True)  53.6 us
    pallas_call x13, Pallas kernels, call(): pl.pallas_call(kernel, out_shape=[jax.ShapeDtypeStruct(s, jnp.float32) fo...  20.3 us
    ppermute x9, starting transfers between devices, spread(): lax.ppermute(part, axis, [(i, i ^ s) for i in range(count)])  12.5 us
    ppermute x9, waiting for transfers between devices, spread(): lax.ppermute(part, axis, [(i, i ^ s) for i in range(count)])  10.2 us
    ppermute x2, starting transfers between devices, pair_up(): lax.ppermute(first, axis, [(i, i ^ 1) for i in range(lax.axis_size(axis))])  4.93 us
  transfers between devices with their start and end apart: 13, of which 9 were waited for; matrix products, arithmetic and copies ran while one was open for 0% of the time, Pallas kernels for 8%

profile of v7, /device:TPU:8, one launch (start us, length us, event | category | flops | bytes accessed | tf_op | source)
XLA Modules:
  0.0 104.8 jit_solution(10520846706100522163)
XLA Ops:
  0.6 0.0 copy-start.3
  0.6 0.0 copy-start
  0.7 0.0 copy-start.1
  0.7 1.4 %pack_rows.1 = (f32[35,8,256]{2,1,0:T(8,128)S(1)}, f32[35,8,256]{2,1,0:T(8,128)S(1)}) custom-call(f32[48]{0:T(128)} %flux.1, bf16[16,48,256]{2,1,0:T(8,128)(2,1)} %opacity.3, f32[16,48,256]{2,1,0:T(8,128)} %old.3, f32[48,256]{1,0:T(8,128)} %density.3, f32[48,256]{1,0:T(8,128)} %material.4), custom_call_target="tpu_custom_call" | custom-call | flops 1000000 | bytes 1000000 | tf_op jit(solution)/shard_map/pack_rows/pallas_call | solution.py:33
  2.0 0.0 copy-start.4
  2.1 0.7 collective-permute-start
  2.7 3.3 %collective-permute-start.1 = (f32[35,8,256]{2,1,0:T(8,128)S(1)}, f32[35,8,256]{2,1,0:T(8,128)S(1)}, u32[]{:S(2)}, u32[]{:S(2)}) collective-permute-start(f32[35,8,256]{2,1,0:T(8,128)S(1)} %get-tuple-element.60), channel_id=1, source_target_pairs={{0,16},{16,0},{32,48},{48,32},{64,80},{80,64},{96,112},{112,96},{1... | collective-permute-start | bytes 860168 | tf_op jit(solution)/shard_map/ppermute | solution.py:495
  6.1 0.0 collective-permute-done.got_second
  6.1 1.2 %collective-permute-done.1.got_first = f32[35,8,256]{2,1,0:T(8,128)S(1)} collective-permute-done((f32[35,8,256]{2,1,0:T(8,128)S(1)}, f32[35,8,256]{2,1,0:T(8,128)S(1)}, u32[]{:S(2)}, u32[]{:S(2)}) %collective-permute-start.1) | collective-permute-done | bytes 286752 | tf_op jit(solution)/shard_map/ppermute | solution.py:495
  7.3 0.0 copy-done
  7.3 0.7 turn.1
  8.0 1.6 %collective-permute-start.2 = (f32[18,8,128]{2,1,0:T(8,128)S(1)}, f32[18,8,128]{2,1,0:T(8,128)S(1)}, u32[]{:S(2)}, u32[]{:S(2)}) collective-permute-start(f32[18,8,128]{2,1,0:T(8,128)S(1)} %get-tuple-element.61), channel_id=1, source_target_pairs={{0,4},{4,0},{8,12},{12,8},{1,5},{5,1},{9,13},{13,9},{2,6},{6,2},{1... | collective-permute-start | bytes 221192 | tf_op jit(solution)/shard_map/ppermute | solution.py:495
  9.6 1.7 %inner_first.1 = (f32[8,272,128]{2,1,0:T(8,128)S(1)}, f32[8,272,128]{2,1,0:T(8,128)S(1)}, f32[8,272,128]{2,1,0:T(8,128)S(1)}, f32[8,272,128]{2,1,0:T(8,128)S(1)}...) custom-call(f32[16]{0:T(128)S(1)} %copy-done.4, ...), custom_call_target="tpu_custom_call" | custom-call | flops 1000000 | bytes 1000000 | tf_op jit(solution)/shard_map/inner_first/pallas_call | solution.py:33
  11.3 0.7 collective-permute-start.3
  12.0 3.9 %inner_second.1 = (f32[8,272,128]{2,1,0:T(8,128)S(1)}, f32[8,272,128]{2,1,0:T(8,128)S(1)}, f32[8,272,128]{2,1,0:T(8,128)S(1)}, f32[8,272,128]{2,1,0:T(8,128)S(1)...) custom-call(f32[16]{0:T(128)S(1)} %copy-done.4, ...), custom_call_target="tpu_custom_call", output_to_operand_aliasing={{0}: (5, {}), {1}: (6, {}), {2}: (7, {}), {3}: (8, {}), {4}... | custom-call | flops 1000000 | bytes 1000000 | tf_op jit(solution)/shard_map/inner_second/pallas_call | solution.py:33
  15.9 0.0 collective-permute-done.2.got_first
  15.9 0.0 collective-permute-done.3.got_second
  15.9 1.4 %frame.1 = (f32[8,272,128]{2,1,0:T(8,128)S(1)}, f32[8,272,128]{2,1,0:T(8,128)S(1)}, f32[8,272,128]{2,1,0:T(8,128)S(1)}, f32[8,272,128]{2,1,0:T(8,128)S(1)}, f32[...) custom-call(f32[16]{0:T(128)S(1)} %copy-done.4, ...), custom_call_target="tpu_custom_call", output_to_operand_aliasing={{0}: (5, {}), {1}: (6, {}), {2}: (7, {}), {3}: (8, {}), {4}... | custom-call | flops 1000000 | bytes 1000000 | tf_op jit(solution)/shard_map/frame/pallas_call | solution.py:33
  17.3 26.7 %all_to_all.33 = f32[64,1,128]{2,1,0:T(1,128)S(1)} all-to-all(f32[64,1,128]{2,1,0:T(1,128)S(1)} %bitcast.16), channel_id=1, replica_groups=mesh['radius'=16,'polar'=4,'group'=4] {'radius','polar'}, dimensions={0} | all-to-all | bytes 65536 | tf_op jit(solution)/shard_map/all_to_all | solution.py:573
  44.0 0.5 update.2
  44.4 1.6 %collective-permute-start.6 = (f32[2,136,128]{2,1,0:T(8,128)S(1)}, f32[2,136,128]{2,1,0:T(8,128)S(1)}, u32[]{:S(2)}, u32[]{:S(2)}) collective-permute-start(f32[2,136,128]{2,1,0:T(8,128)S(1)} %get-tuple-element.97.rest_0_), channel_id=1, source_target_pairs={{0,3},{1,2},{2,1},{3,0},{4,7},{5,6},{6,5},{7,4},{8,11},{9,10},{10,... | collective-permute-start | bytes 417800 | tf_op jit(solution)/shard_map/ppermute | solution.py:491
  46.1 0.9 collective-permute-start.5
  47.0 1.6 %collective-permute-start.4 = (f32[2,136,128]{2,1,0:T(8,128)S(1)}, f32[2,136,128]{2,1,0:T(8,128)S(1)}, u32[]{:S(2)}, u32[]{:S(2)}) collective-permute-start(f32[2,136,128]{2,1,0:T(8,128)S(1)} %get-tuple-element.97.rest_0_), channel_id=1, source_target_pairs={{0,1},{1,0},{2,3},{3,2},{4,5},{5,4},{6,7},{7,6},{8,9},{9,8},{10,11... | collective-permute-start | bytes 417800 | tf_op jit(solution)/shard_map/ppermute | solution.py:491
  48.6 0.0 copy-done.5
  48.6 1.7 %heating.1 = (f32[48,256]{1,0:T(8,128)}, f32[272,128]{1,0:T(8,128)S(1)}) custom-call(f32[48]{0:T(128)S(1)} %copy-done.5, f32[64,128]{1,0:T(8,128)S(1)} %bitcast.13, f32[272,128]{1,0:T(8,128)S(1)} %get-tuple-element.93.dens_ref.cap_in, f32[272,128]{1,0:T(8,128)S(1)} %get-tuple-element.94.mat_ref, f32[8,128]{1,0:T(8,128)S(1)} %get-tuple-element.95.flux_ref), custom_call_target="tpu_custom_call" | custom-call | flops 1000000 | bytes 1000000 | tf_op jit(solution)/shard_map/heating/pallas_call | solution.py:33
  50.3 0.9 collective-permute-done.6.rest_3_
  51.2 2.8 %collective-permute-done.5.rest_2_ = f32[2,136,128]{2,1,0:T(8,128)S(1)} collective-permute-done((f32[2,136,128]{2,1,0:T(8,128)S(1)}, f32[2,136,128]{2,1,0:T(8,128)S(1)}, u32[]{:S(2)}, u32[]{:S(2)}) %collective-permute-start.5) | collective-permute-done | bytes 139296 | tf_op jit(solution)/shard_map/ppermute | solution.py:491
  54.0 0.5 collective-permute-done.4.rest_1_
  54.5 3.1 %next.2 = (f32[8,272,128]{2,1,0:T(8,128)S(1)}, f32[8,272,128]{2,1,0:T(8,128)S(1)}, f32[64,128]{1,0:T(8,128)S(1)}, f32[8,272,128]{2,1,0:T(8,128)S(1)}, f32[272,128]{1,0:T(8,128)S(1)}, /*index=5*/f32[272,128]{1,0:T(8,128)S(1)}) custom-call(f32[16]{0:T(128)S(1)} %copy-done.4, f32[8,128]{1,0:T(8,128)S(1)} %get-tuple-element.88.c1_ref, ...), custom_call_target="tpu_custom_call" | custom-call | flops 1000000 | bytes 1000000 | tf_op jit(solution)/shard_map/next/pallas_call | solution.py:33
  57.6 13.5 %all_to_all.34 = f32[64,1,128]{2,1,0:T(1,128)S(1)} all-to-all(f32[64,1,128]{2,1,0:T(1,128)S(1)} %bitcast.17), channel_id=1, replica_groups=mesh['radius'=16,'polar'=4,'group'=4] {'radius','polar'}, dimensions={0} | all-to-all | bytes 65536 | tf_op jit(solution)/shard_map/all_to_all | solution.py:573
  71.1 0.5 update.3
  71.5 1.6 %collective-permute-start.9 = (f32[1,136,128]{2,1,0:T(8,128)S(1)}, f32[1,136,128]{2,1,0:T(8,128)S(1)}, u32[]{:S(2)}, u32[]{:S(2)}) collective-permute-start(f32[1,136,128]{2,1,0:T(8,128)S(1)} %get-tuple-element.107.rest_0_), channel_id=1, source_target_pairs={{0,3},{1,2},{2,1},{3,0},{4,7},{5,6},{6,5},{7,4},{8,11},{9,10},{10,... | collective-permute-start | bytes 208904 | tf_op jit(solution)/shard_map/ppermute | solution.py:491
  73.2 1.9 %collective-permute-start.8 = (f32[1,136,128]{2,1,0:T(8,128)S(1)}, f32[1,136,128]{2,1,0:T(8,128)S(1)}, u32[]{:S(2)}, u32[]{:S(2)}) collective-permute-start(f32[1,136,128]{2,1,0:T(8,128)S(1)} %get-tuple-element.107.rest_0_), channel_id=1, source_target_pairs={{0,2},{1,3},{2,0},{3,1},{4,6},{5,7},{6,4},{7,5},{8,10},{9,11},{10,... | collective-permute-start | bytes 208904 | tf_op jit(solution)/shard_map/ppermute | solution.py:491
  75.0 0.7 collective-permute-start.7
  75.7 0.2 collective-permute-done.9.rest_3_
  75.9 3.1 %collective-permute-done.8.rest_2_ = f32[1,136,128]{2,1,0:T(8,128)S(1)} collective-permute-done((f32[1,136,128]{2,1,0:T(8,128)S(1)}, f32[1,136,128]{2,1,0:T(8,128)S(1)}, u32[]{:S(2)}, u32[]{:S(2)}) %collective-permute-start.8) | collective-permute-done | bytes 69664 | tf_op jit(solution)/shard_map/ppermute | solution.py:491
  79.1 0.3 collective-permute-done.7.rest_1_
  79.4 2.9 %next.3 = (f32[8,272,128]{2,1,0:T(8,128)S(1)}, f32[8,272,128]{2,1,0:T(8,128)S(1)}, f32[64,128]{1,0:T(8,128)S(1)}) custom-call(f32[16]{0:T(128)S(1)} %copy-done.4, f32[8,128]{1,0:T(8,128)S(1)} %get-tuple-element.102.c1_ref, f32[8,128]{1,0:T(8,128)S(1)} %get-tuple-element.103.c2_ref, f32[8,272,128]{2,1,0:T(8,128)S(1)} %get-tuple-element.83.a_ref, ...), custom_call_target="tpu_custom_call" | custom-call | flops 1000000 | bytes 1000000 | tf_op jit(solution)/shard_map/next/pallas_call | solution.py:33
  82.3 13.5 %all_to_all.35 = f32[64,1,128]{2,1,0:T(1,128)S(1)} all-to-all(f32[64,1,128]{2,1,0:T(1,128)S(1)} %bitcast.18), channel_id=1, replica_groups=mesh['radius'=16,'polar'=4,'group'=4] {'radius','polar'}, dimensions={0} | all-to-all | bytes 65536 | tf_op jit(solution)/shard_map/all_to_all | solution.py:573
  95.8 0.4 last_update.1
  96.2 1.5 %collective-permute-start.12 = (f32[128,128]{1,0:T(8,128)S(1)}, f32[128,128]{1,0:T(8,128)S(1)}, u32[]{:S(2)}, u32[]{:S(2)}) collective-permute-start(f32[128,128]{1,0:T(8,128)S(1)} %get-tuple-element.113.rest_0_), channel_id=1, source_target_pairs={{0,3},{1,2},{2,1},{3,0},{4,7},{5,6},{6,5},{7,4},{8,11},{9,10},{10,... | collective-permute-start | bytes 196616 | tf_op jit(solution)/shard_map/ppermute | solution.py:491
  97.7 2.1 %collective-permute-start.11 = (f32[128,128]{1,0:T(8,128)S(1)}, f32[128,128]{1,0:T(8,128)S(1)}, u32[]{:S(2)}, u32[]{:S(2)}) collective-permute-start(f32[128,128]{1,0:T(8,128)S(1)} %get-tuple-element.113.rest_0_), channel_id=1, source_target_pairs={{0,2},{1,3},{2,0},{3,1},{4,6},{5,7},{6,4},{7,5},{8,10},{9,11},{10,... | collective-permute-start | bytes 196616 | tf_op jit(solution)/shard_map/ppermute | solution.py:491
  99.8 0.5 collective-permute-start.10
  100.3 1.3 %energy.1 = f32[16,48,256]{2,1,0:T(8,128)} custom-call(f32[8,272,128]{2,1,0:T(8,128)S(1)} %get-tuple-element.112.e_ref), custom_call_target="tpu_custom_call" | custom-call | flops 1000000 | bytes 1000000 | tf_op jit(solution)/shard_map/energy/pallas_call | solution.py:33
  101.6 0.0 collective-permute-done.12.rest_3_
  101.6 1.8 %collective-permute-done.11.rest_2_ = f32[128,128]{1,0:T(8,128)S(1)} collective-permute-done((f32[128,128]{1,0:T(8,128)S(1)}, f32[128,128]{1,0:T(8,128)S(1)}, u32[]{:S(2)}, u32[]{:S(2)}) %collective-permute-start.11) | collective-permute-done | bytes 65568 | tf_op jit(solution)/shard_map/ppermute | solution.py:491
  103.5 0.6 collective-permute-done.10.rest_1_
  104.1 0.8 material.5
  (6 shorter events, 0.0 us)
Async XLA Ops:
  0.6 6.7 %copy-start.3 = (f32[48,256]{1,0:T(8,128)S(1)}, f32[48,256]{1,0:T(8,128)}, u32[]{:S(2)}) copy-start(f32[48,256]{1,0:T(8,128)} %material.4) | copy-start | bytes 147460
  0.6 6.7 %copy-start = (f32[16,48,256]{2,1,0:T(8,128)S(1)}, f32[16,48,256]{2,1,0:T(8,128)}, u32[]{:S(2)}) copy-start(f32[16,48,256]{2,1,0:T(8,128)} %old.3) | copy-start | bytes 2359300
  0.7 6.6 %copy-start.1 = (bf16[16,48,256]{2,1,0:T(8,128)(2,1)S(1)}, bf16[16,48,256]{2,1,0:T(8,128)(2,1)}, u32[]{:S(2)}) copy-start(bf16[16,48,256]{2,1,0:T(8,128)(2,1)} %opacity.3) | copy-start | bytes 1179652
  0.7 6.6 %copy-start.2 = (f32[48,256]{1,0:T(8,128)S(1)}, f32[48,256]{1,0:T(8,128)}, u32[]{:S(2)}) copy-start(f32[48,256]{1,0:T(8,128)} %density.3) | copy-start | bytes 147460
  2.0 7.5 %copy-start.4 = (f32[16]{0:T(128)S(1)}, f32[16]{0:T(128)}, u32[]{:S(2)}) copy-start(f32[16]{0:T(128)} %weights.9) | copy-start | bytes 196
  2.1 4.0 %collective-permute-start = (f32[35,8,256]{2,1,0:T(8,128)S(1)}, f32[35,8,256]{2,1,0:T(8,128)S(1)}, u32[]{:S(2)}, u32[]{:S(2)}) collective-permute-start(f32[35,8,256]{2,1,0:T(8,128)S(1)} %get-tuple-element.59), channel_id=1, source_target_pairs={{16,32},{48,64},{80,96},{112,128},{144,160},{176,192},{208,224},{3... | collective-permute-start | bytes 860168 | tf_op jit(solution)/shard_map/ppermute | solution.py:500
  2.7 4.5 %collective-permute-start.1 = (f32[35,8,256]{2,1,0:T(8,128)S(1)}, f32[35,8,256]{2,1,0:T(8,128)S(1)}, u32[]{:S(2)}, u32[]{:S(2)}) collective-permute-start(f32[35,8,256]{2,1,0:T(8,128)S(1)} %get-tuple-element.60), channel_id=1, source_target_pairs={{0,16},{16,0},{32,48},{48,32},{64,80},{80,64},{96,112},{112,96},{1... | collective-permute-start | bytes 860168 | tf_op jit(solution)/shard_map/ppermute | solution.py:495
  8.0 7.9 %collective-permute-start.2 = (f32[18,8,128]{2,1,0:T(8,128)S(1)}, f32[18,8,128]{2,1,0:T(8,128)S(1)}, u32[]{:S(2)}, u32[]{:S(2)}) collective-permute-start(f32[18,8,128]{2,1,0:T(8,128)S(1)} %get-tuple-element.61), channel_id=1, source_target_pairs={{0,4},{4,0},{8,12},{12,8},{1,5},{5,1},{9,13},{13,9},{2,6},{6,2},{1... | collective-permute-start | bytes 221192 | tf_op jit(solution)/shard_map/ppermute | solution.py:495
  11.3 4.6 %collective-permute-start.3 = (f32[18,8,128]{2,1,0:T(8,128)S(1)}, f32[18,8,128]{2,1,0:T(8,128)S(1)}, u32[]{:S(2)}, u32[]{:S(2)}) collective-permute-start(f32[18,8,128]{2,1,0:T(8,128)S(1)} %get-tuple-element.67), channel_id=1, source_target_pairs={{4,8},{8,4},{5,9},{9,5},{6,10},{10,6},{7,11},{11,7},{20,24},{24,20... | collective-permute-start | bytes 221192 | tf_op jit(solution)/shard_map/ppermute | solution.py:500
  44.0 4.6 %copy-start.5 = (f32[48]{0:T(128)S(1)}, f32[48]{0:T(128)}, u32[]{:S(2)}) copy-start(f32[48]{0:T(128)} %flux.1) | copy-start | bytes 580
  44.4 6.8 %collective-permute-start.6 = (f32[2,136,128]{2,1,0:T(8,128)S(1)}, f32[2,136,128]{2,1,0:T(8,128)S(1)}, u32[]{:S(2)}, u32[]{:S(2)}) collective-permute-start(f32[2,136,128]{2,1,0:T(8,128)S(1)} %get-tuple-element.97.rest_0_), channel_id=1, source_target_pairs={{0,3},{1,2},{2,1},{3,0},{4,7},{5,6},{6,5},{7,4},{8,11},{9,10},{10,... | collective-permute-start | bytes 417800 | tf_op jit(solution)/shard_map/ppermute | solution.py:491
  46.1 7.9 %collective-permute-start.5 = (f32[2,136,128]{2,1,0:T(8,128)S(1)}, f32[2,136,128]{2,1,0:T(8,128)S(1)}, u32[]{:S(2)}, u32[]{:S(2)}) collective-permute-start(f32[2,136,128]{2,1,0:T(8,128)S(1)} %get-tuple-element.97.rest_0_), channel_id=1, source_target_pairs={{0,2},{1,3},{2,0},{3,1},{4,6},{5,7},{6,4},{7,5},{8,10},{9,11},{10,... | collective-permute-start | bytes 417800 | tf_op jit(solution)/shard_map/ppermute | solution.py:491
  47.0 7.4 %collective-permute-start.4 = (f32[2,136,128]{2,1,0:T(8,128)S(1)}, f32[2,136,128]{2,1,0:T(8,128)S(1)}, u32[]{:S(2)}, u32[]{:S(2)}) collective-permute-start(f32[2,136,128]{2,1,0:T(8,128)S(1)} %get-tuple-element.97.rest_0_), channel_id=1, source_target_pairs={{0,1},{1,0},{2,3},{3,2},{4,5},{5,4},{6,7},{7,6},{8,9},{9,8},{10,11... | collective-permute-start | bytes 417800 | tf_op jit(solution)/shard_map/ppermute | solution.py:491
  71.5 4.4 %collective-permute-start.9 = (f32[1,136,128]{2,1,0:T(8,128)S(1)}, f32[1,136,128]{2,1,0:T(8,128)S(1)}, u32[]{:S(2)}, u32[]{:S(2)}) collective-permute-start(f32[1,136,128]{2,1,0:T(8,128)S(1)} %get-tuple-element.107.rest_0_), channel_id=1, source_target_pairs={{0,3},{1,2},{2,1},{3,0},{4,7},{5,6},{6,5},{7,4},{8,11},{9,10},{10,... | collective-permute-start | bytes 208904 | tf_op jit(solution)/shard_map/ppermute | solution.py:491
  73.2 5.9 %collective-permute-start.8 = (f32[1,136,128]{2,1,0:T(8,128)S(1)}, f32[1,136,128]{2,1,0:T(8,128)S(1)}, u32[]{:S(2)}, u32[]{:S(2)}) collective-permute-start(f32[1,136,128]{2,1,0:T(8,128)S(1)} %get-tuple-element.107.rest_0_), channel_id=1, source_target_pairs={{0,2},{1,3},{2,0},{3,1},{4,6},{5,7},{6,4},{7,5},{8,10},{9,11},{10,... | collective-permute-start | bytes 208904 | tf_op jit(solution)/shard_map/ppermute | solution.py:491
  75.0 4.3 %collective-permute-start.7 = (f32[1,136,128]{2,1,0:T(8,128)S(1)}, f32[1,136,128]{2,1,0:T(8,128)S(1)}, u32[]{:S(2)}, u32[]{:S(2)}) collective-permute-start(f32[1,136,128]{2,1,0:T(8,128)S(1)} %get-tuple-element.107.rest_0_), channel_id=1, source_target_pairs={{0,1},{1,0},{2,3},{3,2},{4,5},{5,4},{6,7},{7,6},{8,9},{9,8},{10,11... | collective-permute-start | bytes 208904 | tf_op jit(solution)/shard_map/ppermute | solution.py:491
  96.2 5.4 %collective-permute-start.12 = (f32[128,128]{1,0:T(8,128)S(1)}, f32[128,128]{1,0:T(8,128)S(1)}, u32[]{:S(2)}, u32[]{:S(2)}) collective-permute-start(f32[128,128]{1,0:T(8,128)S(1)} %get-tuple-element.113.rest_0_), channel_id=1, source_target_pairs={{0,3},{1,2},{2,1},{3,0},{4,7},{5,6},{6,5},{7,4},{8,11},{9,10},{10,... | collective-permute-start | bytes 196616 | tf_op jit(solution)/shard_map/ppermute | solution.py:491
  97.7 5.8 %collective-permute-start.11 = (f32[128,128]{1,0:T(8,128)S(1)}, f32[128,128]{1,0:T(8,128)S(1)}, u32[]{:S(2)}, u32[]{:S(2)}) collective-permute-start(f32[128,128]{1,0:T(8,128)S(1)} %get-tuple-element.113.rest_0_), channel_id=1, source_target_pairs={{0,2},{1,3},{2,0},{3,1},{4,6},{5,7},{6,4},{7,5},{8,10},{9,11},{10,... | collective-permute-start | bytes 196616 | tf_op jit(solution)/shard_map/ppermute | solution.py:491
  99.8 4.3 %collective-permute-start.10 = (f32[128,128]{1,0:T(8,128)S(1)}, f32[128,128]{1,0:T(8,128)S(1)}, u32[]{:S(2)}, u32[]{:S(2)}) collective-permute-start(f32[128,128]{1,0:T(8,128)S(1)} %get-tuple-element.113.rest_0_), channel_id=1, source_target_pairs={{0,1},{1,0},{2,3},{3,2},{4,5},{5,4},{6,7},{7,6},{8,9},{9,8},{10,11... | collective-permute-start | bytes 196616 | tf_op jit(solution)/shard_map/ppermute | solution.py:491

commit v8 on v7

--- a/solution.py
+++ b/solution.py
@@ -185,11 +185,11 @@
     return acc
 
 
-def krylov(p, pairs, parts, span, own, a_ref, fr_ref, fp_ref, r_ref, q_ref, t_ref, mom, old_mom=None):
+def krylov(p, pairs, parts, span, own, b_ref, fr_ref, fp_ref, r_ref, q_ref, t_ref, mom, old_mom=None):
     sums = [jnp.zeros((HALO, LANES), jnp.float32) for _ in range(4)]
     for lo, hi in parts:
         r = r_ref[(p, *at(lo, hi))]
-        q = r + a_ref[(p, *at(lo, hi))] * r + flux_sum(p, lo, hi, r_ref, r, fr_ref, fp_ref, span)
+        q = b_ref[(p, *at(lo, hi))] * r + flux_sum(p, lo, hi, r_ref, r, fr_ref, fp_ref, span)
         q_ref[(p, *at(lo, hi))] = q
         if lo >= own[0] and hi <= own[1]:
             sums[0] = sums[0] + tile_sum(r * r)
@@ -200,7 +200,7 @@
         if not inside and t_ref is None:
             continue
         q = q_ref[(p, *at(lo, hi))]
-        t = q + a_ref[(p, *at(lo, hi))] * q + flux_sum(p, lo, hi, q_ref, q, fr_ref, fp_ref, span)
+        t = b_ref[(p, *at(lo, hi))] * q + flux_sum(p, lo, hi, q_ref, q, fr_ref, fp_ref, span)
         if t_ref is not None:
             t_ref[(p, *at(lo, hi))] = t
         if inside:
@@ -248,16 +248,16 @@
     begin, end = span
     for lo, hi in inverse_parts:
         a, e = a_ref[(p, *at(lo, hi))], e_ref[(p, *at(lo, hi))]
-        slope_r = 0.5 * (next_row(e) - prev_row(e))
-        slope_p = 0.5 * (after(e_ref, (p,), lo, hi, e, end) - before(e_ref, (p,), lo, hi, e, begin))
+        slope_r = next_row(e) - prev_row(e)
+        slope_p = after(e_ref, (p,), lo, hi, e, end) - before(e_ref, (p,), lo, hi, e, begin)
         n2 = slope_r * slope_r + slope_p * slope_p
         u = a * e
-        s = 2.0 * u + jnp.sqrt(n2)
-        inv[lo:hi, :] = jnp.where(dens_ref[lo:hi, :] > 0.0, (n2 + 3.0 * u * s) / (e * s), OUTSIDE)
+        s = 4.0 * u + n2 * lax.rsqrt(n2 + 1e-37)
+        inv[lo:hi, :] = jnp.where(dens_ref[lo:hi, :] > 0.0, (n2 + 6.0 * u * s) / (e * s), OUTSIDE)
     for lo, hi in parts:
         d = inv[lo:hi, :]
-        fr_ref[(p, *at(lo, hi))] = 2.0 / (d + next_row(d))
-        fp_ref[(p, *at(lo, hi))] = 2.0 / (d + after(inv, (), lo, hi, d, end))
+        fr_ref[(p, *at(lo, hi))] = 4.0 / (d + next_row(d))
+        fp_ref[(p, *at(lo, hi))] = 4.0 / (d + after(inv, (), lo, hi, d, end))
     for lo, hi in parts:
         a, e = a_ref[(p, *at(lo, hi))], e_ref[(p, *at(lo, hi))]
         r_ref[(p, *at(lo, hi))] = a * (w * mat_ref[lo:hi, :] - e) - flux_sum(
@@ -265,32 +265,32 @@
         )
 
 
-def inner_kernel(groups, cols, half, weights, a_ref, e_ref, dens_ref, mat_ref, *rest):
+def inner_kernel(
+    groups, cols, weights, a_ref, e_ref, dens_ref, mat_ref,
+    fr_ref, fp_ref, r_ref, q_ref, t_ref, b_ref, emit, mom, inv,
+):
     pairs = groups // 2
-    if half == 0:
-        edge, fr_ref, fp_ref, r_ref, q_ref, t_ref, emit, mom, edge_out, inv = rest
-        edge_out[...] = edge[...]
-        emit[...] = jnp.zeros(emit.shape, jnp.float32)
-    else:
-        fr_ref, fp_ref, r_ref, q_ref, t_ref, emit, mom, inv = rest[7:]
-    bounds = (0, pairs // 4) if half == 0 else (pairs // 4, pairs)
     span = (HALO, HALO + cols)
     parts = [(lo + HALO, hi + HALO) for lo, hi in pieces(cols)]
     own = (2 * HALO, cols)
+    emit[...] = jnp.zeros(emit.shape, jnp.float32)
 
     def one(p, carry):
         w = weight_of(weights, p)
         for lo, hi in parts:
-            emit[lo:hi, :] += a_ref[(p, *at(lo, hi))] * w
+            a = a_ref[(p, *at(lo, hi))]
+            b_ref[(p, *at(lo, hi))] = 1.0 + a
+            emit[lo:hi, :] += a * w
         first_residual(p, w, parts, parts, span, dens_ref, mat_ref, a_ref, e_ref, fr_ref, fp_ref, r_ref, inv)
-        krylov(p, pairs, parts, span, own, a_ref, fr_ref, fp_ref, r_ref, q_ref, t_ref, mom)
+        krylov(p, pairs, parts, span, own, b_ref, fr_ref, fp_ref, r_ref, q_ref, t_ref, mom)
         return carry
 
-    lax.fori_loop(*bounds, one, 0, unroll=2)
+    lax.fori_loop(0, pairs, one, 0, unroll=2)
 
 
 def frame_kernel(groups, rows, cols, weights, got_first, got_second, emit, old_mom, *rest):
-    a_ref, e_ref, fr_ref, fp_ref, r_ref, q_ref, t_ref, dens_ref, mat_ref, emit_out, out, inv, mom = rest[9:]
+    a_ref, e_ref, fr_ref, fp_ref, r_ref, q_ref, t_ref, b_ref, dens_ref, mat_ref = rest[10:20]
+    emit_out, out, inv, mom = rest[20:]
     pairs = groups // 2
     tall = cols + 2 * HALO
     span = (0, tall)
@@ -313,13 +313,14 @@
         for side, (lo, hi) in enumerate(ends):
             a = jnp.where(dens_ref[lo:hi, :] > 0.0, halo(side, p), 1.0)
             a_ref[(p, *at(lo, hi))] = a
+            b_ref[(p, *at(lo, hi))] = 1.0 + a
             e_ref[(p, *at(lo, hi))] = halo(side, pairs + p)
             sums.append(emitted[side] + a * w)
         first_residual(
             p, w, inverse_parts, parts, span, dens_ref, mat_ref, a_ref, e_ref, fr_ref, fp_ref, r_ref, inv
         )
         krylov(
-            p, pairs, parts, span, (HALO, HALO + cols), a_ref, fr_ref, fp_ref, r_ref, q_ref, t_ref, mom, old_mom
+            p, pairs, parts, span, (HALO, HALO + cols), b_ref, fr_ref, fp_ref, r_ref, q_ref, t_ref, mom, old_mom
         )
         return tuple(sums)
 
@@ -438,7 +439,7 @@
     return total
 
 
-def next_kernel(groups, rows, count, turn, last, weights, c1_ref, c2_ref, a_ref, fr_ref, fp_ref, r_in, q_in, t_in, fixed, cap_in, mat_ref, *rest):
+def next_kernel(groups, rows, count, turn, last, weights, c1_ref, c2_ref, a_ref, b_ref, fr_ref, fp_ref, r_in, q_in, t_in, fixed, cap_in, mat_ref, *rest):
     pairs = groups // 2
     sums = rest[:count]
     rest = rest[count:]
@@ -472,7 +473,7 @@
             r_ref[here] = (
                 r_in[here] - c1 * q_in[here] + c2 * t_in[here] + a_ref[here] * (w * delta[lo:hi, :])
             )
-        krylov(p, pairs, parts, (0, tall), (HALO, tall - HALO), a_ref, fr_ref, fp_ref, r_ref, q_ref, t_ref, mom)
+        krylov(p, pairs, parts, (0, tall), (HALO, tall - HALO), b_ref, fr_ref, fp_ref, r_ref, q_ref, t_ref, mom)
         return carry
 
     lax.fori_loop(0, pairs, one, 0, unroll=2)
@@ -540,33 +541,23 @@
         [vspec()] * 6,
         name="turn",
     )
-    first = pair_up(first, "polar")
-    *state, second = call(
-        functools.partial(inner_kernel, groups, cols, 0),
-        [big] * 5 + [flat, (4 * pairs, LANES), edge],
-        (weights, a, e, dens, mat, second),
-        [sspec()] + [vspec()] * 5,
+    first, second = pair_up(first, "polar"), pair_across(second, "polar")
+    fr, fp, r, q, t, b, emit, mom = call(
+        functools.partial(inner_kernel, groups, cols),
+        [big] * 6 + [flat, (4 * pairs, LANES)],
+        (weights, a, e, dens, mat),
+        [sspec()] + [vspec()] * 4,
         scratch=[vmem(flat)],
-        name="inner_first",
-    )
-    second = pair_across(second, "polar")
-    fr, fp, r, q, t, emit, mom = call(
-        functools.partial(inner_kernel, groups, cols, 1),
-        [big] * 5 + [flat, (4 * pairs, LANES)],
-        (weights, a, e, dens, mat, *state),
-        [sspec()] + [vspec()] * 11,
-        scratch=[vmem(flat)],
-        name="inner_second",
-        aliases={5 + k: k for k in range(7)},
-    )
-    a, e, fr, fp, r, q, t, dens, mat, emit, out = call(
+        name="inner",
+    )
+    a, e, fr, fp, r, q, t, b, dens, mat, emit, out = call(
         functools.partial(frame_kernel, groups, rows, cols),
-        [big] * 7 + [flat, flat, (tall // 2, LANES), line],
-        (weights, first, second, emit, mom, a, e, fr, fp, r, q, t, dens, mat),
-        [sspec()] + [vspec()] * 13,
+        [big] * 8 + [flat, flat, (tall // 2, LANES), line],
+        (weights, first, second, emit, mom, a, e, fr, fp, r, q, t, b, dens, mat),
+        [sspec()] + [vspec()] * 14,
         scratch=[vmem(flat), vmem((4 * pairs, LANES))],
         name="frame",
-        aliases={5 + k: k for k in range(9)},
+        aliases={5 + k: k for k in range(10)},
     )
     capacity = dens
     for turn in range(ITERS):
@@ -618,8 +609,8 @@
         r, q, out, *more = call(
             functools.partial(next_kernel, groups, rows, count, turn, last),
             [big, big, line] + ([] if last else [big, flat]) + ([flat] if first else []),
-            (weights, c1, c2, a, fr, fp, r, q, t, fixed, capacity, mat, *sums),
-            [sspec()] + [vspec()] * (11 + count),
+            (weights, c1, c2, a, b, fr, fp, r, q, t, fixed, capacity, mat, *sums),
+            [sspec()] + [vspec()] * (12 + count),
             scratch=[vmem(flat), vmem((4 * pairs, LANES))],
             name="next",
         )

time: 105 us -> 104 us (level)
    pallas_call x13 -> x12, Pallas kernels: 20.3 us -> 19.8 us  [call(): pl.pallas_call(kernel, out_shape=[jax.ShapeDtypeStruct(s, jnp.float32) fo...]
where the time goes in v8:
time: 104 us
  blocking collectives  53.4 us (51%)
  Pallas kernels  19.8 us (19%)
  starting transfers between devices  18.7 us (18%)
  waiting for transfers between devices  11.4 us (11%)
    all_to_all x3, blocking collectives, per_device(): gathered = lax.all_to_all(out, ('radius', 'polar'), 0, 0, tiled=True)  53.4 us
    pallas_call x12, Pallas kernels, call(): pl.pallas_call(kernel, out_shape=[jax.ShapeDtypeStruct(s, jnp.float32) fo...  19.8 us
    ppermute x9, starting transfers between devices, spread(): lax.ppermute(part, axis, [(i, i ^ s) for i in range(count)])  12.5 us
    ppermute x9, waiting for transfers between devices, spread(): lax.ppermute(part, axis, [(i, i ^ s) for i in range(count)])  10.2 us
    ppermute x2, starting transfers between devices, pair_up(): lax.ppermute(first, axis, [(i, i ^ 1) for i in range(lax.axis_size(axis))])  4.92 us
  transfers between devices with their start and end apart: 13, of which 9 were waited for; matrix products, arithmetic and copies ran while one was open for 0% of the time, Pallas kernels for 8%

profile of v8, /device:TPU:8, one launch (start us, length us, event | category | flops | bytes accessed | tf_op | source)
XLA Modules:
  0.0 104.2 jit_solution(4012508958727734667)
XLA Ops:
  0.6 0.0 copy-start.3
  0.6 0.0 copy-start
  0.7 0.0 copy-start.1
  0.7 0.0 copy-start.2
  0.7 1.4 %pack_rows.1 = (f32[35,8,256]{2,1,0:T(8,128)S(1)}, f32[35,8,256]{2,1,0:T(8,128)S(1)}) custom-call(f32[48]{0:T(128)} %flux.1, bf16[16,48,256]{2,1,0:T(8,128)(2,1)} %opacity.3, f32[16,48,256]{2,1,0:T(8,128)} %old.3, f32[48,256]{1,0:T(8,128)} %density.3, f32[48,256]{1,0:T(8,128)} %material.4), custom_call_target="tpu_custom_call" | custom-call | flops 1000000 | bytes 1000000 | tf_op jit(solution)/shard_map/pack_rows/pallas_call | solution.py:33
  2.0 0.0 copy-start.4
  2.1 0.7 collective-permute-start
  2.7 3.3 %collective-permute-start.1 = (f32[35,8,256]{2,1,0:T(8,128)S(1)}, f32[35,8,256]{2,1,0:T(8,128)S(1)}, u32[]{:S(2)}, u32[]{:S(2)}) collective-permute-start(f32[35,8,256]{2,1,0:T(8,128)S(1)} %get-tuple-element.54), channel_id=1, source_target_pairs={{0,16},{16,0},{32,48},{48,32},{64,80},{80,64},{96,112},{112,96},{1... | collective-permute-start | bytes 860168 | tf_op jit(solution)/shard_map/ppermute | solution.py:496
  6.1 0.0 collective-permute-done.got_second
  6.1 1.2 %collective-permute-done.1.got_first = f32[35,8,256]{2,1,0:T(8,128)S(1)} collective-permute-done((f32[35,8,256]{2,1,0:T(8,128)S(1)}, f32[35,8,256]{2,1,0:T(8,128)S(1)}, u32[]{:S(2)}, u32[]{:S(2)}) %collective-permute-start.1) | collective-permute-done | bytes 286752 | tf_op jit(solution)/shard_map/ppermute | solution.py:496
  7.3 0.0 copy-done
  7.3 0.7 turn.1
  8.0 1.6 %collective-permute-start.2 = (f32[18,8,128]{2,1,0:T(8,128)S(1)}, f32[18,8,128]{2,1,0:T(8,128)S(1)}, u32[]{:S(2)}, u32[]{:S(2)}) collective-permute-start(f32[18,8,128]{2,1,0:T(8,128)S(1)} %get-tuple-element.55), channel_id=1, source_target_pairs={{0,4},{4,0},{8,12},{12,8},{1,5},{5,1},{9,13},{13,9},{2,6},{6,2},{1... | collective-permute-start | bytes 221192 | tf_op jit(solution)/shard_map/ppermute | solution.py:496
  9.6 0.7 collective-permute-start.3
  10.2 0.0 copy-done.4
  10.3 5.0 %inner.1 = (f32[8,272,128]{2,1,0:T(8,128)S(1)}, f32[8,272,128]{2,1,0:T(8,128)S(1)}, f32[8,272,128]{2,1,0:T(8,128)S(1)}, f32[8,272,128]{2,1,0:T(8,128)S(1)}, f32[...) custom-call(f32[16]{0:T(128)S(1)} %copy-done.4, ...), custom_call_target="tpu_custom_call" | custom-call | flops 1000000 | bytes 1000000 | tf_op jit(solution)/shard_map/inner/pallas_call | solution.py:33
  15.2 0.0 collective-permute-done.2.got_first
  15.2 0.0 collective-permute-done.3.got_second
  15.3 1.4 %frame.1 = (f32[8,272,128]{2,1,0:T(8,128)S(1)}, f32[8,272,128]{2,1,0:T(8,128)S(1)}, f32[8,272,128]{2,1,0:T(8,128)S(1)}, f32[8,272,128]{2,1,0:T(8,128)S(1)}, f32[...) custom-call(f32[16]{0:T(128)S(1)} %copy-done.4, ...), custom_call_target="tpu_custom_call", output_to_operand_aliasing={{0}: (5, {}), {1}: (6, {}), {2}: (7, {}), {3}: (8, {}), {4}... | custom-call | flops 1000000 | bytes 1000000 | tf_op jit(solution)/shard_map/frame/pallas_call | solution.py:33
  16.6 26.3 %all_to_all.33 = f32[64,1,128]{2,1,0:T(1,128)S(1)} all-to-all(f32[64,1,128]{2,1,0:T(1,128)S(1)} %bitcast.16), channel_id=1, replica_groups=mesh['radius'=16,'polar'=4,'group'=4] {'radius','polar'}, dimensions={0} | all-to-all | bytes 65536 | tf_op jit(solution)/shard_map/all_to_all | solution.py:564
  43.0 0.4 update.2
  43.4 1.6 %collective-permute-start.6 = (f32[2,136,128]{2,1,0:T(8,128)S(1)}, f32[2,136,128]{2,1,0:T(8,128)S(1)}, u32[]{:S(2)}, u32[]{:S(2)}) collective-permute-start(f32[2,136,128]{2,1,0:T(8,128)S(1)} %get-tuple-element.85.rest_0_), channel_id=1, source_target_pairs={{0,3},{1,2},{2,1},{3,0},{4,7},{5,6},{6,5},{7,4},{8,11},{9,10},{10,... | collective-permute-start | bytes 417800 | tf_op jit(solution)/shard_map/ppermute | solution.py:492
  45.0 0.9 collective-permute-start.5
  46.0 1.6 %collective-permute-start.4 = (f32[2,136,128]{2,1,0:T(8,128)S(1)}, f32[2,136,128]{2,1,0:T(8,128)S(1)}, u32[]{:S(2)}, u32[]{:S(2)}) collective-permute-start(f32[2,136,128]{2,1,0:T(8,128)S(1)} %get-tuple-element.85.rest_0_), channel_id=1, source_target_pairs={{0,1},{1,0},{2,3},{3,2},{4,5},{5,4},{6,7},{7,6},{8,9},{9,8},{10,11... | collective-permute-start | bytes 417800 | tf_op jit(solution)/shard_map/ppermute | solution.py:492
  47.5 1.7 %heating.1 = (f32[48,256]{1,0:T(8,128)}, f32[272,128]{1,0:T(8,128)S(1)}) custom-call(f32[48]{0:T(128)S(1)} %copy-done.5, f32[64,128]{1,0:T(8,128)S(1)} %bitcast.13, f32[272,128]{1,0:T(8,128)S(1)} %get-tuple-element.81.dens_ref.cap_in, f32[272,128]{1,0:T(8,128)S(1)} %get-tuple-element.82.mat_ref, f32[8,128]{1,0:T(8,128)S(1)} %get-tuple-element.83.flux_ref), custom_call_target="tpu_custom_call" | custom-call | flops 1000000 | bytes 1000000 | tf_op jit(solution)/shard_map/heating/pallas_call | solution.py:33
  49.3 0.9 collective-permute-done.6.rest_3_
  50.2 2.8 %collective-permute-done.5.rest_2_ = f32[2,136,128]{2,1,0:T(8,128)S(1)} collective-permute-done((f32[2,136,128]{2,1,0:T(8,128)S(1)}, f32[2,136,128]{2,1,0:T(8,128)S(1)}, u32[]{:S(2)}, u32[]{:S(2)}) %collective-permute-start.5) | collective-permute-done | bytes 139296 | tf_op jit(solution)/shard_map/ppermute | solution.py:492
  52.9 0.5 collective-permute-done.4.rest_1_
  53.4 3.2 %next.2 = (f32[8,272,128]{2,1,0:T(8,128)S(1)}, f32[8,272,128]{2,1,0:T(8,128)S(1)}, f32[64,128]{1,0:T(8,128)S(1)}, f32[8,272,128]{2,1,0:T(8,128)S(1)}, f32[272,128]{1,0:T(8,128)S(1)}, /*index=5*/f32[272,128]{1,0:T(8,128)S(1)}) custom-call(f32[16]{0:T(128)S(1)} %copy-done.4, f32[8,128]{1,0:T(8,128)S(1)} %get-tuple-element.75.c1_ref, ...), custom_call_target="tpu_custom_call" | custom-call | flops 1000000 | bytes 1000000 | tf_op jit(solution)/shard_map/next/pallas_call | solution.py:33
  56.6 13.5 %all_to_all.34 = f32[64,1,128]{2,1,0:T(1,128)S(1)} all-to-all(f32[64,1,128]{2,1,0:T(1,128)S(1)} %bitcast.17), channel_id=1, replica_groups=mesh['radius'=16,'polar'=4,'group'=4] {'radius','polar'}, dimensions={0} | all-to-all | bytes 65536 | tf_op jit(solution)/shard_map/all_to_all | solution.py:564
  70.1 0.5 update.3
  70.5 1.6 %collective-permute-start.9 = (f32[1,136,128]{2,1,0:T(8,128)S(1)}, f32[1,136,128]{2,1,0:T(8,128)S(1)}, u32[]{:S(2)}, u32[]{:S(2)}) collective-permute-start(f32[1,136,128]{2,1,0:T(8,128)S(1)} %get-tuple-element.95.rest_0_), channel_id=1, source_target_pairs={{0,3},{1,2},{2,1},{3,0},{4,7},{5,6},{6,5},{7,4},{8,11},{9,10},{10,... | collective-permute-start | bytes 208904 | tf_op jit(solution)/shard_map/ppermute | solution.py:492
  72.2 1.9 %collective-permute-start.8 = (f32[1,136,128]{2,1,0:T(8,128)S(1)}, f32[1,136,128]{2,1,0:T(8,128)S(1)}, u32[]{:S(2)}, u32[]{:S(2)}) collective-permute-start(f32[1,136,128]{2,1,0:T(8,128)S(1)} %get-tuple-element.95.rest_0_), channel_id=1, source_target_pairs={{0,2},{1,3},{2,0},{3,1},{4,6},{5,7},{6,4},{7,5},{8,10},{9,11},{10,... | collective-permute-start | bytes 208904 | tf_op jit(solution)/shard_map/ppermute | solution.py:492
  74.1 0.7 collective-permute-start.7
  74.7 0.2 collective-permute-done.9.rest_3_
  74.9 3.1 %collective-permute-done.8.rest_2_ = f32[1,136,128]{2,1,0:T(8,128)S(1)} collective-permute-done((f32[1,136,128]{2,1,0:T(8,128)S(1)}, f32[1,136,128]{2,1,0:T(8,128)S(1)}, u32[]{:S(2)}, u32[]{:S(2)}) %collective-permute-start.8) | collective-permute-done | bytes 69664 | tf_op jit(solution)/shard_map/ppermute | solution.py:492
  78.1 0.3 collective-permute-done.7.rest_1_
  78.4 3.0 %next.3 = (f32[8,272,128]{2,1,0:T(8,128)S(1)}, f32[8,272,128]{2,1,0:T(8,128)S(1)}, f32[64,128]{1,0:T(8,128)S(1)}) custom-call(f32[16]{0:T(128)S(1)} %copy-done.4, f32[8,128]{1,0:T(8,128)S(1)} %get-tuple-element.90.c1_ref, f32[8,128]{1,0:T(8,128)S(1)} %get-tuple-element.91.c2_ref, f32[8,272,128]{2,1,0:T(8,128)S(1)} %get-tuple-element.70.a_ref, ...), custom_call_target="tpu_custom_call" | custom-call | flops 1000000 | bytes 1000000 | tf_op jit(solution)/shard_map/next/pallas_call | solution.py:33
  81.4 13.7 %all_to_all.35 = f32[64,1,128]{2,1,0:T(1,128)S(1)} all-to-all(f32[64,1,128]{2,1,0:T(1,128)S(1)} %bitcast.18), channel_id=1, replica_groups=mesh['radius'=16,'polar'=4,'group'=4] {'radius','polar'}, dimensions={0} | all-to-all | bytes 65536 | tf_op jit(solution)/shard_map/all_to_all | solution.py:564
  95.0 0.5 last_update.1
  95.6 1.5 %collective-permute-start.12 = (f32[128,128]{1,0:T(8,128)S(1)}, f32[128,128]{1,0:T(8,128)S(1)}, u32[]{:S(2)}, u32[]{:S(2)}) collective-permute-start(f32[128,128]{1,0:T(8,128)S(1)} %get-tuple-element.101.rest_0_), channel_id=1, source_target_pairs={{0,3},{1,2},{2,1},{3,0},{4,7},{5,6},{6,5},{7,4},{8,11},{9,10},{10,... | collective-permute-start | bytes 196616 | tf_op jit(solution)/shard_map/ppermute | solution.py:492
  97.1 2.1 %collective-permute-start.11 = (f32[128,128]{1,0:T(8,128)S(1)}, f32[128,128]{1,0:T(8,128)S(1)}, u32[]{:S(2)}, u32[]{:S(2)}) collective-permute-start(f32[128,128]{1,0:T(8,128)S(1)} %get-tuple-element.101.rest_0_), channel_id=1, source_target_pairs={{0,2},{1,3},{2,0},{3,1},{4,6},{5,7},{6,4},{7,5},{8,10},{9,11},{10,... | collective-permute-start | bytes 196616 | tf_op jit(solution)/shard_map/ppermute | solution.py:492
  99.2 0.5 collective-permute-start.10
  99.7 1.3 %energy.1 = f32[16,48,256]{2,1,0:T(8,128)} custom-call(f32[8,272,128]{2,1,0:T(8,128)S(1)} %get-tuple-element.100.e_ref), custom_call_target="tpu_custom_call" | custom-call | flops 1000000 | bytes 1000000 | tf_op jit(solution)/shard_map/energy/pallas_call | solution.py:33
  101.0 0.0 collective-permute-done.12.rest_3_
  101.0 1.8 %collective-permute-done.11.rest_2_ = f32[128,128]{1,0:T(8,128)S(1)} collective-permute-done((f32[128,128]{1,0:T(8,128)S(1)}, f32[128,128]{1,0:T(8,128)S(1)}, u32[]{:S(2)}, u32[]{:S(2)}) %collective-permute-start.11) | collective-permute-done | bytes 65568 | tf_op jit(solution)/shard_map/ppermute | solution.py:492
  102.8 0.6 collective-permute-done.10.rest_1_
  103.4 0.8 material.5
  (5 shorter events, 0.0 us)
Async XLA Ops:
  0.6 6.7 %copy-start.3 = (f32[48,256]{1,0:T(8,128)S(1)}, f32[48,256]{1,0:T(8,128)}, u32[]{:S(2)}) copy-start(f32[48,256]{1,0:T(8,128)} %material.4) | copy-start | bytes 147460
  0.6 6.7 %copy-start = (f32[16,48,256]{2,1,0:T(8,128)S(1)}, f32[16,48,256]{2,1,0:T(8,128)}, u32[]{:S(2)}) copy-start(f32[16,48,256]{2,1,0:T(8,128)} %old.3) | copy-start | bytes 2359300
  0.7 6.6 %copy-start.1 = (bf16[16,48,256]{2,1,0:T(8,128)(2,1)S(1)}, bf16[16,48,256]{2,1,0:T(8,128)(2,1)}, u32[]{:S(2)}) copy-start(bf16[16,48,256]{2,1,0:T(8,128)(2,1)} %opacity.3) | copy-start | bytes 1179652
  0.7 6.6 %copy-start.2 = (f32[48,256]{1,0:T(8,128)S(1)}, f32[48,256]{1,0:T(8,128)}, u32[]{:S(2)}) copy-start(f32[48,256]{1,0:T(8,128)} %density.3) | copy-start | bytes 147460
  2.0 8.2 %copy-start.4 = (f32[16]{0:T(128)S(1)}, f32[16]{0:T(128)}, u32[]{:S(2)}) copy-start(f32[16]{0:T(128)} %weights.7) | copy-start | bytes 196
  2.1 4.0 %collective-permute-start = (f32[35,8,256]{2,1,0:T(8,128)S(1)}, f32[35,8,256]{2,1,0:T(8,128)S(1)}, u32[]{:S(2)}, u32[]{:S(2)}) collective-permute-start(f32[35,8,256]{2,1,0:T(8,128)S(1)} %get-tuple-element.53), channel_id=1, source_target_pairs={{16,32},{48,64},{80,96},{112,128},{144,160},{176,192},{208,224},{3... | collective-permute-start | bytes 860168 | tf_op jit(solution)/shard_map/ppermute | solution.py:501
  2.7 4.5 %collective-permute-start.1 = (f32[35,8,256]{2,1,0:T(8,128)S(1)}, f32[35,8,256]{2,1,0:T(8,128)S(1)}, u32[]{:S(2)}, u32[]{:S(2)}) collective-permute-start(f32[35,8,256]{2,1,0:T(8,128)S(1)} %get-tuple-element.54), channel_id=1, source_target_pairs={{0,16},{16,0},{32,48},{48,32},{64,80},{80,64},{96,112},{112,96},{1... | collective-permute-start | bytes 860168 | tf_op jit(solution)/shard_map/ppermute | solution.py:496
  8.0 7.2 %collective-permute-start.2 = (f32[18,8,128]{2,1,0:T(8,128)S(1)}, f32[18,8,128]{2,1,0:T(8,128)S(1)}, u32[]{:S(2)}, u32[]{:S(2)}) collective-permute-start(f32[18,8,128]{2,1,0:T(8,128)S(1)} %get-tuple-element.55), channel_id=1, source_target_pairs={{0,4},{4,0},{8,12},{12,8},{1,5},{5,1},{9,13},{13,9},{2,6},{6,2},{1... | collective-permute-start | bytes 221192 | tf_op jit(solution)/shard_map/ppermute | solution.py:496
  9.6 5.7 %collective-permute-start.3 = (f32[18,8,128]{2,1,0:T(8,128)S(1)}, f32[18,8,128]{2,1,0:T(8,128)S(1)}, u32[]{:S(2)}, u32[]{:S(2)}) collective-permute-start(f32[18,8,128]{2,1,0:T(8,128)S(1)} %get-tuple-element.56), channel_id=1, source_target_pairs={{4,8},{8,4},{5,9},{9,5},{6,10},{10,6},{7,11},{11,7},{20,24},{24,20... | collective-permute-start | bytes 221192 | tf_op jit(solution)/shard_map/ppermute | solution.py:501
  43.0 4.6 %copy-start.5 = (f32[48]{0:T(128)S(1)}, f32[48]{0:T(128)}, u32[]{:S(2)}) copy-start(f32[48]{0:T(128)} %flux.1) | copy-start | bytes 580
  43.4 6.8 %collective-permute-start.6 = (f32[2,136,128]{2,1,0:T(8,128)S(1)}, f32[2,136,128]{2,1,0:T(8,128)S(1)}, u32[]{:S(2)}, u32[]{:S(2)}) collective-permute-start(f32[2,136,128]{2,1,0:T(8,128)S(1)} %get-tuple-element.85.rest_0_), channel_id=1, source_target_pairs={{0,3},{1,2},{2,1},{3,0},{4,7},{5,6},{6,5},{7,4},{8,11},{9,10},{10,... | collective-permute-start | bytes 417800 | tf_op jit(solution)/shard_map/ppermute | solution.py:492
  45.0 7.9 %collective-permute-start.5 = (f32[2,136,128]{2,1,0:T(8,128)S(1)}, f32[2,136,128]{2,1,0:T(8,128)S(1)}, u32[]{:S(2)}, u32[]{:S(2)}) collective-permute-start(f32[2,136,128]{2,1,0:T(8,128)S(1)} %get-tuple-element.85.rest_0_), channel_id=1, source_target_pairs={{0,2},{1,3},{2,0},{3,1},{4,6},{5,7},{6,4},{7,5},{8,10},{9,11},{10,... | collective-permute-start | bytes 417800 | tf_op jit(solution)/shard_map/ppermute | solution.py:492
  46.0 7.4 %collective-permute-start.4 = (f32[2,136,128]{2,1,0:T(8,128)S(1)}, f32[2,136,128]{2,1,0:T(8,128)S(1)}, u32[]{:S(2)}, u32[]{:S(2)}) collective-permute-start(f32[2,136,128]{2,1,0:T(8,128)S(1)} %get-tuple-element.85.rest_0_), channel_id=1, source_target_pairs={{0,1},{1,0},{2,3},{3,2},{4,5},{5,4},{6,7},{7,6},{8,9},{9,8},{10,11... | collective-permute-start | bytes 417800 | tf_op jit(solution)/shard_map/ppermute | solution.py:492
  70.5 4.4 %collective-permute-start.9 = (f32[1,136,128]{2,1,0:T(8,128)S(1)}, f32[1,136,128]{2,1,0:T(8,128)S(1)}, u32[]{:S(2)}, u32[]{:S(2)}) collective-permute-start(f32[1,136,128]{2,1,0:T(8,128)S(1)} %get-tuple-element.95.rest_0_), channel_id=1, source_target_pairs={{0,3},{1,2},{2,1},{3,0},{4,7},{5,6},{6,5},{7,4},{8,11},{9,10},{10,... | collective-permute-start | bytes 208904 | tf_op jit(solution)/shard_map/ppermute | solution.py:492
  72.2 5.9 %collective-permute-start.8 = (f32[1,136,128]{2,1,0:T(8,128)S(1)}, f32[1,136,128]{2,1,0:T(8,128)S(1)}, u32[]{:S(2)}, u32[]{:S(2)}) collective-permute-start(f32[1,136,128]{2,1,0:T(8,128)S(1)} %get-tuple-element.95.rest_0_), channel_id=1, source_target_pairs={{0,2},{1,3},{2,0},{3,1},{4,6},{5,7},{6,4},{7,5},{8,10},{9,11},{10,... | collective-permute-start | bytes 208904 | tf_op jit(solution)/shard_map/ppermute | solution.py:492
  74.1 4.3 %collective-permute-start.7 = (f32[1,136,128]{2,1,0:T(8,128)S(1)}, f32[1,136,128]{2,1,0:T(8,128)S(1)}, u32[]{:S(2)}, u32[]{:S(2)}) collective-permute-start(f32[1,136,128]{2,1,0:T(8,128)S(1)} %get-tuple-element.95.rest_0_), channel_id=1, source_target_pairs={{0,1},{1,0},{2,3},{3,2},{4,5},{5,4},{6,7},{7,6},{8,9},{9,8},{10,11... | collective-permute-start | bytes 208904 | tf_op jit(solution)/shard_map/ppermute | solution.py:492
  95.6 5.4 %collective-permute-start.12 = (f32[128,128]{1,0:T(8,128)S(1)}, f32[128,128]{1,0:T(8,128)S(1)}, u32[]{:S(2)}, u32[]{:S(2)}) collective-permute-start(f32[128,128]{1,0:T(8,128)S(1)} %get-tuple-element.101.rest_0_), channel_id=1, source_target_pairs={{0,3},{1,2},{2,1},{3,0},{4,7},{5,6},{6,5},{7,4},{8,11},{9,10},{10,... | collective-permute-start | bytes 196616 | tf_op jit(solution)/shard_map/ppermute | solution.py:492
  97.1 5.8 %collective-permute-start.11 = (f32[128,128]{1,0:T(8,128)S(1)}, f32[128,128]{1,0:T(8,128)S(1)}, u32[]{:S(2)}, u32[]{:S(2)}) collective-permute-start(f32[128,128]{1,0:T(8,128)S(1)} %get-tuple-element.101.rest_0_), channel_id=1, source_target_pairs={{0,2},{1,3},{2,0},{3,1},{4,6},{5,7},{6,4},{7,5},{8,10},{9,11},{10,... | collective-permute-start | bytes 196616 | tf_op jit(solution)/shard_map/ppermute | solution.py:492
  99.2 4.3 %collective-permute-start.10 = (f32[128,128]{1,0:T(8,128)S(1)}, f32[128,128]{1,0:T(8,128)S(1)}, u32[]{:S(2)}, u32[]{:S(2)}) collective-permute-start(f32[128,128]{1,0:T(8,128)S(1)} %get-tuple-element.101.rest_0_), channel_id=1, source_target_pairs={{0,1},{1,0},{2,3},{3,2},{4,5},{5,4},{6,7},{7,6},{8,9},{9,8},{10,11... | collective-permute-start | bytes 196616 | tf_op jit(solution)/shard_map/ppermute | solution.py:492

commit v9 on v8

--- a/solution.py
+++ b/solution.py
@@ -383,13 +383,19 @@
         s_out[1] = emit[...]
 
 
-def last_update_kernel(pairs, cols, gathered, a_ref, e_ref, r_ref, q_ref, e_out, s_out, s):
+def turned_back(v, rows):
+    parts = [v[lo : lo + LANES].T[HALO : HALO + rows] for lo in range(0, v.shape[0], LANES)]
+    return jnp.concatenate(parts, axis=1)
+
+
+def last_update_kernel(pairs, rows, cols, gathered, a_ref, e_ref, r_ref, q_ref, e_out, s_out, s):
     c1, c2 = steps(pairs, gathered)
     absorbed(pairs, c1, c2, a_ref, e_ref, r_ref, q_ref, e_out, s)
-    s_out[...] = fold(s[HALO : HALO + cols, :])
-
-
-def energy_kernel(pairs, rows, cols, e_ref, out):
+    total = s[HALO : HALO + cols, :]
+    s_out[...] = turned_back(total + pltpu.roll(total, HALF, 1), rows)
+
+
+def energy_kernel(pairs, rows, cols, e_ref, fixed, capacity, out, fixed_out, capacity_out):
     def one(p, carry):
         for lo in range(0, cols, LANES):
             block = e_ref[p, HALO + lo : HALO + lo + LANES, :].T
@@ -398,11 +404,8 @@
         return carry
 
     lax.fori_loop(0, pairs, one, 0, unroll=4)
-
-
-def turned_back(v, rows):
-    parts = [v[lo : lo + LANES].T[HALO : HALO + rows] for lo in range(0, v.shape[0], LANES)]
-    return jnp.concatenate(parts, axis=1)
+    fixed_out[...] = turned_back(fixed[HALO : HALO + cols, :], rows)
+    capacity_out[...] = turned_back(capacity[HALO : HALO + cols, :], rows)
 
 
 def heating_kernel(
@@ -480,11 +483,9 @@
     send_moments(pairs, rows, mom, out, None)
 
 
-def material_kernel(count, rows, cols, fixed, capacity, *rest):
-    sums, out = rest[:count], rest[count]
-    total = jnp.concatenate(unfold(summed(sums)), axis=0)
-    here = at(HALO, HALO + cols)
-    out[...] = turned_back((fixed[here] + total) / capacity[here], rows)
+def material_kernel(fixed, capacity, *rest):
+    sums, out = rest[:-1], rest[-1]
+    out[...] = (fixed[...] + summed(sums)) / capacity[...]
 
 
 def spread(part, axis):
@@ -564,23 +565,23 @@
         gathered = lax.all_to_all(out, ("radius", "polar"), 0, 0, tiled=True)
         if turn + 1 == ITERS:
             e, part = call(
-                functools.partial(last_update_kernel, pairs, cols),
-                [big, (cols // 2, LANES)],
+                functools.partial(last_update_kernel, pairs, rows, cols),
+                [big, (rows, cols)],
                 (gathered, a, e, r, q),
                 [vspec()] * 5,
                 scratch=[vmem(flat)],
                 name="last_update",
             )
             sums = spread(part, "group")
-            (energy,) = call(
+            energy, fixed, capacity = call(
                 functools.partial(energy_kernel, pairs, rows, cols),
-                [(groups, rows, cols)],
-                (e,),
-                [vspec()],
+                [(groups, rows, cols), (rows, cols), (rows, cols)],
+                (e, fixed, capacity),
+                [vspec()] * 3,
                 name="energy",
             )
             (mat,) = call(
-                functools.partial(material_kernel, count, rows, cols),
+                material_kernel,
                 [(rows, cols)],
                 (fixed, capacity, *sums),
                 [vspec()] * (2 + count),

time: 104 us -> 104 us (level)
  no operation moved by 1% of the time
where the time goes in v9:
time: 104 us
  blocking collectives  53.4 us (51%)
  Pallas kernels  19.8 us (19%)
  starting transfers between devices  18.8 us (18%)
  waiting for transfers between devices  11.3 us (11%)
    all_to_all x3, blocking collectives, per_device(): gathered = lax.all_to_all(out, ('radius', 'polar'), 0, 0, tiled=True)  53.4 us
    pallas_call x12, Pallas kernels, call(): pl.pallas_call(kernel, out_shape=[jax.ShapeDtypeStruct(s, jnp.float32) fo...  19.8 us
    ppermute x9, starting transfers between devices, spread(): lax.ppermute(part, axis, [(i, i ^ s) for i in range(count)])  12.5 us
    ppermute x9, waiting for transfers between devices, spread(): lax.ppermute(part, axis, [(i, i ^ s) for i in range(count)])  10.1 us
    ppermute x2, starting transfers between devices, pair_up(): lax.ppermute(first, axis, [(i, i ^ 1) for i in range(lax.axis_size(axis))])  4.92 us
  transfers between devices with their start and end apart: 13, of which 9 were waited for; matrix products, arithmetic and copies ran while one was open for 0% of the time, Pallas kernels for 8%

profile of v9, /device:TPU:8, one launch (start us, length us, event | category | flops | bytes accessed | tf_op | source)
XLA Modules:
  0.0 104.0 jit_solution(17181598030429995218)
XLA Ops:
  0.6 0.0 copy-start.3
  0.6 0.0 copy-start
  0.7 0.0 copy-start.1
  0.7 0.0 copy-start.2
  0.7 1.4 %pack_rows.1 = (f32[35,8,256]{2,1,0:T(8,128)S(1)}, f32[35,8,256]{2,1,0:T(8,128)S(1)}) custom-call(f32[48]{0:T(128)} %flux.1, bf16[16,48,256]{2,1,0:T(8,128)(2,1)} %opacity.3, f32[16,48,256]{2,1,0:T(8,128)} %old.3, f32[48,256]{1,0:T(8,128)} %density.3, f32[48,256]{1,0:T(8,128)} %material.4), custom_call_target="tpu_custom_call" | custom-call | flops 1000000 | bytes 1000000 | tf_op jit(solution)/shard_map/pack_rows/pallas_call | solution.py:33
  2.0 0.0 copy-start.4
  2.1 0.7 collective-permute-start
  2.7 3.3 %collective-permute-start.1 = (f32[35,8,256]{2,1,0:T(8,128)S(1)}, f32[35,8,256]{2,1,0:T(8,128)S(1)}, u32[]{:S(2)}, u32[]{:S(2)}) collective-permute-start(f32[35,8,256]{2,1,0:T(8,128)S(1)} %get-tuple-element.57), channel_id=1, source_target_pairs={{0,16},{16,0},{32,48},{48,32},{64,80},{80,64},{96,112},{112,96},{1... | collective-permute-start | bytes 860168 | tf_op jit(solution)/shard_map/ppermute | solution.py:497
  6.1 0.0 collective-permute-done.got_second
  6.1 1.2 %collective-permute-done.1.got_first = f32[35,8,256]{2,1,0:T(8,128)S(1)} collective-permute-done((f32[35,8,256]{2,1,0:T(8,128)S(1)}, f32[35,8,256]{2,1,0:T(8,128)S(1)}, u32[]{:S(2)}, u32[]{:S(2)}) %collective-permute-start.1) | collective-permute-done | bytes 286752 | tf_op jit(solution)/shard_map/ppermute | solution.py:497
  7.3 0.0 copy-done.3
  7.3 0.0 copy-done.1
  7.3 0.7 turn.1
  8.0 1.6 %collective-permute-start.2 = (f32[18,8,128]{2,1,0:T(8,128)S(1)}, f32[18,8,128]{2,1,0:T(8,128)S(1)}, u32[]{:S(2)}, u32[]{:S(2)}) collective-permute-start(f32[18,8,128]{2,1,0:T(8,128)S(1)} %get-tuple-element.58), channel_id=1, source_target_pairs={{0,4},{4,0},{8,12},{12,8},{1,5},{5,1},{9,13},{13,9},{2,6},{6,2},{1... | collective-permute-start | bytes 221192 | tf_op jit(solution)/shard_map/ppermute | solution.py:497
  9.6 0.7 collective-permute-start.3
  10.3 5.0 %inner.1 = (f32[8,272,128]{2,1,0:T(8,128)S(1)}, f32[8,272,128]{2,1,0:T(8,128)S(1)}, f32[8,272,128]{2,1,0:T(8,128)S(1)}, f32[8,272,128]{2,1,0:T(8,128)S(1)}, f32[...) custom-call(f32[16]{0:T(128)S(1)} %copy-done.4, ...), custom_call_target="tpu_custom_call" | custom-call | flops 1000000 | bytes 1000000 | tf_op jit(solution)/shard_map/inner/pallas_call | solution.py:33
  15.2 0.0 collective-permute-done.2.got_first
  15.2 0.0 collective-permute-done.3.got_second
  15.3 1.4 %frame.1 = (f32[8,272,128]{2,1,0:T(8,128)S(1)}, f32[8,272,128]{2,1,0:T(8,128)S(1)}, f32[8,272,128]{2,1,0:T(8,128)S(1)}, f32[8,272,128]{2,1,0:T(8,128)S(1)}, f32[...) custom-call(f32[16]{0:T(128)S(1)} %copy-done.4, ...), custom_call_target="tpu_custom_call", output_to_operand_aliasing={{0}: (5, {}), {1}: (6, {}), {2}: (7, {}), {3}: (8, {}), {4}... | custom-call | flops 1000000 | bytes 1000000 | tf_op jit(solution)/shard_map/frame/pallas_call | solution.py:33
  16.6 26.3 %all_to_all.33 = f32[64,1,128]{2,1,0:T(1,128)S(1)} all-to-all(f32[64,1,128]{2,1,0:T(1,128)S(1)} %bitcast.16), channel_id=1, replica_groups=mesh['radius'=16,'polar'=4,'group'=4] {'radius','polar'}, dimensions={0} | all-to-all | bytes 65536 | tf_op jit(solution)/shard_map/all_to_all | solution.py:565
  43.0 0.4 update.2
  43.4 1.6 %collective-permute-start.6 = (f32[2,136,128]{2,1,0:T(8,128)S(1)}, f32[2,136,128]{2,1,0:T(8,128)S(1)}, u32[]{:S(2)}, u32[]{:S(2)}) collective-permute-start(f32[2,136,128]{2,1,0:T(8,128)S(1)} %get-tuple-element.88.rest_0_), channel_id=1, source_target_pairs={{0,3},{1,2},{2,1},{3,0},{4,7},{5,6},{6,5},{7,4},{8,11},{9,10},{10,... | collective-permute-start | bytes 417800 | tf_op jit(solution)/shard_map/ppermute | solution.py:493
  45.0 0.9 collective-permute-start.5
  46.0 1.6 %collective-permute-start.4 = (f32[2,136,128]{2,1,0:T(8,128)S(1)}, f32[2,136,128]{2,1,0:T(8,128)S(1)}, u32[]{:S(2)}, u32[]{:S(2)}) collective-permute-start(f32[2,136,128]{2,1,0:T(8,128)S(1)} %get-tuple-element.88.rest_0_), channel_id=1, source_target_pairs={{0,1},{1,0},{2,3},{3,2},{4,5},{5,4},{6,7},{7,6},{8,9},{9,8},{10,11... | collective-permute-start | bytes 417800 | tf_op jit(solution)/shard_map/ppermute | solution.py:493
  47.5 1.7 %heating.1 = (f32[48,256]{1,0:T(8,128)}, f32[272,128]{1,0:T(8,128)S(1)}) custom-call(f32[48]{0:T(128)S(1)} %copy-done.5, f32[64,128]{1,0:T(8,128)S(1)} %bitcast.13, f32[272,128]{1,0:T(8,128)S(1)} %get-tuple-element.84.dens_ref.cap_in, f32[272,128]{1,0:T(8,128)S(1)} %get-tuple-element.85.mat_ref, f32[8,128]{1,0:T(8,128)S(1)} %get-tuple-element.86.flux_ref), custom_call_target="tpu_custom_call" | custom-call | flops 1000000 | bytes 1000000 | tf_op jit(solution)/shard_map/heating/pallas_call | solution.py:33
  49.3 0.9 collective-permute-done.6.rest_3_
  50.2 2.8 %collective-permute-done.5.rest_2_ = f32[2,136,128]{2,1,0:T(8,128)S(1)} collective-permute-done((f32[2,136,128]{2,1,0:T(8,128)S(1)}, f32[2,136,128]{2,1,0:T(8,128)S(1)}, u32[]{:S(2)}, u32[]{:S(2)}) %collective-permute-start.5) | collective-permute-done | bytes 139296 | tf_op jit(solution)/shard_map/ppermute | solution.py:493
  52.9 0.5 collective-permute-done.4.rest_1_
  53.4 3.2 %next.2 = (f32[8,272,128]{2,1,0:T(8,128)S(1)}, f32[8,272,128]{2,1,0:T(8,128)S(1)}, f32[64,128]{1,0:T(8,128)S(1)}, f32[8,272,128]{2,1,0:T(8,128)S(1)}, f32[272,128]{1,0:T(8,128)S(1)}, /*index=5*/f32[272,128]{1,0:T(8,128)S(1)}) custom-call(f32[16]{0:T(128)S(1)} %copy-done.4, f32[8,128]{1,0:T(8,128)S(1)} %get-tuple-element.78.c1_ref, ...), custom_call_target="tpu_custom_call" | custom-call | flops 1000000 | bytes 1000000 | tf_op jit(solution)/shard_map/next/pallas_call | solution.py:33
  56.6 13.5 %all_to_all.34 = f32[64,1,128]{2,1,0:T(1,128)S(1)} all-to-all(f32[64,1,128]{2,1,0:T(1,128)S(1)} %bitcast.17), channel_id=1, replica_groups=mesh['radius'=16,'polar'=4,'group'=4] {'radius','polar'}, dimensions={0} | all-to-all | bytes 65536 | tf_op jit(solution)/shard_map/all_to_all | solution.py:565
  70.1 0.5 update.3
  70.6 1.6 %collective-permute-start.9 = (f32[1,136,128]{2,1,0:T(8,128)S(1)}, f32[1,136,128]{2,1,0:T(8,128)S(1)}, u32[]{:S(2)}, u32[]{:S(2)}) collective-permute-start(f32[1,136,128]{2,1,0:T(8,128)S(1)} %get-tuple-element.98.rest_0_), channel_id=1, source_target_pairs={{0,3},{1,2},{2,1},{3,0},{4,7},{5,6},{6,5},{7,4},{8,11},{9,10},{10,... | collective-permute-start | bytes 208904 | tf_op jit(solution)/shard_map/ppermute | solution.py:493
  72.2 1.9 %collective-permute-start.8 = (f32[1,136,128]{2,1,0:T(8,128)S(1)}, f32[1,136,128]{2,1,0:T(8,128)S(1)}, u32[]{:S(2)}, u32[]{:S(2)}) collective-permute-start(f32[1,136,128]{2,1,0:T(8,128)S(1)} %get-tuple-element.98.rest_0_), channel_id=1, source_target_pairs={{0,2},{1,3},{2,0},{3,1},{4,6},{5,7},{6,4},{7,5},{8,10},{9,11},{10,... | collective-permute-start | bytes 208904 | tf_op jit(solution)/shard_map/ppermute | solution.py:493
  74.1 0.7 collective-permute-start.7
  74.7 0.2 collective-permute-done.9.rest_3_
  74.9 3.1 %collective-permute-done.8.rest_2_ = f32[1,136,128]{2,1,0:T(8,128)S(1)} collective-permute-done((f32[1,136,128]{2,1,0:T(8,128)S(1)}, f32[1,136,128]{2,1,0:T(8,128)S(1)}, u32[]{:S(2)}, u32[]{:S(2)}) %collective-permute-start.8) | collective-permute-done | bytes 69664 | tf_op jit(solution)/shard_map/ppermute | solution.py:493
  78.1 0.3 collective-permute-done.7.rest_1_
  78.4 3.1 %next.3 = (f32[8,272,128]{2,1,0:T(8,128)S(1)}, f32[8,272,128]{2,1,0:T(8,128)S(1)}, f32[64,128]{1,0:T(8,128)S(1)}) custom-call(f32[16]{0:T(128)S(1)} %copy-done.4, f32[8,128]{1,0:T(8,128)S(1)} %get-tuple-element.93.c1_ref, f32[8,128]{1,0:T(8,128)S(1)} %get-tuple-element.94.c2_ref, f32[8,272,128]{2,1,0:T(8,128)S(1)} %get-tuple-element.73.a_ref, ...), custom_call_target="tpu_custom_call" | custom-call | flops 1000000 | bytes 1000000 | tf_op jit(solution)/shard_map/next/pallas_call | solution.py:33
  81.5 13.7 %all_to_all.35 = f32[64,1,128]{2,1,0:T(1,128)S(1)} all-to-all(f32[64,1,128]{2,1,0:T(1,128)S(1)} %bitcast.18), channel_id=1, replica_groups=mesh['radius'=16,'polar'=4,'group'=4] {'radius','polar'}, dimensions={0} | all-to-all | bytes 65536 | tf_op jit(solution)/shard_map/all_to_all | solution.py:565
  95.1 0.5 last_update.1
  95.6 1.5 %collective-permute-start.12 = (f32[48,256]{1,0:T(8,128)S(1)}, f32[48,256]{1,0:T(8,128)S(1)}, u32[]{:S(2)}, u32[]{:S(2)}) collective-permute-start(f32[48,256]{1,0:T(8,128)S(1)} %get-tuple-element.107.rest_0_), channel_id=1, source_target_pairs={{0,3},{1,2},{2,1},{3,0},{4,7},{5,6},{6,5},{7,4},{8,11},{9,10},{10,... | collective-permute-start | bytes 147464 | tf_op jit(solution)/shard_map/ppermute | solution.py:493
  97.2 2.1 %collective-permute-start.11 = (f32[48,256]{1,0:T(8,128)S(1)}, f32[48,256]{1,0:T(8,128)S(1)}, u32[]{:S(2)}, u32[]{:S(2)}) collective-permute-start(f32[48,256]{1,0:T(8,128)S(1)} %get-tuple-element.107.rest_0_), channel_id=1, source_target_pairs={{0,2},{1,3},{2,0},{3,1},{4,6},{5,7},{6,4},{7,5},{8,10},{9,11},{10,... | collective-permute-start | bytes 147464 | tf_op jit(solution)/shard_map/ppermute | solution.py:493
  99.3 0.5 collective-permute-start.10
  99.8 1.3 %energy.1 = (f32[16,48,256]{2,1,0:T(8,128)}, f32[48,256]{1,0:T(8,128)S(1)}, f32[48,256]{1,0:T(8,128)S(1)}) custom-call(f32[8,272,128]{2,1,0:T(8,128)S(1)} %get-tuple-element.103.e_ref, f32[272,128]{1,0:T(8,128)S(1)} %get-tuple-element.87.fixed, f32[272,128]{1,0:T(8,128)S(1)} %get-tuple-element.96.cap_in.capacity), custom_call_target="tpu_custom_call" | custom-call | flops 1000000 | bytes 1000000 | tf_op jit(solution)/shard_map/energy/pallas_call | solution.py:33
  101.1 0.0 collective-permute-done.12.rest_3_
  101.1 1.7 %collective-permute-done.11.rest_2_ = f32[48,256]{1,0:T(8,128)S(1)} collective-permute-done((f32[48,256]{1,0:T(8,128)S(1)}, f32[48,256]{1,0:T(8,128)S(1)}, u32[]{:S(2)}, u32[]{:S(2)}) %collective-permute-start.11) | collective-permute-done | bytes 49184 | tf_op jit(solution)/shard_map/ppermute | solution.py:493
  102.8 0.6 collective-permute-done.10.rest_1_
  103.4 0.6 material.5
  (5 shorter events, 0.0 us)
Async XLA Ops:
  0.6 6.7 %copy-start.3 = (f32[48,256]{1,0:T(8,128)S(1)}, f32[48,256]{1,0:T(8,128)}, u32[]{:S(2)}) copy-start(f32[48,256]{1,0:T(8,128)} %material.4) | copy-start | bytes 147460
  0.6 6.7 %copy-start = (f32[16,48,256]{2,1,0:T(8,128)S(1)}, f32[16,48,256]{2,1,0:T(8,128)}, u32[]{:S(2)}) copy-start(f32[16,48,256]{2,1,0:T(8,128)} %old.3) | copy-start | bytes 2359300
  0.7 6.6 %copy-start.1 = (bf16[16,48,256]{2,1,0:T(8,128)(2,1)S(1)}, bf16[16,48,256]{2,1,0:T(8,128)(2,1)}, u32[]{:S(2)}) copy-start(bf16[16,48,256]{2,1,0:T(8,128)(2,1)} %opacity.3) | copy-start | bytes 1179652
  0.7 6.6 %copy-start.2 = (f32[48,256]{1,0:T(8,128)S(1)}, f32[48,256]{1,0:T(8,128)}, u32[]{:S(2)}) copy-start(f32[48,256]{1,0:T(8,128)} %density.3) | copy-start | bytes 147460
  2.0 8.2 %copy-start.4 = (f32[16]{0:T(128)S(1)}, f32[16]{0:T(128)}, u32[]{:S(2)}) copy-start(f32[16]{0:T(128)} %weights.7) | copy-start | bytes 196
  2.1 4.0 %collective-permute-start = (f32[35,8,256]{2,1,0:T(8,128)S(1)}, f32[35,8,256]{2,1,0:T(8,128)S(1)}, u32[]{:S(2)}, u32[]{:S(2)}) collective-permute-start(f32[35,8,256]{2,1,0:T(8,128)S(1)} %get-tuple-element.56), channel_id=1, source_target_pairs={{16,32},{48,64},{80,96},{112,128},{144,160},{176,192},{208,224},{3... | collective-permute-start | bytes 860168 | tf_op jit(solution)/shard_map/ppermute | solution.py:502
  2.7 4.5 %collective-permute-start.1 = (f32[35,8,256]{2,1,0:T(8,128)S(1)}, f32[35,8,256]{2,1,0:T(8,128)S(1)}, u32[]{:S(2)}, u32[]{:S(2)}) collective-permute-start(f32[35,8,256]{2,1,0:T(8,128)S(1)} %get-tuple-element.57), channel_id=1, source_target_pairs={{0,16},{16,0},{32,48},{48,32},{64,80},{80,64},{96,112},{112,96},{1... | collective-permute-start | bytes 860168 | tf_op jit(solution)/shard_map/ppermute | solution.py:497
  8.0 7.2 %collective-permute-start.2 = (f32[18,8,128]{2,1,0:T(8,128)S(1)}, f32[18,8,128]{2,1,0:T(8,128)S(1)}, u32[]{:S(2)}, u32[]{:S(2)}) collective-permute-start(f32[18,8,128]{2,1,0:T(8,128)S(1)} %get-tuple-element.58), channel_id=1, source_target_pairs={{0,4},{4,0},{8,12},{12,8},{1,5},{5,1},{9,13},{13,9},{2,6},{6,2},{1... | collective-permute-start | bytes 221192 | tf_op jit(solution)/shard_map/ppermute | solution.py:497
  9.6 5.7 %collective-permute-start.3 = (f32[18,8,128]{2,1,0:T(8,128)S(1)}, f32[18,8,128]{2,1,0:T(8,128)S(1)}, u32[]{:S(2)}, u32[]{:S(2)}) collective-permute-start(f32[18,8,128]{2,1,0:T(8,128)S(1)} %get-tuple-element.59), channel_id=1, source_target_pairs={{4,8},{8,4},{5,9},{9,5},{6,10},{10,6},{7,11},{11,7},{20,24},{24,20... | collective-permute-start | bytes 221192 | tf_op jit(solution)/shard_map/ppermute | solution.py:502
  43.0 4.6 %copy-start.5 = (f32[48]{0:T(128)S(1)}, f32[48]{0:T(128)}, u32[]{:S(2)}) copy-start(f32[48]{0:T(128)} %flux.1) | copy-start | bytes 580
  43.4 6.8 %collective-permute-start.6 = (f32[2,136,128]{2,1,0:T(8,128)S(1)}, f32[2,136,128]{2,1,0:T(8,128)S(1)}, u32[]{:S(2)}, u32[]{:S(2)}) collective-permute-start(f32[2,136,128]{2,1,0:T(8,128)S(1)} %get-tuple-element.88.rest_0_), channel_id=1, source_target_pairs={{0,3},{1,2},{2,1},{3,0},{4,7},{5,6},{6,5},{7,4},{8,11},{9,10},{10,... | collective-permute-start | bytes 417800 | tf_op jit(solution)/shard_map/ppermute | solution.py:493
  45.0 7.9 %collective-permute-start.5 = (f32[2,136,128]{2,1,0:T(8,128)S(1)}, f32[2,136,128]{2,1,0:T(8,128)S(1)}, u32[]{:S(2)}, u32[]{:S(2)}) collective-permute-start(f32[2,136,128]{2,1,0:T(8,128)S(1)} %get-tuple-element.88.rest_0_), channel_id=1, source_target_pairs={{0,2},{1,3},{2,0},{3,1},{4,6},{5,7},{6,4},{7,5},{8,10},{9,11},{10,... | collective-permute-start | bytes 417800 | tf_op jit(solution)/shard_map/ppermute | solution.py:493
  46.0 7.4 %collective-permute-start.4 = (f32[2,136,128]{2,1,0:T(8,128)S(1)}, f32[2,136,128]{2,1,0:T(8,128)S(1)}, u32[]{:S(2)}, u32[]{:S(2)}) collective-permute-start(f32[2,136,128]{2,1,0:T(8,128)S(1)} %get-tuple-element.88.rest_0_), channel_id=1, source_target_pairs={{0,1},{1,0},{2,3},{3,2},{4,5},{5,4},{6,7},{7,6},{8,9},{9,8},{10,11... | collective-permute-start | bytes 417800 | tf_op jit(solution)/shard_map/ppermute | solution.py:493
  70.6 4.4 %collective-permute-start.9 = (f32[1,136,128]{2,1,0:T(8,128)S(1)}, f32[1,136,128]{2,1,0:T(8,128)S(1)}, u32[]{:S(2)}, u32[]{:S(2)}) collective-permute-start(f32[1,136,128]{2,1,0:T(8,128)S(1)} %get-tuple-element.98.rest_0_), channel_id=1, source_target_pairs={{0,3},{1,2},{2,1},{3,0},{4,7},{5,6},{6,5},{7,4},{8,11},{9,10},{10,... | collective-permute-start | bytes 208904 | tf_op jit(solution)/shard_map/ppermute | solution.py:493
  72.2 5.9 %collective-permute-start.8 = (f32[1,136,128]{2,1,0:T(8,128)S(1)}, f32[1,136,128]{2,1,0:T(8,128)S(1)}, u32[]{:S(2)}, u32[]{:S(2)}) collective-permute-start(f32[1,136,128]{2,1,0:T(8,128)S(1)} %get-tuple-element.98.rest_0_), channel_id=1, source_target_pairs={{0,2},{1,3},{2,0},{3,1},{4,6},{5,7},{6,4},{7,5},{8,10},{9,11},{10,... | collective-permute-start | bytes 208904 | tf_op jit(solution)/shard_map/ppermute | solution.py:493
  74.1 4.3 %collective-permute-start.7 = (f32[1,136,128]{2,1,0:T(8,128)S(1)}, f32[1,136,128]{2,1,0:T(8,128)S(1)}, u32[]{:S(2)}, u32[]{:S(2)}) collective-permute-start(f32[1,136,128]{2,1,0:T(8,128)S(1)} %get-tuple-element.98.rest_0_), channel_id=1, source_target_pairs={{0,1},{1,0},{2,3},{3,2},{4,5},{5,4},{6,7},{7,6},{8,9},{9,8},{10,11... | collective-permute-start | bytes 208904 | tf_op jit(solution)/shard_map/ppermute | solution.py:493
  95.6 5.5 %collective-permute-start.12 = (f32[48,256]{1,0:T(8,128)S(1)}, f32[48,256]{1,0:T(8,128)S(1)}, u32[]{:S(2)}, u32[]{:S(2)}) collective-permute-start(f32[48,256]{1,0:T(8,128)S(1)} %get-tuple-element.107.rest_0_), channel_id=1, source_target_pairs={{0,3},{1,2},{2,1},{3,0},{4,7},{5,6},{6,5},{7,4},{8,11},{9,10},{10,... | collective-permute-start | bytes 147464 | tf_op jit(solution)/shard_map/ppermute | solution.py:493
  97.2 5.6 %collective-permute-start.11 = (f32[48,256]{1,0:T(8,128)S(1)}, f32[48,256]{1,0:T(8,128)S(1)}, u32[]{:S(2)}, u32[]{:S(2)}) collective-permute-start(f32[48,256]{1,0:T(8,128)S(1)} %get-tuple-element.107.rest_0_), channel_id=1, source_target_pairs={{0,2},{1,3},{2,0},{3,1},{4,6},{5,7},{6,4},{7,5},{8,10},{9,11},{10,... | collective-permute-start | bytes 147464 | tf_op jit(solution)/shard_map/ppermute | solution.py:493
  99.3 4.1 %collective-permute-start.10 = (f32[48,256]{1,0:T(8,128)S(1)}, f32[48,256]{1,0:T(8,128)S(1)}, u32[]{:S(2)}, u32[]{:S(2)}) collective-permute-start(f32[48,256]{1,0:T(8,128)S(1)} %get-tuple-element.107.rest_0_), channel_id=1, source_target_pairs={{0,1},{1,0},{2,3},{3,2},{4,5},{5,4},{6,7},{7,6},{8,9},{9,8},{10,11... | collective-permute-start | bytes 147464 | tf_op jit(solution)/shard_map/ppermute | solution.py:493

commit v10 on v9

--- a/solution.py
+++ b/solution.py
@@ -267,20 +267,17 @@
 
 def inner_kernel(
     groups, cols, weights, a_ref, e_ref, dens_ref, mat_ref,
-    fr_ref, fp_ref, r_ref, q_ref, t_ref, b_ref, emit, mom, inv,
+    fr_ref, fp_ref, r_ref, q_ref, t_ref, b_ref, mom, inv,
 ):
     pairs = groups // 2
     span = (HALO, HALO + cols)
     parts = [(lo + HALO, hi + HALO) for lo, hi in pieces(cols)]
     own = (2 * HALO, cols)
-    emit[...] = jnp.zeros(emit.shape, jnp.float32)
 
     def one(p, carry):
         w = weight_of(weights, p)
         for lo, hi in parts:
-            a = a_ref[(p, *at(lo, hi))]
-            b_ref[(p, *at(lo, hi))] = 1.0 + a
-            emit[lo:hi, :] += a * w
+            b_ref[(p, *at(lo, hi))] = 1.0 + a_ref[(p, *at(lo, hi))]
         first_residual(p, w, parts, parts, span, dens_ref, mat_ref, a_ref, e_ref, fr_ref, fp_ref, r_ref, inv)
         krylov(p, pairs, parts, span, own, b_ref, fr_ref, fp_ref, r_ref, q_ref, t_ref, mom)
         return carry
@@ -288,9 +285,9 @@
     lax.fori_loop(0, pairs, one, 0, unroll=2)
 
 
-def frame_kernel(groups, rows, cols, weights, got_first, got_second, emit, old_mom, *rest):
+def frame_kernel(groups, rows, cols, weights, got_first, got_second, old_mom, *rest):
     a_ref, e_ref, fr_ref, fp_ref, r_ref, q_ref, t_ref, b_ref, dens_ref, mat_ref = rest[10:20]
-    emit_out, out, inv, mom = rest[20:]
+    out, inv, mom = rest[20:]
     pairs = groups // 2
     tall = cols + 2 * HALO
     span = (0, tall)
@@ -307,26 +304,22 @@
     parts = [(0, HALO), (HALO, 2 * HALO), (cols, cols + HALO), (cols + HALO, tall)]
     inverse_parts = parts[:2] + [(2 * HALO, 3 * HALO)] + parts[2:]
 
-    def one(p, emitted):
+    def one(p, carry):
         w = weight_of(weights, p)
-        sums = []
         for side, (lo, hi) in enumerate(ends):
             a = jnp.where(dens_ref[lo:hi, :] > 0.0, halo(side, p), 1.0)
             a_ref[(p, *at(lo, hi))] = a
             b_ref[(p, *at(lo, hi))] = 1.0 + a
             e_ref[(p, *at(lo, hi))] = halo(side, pairs + p)
-            sums.append(emitted[side] + a * w)
         first_residual(
             p, w, inverse_parts, parts, span, dens_ref, mat_ref, a_ref, e_ref, fr_ref, fp_ref, r_ref, inv
         )
         krylov(
             p, pairs, parts, span, (HALO, HALO + cols), b_ref, fr_ref, fp_ref, r_ref, q_ref, t_ref, mom, old_mom
         )
-        return tuple(sums)
-
-    zero = jnp.zeros((HALO, LANES), jnp.float32)
-    low, high = lax.fori_loop(0, pairs, one, (zero, zero), unroll=8)
-    emit_out[...] = fold(jnp.concatenate([low, emit[HALO : HALO + cols, :], high], axis=0))
+        return carry
+
+    lax.fori_loop(0, pairs, one, 0, unroll=8)
     row_sums = jnp.sum(tile_sum(dens_ref[HALO : HALO + cols, :]), axis=0, keepdims=True)
     send_moments(pairs, rows, mom, out, row_sums)
 
@@ -353,34 +346,36 @@
     return first + second * (1.0 + beta), first * second
 
 
-def absorbed(pairs, c1, c2, a_ref, e_ref, r_ref, q_ref, e_out, s):
+def absorbed(pairs, c1, c2, a_ref, e_ref, r_ref, q_ref, e_out, s, weights=None, emit=None):
     tall = a_ref.shape[1]
     for lo, hi in pieces(tall):
-        total = jnp.zeros((hi - lo, LANES), jnp.float32)
+        total = emitted = jnp.zeros((hi - lo, LANES), jnp.float32)
         for p in range(pairs):
+            a = a_ref[(p, *at(lo, hi))]
             e = (
                 e_ref[(p, *at(lo, hi))]
                 + c1[p : p + 1, :] * r_ref[(p, *at(lo, hi))]
                 - c2[p : p + 1, :] * q_ref[(p, *at(lo, hi))]
             )
             e_out[(p, *at(lo, hi))] = e
-            total = total + a_ref[(p, *at(lo, hi))] * e
+            total = total + a * e
+            if emit is not None:
+                emitted = emitted + a * weight_of(weights, p)
         s[lo:hi, :] = total
-
-
-def update_kernel(pairs, gathered, a_ref, e_ref, r_ref, q_ref, *rest):
-    if len(rest) == 6:
-        emit, *rest = rest
-    else:
-        emit = None
-    e_out, s_out, c1_ref, c2_ref, s = rest
+        if emit is not None:
+            emit[lo:hi, :] = emitted
+
+
+def update_kernel(pairs, first, weights, gathered, a_ref, e_ref, r_ref, q_ref, e_out, s_out, c1_ref, c2_ref, s, emit):
     c1, c2 = steps(pairs, gathered)
     c1_ref[...] = c1
     c2_ref[...] = c2
-    absorbed(pairs, c1, c2, a_ref, e_ref, r_ref, q_ref, e_out, s)
+    if first:
+        absorbed(pairs, c1, c2, a_ref, e_ref, r_ref, q_ref, e_out, s, weights, emit)
+        s_out[1] = fold(emit[...])
+    else:
+        absorbed(pairs, c1, c2, a_ref, e_ref, r_ref, q_ref, e_out, s)
     s_out[0] = fold(s[...])
-    if emit is not None:
-        s_out[1] = emit[...]
 
 
 def turned_back(v, rows):
@@ -543,22 +538,22 @@
         name="turn",
     )
     first, second = pair_up(first, "polar"), pair_across(second, "polar")
-    fr, fp, r, q, t, b, emit, mom = call(
+    fr, fp, r, q, t, b, mom = call(
         functools.partial(inner_kernel, groups, cols),
-        [big] * 6 + [flat, (4 * pairs, LANES)],
+        [big] * 6 + [(4 * pairs, LANES)],
         (weights, a, e, dens, mat),
         [sspec()] + [vspec()] * 4,
         scratch=[vmem(flat)],
         name="inner",
     )
-    a, e, fr, fp, r, q, t, b, dens, mat, emit, out = call(
+    a, e, fr, fp, r, q, t, b, dens, mat, out = call(
         functools.partial(frame_kernel, groups, rows, cols),
-        [big] * 8 + [flat, flat, (tall // 2, LANES), line],
-        (weights, first, second, emit, mom, a, e, fr, fp, r, q, t, b, dens, mat),
-        [sspec()] + [vspec()] * 14,
+        [big] * 8 + [flat, flat, line],
+        (weights, first, second, mom, a, e, fr, fp, r, q, t, b, dens, mat),
+        [sspec()] + [vspec()] * 13,
         scratch=[vmem(flat), vmem((4 * pairs, LANES))],
         name="frame",
-        aliases={5 + k: k for k in range(10)},
+        aliases={4 + k: k for k in range(10)},
     )
     capacity = dens
     for turn in range(ITERS):
@@ -589,13 +584,12 @@
             )
             break
         first, last = turn == 0, turn + 2 == ITERS
-        extra = [emit] if first else []
         e, part, c1, c2 = call(
-            functools.partial(update_kernel, pairs),
-            [big, (1 + len(extra), tall // 2, LANES), (pairs, LANES), (pairs, LANES)],
-            (gathered, a, e, r, q, *extra),
-            [vspec()] * (5 + len(extra)),
-            scratch=[vmem(flat)],
+            functools.partial(update_kernel, pairs, first),
+            [big, (2 if first else 1, tall // 2, LANES), (pairs, LANES), (pairs, LANES)],
+            (weights, gathered, a, e, r, q),
+            [sspec()] + [vspec()] * 5,
+            scratch=[vmem(flat)] * 2,
             name="update",
         )
         sums = spread(part, "group")

time: 104 us -> 105 us (level)
  no operation moved by 1% of the time
where the time goes in v10:
time: 105 us
  blocking collectives  53.4 us (51%)
  Pallas kernels  20.6 us (20%)
  starting transfers between devices  18.8 us (18%)
  waiting for transfers between devices  11.3 us (11%)
    all_to_all x3, blocking collectives, per_device(): gathered = lax.all_to_all(out, ('radius', 'polar'), 0, 0, tiled=True)  53.4 us
    pallas_call x12, Pallas kernels, call(): pl.pallas_call(kernel, out_shape=[jax.ShapeDtypeStruct(s, jnp.float32) fo...  20.6 us
    ppermute x9, starting transfers between devices, spread(): lax.ppermute(part, axis, [(i, i ^ s) for i in range(count)])  12.5 us
    ppermute x9, waiting for transfers between devices, spread(): lax.ppermute(part, axis, [(i, i ^ s) for i in range(count)])  10.1 us
    ppermute x2, starting transfers between devices, pair_up(): lax.ppermute(first, axis, [(i, i ^ 1) for i in range(lax.axis_size(axis))])  4.92 us
  transfers between devices with their start and end apart: 13, of which 9 were waited for; matrix products, arithmetic and copies ran while one was open for 0% of the time, Pallas kernels for 8%

profile of v10, /device:TPU:8, one launch (start us, length us, event | category | flops | bytes accessed | tf_op | source)
XLA Modules:
  0.0 104.9 jit_solution(989202950391574453)
XLA Ops:
  0.6 0.0 copy-start.3
  0.6 0.0 copy-start
  0.7 0.0 copy-start.1
  0.7 0.0 copy-start.2
  0.7 1.4 %pack_rows.1 = (f32[35,8,256]{2,1,0:T(8,128)S(1)}, f32[35,8,256]{2,1,0:T(8,128)S(1)}) custom-call(f32[48]{0:T(128)} %flux.1, bf16[16,48,256]{2,1,0:T(8,128)(2,1)} %opacity.3, f32[16,48,256]{2,1,0:T(8,128)} %old.3, f32[48,256]{1,0:T(8,128)} %density.3, f32[48,256]{1,0:T(8,128)} %material.4), custom_call_target="tpu_custom_call" | custom-call | flops 1000000 | bytes 1000000 | tf_op jit(solution)/shard_map/pack_rows/pallas_call | solution.py:33
  2.0 0.0 copy-start.4
  2.1 0.7 collective-permute-start
  2.7 3.3 %collective-permute-start.1 = (f32[35,8,256]{2,1,0:T(8,128)S(1)}, f32[35,8,256]{2,1,0:T(8,128)S(1)}, u32[]{:S(2)}, u32[]{:S(2)}) collective-permute-start(f32[35,8,256]{2,1,0:T(8,128)S(1)} %get-tuple-element.55), channel_id=1, source_target_pairs={{0,16},{16,0},{32,48},{48,32},{64,80},{80,64},{96,112},{112,96},{1... | collective-permute-start | bytes 860168 | tf_op jit(solution)/shard_map/ppermute | solution.py:492
  6.1 0.0 collective-permute-done.got_second
  6.1 1.2 %collective-permute-done.1.got_first = f32[35,8,256]{2,1,0:T(8,128)S(1)} collective-permute-done((f32[35,8,256]{2,1,0:T(8,128)S(1)}, f32[35,8,256]{2,1,0:T(8,128)S(1)}, u32[]{:S(2)}, u32[]{:S(2)}) %collective-permute-start.1) | collective-permute-done | bytes 286752 | tf_op jit(solution)/shard_map/ppermute | solution.py:492
  7.3 0.0 copy-done.3
  7.3 0.0 copy-done.1
  7.3 0.7 turn.1
  8.0 1.6 %collective-permute-start.2 = (f32[18,8,128]{2,1,0:T(8,128)S(1)}, f32[18,8,128]{2,1,0:T(8,128)S(1)}, u32[]{:S(2)}, u32[]{:S(2)}) collective-permute-start(f32[18,8,128]{2,1,0:T(8,128)S(1)} %get-tuple-element.56), channel_id=1, source_target_pairs={{0,4},{4,0},{8,12},{12,8},{1,5},{5,1},{9,13},{13,9},{2,6},{6,2},{1... | collective-permute-start | bytes 221192 | tf_op jit(solution)/shard_map/ppermute | solution.py:492
  9.6 0.7 collective-permute-start.3
  10.3 4.9 %inner.1 = (f32[8,272,128]{2,1,0:T(8,128)S(1)}, f32[8,272,128]{2,1,0:T(8,128)S(1)}, f32[8,272,128]{2,1,0:T(8,128)S(1)}, f32[8,272,128]{2,1,0:T(8,128)S(1)}, f32[...) custom-call(f32[16]{0:T(128)S(1)} %copy-done.4, ...), custom_call_target="tpu_custom_call" | custom-call | flops 1000000 | bytes 1000000 | tf_op jit(solution)/shard_map/inner/pallas_call | solution.py:33
  15.2 0.0 collective-permute-done.2.got_first
  15.2 0.0 collective-permute-done.3.got_second
  15.2 1.4 %frame.1 = (f32[8,272,128]{2,1,0:T(8,128)S(1)}, f32[8,272,128]{2,1,0:T(8,128)S(1)}, f32[8,272,128]{2,1,0:T(8,128)S(1)}, f32[8,272,128]{2,1,0:T(8,128)S(1)}, f32[...) custom-call(f32[16]{0:T(128)S(1)} %copy-done.4, ...), custom_call_target="tpu_custom_call", output_to_operand_aliasing={{0}: (4, {}), {1}: (5, {}), {2}: (6, {}), {3}: (7, {}), {4}... | custom-call | flops 1000000 | bytes 1000000 | tf_op jit(solution)/shard_map/frame/pallas_call | solution.py:33
  16.6 26.3 %all_to_all.33 = f32[64,1,128]{2,1,0:T(1,128)S(1)} all-to-all(f32[64,1,128]{2,1,0:T(1,128)S(1)} %bitcast.16), channel_id=1, replica_groups=mesh['radius'=16,'polar'=4,'group'=4] {'radius','polar'}, dimensions={0} | all-to-all | bytes 65536 | tf_op jit(solution)/shard_map/all_to_all | solution.py:560
  42.9 1.0 update.2
  43.8 1.6 %collective-permute-start.6 = (f32[2,136,128]{2,1,0:T(8,128)S(1)}, f32[2,136,128]{2,1,0:T(8,128)S(1)}, u32[]{:S(2)}, u32[]{:S(2)}) collective-permute-start(f32[2,136,128]{2,1,0:T(8,128)S(1)} %get-tuple-element.84.rest_0_), channel_id=1, source_target_pairs={{0,3},{1,2},{2,1},{3,0},{4,7},{5,6},{6,5},{7,4},{8,11},{9,10},{10,... | collective-permute-start | bytes 417800 | tf_op jit(solution)/shard_map/ppermute | solution.py:488
  45.5 0.9 collective-permute-start.5
  46.4 1.6 %collective-permute-start.4 = (f32[2,136,128]{2,1,0:T(8,128)S(1)}, f32[2,136,128]{2,1,0:T(8,128)S(1)}, u32[]{:S(2)}, u32[]{:S(2)}) collective-permute-start(f32[2,136,128]{2,1,0:T(8,128)S(1)} %get-tuple-element.84.rest_0_), channel_id=1, source_target_pairs={{0,1},{1,0},{2,3},{3,2},{4,5},{5,4},{6,7},{7,6},{8,9},{9,8},{10,11... | collective-permute-start | bytes 417800 | tf_op jit(solution)/shard_map/ppermute | solution.py:488
  48.0 1.7 %heating.1 = (f32[48,256]{1,0:T(8,128)}, f32[272,128]{1,0:T(8,128)S(1)}) custom-call(f32[48]{0:T(128)S(1)} %copy-done.5, f32[64,128]{1,0:T(8,128)S(1)} %bitcast.13, f32[272,128]{1,0:T(8,128)S(1)} %get-tuple-element.80.dens_ref.cap_in, f32[272,128]{1,0:T(8,128)S(1)} %get-tuple-element.81.mat_ref, f32[8,128]{1,0:T(8,128)S(1)} %get-tuple-element.82.flux_ref), custom_call_target="tpu_custom_call" | custom-call | flops 1000000 | bytes 1000000 | tf_op jit(solution)/shard_map/heating/pallas_call | solution.py:33
  49.7 0.9 collective-permute-done.6.rest_3_
  50.6 2.8 %collective-permute-done.5.rest_2_ = f32[2,136,128]{2,1,0:T(8,128)S(1)} collective-permute-done((f32[2,136,128]{2,1,0:T(8,128)S(1)}, f32[2,136,128]{2,1,0:T(8,128)S(1)}, u32[]{:S(2)}, u32[]{:S(2)}) %collective-permute-start.5) | collective-permute-done | bytes 139296 | tf_op jit(solution)/shard_map/ppermute | solution.py:488
  53.4 0.5 collective-permute-done.4.rest_1_
  53.9 3.1 %next.2 = (f32[8,272,128]{2,1,0:T(8,128)S(1)}, f32[8,272,128]{2,1,0:T(8,128)S(1)}, f32[64,128]{1,0:T(8,128)S(1)}, f32[8,272,128]{2,1,0:T(8,128)S(1)}, f32[272,128]{1,0:T(8,128)S(1)}, /*index=5*/f32[272,128]{1,0:T(8,128)S(1)}) custom-call(f32[16]{0:T(128)S(1)} %copy-done.4, f32[8,128]{1,0:T(8,128)S(1)} %get-tuple-element.74.c1_ref, ...), custom_call_target="tpu_custom_call" | custom-call | flops 1000000 | bytes 1000000 | tf_op jit(solution)/shard_map/next/pallas_call | solution.py:33
  57.0 13.5 %all_to_all.34 = f32[64,1,128]{2,1,0:T(1,128)S(1)} all-to-all(f32[64,1,128]{2,1,0:T(1,128)S(1)} %bitcast.17), channel_id=1, replica_groups=mesh['radius'=16,'polar'=4,'group'=4] {'radius','polar'}, dimensions={0} | all-to-all | bytes 65536 | tf_op jit(solution)/shard_map/all_to_all | solution.py:560
  70.4 1.0 update.3
  71.4 1.6 %collective-permute-start.9 = (f32[1,136,128]{2,1,0:T(8,128)S(1)}, f32[1,136,128]{2,1,0:T(8,128)S(1)}, u32[]{:S(2)}, u32[]{:S(2)}) collective-permute-start(f32[1,136,128]{2,1,0:T(8,128)S(1)} %get-tuple-element.94.rest_0_), channel_id=1, source_target_pairs={{0,3},{1,2},{2,1},{3,0},{4,7},{5,6},{6,5},{7,4},{8,11},{9,10},{10,... | collective-permute-start | bytes 208904 | tf_op jit(solution)/shard_map/ppermute | solution.py:488
  73.1 1.9 %collective-permute-start.8 = (f32[1,136,128]{2,1,0:T(8,128)S(1)}, f32[1,136,128]{2,1,0:T(8,128)S(1)}, u32[]{:S(2)}, u32[]{:S(2)}) collective-permute-start(f32[1,136,128]{2,1,0:T(8,128)S(1)} %get-tuple-element.94.rest_0_), channel_id=1, source_target_pairs={{0,2},{1,3},{2,0},{3,1},{4,6},{5,7},{6,4},{7,5},{8,10},{9,11},{10,... | collective-permute-start | bytes 208904 | tf_op jit(solution)/shard_map/ppermute | solution.py:488
  74.9 0.7 collective-permute-start.7
  75.6 0.2 collective-permute-done.9.rest_3_
  75.8 3.1 %collective-permute-done.8.rest_2_ = f32[1,136,128]{2,1,0:T(8,128)S(1)} collective-permute-done((f32[1,136,128]{2,1,0:T(8,128)S(1)}, f32[1,136,128]{2,1,0:T(8,128)S(1)}, u32[]{:S(2)}, u32[]{:S(2)}) %collective-permute-start.8) | collective-permute-done | bytes 69664 | tf_op jit(solution)/shard_map/ppermute | solution.py:488
  79.0 0.3 collective-permute-done.7.rest_1_
  79.3 3.1 %next.3 = (f32[8,272,128]{2,1,0:T(8,128)S(1)}, f32[8,272,128]{2,1,0:T(8,128)S(1)}, f32[64,128]{1,0:T(8,128)S(1)}) custom-call(f32[16]{0:T(128)S(1)} %copy-done.4, f32[8,128]{1,0:T(8,128)S(1)} %get-tuple-element.89.c1_ref, f32[8,128]{1,0:T(8,128)S(1)} %get-tuple-element.90.c2_ref, f32[8,272,128]{2,1,0:T(8,128)S(1)} %get-tuple-element.70.a_ref, ...), custom_call_target="tpu_custom_call" | custom-call | flops 1000000 | bytes 1000000 | tf_op jit(solution)/shard_map/next/pallas_call | solution.py:33
  82.4 13.7 %all_to_all.35 = f32[64,1,128]{2,1,0:T(1,128)S(1)} all-to-all(f32[64,1,128]{2,1,0:T(1,128)S(1)} %bitcast.18), channel_id=1, replica_groups=mesh['radius'=16,'polar'=4,'group'=4] {'radius','polar'}, dimensions={0} | all-to-all | bytes 65536 | tf_op jit(solution)/shard_map/all_to_all | solution.py:560
  96.0 0.5 last_update.1
  96.5 1.5 %collective-permute-start.12 = (f32[48,256]{1,0:T(8,128)S(1)}, f32[48,256]{1,0:T(8,128)S(1)}, u32[]{:S(2)}, u32[]{:S(2)}) collective-permute-start(f32[48,256]{1,0:T(8,128)S(1)} %get-tuple-element.103.rest_0_), channel_id=1, source_target_pairs={{0,3},{1,2},{2,1},{3,0},{4,7},{5,6},{6,5},{7,4},{8,11},{9,10},{10,... | collective-permute-start | bytes 147464 | tf_op jit(solution)/shard_map/ppermute | solution.py:488
  98.0 2.1 %collective-permute-start.11 = (f32[48,256]{1,0:T(8,128)S(1)}, f32[48,256]{1,0:T(8,128)S(1)}, u32[]{:S(2)}, u32[]{:S(2)}) collective-permute-start(f32[48,256]{1,0:T(8,128)S(1)} %get-tuple-element.103.rest_0_), channel_id=1, source_target_pairs={{0,2},{1,3},{2,0},{3,1},{4,6},{5,7},{6,4},{7,5},{8,10},{9,11},{10,... | collective-permute-start | bytes 147464 | tf_op jit(solution)/shard_map/ppermute | solution.py:488
  100.2 0.5 collective-permute-start.10
  100.7 1.3 %energy.1 = (f32[16,48,256]{2,1,0:T(8,128)}, f32[48,256]{1,0:T(8,128)S(1)}, f32[48,256]{1,0:T(8,128)S(1)}) custom-call(f32[8,272,128]{2,1,0:T(8,128)S(1)} %get-tuple-element.99.e_ref, f32[272,128]{1,0:T(8,128)S(1)} %get-tuple-element.83.fixed, f32[272,128]{1,0:T(8,128)S(1)} %get-tuple-element.92.cap_in.capacity), custom_call_target="tpu_custom_call" | custom-call | flops 1000000 | bytes 1000000 | tf_op jit(solution)/shard_map/energy/pallas_call | solution.py:33
  102.0 0.0 collective-permute-done.12.rest_3_
  102.0 1.7 %collective-permute-done.11.rest_2_ = f32[48,256]{1,0:T(8,128)S(1)} collective-permute-done((f32[48,256]{1,0:T(8,128)S(1)}, f32[48,256]{1,0:T(8,128)S(1)}, u32[]{:S(2)}, u32[]{:S(2)}) %collective-permute-start.11) | collective-permute-done | bytes 49184 | tf_op jit(solution)/shard_map/ppermute | solution.py:488
  103.6 0.6 collective-permute-done.10.rest_1_
  104.2 0.6 material.5
  (5 shorter events, 0.0 us)
Async XLA Ops:
  0.6 6.7 %copy-start.3 = (f32[48,256]{1,0:T(8,128)S(1)}, f32[48,256]{1,0:T(8,128)}, u32[]{:S(2)}) copy-start(f32[48,256]{1,0:T(8,128)} %material.4) | copy-start | bytes 147460
  0.6 6.7 %copy-start = (f32[16,48,256]{2,1,0:T(8,128)S(1)}, f32[16,48,256]{2,1,0:T(8,128)}, u32[]{:S(2)}) copy-start(f32[16,48,256]{2,1,0:T(8,128)} %old.3) | copy-start | bytes 2359300
  0.7 6.6 %copy-start.1 = (bf16[16,48,256]{2,1,0:T(8,128)(2,1)S(1)}, bf16[16,48,256]{2,1,0:T(8,128)(2,1)}, u32[]{:S(2)}) copy-start(bf16[16,48,256]{2,1,0:T(8,128)(2,1)} %opacity.3) | copy-start | bytes 1179652
  0.7 6.6 %copy-start.2 = (f32[48,256]{1,0:T(8,128)S(1)}, f32[48,256]{1,0:T(8,128)}, u32[]{:S(2)}) copy-start(f32[48,256]{1,0:T(8,128)} %density.3) | copy-start | bytes 147460
  2.0 8.2 %copy-start.4 = (f32[16]{0:T(128)S(1)}, f32[16]{0:T(128)}, u32[]{:S(2)}) copy-start(f32[16]{0:T(128)} %weights.11) | copy-start | bytes 196
  2.1 4.0 %collective-permute-start = (f32[35,8,256]{2,1,0:T(8,128)S(1)}, f32[35,8,256]{2,1,0:T(8,128)S(1)}, u32[]{:S(2)}, u32[]{:S(2)}) collective-permute-start(f32[35,8,256]{2,1,0:T(8,128)S(1)} %get-tuple-element.54), channel_id=1, source_target_pairs={{16,32},{48,64},{80,96},{112,128},{144,160},{176,192},{208,224},{3... | collective-permute-start | bytes 860168 | tf_op jit(solution)/shard_map/ppermute | solution.py:497
  2.7 4.5 %collective-permute-start.1 = (f32[35,8,256]{2,1,0:T(8,128)S(1)}, f32[35,8,256]{2,1,0:T(8,128)S(1)}, u32[]{:S(2)}, u32[]{:S(2)}) collective-permute-start(f32[35,8,256]{2,1,0:T(8,128)S(1)} %get-tuple-element.55), channel_id=1, source_target_pairs={{0,16},{16,0},{32,48},{48,32},{64,80},{80,64},{96,112},{112,96},{1... | collective-permute-start | bytes 860168 | tf_op jit(solution)/shard_map/ppermute | solution.py:492
  8.0 7.2 %collective-permute-start.2 = (f32[18,8,128]{2,1,0:T(8,128)S(1)}, f32[18,8,128]{2,1,0:T(8,128)S(1)}, u32[]{:S(2)}, u32[]{:S(2)}) collective-permute-start(f32[18,8,128]{2,1,0:T(8,128)S(1)} %get-tuple-element.56), channel_id=1, source_target_pairs={{0,4},{4,0},{8,12},{12,8},{1,5},{5,1},{9,13},{13,9},{2,6},{6,2},{1... | collective-permute-start | bytes 221192 | tf_op jit(solution)/shard_map/ppermute | solution.py:492
  9.6 5.6 %collective-permute-start.3 = (f32[18,8,128]{2,1,0:T(8,128)S(1)}, f32[18,8,128]{2,1,0:T(8,128)S(1)}, u32[]{:S(2)}, u32[]{:S(2)}) collective-permute-start(f32[18,8,128]{2,1,0:T(8,128)S(1)} %get-tuple-element.57), channel_id=1, source_target_pairs={{4,8},{8,4},{5,9},{9,5},{6,10},{10,6},{7,11},{11,7},{20,24},{24,20... | collective-permute-start | bytes 221192 | tf_op jit(solution)/shard_map/ppermute | solution.py:497
  42.9 5.1 %copy-start.5 = (f32[48]{0:T(128)S(1)}, f32[48]{0:T(128)}, u32[]{:S(2)}) copy-start(f32[48]{0:T(128)} %flux.1) | copy-start | bytes 580
  43.8 6.8 %collective-permute-start.6 = (f32[2,136,128]{2,1,0:T(8,128)S(1)}, f32[2,136,128]{2,1,0:T(8,128)S(1)}, u32[]{:S(2)}, u32[]{:S(2)}) collective-permute-start(f32[2,136,128]{2,1,0:T(8,128)S(1)} %get-tuple-element.84.rest_0_), channel_id=1, source_target_pairs={{0,3},{1,2},{2,1},{3,0},{4,7},{5,6},{6,5},{7,4},{8,11},{9,10},{10,... | collective-permute-start | bytes 417800 | tf_op jit(solution)/shard_map/ppermute | solution.py:488
  45.5 7.9 %collective-permute-start.5 = (f32[2,136,128]{2,1,0:T(8,128)S(1)}, f32[2,136,128]{2,1,0:T(8,128)S(1)}, u32[]{:S(2)}, u32[]{:S(2)}) collective-permute-start(f32[2,136,128]{2,1,0:T(8,128)S(1)} %get-tuple-element.84.rest_0_), channel_id=1, source_target_pairs={{0,2},{1,3},{2,0},{3,1},{4,6},{5,7},{6,4},{7,5},{8,10},{9,11},{10,... | collective-permute-start | bytes 417800 | tf_op jit(solution)/shard_map/ppermute | solution.py:488
  46.4 7.4 %collective-permute-start.4 = (f32[2,136,128]{2,1,0:T(8,128)S(1)}, f32[2,136,128]{2,1,0:T(8,128)S(1)}, u32[]{:S(2)}, u32[]{:S(2)}) collective-permute-start(f32[2,136,128]{2,1,0:T(8,128)S(1)} %get-tuple-element.84.rest_0_), channel_id=1, source_target_pairs={{0,1},{1,0},{2,3},{3,2},{4,5},{5,4},{6,7},{7,6},{8,9},{9,8},{10,11... | collective-permute-start | bytes 417800 | tf_op jit(solution)/shard_map/ppermute | solution.py:488
  71.4 4.4 %collective-permute-start.9 = (f32[1,136,128]{2,1,0:T(8,128)S(1)}, f32[1,136,128]{2,1,0:T(8,128)S(1)}, u32[]{:S(2)}, u32[]{:S(2)}) collective-permute-start(f32[1,136,128]{2,1,0:T(8,128)S(1)} %get-tuple-element.94.rest_0_), channel_id=1, source_target_pairs={{0,3},{1,2},{2,1},{3,0},{4,7},{5,6},{6,5},{7,4},{8,11},{9,10},{10,... | collective-permute-start | bytes 208904 | tf_op jit(solution)/shard_map/ppermute | solution.py:488
  73.1 5.9 %collective-permute-start.8 = (f32[1,136,128]{2,1,0:T(8,128)S(1)}, f32[1,136,128]{2,1,0:T(8,128)S(1)}, u32[]{:S(2)}, u32[]{:S(2)}) collective-permute-start(f32[1,136,128]{2,1,0:T(8,128)S(1)} %get-tuple-element.94.rest_0_), channel_id=1, source_target_pairs={{0,2},{1,3},{2,0},{3,1},{4,6},{5,7},{6,4},{7,5},{8,10},{9,11},{10,... | collective-permute-start | bytes 208904 | tf_op jit(solution)/shard_map/ppermute | solution.py:488
  74.9 4.3 %collective-permute-start.7 = (f32[1,136,128]{2,1,0:T(8,128)S(1)}, f32[1,136,128]{2,1,0:T(8,128)S(1)}, u32[]{:S(2)}, u32[]{:S(2)}) collective-permute-start(f32[1,136,128]{2,1,0:T(8,128)S(1)} %get-tuple-element.94.rest_0_), channel_id=1, source_target_pairs={{0,1},{1,0},{2,3},{3,2},{4,5},{5,4},{6,7},{7,6},{8,9},{9,8},{10,11... | collective-permute-start | bytes 208904 | tf_op jit(solution)/shard_map/ppermute | solution.py:488
  96.5 5.5 %collective-permute-start.12 = (f32[48,256]{1,0:T(8,128)S(1)}, f32[48,256]{1,0:T(8,128)S(1)}, u32[]{:S(2)}, u32[]{:S(2)}) collective-permute-start(f32[48,256]{1,0:T(8,128)S(1)} %get-tuple-element.103.rest_0_), channel_id=1, source_target_pairs={{0,3},{1,2},{2,1},{3,0},{4,7},{5,6},{6,5},{7,4},{8,11},{9,10},{10,... | collective-permute-start | bytes 147464 | tf_op jit(solution)/shard_map/ppermute | solution.py:488
  98.0 5.6 %collective-permute-start.11 = (f32[48,256]{1,0:T(8,128)S(1)}, f32[48,256]{1,0:T(8,128)S(1)}, u32[]{:S(2)}, u32[]{:S(2)}) collective-permute-start(f32[48,256]{1,0:T(8,128)S(1)} %get-tuple-element.103.rest_0_), channel_id=1, source_target_pairs={{0,2},{1,3},{2,0},{3,1},{4,6},{5,7},{6,4},{7,5},{8,10},{9,11},{10,... | collective-permute-start | bytes 147464 | tf_op jit(solution)/shard_map/ppermute | solution.py:488
  100.2 4.1 %collective-permute-start.10 = (f32[48,256]{1,0:T(8,128)S(1)}, f32[48,256]{1,0:T(8,128)S(1)}, u32[]{:S(2)}, u32[]{:S(2)}) collective-permute-start(f32[48,256]{1,0:T(8,128)S(1)} %get-tuple-element.103.rest_0_), channel_id=1, source_target_pairs={{0,1},{1,0},{2,3},{3,2},{4,5},{5,4},{6,7},{7,6},{8,9},{9,8},{10,11... | collective-permute-start | bytes 147464 | tf_op jit(solution)/shard_map/ppermute | solution.py:488

commit v11 on v10

--- a/solution.py
+++ b/solution.py
@@ -60,11 +60,16 @@
     return even, jnp.where(even, inner, outer), jnp.where(even, outer, inner)
 
 
-def pack_rows_kernel(groups, rows, flux_in, opacity, old, density, material, first, second, *scratch):
+def pack_rows_kernel(
+    groups, rows, weights_in, flux_in, opacity, old, density, material, first, second, weight_lanes, *scratch
+):
     even, lo_first, lo_second = partner("radius", rows - HALO, 0)
-    flux, sems = scratch[-2:]
+    weights, flux, sems = scratch[-3:]
     sides = ((first, lo_first, even), (second, lo_second, jnp.logical_not(even)))
-    copies = [pltpu.make_async_copy(flux_in, flux, sems.at[8])]
+    copies = [
+        pltpu.make_async_copy(flux_in, flux, sems.at[8]),
+        pltpu.make_async_copy(weights_in, weights, sems.at[9]),
+    ]
     for side, (_, lo, at_end) in enumerate(sides):
         op_buf, old_buf, dens_buf, mat_buf = scratch[4 * side : 4 * side + 4]
         lo = pl.multiple_of(lo, HALO)
@@ -81,6 +86,9 @@
         c.start()
     for c in copies:
         c.wait()
+    half = lane_of() < HALF
+    for p in range(groups // 2):
+        weight_lanes[p : p + 1, :] = jnp.where(half, weights[2 * p], weights[2 * p + 1])
     lane = lane_of(HALO) % HALF
     for side, (out, lo, at_end) in enumerate(sides):
         op_buf, old_buf, dens_buf, mat_buf = scratch[4 * side : 4 * side + 4]
@@ -229,7 +237,7 @@
 
 
 def weight_of(weights, p):
-    return jnp.where(lane_of(HALO) < HALF, weights[2 * p], weights[2 * p + 1])[:1]
+    return weights[pl.ds(p, 1), :]
 
 
 def fold(s):
@@ -516,15 +524,17 @@
         vmem((HALO, cols)),
         vmem((HALO, cols)),
     ]
-    first, second = call(
+    first, second, weights = call(
         functools.partial(pack_rows_kernel, groups, rows),
-        [(planes, HALO, cols)] * 2,
+        [(planes, HALO, cols)] * 2 + [(pairs, LANES)],
         tuple(
             pltpu.with_memory_space_constraint(v, pltpu.HBM)
-            for v in (stellar_flux, opacity, radiation_old, density, material_old)
+            for v in (weights, stellar_flux, opacity, radiation_old, density, material_old)
         ),
-        [hspec()] * 5,
-        scratch=strips * 2 + [pltpu.SMEM((rows,), jnp.float32), pltpu.SemaphoreType.DMA((9,))],
+        [hspec()] * 6,
+        scratch=strips * 2
+        + [pltpu.SMEM((size,), jnp.float32) for size in (groups, rows)]
+        + [pltpu.SemaphoreType.DMA((10,))],
         name="pack_rows",
         limit=20 * 1024 * 1024,
     )
@@ -542,7 +552,7 @@
         functools.partial(inner_kernel, groups, cols),
         [big] * 6 + [(4 * pairs, LANES)],
         (weights, a, e, dens, mat),
-        [sspec()] + [vspec()] * 4,
+        [vspec()] * 5,
         scratch=[vmem(flat)],
         name="inner",
     )
@@ -550,7 +560,7 @@
         functools.partial(frame_kernel, groups, rows, cols),
         [big] * 8 + [flat, flat, line],
         (weights, first, second, mom, a, e, fr, fp, r, q, t, b, dens, mat),
-        [sspec()] + [vspec()] * 13,
+        [vspec()] * 14,
         scratch=[vmem(flat), vmem((4 * pairs, LANES))],
         name="frame",
         aliases={4 + k: k for k in range(10)},
@@ -588,7 +598,7 @@
             functools.partial(update_kernel, pairs, first),
             [big, (2 if first else 1, tall // 2, LANES), (pairs, LANES), (pairs, LANES)],
             (weights, gathered, a, e, r, q),
-            [sspec()] + [vspec()] * 5,
+            [vspec()] * 6,
             scratch=[vmem(flat)] * 2,
             name="update",
         )
@@ -605,7 +615,7 @@
             functools.partial(next_kernel, groups, rows, count, turn, last),
             [big, big, line] + ([] if last else [big, flat]) + ([flat] if first else []),
             (weights, c1, c2, a, b, fr, fp, r, q, t, fixed, capacity, mat, *sums),
-            [sspec()] + [vspec()] * (12 + count),
+            [vspec()] * (13 + count),
             scratch=[vmem(flat), vmem((4 * pairs, LANES))],
             name="next",
         )

time: 105 us -> 102 us (0.971)
  Pallas kernels: 20.6 us -> 17.4 us
    pallas_call x12, Pallas kernels: 20.6 us -> 17.4 us  [call(): pl.pallas_call(kernel, out_shape=[jax.ShapeDtypeStruct(s, jnp.float32) fo...]
  transfers between devices with their start and end apart: 13 -> 13, of which waited for: 9 -> 9; matrix products, arithmetic and copies ran while one was open for 0% -> 0% of each run, Pallas kernels for 8% -> 7%
where the time goes in v11:
time: 102 us
  blocking collectives  53.4 us (52%)
  starting transfers between devices  18.8 us (18%)
  Pallas kernels  17.4 us (17%)
  waiting for transfers between devices  11.3 us (11%)
    all_to_all x3, blocking collectives, per_device(): gathered = lax.all_to_all(out, ('radius', 'polar'), 0, 0, tiled=True)  53.4 us
    pallas_call x12, Pallas kernels, call(): pl.pallas_call(kernel, out_shape=[jax.ShapeDtypeStruct(s, jnp.float32) fo...  17.4 us
    ppermute x9, starting transfers between devices, spread(): lax.ppermute(part, axis, [(i, i ^ s) for i in range(count)])  12.5 us
    ppermute x9, waiting for transfers between devices, spread(): lax.ppermute(part, axis, [(i, i ^ s) for i in range(count)])  10.1 us
    ppermute x2, starting transfers between devices, pair_up(): lax.ppermute(first, axis, [(i, i ^ 1) for i in range(lax.axis_size(axis))])  4.92 us
  transfers between devices with their start and end apart: 13, of which 9 were waited for; matrix products, arithmetic and copies ran while one was open for 0% of the time, Pallas kernels for 7%

profile of v11, /device:TPU:8, one launch (start us, length us, event | category | flops | bytes accessed | tf_op | source)
XLA Modules:
  0.0 101.7 jit_solution(12994063376359316000)
XLA Ops:
  0.6 0.0 copy-start.3
  0.6 0.0 copy-start
  0.7 0.0 copy-start.1
  0.7 0.0 copy-start.2
  0.7 1.4 %pack_rows.1 = (f32[35,8,256]{2,1,0:T(8,128)S(1)}, f32[35,8,256]{2,1,0:T(8,128)S(1)}, f32[8,128]{1,0:T(8,128)S(1)}) custom-call(f32[16]{0:T(128)} %weights_in.1, f32[48]{0:T(128)} %flux.1, bf16[16,48,256]{2,1,0:T(8,128)(2,1)} %opacity.3, f32[16,48,256]{2,1,0:T(8,128)} %old.3, f32[48,256]{1,0:T(8,128)} %density.3, f32[48,256]{1,0:T(8,128)} %material.4), custom_call_target="tpu_custom_call" | custom-call | flops 1000000 | bytes 1000000 | tf_op jit(solution)/shard_map/pack_rows/pallas_call | solution.py:33
  2.1 0.7 collective-permute-start
  2.7 3.3 %collective-permute-start.1 = (f32[35,8,256]{2,1,0:T(8,128)S(1)}, f32[35,8,256]{2,1,0:T(8,128)S(1)}, u32[]{:S(2)}, u32[]{:S(2)}) collective-permute-start(f32[35,8,256]{2,1,0:T(8,128)S(1)} %get-tuple-element.57), channel_id=1, source_target_pairs={{0,16},{16,0},{32,48},{48,32},{64,80},{80,64},{96,112},{112,96},{1... | collective-permute-start | bytes 860168 | tf_op jit(solution)/shard_map/ppermute | solution.py:500
  6.1 0.0 collective-permute-done.got_second
  6.1 1.2 %collective-permute-done.1.got_first = f32[35,8,256]{2,1,0:T(8,128)S(1)} collective-permute-done((f32[35,8,256]{2,1,0:T(8,128)S(1)}, f32[35,8,256]{2,1,0:T(8,128)S(1)}, u32[]{:S(2)}, u32[]{:S(2)}) %collective-permute-start.1) | collective-permute-done | bytes 286752 | tf_op jit(solution)/shard_map/ppermute | solution.py:500
  7.3 0.0 copy-done.3
  7.3 0.0 copy-done
  7.3 0.0 copy-done.1
  7.3 0.7 turn.1
  8.0 1.6 %collective-permute-start.2 = (f32[18,8,128]{2,1,0:T(8,128)S(1)}, f32[18,8,128]{2,1,0:T(8,128)S(1)}, u32[]{:S(2)}, u32[]{:S(2)}) collective-permute-start(f32[18,8,128]{2,1,0:T(8,128)S(1)} %get-tuple-element.58), channel_id=1, source_target_pairs={{0,4},{4,0},{8,12},{12,8},{1,5},{5,1},{9,13},{13,9},{2,6},{6,2},{1... | collective-permute-start | bytes 221192 | tf_op jit(solution)/shard_map/ppermute | solution.py:500
  9.6 0.7 collective-permute-start.3
  10.2 4.4 %inner.1 = (f32[8,272,128]{2,1,0:T(8,128)S(1)}, f32[8,272,128]{2,1,0:T(8,128)S(1)}, f32[8,272,128]{2,1,0:T(8,128)S(1)}, f32[8,272,128]{2,1,0:T(8,128)S(1)}, f32[...) custom-call(f32[8,128]{1,0:T(8,128)S(1)} %get-tuple-element.55.weights, ...), custom_call_target="tpu_custom_call" | custom-call | flops 1000000 | bytes 1000000 | tf_op jit(solution)/shard_map/inner/pallas_call | solution.py:33
  14.6 0.0 collective-permute-done.2.got_first
  14.6 0.0 collective-permute-done.3.got_second
  14.7 0.8 frame.1
  15.5 26.3 %all_to_all.33 = f32[64,1,128]{2,1,0:T(1,128)S(1)} all-to-all(f32[64,1,128]{2,1,0:T(1,128)S(1)} %bitcast.16), channel_id=1, replica_groups=mesh['radius'=16,'polar'=4,'group'=4] {'radius','polar'}, dimensions={0} | all-to-all | bytes 65536 | tf_op jit(solution)/shard_map/all_to_all | solution.py:570
  41.8 0.4 update.2
  42.3 1.6 %collective-permute-start.6 = (f32[2,136,128]{2,1,0:T(8,128)S(1)}, f32[2,136,128]{2,1,0:T(8,128)S(1)}, u32[]{:S(2)}, u32[]{:S(2)}) collective-permute-start(f32[2,136,128]{2,1,0:T(8,128)S(1)} %get-tuple-element.86.rest_0_), channel_id=1, source_target_pairs={{0,3},{1,2},{2,1},{3,0},{4,7},{5,6},{6,5},{7,4},{8,11},{9,10},{10,... | collective-permute-start | bytes 417800 | tf_op jit(solution)/shard_map/ppermute | solution.py:496
  43.9 0.9 collective-permute-start.5
  44.8 1.6 %collective-permute-start.4 = (f32[2,136,128]{2,1,0:T(8,128)S(1)}, f32[2,136,128]{2,1,0:T(8,128)S(1)}, u32[]{:S(2)}, u32[]{:S(2)}) collective-permute-start(f32[2,136,128]{2,1,0:T(8,128)S(1)} %get-tuple-element.86.rest_0_), channel_id=1, source_target_pairs={{0,1},{1,0},{2,3},{3,2},{4,5},{5,4},{6,7},{7,6},{8,9},{9,8},{10,11... | collective-permute-start | bytes 417800 | tf_op jit(solution)/shard_map/ppermute | solution.py:496
  46.4 1.7 %heating.1 = (f32[48,256]{1,0:T(8,128)}, f32[272,128]{1,0:T(8,128)S(1)}) custom-call(f32[48]{0:T(128)S(1)} %copy-done.4, f32[64,128]{1,0:T(8,128)S(1)} %bitcast.13, f32[272,128]{1,0:T(8,128)S(1)} %get-tuple-element.82.dens_ref.cap_in, f32[272,128]{1,0:T(8,128)S(1)} %get-tuple-element.83.mat_ref, f32[8,128]{1,0:T(8,128)S(1)} %get-tuple-element.84.flux_ref), custom_call_target="tpu_custom_call" | custom-call | flops 1000000 | bytes 1000000 | tf_op jit(solution)/shard_map/heating/pallas_call | solution.py:33
  48.2 0.9 collective-permute-done.6.rest_3_
  49.0 2.8 %collective-permute-done.5.rest_2_ = f32[2,136,128]{2,1,0:T(8,128)S(1)} collective-permute-done((f32[2,136,128]{2,1,0:T(8,128)S(1)}, f32[2,136,128]{2,1,0:T(8,128)S(1)}, u32[]{:S(2)}, u32[]{:S(2)}) %collective-permute-start.5) | collective-permute-done | bytes 139296 | tf_op jit(solution)/shard_map/ppermute | solution.py:496
  51.8 0.5 collective-permute-done.4.rest_1_
  52.3 2.5 %next.2 = (f32[8,272,128]{2,1,0:T(8,128)S(1)}, f32[8,272,128]{2,1,0:T(8,128)S(1)}, f32[64,128]{1,0:T(8,128)S(1)}, f32[8,272,128]{2,1,0:T(8,128)S(1)}, f32[272,128]{1,0:T(8,128)S(1)}, /*index=5*/f32[272,128]{1,0:T(8,128)S(1)}) custom-call(f32[8,128]{1,0:T(8,128)S(1)} %get-tuple-element.55.weights, f32[8,128]{1,0:T(8,128)S(1)} %get-tuple-element.76.c1_ref, ...), custom_call_target="tpu_custom_call" | custom-call | flops 1000000 | bytes 1000000 | tf_op jit(solution)/shard_map/next/pallas_call | solution.py:33
  54.8 13.5 %all_to_all.34 = f32[64,1,128]{2,1,0:T(1,128)S(1)} all-to-all(f32[64,1,128]{2,1,0:T(1,128)S(1)} %bitcast.17), channel_id=1, replica_groups=mesh['radius'=16,'polar'=4,'group'=4] {'radius','polar'}, dimensions={0} | all-to-all | bytes 65536 | tf_op jit(solution)/shard_map/all_to_all | solution.py:570
  68.3 0.4 update.3
  68.7 1.6 %collective-permute-start.9 = (f32[1,136,128]{2,1,0:T(8,128)S(1)}, f32[1,136,128]{2,1,0:T(8,128)S(1)}, u32[]{:S(2)}, u32[]{:S(2)}) collective-permute-start(f32[1,136,128]{2,1,0:T(8,128)S(1)} %get-tuple-element.96.rest_0_), channel_id=1, source_target_pairs={{0,3},{1,2},{2,1},{3,0},{4,7},{5,6},{6,5},{7,4},{8,11},{9,10},{10,... | collective-permute-start | bytes 208904 | tf_op jit(solution)/shard_map/ppermute | solution.py:496
  70.3 1.9 %collective-permute-start.8 = (f32[1,136,128]{2,1,0:T(8,128)S(1)}, f32[1,136,128]{2,1,0:T(8,128)S(1)}, u32[]{:S(2)}, u32[]{:S(2)}) collective-permute-start(f32[1,136,128]{2,1,0:T(8,128)S(1)} %get-tuple-element.96.rest_0_), channel_id=1, source_target_pairs={{0,2},{1,3},{2,0},{3,1},{4,6},{5,7},{6,4},{7,5},{8,10},{9,11},{10,... | collective-permute-start | bytes 208904 | tf_op jit(solution)/shard_map/ppermute | solution.py:496
  72.2 0.7 collective-permute-start.7
  72.8 0.2 collective-permute-done.9.rest_3_
  73.0 3.1 %collective-permute-done.8.rest_2_ = f32[1,136,128]{2,1,0:T(8,128)S(1)} collective-permute-done((f32[1,136,128]{2,1,0:T(8,128)S(1)}, f32[1,136,128]{2,1,0:T(8,128)S(1)}, u32[]{:S(2)}, u32[]{:S(2)}) %collective-permute-start.8) | collective-permute-done | bytes 69664 | tf_op jit(solution)/shard_map/ppermute | solution.py:496
  76.2 0.3 collective-permute-done.7.rest_1_
  76.5 2.6 %next.3 = (f32[8,272,128]{2,1,0:T(8,128)S(1)}, f32[8,272,128]{2,1,0:T(8,128)S(1)}, f32[64,128]{1,0:T(8,128)S(1)}) custom-call(f32[8,128]{1,0:T(8,128)S(1)} %get-tuple-element.55.weights, f32[8,128]{1,0:T(8,128)S(1)} %get-tuple-element.91.c1_ref, f32[8,128]{1,0:T(8,128)S(1)} %get-tuple-element.92.c2_ref, f32[8,272,128]{2,1,0:T(8,128)S(1)} %get-tuple-element.72.a_ref, ...), custom_call_target="tpu_custom_call" | custom-call | flops 1000000 | bytes 1000000 | tf_op jit(solution)/shard_map/next/pallas_call | solution.py:33
  79.1 13.7 %all_to_all.35 = f32[64,1,128]{2,1,0:T(1,128)S(1)} all-to-all(f32[64,1,128]{2,1,0:T(1,128)S(1)} %bitcast.18), channel_id=1, replica_groups=mesh['radius'=16,'polar'=4,'group'=4] {'radius','polar'}, dimensions={0} | all-to-all | bytes 65536 | tf_op jit(solution)/shard_map/all_to_all | solution.py:570
  92.8 0.5 last_update.1
  93.3 1.5 %collective-permute-start.12 = (f32[48,256]{1,0:T(8,128)S(1)}, f32[48,256]{1,0:T(8,128)S(1)}, u32[]{:S(2)}, u32[]{:S(2)}) collective-permute-start(f32[48,256]{1,0:T(8,128)S(1)} %get-tuple-element.105.rest_0_), channel_id=1, source_target_pairs={{0,3},{1,2},{2,1},{3,0},{4,7},{5,6},{6,5},{7,4},{8,11},{9,10},{10,... | collective-permute-start | bytes 147464 | tf_op jit(solution)/shard_map/ppermute | solution.py:496
  94.8 2.1 %collective-permute-start.11 = (f32[48,256]{1,0:T(8,128)S(1)}, f32[48,256]{1,0:T(8,128)S(1)}, u32[]{:S(2)}, u32[]{:S(2)}) collective-permute-start(f32[48,256]{1,0:T(8,128)S(1)} %get-tuple-element.105.rest_0_), channel_id=1, source_target_pairs={{0,2},{1,3},{2,0},{3,1},{4,6},{5,7},{6,4},{7,5},{8,10},{9,11},{10,... | collective-permute-start | bytes 147464 | tf_op jit(solution)/shard_map/ppermute | solution.py:496
  96.9 0.5 collective-permute-start.10
  97.5 1.3 %energy.1 = (f32[16,48,256]{2,1,0:T(8,128)}, f32[48,256]{1,0:T(8,128)S(1)}, f32[48,256]{1,0:T(8,128)S(1)}) custom-call(f32[8,272,128]{2,1,0:T(8,128)S(1)} %get-tuple-element.101.e_ref, f32[272,128]{1,0:T(8,128)S(1)} %get-tuple-element.85.fixed, f32[272,128]{1,0:T(8,128)S(1)} %get-tuple-element.94.cap_in.capacity), custom_call_target="tpu_custom_call" | custom-call | flops 1000000 | bytes 1000000 | tf_op jit(solution)/shard_map/energy/pallas_call | solution.py:33
  98.8 0.0 collective-permute-done.12.rest_3_
  98.8 1.7 %collective-permute-done.11.rest_2_ = f32[48,256]{1,0:T(8,128)S(1)} collective-permute-done((f32[48,256]{1,0:T(8,128)S(1)}, f32[48,256]{1,0:T(8,128)S(1)}, u32[]{:S(2)}, u32[]{:S(2)}) %collective-permute-start.11) | collective-permute-done | bytes 49184 | tf_op jit(solution)/shard_map/ppermute | solution.py:496
  100.4 0.6 collective-permute-done.10.rest_1_
  101.0 0.6 material.5
  (3 shorter events, 0.0 us)
Async XLA Ops:
  0.6 6.7 %copy-start.3 = (f32[48,256]{1,0:T(8,128)S(1)}, f32[48,256]{1,0:T(8,128)}, u32[]{:S(2)}) copy-start(f32[48,256]{1,0:T(8,128)} %material.4) | copy-start | bytes 147460
  0.6 6.7 %copy-start = (f32[16,48,256]{2,1,0:T(8,128)S(1)}, f32[16,48,256]{2,1,0:T(8,128)}, u32[]{:S(2)}) copy-start(f32[16,48,256]{2,1,0:T(8,128)} %old.3) | copy-start | bytes 2359300
  0.7 6.6 %copy-start.1 = (bf16[16,48,256]{2,1,0:T(8,128)(2,1)S(1)}, bf16[16,48,256]{2,1,0:T(8,128)(2,1)}, u32[]{:S(2)}) copy-start(bf16[16,48,256]{2,1,0:T(8,128)(2,1)} %opacity.3) | copy-start | bytes 1179652
  0.7 6.6 %copy-start.2 = (f32[48,256]{1,0:T(8,128)S(1)}, f32[48,256]{1,0:T(8,128)}, u32[]{:S(2)}) copy-start(f32[48,256]{1,0:T(8,128)} %density.3) | copy-start | bytes 147460
  2.1 4.0 %collective-permute-start = (f32[35,8,256]{2,1,0:T(8,128)S(1)}, f32[35,8,256]{2,1,0:T(8,128)S(1)}, u32[]{:S(2)}, u32[]{:S(2)}) collective-permute-start(f32[35,8,256]{2,1,0:T(8,128)S(1)} %get-tuple-element.56), channel_id=1, source_target_pairs={{16,32},{48,64},{80,96},{112,128},{144,160},{176,192},{208,224},{3... | collective-permute-start | bytes 860168 | tf_op jit(solution)/shard_map/ppermute | solution.py:505
  2.7 4.5 %collective-permute-start.1 = (f32[35,8,256]{2,1,0:T(8,128)S(1)}, f32[35,8,256]{2,1,0:T(8,128)S(1)}, u32[]{:S(2)}, u32[]{:S(2)}) collective-permute-start(f32[35,8,256]{2,1,0:T(8,128)S(1)} %get-tuple-element.57), channel_id=1, source_target_pairs={{0,16},{16,0},{32,48},{48,32},{64,80},{80,64},{96,112},{112,96},{1... | collective-permute-start | bytes 860168 | tf_op jit(solution)/shard_map/ppermute | solution.py:500
  8.0 6.6 %collective-permute-start.2 = (f32[18,8,128]{2,1,0:T(8,128)S(1)}, f32[18,8,128]{2,1,0:T(8,128)S(1)}, u32[]{:S(2)}, u32[]{:S(2)}) collective-permute-start(f32[18,8,128]{2,1,0:T(8,128)S(1)} %get-tuple-element.58), channel_id=1, source_target_pairs={{0,4},{4,0},{8,12},{12,8},{1,5},{5,1},{9,13},{13,9},{2,6},{6,2},{1... | collective-permute-start | bytes 221192 | tf_op jit(solution)/shard_map/ppermute | solution.py:500
  9.6 5.1 %collective-permute-start.3 = (f32[18,8,128]{2,1,0:T(8,128)S(1)}, f32[18,8,128]{2,1,0:T(8,128)S(1)}, u32[]{:S(2)}, u32[]{:S(2)}) collective-permute-start(f32[18,8,128]{2,1,0:T(8,128)S(1)} %get-tuple-element.59), channel_id=1, source_target_pairs={{4,8},{8,4},{5,9},{9,5},{6,10},{10,6},{7,11},{11,7},{20,24},{24,20... | collective-permute-start | bytes 221192 | tf_op jit(solution)/shard_map/ppermute | solution.py:505
  41.8 4.6 %copy-start.4 = (f32[48]{0:T(128)S(1)}, f32[48]{0:T(128)}, u32[]{:S(2)}) copy-start(f32[48]{0:T(128)} %flux.1) | copy-start | bytes 580
  42.3 6.8 %collective-permute-start.6 = (f32[2,136,128]{2,1,0:T(8,128)S(1)}, f32[2,136,128]{2,1,0:T(8,128)S(1)}, u32[]{:S(2)}, u32[]{:S(2)}) collective-permute-start(f32[2,136,128]{2,1,0:T(8,128)S(1)} %get-tuple-element.86.rest_0_), channel_id=1, source_target_pairs={{0,3},{1,2},{2,1},{3,0},{4,7},{5,6},{6,5},{7,4},{8,11},{9,10},{10,... | collective-permute-start | bytes 417800 | tf_op jit(solution)/shard_map/ppermute | solution.py:496
  43.9 7.9 %collective-permute-start.5 = (f32[2,136,128]{2,1,0:T(8,128)S(1)}, f32[2,136,128]{2,1,0:T(8,128)S(1)}, u32[]{:S(2)}, u32[]{:S(2)}) collective-permute-start(f32[2,136,128]{2,1,0:T(8,128)S(1)} %get-tuple-element.86.rest_0_), channel_id=1, source_target_pairs={{0,2},{1,3},{2,0},{3,1},{4,6},{5,7},{6,4},{7,5},{8,10},{9,11},{10,... | collective-permute-start | bytes 417800 | tf_op jit(solution)/shard_map/ppermute | solution.py:496
  44.8 7.4 %collective-permute-start.4 = (f32[2,136,128]{2,1,0:T(8,128)S(1)}, f32[2,136,128]{2,1,0:T(8,128)S(1)}, u32[]{:S(2)}, u32[]{:S(2)}) collective-permute-start(f32[2,136,128]{2,1,0:T(8,128)S(1)} %get-tuple-element.86.rest_0_), channel_id=1, source_target_pairs={{0,1},{1,0},{2,3},{3,2},{4,5},{5,4},{6,7},{7,6},{8,9},{9,8},{10,11... | collective-permute-start | bytes 417800 | tf_op jit(solution)/shard_map/ppermute | solution.py:496
  68.7 4.4 %collective-permute-start.9 = (f32[1,136,128]{2,1,0:T(8,128)S(1)}, f32[1,136,128]{2,1,0:T(8,128)S(1)}, u32[]{:S(2)}, u32[]{:S(2)}) collective-permute-start(f32[1,136,128]{2,1,0:T(8,128)S(1)} %get-tuple-element.96.rest_0_), channel_id=1, source_target_pairs={{0,3},{1,2},{2,1},{3,0},{4,7},{5,6},{6,5},{7,4},{8,11},{9,10},{10,... | collective-permute-start | bytes 208904 | tf_op jit(solution)/shard_map/ppermute | solution.py:496
  70.3 5.9 %collective-permute-start.8 = (f32[1,136,128]{2,1,0:T(8,128)S(1)}, f32[1,136,128]{2,1,0:T(8,128)S(1)}, u32[]{:S(2)}, u32[]{:S(2)}) collective-permute-start(f32[1,136,128]{2,1,0:T(8,128)S(1)} %get-tuple-element.96.rest_0_), channel_id=1, source_target_pairs={{0,2},{1,3},{2,0},{3,1},{4,6},{5,7},{6,4},{7,5},{8,10},{9,11},{10,... | collective-permute-start | bytes 208904 | tf_op jit(solution)/shard_map/ppermute | solution.py:496
  72.2 4.3 %collective-permute-start.7 = (f32[1,136,128]{2,1,0:T(8,128)S(1)}, f32[1,136,128]{2,1,0:T(8,128)S(1)}, u32[]{:S(2)}, u32[]{:S(2)}) collective-permute-start(f32[1,136,128]{2,1,0:T(8,128)S(1)} %get-tuple-element.96.rest_0_), channel_id=1, source_target_pairs={{0,1},{1,0},{2,3},{3,2},{4,5},{5,4},{6,7},{7,6},{8,9},{9,8},{10,11... | collective-permute-start | bytes 208904 | tf_op jit(solution)/shard_map/ppermute | solution.py:496
  93.3 5.5 %collective-permute-start.12 = (f32[48,256]{1,0:T(8,128)S(1)}, f32[48,256]{1,0:T(8,128)S(1)}, u32[]{:S(2)}, u32[]{:S(2)}) collective-permute-start(f32[48,256]{1,0:T(8,128)S(1)} %get-tuple-element.105.rest_0_), channel_id=1, source_target_pairs={{0,3},{1,2},{2,1},{3,0},{4,7},{5,6},{6,5},{7,4},{8,11},{9,10},{10,... | collective-permute-start | bytes 147464 | tf_op jit(solution)/shard_map/ppermute | solution.py:496
  94.8 5.6 %collective-permute-start.11 = (f32[48,256]{1,0:T(8,128)S(1)}, f32[48,256]{1,0:T(8,128)S(1)}, u32[]{:S(2)}, u32[]{:S(2)}) collective-permute-start(f32[48,256]{1,0:T(8,128)S(1)} %get-tuple-element.105.rest_0_), channel_id=1, source_target_pairs={{0,2},{1,3},{2,0},{3,1},{4,6},{5,7},{6,4},{7,5},{8,10},{9,11},{10,... | collective-permute-start | bytes 147464 | tf_op jit(solution)/shard_map/ppermute | solution.py:496
  96.9 4.1 %collective-permute-start.10 = (f32[48,256]{1,0:T(8,128)S(1)}, f32[48,256]{1,0:T(8,128)S(1)}, u32[]{:S(2)}, u32[]{:S(2)}) collective-permute-start(f32[48,256]{1,0:T(8,128)S(1)} %get-tuple-element.105.rest_0_), channel_id=1, source_target_pairs={{0,1},{1,0},{2,3},{3,2},{4,5},{5,4},{6,7},{7,6},{8,9},{9,8},{10,11... | collective-permute-start | bytes 147464 | tf_op jit(solution)/shard_map/ppermute | solution.py:496

commit v12 on v11

--- a/solution.py
+++ b/solution.py
@@ -11,7 +11,7 @@
 HALO = 8
 LANES = 128
 HALF = LANES // 2
-STEP = 64
+STEP = 16
 VMEM_LIMIT = 12 * 1024 * 1024
 HIGHEST = lax.Precision.HIGHEST
 OUTSIDE = 1.6e38
@@ -293,7 +293,7 @@
     lax.fori_loop(0, pairs, one, 0, unroll=2)
 
 
-def frame_kernel(groups, rows, cols, weights, got_first, got_second, old_mom, *rest):
+def frame_kernel(groups, rows, cols, weights, got_second, got_first, old_mom, *rest):
     a_ref, e_ref, fr_ref, fp_ref, r_ref, q_ref, t_ref, b_ref, dens_ref, mat_ref = rest[10:20]
     out, inv, mom = rest[20:]
     pairs = groups // 2
@@ -547,7 +547,8 @@
         [vspec()] * 6,
         name="turn",
     )
-    first, second = pair_up(first, "polar"), pair_across(second, "polar")
+    second = pair_across(second, "polar")
+    first = pair_up(first, "polar")
     fr, fp, r, q, t, b, mom = call(
         functools.partial(inner_kernel, groups, cols),
         [big] * 6 + [(4 * pairs, LANES)],
@@ -559,7 +560,7 @@
     a, e, fr, fp, r, q, t, b, dens, mat, out = call(
         functools.partial(frame_kernel, groups, rows, cols),
         [big] * 8 + [flat, flat, line],
-        (weights, first, second, mom, a, e, fr, fp, r, q, t, b, dens, mat),
+        (weights, second, first, mom, a, e, fr, fp, r, q, t, b, dens, mat),
         [vspec()] * 14,
         scratch=[vmem(flat), vmem((4 * pairs, LANES))],
         name="frame",

time: 102 us -> 102 us (level)
  blocking collectives: 53.4 us -> 50.6 us
  starting transfers between devices: 18.8 us -> 21.5 us
    all_to_all x3, blocking collectives: 53.4 us -> 50.6 us  [per_device(): gathered = lax.all_to_all(out, ('radius', 'polar'), 0, 0, tiled=True)]
    ppermute x2, starting transfers between devices: 4.92 us -> 7.66 us  [pair_up(): lax.ppermute(first, axis, [(i, i ^ 1) for i in range(lax.axis_size(axis))])]
where the time goes in v12:
time: 102 us; the launch traced here: 101 us
  blocking collectives  50.6 us (50%)
  starting transfers between devices  21.5 us (21%)
  Pallas kernels  17.2 us (17%)
  waiting for transfers between devices  11.3 us (11%)
    all_to_all x3, blocking collectives, per_device(): gathered = lax.all_to_all(out, ('radius', 'polar'), 0, 0, tiled=True)  50.6 us
    pallas_call x12, Pallas kernels, call(): pl.pallas_call(kernel, out_shape=[jax.ShapeDtypeStruct(s, jnp.float32) fo...  17.2 us
    ppermute x9, starting transfers between devices, spread(): lax.ppermute(part, axis, [(i, i ^ s) for i in range(count)])  12.5 us
    ppermute x9, waiting for transfers between devices, spread(): lax.ppermute(part, axis, [(i, i ^ s) for i in range(count)])  10.1 us
    ppermute x2, starting transfers between devices, pair_up(): lax.ppermute(first, axis, [(i, i ^ 1) for i in range(lax.axis_size(axis))])  7.66 us
  transfers between devices with their start and end apart: 13, of which 9 were waited for; matrix products, arithmetic and copies ran while one was open for 0% of the time, Pallas kernels for 7%

profile of v12, /device:TPU:8, one launch (start us, length us, event | category | flops | bytes accessed | tf_op | source)
XLA Modules:
  0.0 101.3 jit_solution(16031697312203970914)
XLA Ops:
  0.6 0.0 copy-start.3
  0.6 0.0 copy-start
  0.7 0.0 copy-start.1
  0.7 0.0 copy-start.2
  0.7 1.4 %pack_rows.1 = (f32[35,8,256]{2,1,0:T(8,128)S(1)}, f32[35,8,256]{2,1,0:T(8,128)S(1)}, f32[8,128]{1,0:T(8,128)S(1)}) custom-call(f32[16]{0:T(128)} %weights_in.1, f32[48]{0:T(128)} %flux.1, bf16[16,48,256]{2,1,0:T(8,128)(2,1)} %opacity.3, f32[16,48,256]{2,1,0:T(8,128)} %old.3, f32[48,256]{1,0:T(8,128)} %density.3, f32[48,256]{1,0:T(8,128)} %material.4), custom_call_target="tpu_custom_call" | custom-call | flops 1000000 | bytes 1000000 | tf_op jit(solution)/shard_map/pack_rows/pallas_call | solution.py:33
  2.1 0.7 collective-permute-start
  2.7 3.3 %collective-permute-start.1 = (f32[35,8,256]{2,1,0:T(8,128)S(1)}, f32[35,8,256]{2,1,0:T(8,128)S(1)}, u32[]{:S(2)}, u32[]{:S(2)}) collective-permute-start(f32[35,8,256]{2,1,0:T(8,128)S(1)} %get-tuple-element.57), channel_id=1, source_target_pairs={{0,16},{16,0},{32,48},{48,32},{64,80},{80,64},{96,112},{112,96},{1... | collective-permute-start | bytes 860168 | tf_op jit(solution)/shard_map/ppermute | solution.py:500
  6.1 0.0 collective-permute-done.got_second
  6.1 1.2 %collective-permute-done.1.got_first = f32[35,8,256]{2,1,0:T(8,128)S(1)} collective-permute-done((f32[35,8,256]{2,1,0:T(8,128)S(1)}, f32[35,8,256]{2,1,0:T(8,128)S(1)}, u32[]{:S(2)}, u32[]{:S(2)}) %collective-permute-start.1) | collective-permute-done | bytes 286752 | tf_op jit(solution)/shard_map/ppermute | solution.py:500
  7.3 0.0 copy-done.3
  7.3 0.0 copy-done
  7.3 0.0 copy-done.1
  7.3 0.7 turn.1
  8.0 0.7 collective-permute-start.2
  8.7 4.3 %collective-permute-start.3 = (f32[18,8,128]{2,1,0:T(8,128)S(1)}, f32[18,8,128]{2,1,0:T(8,128)S(1)}, u32[]{:S(2)}, u32[]{:S(2)}) collective-permute-start(f32[18,8,128]{2,1,0:T(8,128)S(1)} %get-tuple-element.59), channel_id=1, source_target_pairs={{0,4},{4,0},{8,12},{12,8},{1,5},{5,1},{9,13},{13,9},{2,6},{6,2},{1... | collective-permute-start | bytes 221192 | tf_op jit(solution)/shard_map/ppermute | solution.py:500
  13.0 4.3 %inner.1 = (f32[8,272,128]{2,1,0:T(8,128)S(1)}, f32[8,272,128]{2,1,0:T(8,128)S(1)}, f32[8,272,128]{2,1,0:T(8,128)S(1)}, f32[8,272,128]{2,1,0:T(8,128)S(1)}, f32[...) custom-call(f32[8,128]{1,0:T(8,128)S(1)} %get-tuple-element.55.weights, ...), custom_call_target="tpu_custom_call" | custom-call | flops 1000000 | bytes 1000000 | tf_op jit(solution)/shard_map/inner/pallas_call | solution.py:33
  17.3 0.0 collective-permute-done.2.got_second
  17.3 0.0 collective-permute-done.3.got_first
  17.3 0.8 frame.1
  18.2 23.5 %all_to_all.33 = f32[64,1,128]{2,1,0:T(1,128)S(1)} all-to-all(f32[64,1,128]{2,1,0:T(1,128)S(1)} %bitcast.16), channel_id=1, replica_groups=mesh['radius'=16,'polar'=4,'group'=4] {'radius','polar'}, dimensions={0} | all-to-all | bytes 65536 | tf_op jit(solution)/shard_map/all_to_all | solution.py:571
  41.6 0.4 update.2
  42.1 1.6 %collective-permute-start.6 = (f32[2,136,128]{2,1,0:T(8,128)S(1)}, f32[2,136,128]{2,1,0:T(8,128)S(1)}, u32[]{:S(2)}, u32[]{:S(2)}) collective-permute-start(f32[2,136,128]{2,1,0:T(8,128)S(1)} %get-tuple-element.86.rest_0_), channel_id=1, source_target_pairs={{0,3},{1,2},{2,1},{3,0},{4,7},{5,6},{6,5},{7,4},{8,11},{9,10},{10,... | collective-permute-start | bytes 417800 | tf_op jit(solution)/shard_map/ppermute | solution.py:496
  43.7 0.9 collective-permute-start.5
  44.7 1.6 %collective-permute-start.4 = (f32[2,136,128]{2,1,0:T(8,128)S(1)}, f32[2,136,128]{2,1,0:T(8,128)S(1)}, u32[]{:S(2)}, u32[]{:S(2)}) collective-permute-start(f32[2,136,128]{2,1,0:T(8,128)S(1)} %get-tuple-element.86.rest_0_), channel_id=1, source_target_pairs={{0,1},{1,0},{2,3},{3,2},{4,5},{5,4},{6,7},{7,6},{8,9},{9,8},{10,11... | collective-permute-start | bytes 417800 | tf_op jit(solution)/shard_map/ppermute | solution.py:496
  46.2 1.7 %heating.1 = (f32[48,256]{1,0:T(8,128)}, f32[272,128]{1,0:T(8,128)S(1)}) custom-call(f32[48]{0:T(128)S(1)} %copy-done.4, f32[64,128]{1,0:T(8,128)S(1)} %bitcast.13, f32[272,128]{1,0:T(8,128)S(1)} %get-tuple-element.82.dens_ref.cap_in, f32[272,128]{1,0:T(8,128)S(1)} %get-tuple-element.83.mat_ref, f32[8,128]{1,0:T(8,128)S(1)} %get-tuple-element.84.flux_ref), custom_call_target="tpu_custom_call" | custom-call | flops 1000000 | bytes 1000000 | tf_op jit(solution)/shard_map/heating/pallas_call | solution.py:33
  48.0 0.9 collective-permute-done.6.rest_3_
  48.9 2.8 %collective-permute-done.5.rest_2_ = f32[2,136,128]{2,1,0:T(8,128)S(1)} collective-permute-done((f32[2,136,128]{2,1,0:T(8,128)S(1)}, f32[2,136,128]{2,1,0:T(8,128)S(1)}, u32[]{:S(2)}, u32[]{:S(2)}) %collective-permute-start.5) | collective-permute-done | bytes 139296 | tf_op jit(solution)/shard_map/ppermute | solution.py:496
  51.6 0.5 collective-permute-done.4.rest_1_
  52.1 2.4 %next.2 = (f32[8,272,128]{2,1,0:T(8,128)S(1)}, f32[8,272,128]{2,1,0:T(8,128)S(1)}, f32[64,128]{1,0:T(8,128)S(1)}, f32[8,272,128]{2,1,0:T(8,128)S(1)}, f32[272,128]{1,0:T(8,128)S(1)}, /*index=5*/f32[272,128]{1,0:T(8,128)S(1)}) custom-call(f32[8,128]{1,0:T(8,128)S(1)} %get-tuple-element.55.weights, f32[8,128]{1,0:T(8,128)S(1)} %get-tuple-element.76.c1_ref, ...), custom_call_target="tpu_custom_call" | custom-call | flops 1000000 | bytes 1000000 | tf_op jit(solution)/shard_map/next/pallas_call | solution.py:33
  54.5 13.5 %all_to_all.34 = f32[64,1,128]{2,1,0:T(1,128)S(1)} all-to-all(f32[64,1,128]{2,1,0:T(1,128)S(1)} %bitcast.17), channel_id=1, replica_groups=mesh['radius'=16,'polar'=4,'group'=4] {'radius','polar'}, dimensions={0} | all-to-all | bytes 65536 | tf_op jit(solution)/shard_map/all_to_all | solution.py:571
  68.0 0.4 update.3
  68.4 1.6 %collective-permute-start.9 = (f32[1,136,128]{2,1,0:T(8,128)S(1)}, f32[1,136,128]{2,1,0:T(8,128)S(1)}, u32[]{:S(2)}, u32[]{:S(2)}) collective-permute-start(f32[1,136,128]{2,1,0:T(8,128)S(1)} %get-tuple-element.96.rest_0_), channel_id=1, source_target_pairs={{0,3},{1,2},{2,1},{3,0},{4,7},{5,6},{6,5},{7,4},{8,11},{9,10},{10,... | collective-permute-start | bytes 208904 | tf_op jit(solution)/shard_map/ppermute | solution.py:496
  70.0 1.9 %collective-permute-start.8 = (f32[1,136,128]{2,1,0:T(8,128)S(1)}, f32[1,136,128]{2,1,0:T(8,128)S(1)}, u32[]{:S(2)}, u32[]{:S(2)}) collective-permute-start(f32[1,136,128]{2,1,0:T(8,128)S(1)} %get-tuple-element.96.rest_0_), channel_id=1, source_target_pairs={{0,2},{1,3},{2,0},{3,1},{4,6},{5,7},{6,4},{7,5},{8,10},{9,11},{10,... | collective-permute-start | bytes 208904 | tf_op jit(solution)/shard_map/ppermute | solution.py:496
  71.9 0.7 collective-permute-start.7
  72.5 0.2 collective-permute-done.9.rest_3_
  72.8 3.1 %collective-permute-done.8.rest_2_ = f32[1,136,128]{2,1,0:T(8,128)S(1)} collective-permute-done((f32[1,136,128]{2,1,0:T(8,128)S(1)}, f32[1,136,128]{2,1,0:T(8,128)S(1)}, u32[]{:S(2)}, u32[]{:S(2)}) %collective-permute-start.8) | collective-permute-done | bytes 69664 | tf_op jit(solution)/shard_map/ppermute | solution.py:496
  75.9 0.3 collective-permute-done.7.rest_1_
  76.2 2.6 %next.3 = (f32[8,272,128]{2,1,0:T(8,128)S(1)}, f32[8,272,128]{2,1,0:T(8,128)S(1)}, f32[64,128]{1,0:T(8,128)S(1)}) custom-call(f32[8,128]{1,0:T(8,128)S(1)} %get-tuple-element.55.weights, f32[8,128]{1,0:T(8,128)S(1)} %get-tuple-element.91.c1_ref, f32[8,128]{1,0:T(8,128)S(1)} %get-tuple-element.92.c2_ref, f32[8,272,128]{2,1,0:T(8,128)S(1)} %get-tuple-element.72.a_ref, ...), custom_call_target="tpu_custom_call" | custom-call | flops 1000000 | bytes 1000000 | tf_op jit(solution)/shard_map/next/pallas_call | solution.py:33
  78.7 13.7 %all_to_all.35 = f32[64,1,128]{2,1,0:T(1,128)S(1)} all-to-all(f32[64,1,128]{2,1,0:T(1,128)S(1)} %bitcast.18), channel_id=1, replica_groups=mesh['radius'=16,'polar'=4,'group'=4] {'radius','polar'}, dimensions={0} | all-to-all | bytes 65536 | tf_op jit(solution)/shard_map/all_to_all | solution.py:571
  92.4 0.5 last_update.1
  92.9 1.5 %collective-permute-start.12 = (f32[48,256]{1,0:T(8,128)S(1)}, f32[48,256]{1,0:T(8,128)S(1)}, u32[]{:S(2)}, u32[]{:S(2)}) collective-permute-start(f32[48,256]{1,0:T(8,128)S(1)} %get-tuple-element.105.rest_0_), channel_id=1, source_target_pairs={{0,3},{1,2},{2,1},{3,0},{4,7},{5,6},{6,5},{7,4},{8,11},{9,10},{10,... | collective-permute-start | bytes 147464 | tf_op jit(solution)/shard_map/ppermute | solution.py:496
  94.5 2.1 %collective-permute-start.11 = (f32[48,256]{1,0:T(8,128)S(1)}, f32[48,256]{1,0:T(8,128)S(1)}, u32[]{:S(2)}, u32[]{:S(2)}) collective-permute-start(f32[48,256]{1,0:T(8,128)S(1)} %get-tuple-element.105.rest_0_), channel_id=1, source_target_pairs={{0,2},{1,3},{2,0},{3,1},{4,6},{5,7},{6,4},{7,5},{8,10},{9,11},{10,... | collective-permute-start | bytes 147464 | tf_op jit(solution)/shard_map/ppermute | solution.py:496
  96.6 0.5 collective-permute-start.10
  97.1 1.3 %energy.1 = (f32[16,48,256]{2,1,0:T(8,128)}, f32[48,256]{1,0:T(8,128)S(1)}, f32[48,256]{1,0:T(8,128)S(1)}) custom-call(f32[8,272,128]{2,1,0:T(8,128)S(1)} %get-tuple-element.101.e_ref, f32[272,128]{1,0:T(8,128)S(1)} %get-tuple-element.85.fixed, f32[272,128]{1,0:T(8,128)S(1)} %get-tuple-element.94.cap_in.capacity), custom_call_target="tpu_custom_call" | custom-call | flops 1000000 | bytes 1000000 | tf_op jit(solution)/shard_map/energy/pallas_call | solution.py:33
  98.4 0.0 collective-permute-done.12.rest_3_
  98.4 1.7 %collective-permute-done.11.rest_2_ = f32[48,256]{1,0:T(8,128)S(1)} collective-permute-done((f32[48,256]{1,0:T(8,128)S(1)}, f32[48,256]{1,0:T(8,128)S(1)}, u32[]{:S(2)}, u32[]{:S(2)}) %collective-permute-start.11) | collective-permute-done | bytes 49184 | tf_op jit(solution)/shard_map/ppermute | solution.py:496
  100.0 0.6 collective-permute-done.10.rest_1_
  100.7 0.6 material.5
  (3 shorter events, 0.0 us)
Async XLA Ops:
  0.6 6.7 %copy-start.3 = (f32[48,256]{1,0:T(8,128)S(1)}, f32[48,256]{1,0:T(8,128)}, u32[]{:S(2)}) copy-start(f32[48,256]{1,0:T(8,128)} %material.4) | copy-start | bytes 147460
  0.6 6.7 %copy-start = (f32[16,48,256]{2,1,0:T(8,128)S(1)}, f32[16,48,256]{2,1,0:T(8,128)}, u32[]{:S(2)}) copy-start(f32[16,48,256]{2,1,0:T(8,128)} %old.3) | copy-start | bytes 2359300
  0.7 6.6 %copy-start.1 = (bf16[16,48,256]{2,1,0:T(8,128)(2,1)S(1)}, bf16[16,48,256]{2,1,0:T(8,128)(2,1)}, u32[]{:S(2)}) copy-start(bf16[16,48,256]{2,1,0:T(8,128)(2,1)} %opacity.3) | copy-start | bytes 1179652
  0.7 6.6 %copy-start.2 = (f32[48,256]{1,0:T(8,128)S(1)}, f32[48,256]{1,0:T(8,128)}, u32[]{:S(2)}) copy-start(f32[48,256]{1,0:T(8,128)} %density.3) | copy-start | bytes 147460
  2.1 4.0 %collective-permute-start = (f32[35,8,256]{2,1,0:T(8,128)S(1)}, f32[35,8,256]{2,1,0:T(8,128)S(1)}, u32[]{:S(2)}, u32[]{:S(2)}) collective-permute-start(f32[35,8,256]{2,1,0:T(8,128)S(1)} %get-tuple-element.56), channel_id=1, source_target_pairs={{16,32},{48,64},{80,96},{112,128},{144,160},{176,192},{208,224},{3... | collective-permute-start | bytes 860168 | tf_op jit(solution)/shard_map/ppermute | solution.py:505
  2.7 4.5 %collective-permute-start.1 = (f32[35,8,256]{2,1,0:T(8,128)S(1)}, f32[35,8,256]{2,1,0:T(8,128)S(1)}, u32[]{:S(2)}, u32[]{:S(2)}) collective-permute-start(f32[35,8,256]{2,1,0:T(8,128)S(1)} %get-tuple-element.57), channel_id=1, source_target_pairs={{0,16},{16,0},{32,48},{48,32},{64,80},{80,64},{96,112},{112,96},{1... | collective-permute-start | bytes 860168 | tf_op jit(solution)/shard_map/ppermute | solution.py:500
  8.0 9.3 %collective-permute-start.2 = (f32[18,8,128]{2,1,0:T(8,128)S(1)}, f32[18,8,128]{2,1,0:T(8,128)S(1)}, u32[]{:S(2)}, u32[]{:S(2)}) collective-permute-start(f32[18,8,128]{2,1,0:T(8,128)S(1)} %get-tuple-element.58), channel_id=1, source_target_pairs={{4,8},{8,4},{5,9},{9,5},{6,10},{10,6},{7,11},{11,7},{20,24},{24,20... | collective-permute-start | bytes 221192 | tf_op jit(solution)/shard_map/ppermute | solution.py:505
  8.7 8.6 %collective-permute-start.3 = (f32[18,8,128]{2,1,0:T(8,128)S(1)}, f32[18,8,128]{2,1,0:T(8,128)S(1)}, u32[]{:S(2)}, u32[]{:S(2)}) collective-permute-start(f32[18,8,128]{2,1,0:T(8,128)S(1)} %get-tuple-element.59), channel_id=1, source_target_pairs={{0,4},{4,0},{8,12},{12,8},{1,5},{5,1},{9,13},{13,9},{2,6},{6,2},{1... | collective-permute-start | bytes 221192 | tf_op jit(solution)/shard_map/ppermute | solution.py:500
  41.6 4.6 %copy-start.4 = (f32[48]{0:T(128)S(1)}, f32[48]{0:T(128)}, u32[]{:S(2)}) copy-start(f32[48]{0:T(128)} %flux.1) | copy-start | bytes 580
  42.1 6.8 %collective-permute-start.6 = (f32[2,136,128]{2,1,0:T(8,128)S(1)}, f32[2,136,128]{2,1,0:T(8,128)S(1)}, u32[]{:S(2)}, u32[]{:S(2)}) collective-permute-start(f32[2,136,128]{2,1,0:T(8,128)S(1)} %get-tuple-element.86.rest_0_), channel_id=1, source_target_pairs={{0,3},{1,2},{2,1},{3,0},{4,7},{5,6},{6,5},{7,4},{8,11},{9,10},{10,... | collective-permute-start | bytes 417800 | tf_op jit(solution)/shard_map/ppermute | solution.py:496
  43.7 7.9 %collective-permute-start.5 = (f32[2,136,128]{2,1,0:T(8,128)S(1)}, f32[2,136,128]{2,1,0:T(8,128)S(1)}, u32[]{:S(2)}, u32[]{:S(2)}) collective-permute-start(f32[2,136,128]{2,1,0:T(8,128)S(1)} %get-tuple-element.86.rest_0_), channel_id=1, source_target_pairs={{0,2},{1,3},{2,0},{3,1},{4,6},{5,7},{6,4},{7,5},{8,10},{9,11},{10,... | collective-permute-start | bytes 417800 | tf_op jit(solution)/shard_map/ppermute | solution.py:496
  44.7 7.4 %collective-permute-start.4 = (f32[2,136,128]{2,1,0:T(8,128)S(1)}, f32[2,136,128]{2,1,0:T(8,128)S(1)}, u32[]{:S(2)}, u32[]{:S(2)}) collective-permute-start(f32[2,136,128]{2,1,0:T(8,128)S(1)} %get-tuple-element.86.rest_0_), channel_id=1, source_target_pairs={{0,1},{1,0},{2,3},{3,2},{4,5},{5,4},{6,7},{7,6},{8,9},{9,8},{10,11... | collective-permute-start | bytes 417800 | tf_op jit(solution)/shard_map/ppermute | solution.py:496
  68.4 4.4 %collective-permute-start.9 = (f32[1,136,128]{2,1,0:T(8,128)S(1)}, f32[1,136,128]{2,1,0:T(8,128)S(1)}, u32[]{:S(2)}, u32[]{:S(2)}) collective-permute-start(f32[1,136,128]{2,1,0:T(8,128)S(1)} %get-tuple-element.96.rest_0_), channel_id=1, source_target_pairs={{0,3},{1,2},{2,1},{3,0},{4,7},{5,6},{6,5},{7,4},{8,11},{9,10},{10,... | collective-permute-start | bytes 208904 | tf_op jit(solution)/shard_map/ppermute | solution.py:496
  70.0 5.9 %collective-permute-start.8 = (f32[1,136,128]{2,1,0:T(8,128)S(1)}, f32[1,136,128]{2,1,0:T(8,128)S(1)}, u32[]{:S(2)}, u32[]{:S(2)}) collective-permute-start(f32[1,136,128]{2,1,0:T(8,128)S(1)} %get-tuple-element.96.rest_0_), channel_id=1, source_target_pairs={{0,2},{1,3},{2,0},{3,1},{4,6},{5,7},{6,4},{7,5},{8,10},{9,11},{10,... | collective-permute-start | bytes 208904 | tf_op jit(solution)/shard_map/ppermute | solution.py:496
  71.9 4.3 %collective-permute-start.7 = (f32[1,136,128]{2,1,0:T(8,128)S(1)}, f32[1,136,128]{2,1,0:T(8,128)S(1)}, u32[]{:S(2)}, u32[]{:S(2)}) collective-permute-start(f32[1,136,128]{2,1,0:T(8,128)S(1)} %get-tuple-element.96.rest_0_), channel_id=1, source_target_pairs={{0,1},{1,0},{2,3},{3,2},{4,5},{5,4},{6,7},{7,6},{8,9},{9,8},{10,11... | collective-permute-start | bytes 208904 | tf_op jit(solution)/shard_map/ppermute | solution.py:496
  92.9 5.5 %collective-permute-start.12 = (f32[48,256]{1,0:T(8,128)S(1)}, f32[48,256]{1,0:T(8,128)S(1)}, u32[]{:S(2)}, u32[]{:S(2)}) collective-permute-start(f32[48,256]{1,0:T(8,128)S(1)} %get-tuple-element.105.rest_0_), channel_id=1, source_target_pairs={{0,3},{1,2},{2,1},{3,0},{4,7},{5,6},{6,5},{7,4},{8,11},{9,10},{10,... | collective-permute-start | bytes 147464 | tf_op jit(solution)/shard_map/ppermute | solution.py:496
  94.5 5.6 %collective-permute-start.11 = (f32[48,256]{1,0:T(8,128)S(1)}, f32[48,256]{1,0:T(8,128)S(1)}, u32[]{:S(2)}, u32[]{:S(2)}) collective-permute-start(f32[48,256]{1,0:T(8,128)S(1)} %get-tuple-element.105.rest_0_), channel_id=1, source_target_pairs={{0,2},{1,3},{2,0},{3,1},{4,6},{5,7},{6,4},{7,5},{8,10},{9,11},{10,... | collective-permute-start | bytes 147464 | tf_op jit(solution)/shard_map/ppermute | solution.py:496
  96.6 4.1 %collective-permute-start.10 = (f32[48,256]{1,0:T(8,128)S(1)}, f32[48,256]{1,0:T(8,128)S(1)}, u32[]{:S(2)}, u32[]{:S(2)}) collective-permute-start(f32[48,256]{1,0:T(8,128)S(1)} %get-tuple-element.105.rest_0_), channel_id=1, source_target_pairs={{0,1},{1,0},{2,3},{3,2},{4,5},{5,4},{6,7},{7,6},{8,9},{9,8},{10,11... | collective-permute-start | bytes 147464 | tf_op jit(solution)/shard_map/ppermute | solution.py:496
